TPU v7x, 256 devices: a whole 4x4x8 slice. The times are simulated.
256 devices in a mesh: blk: 32 (over x, y, z_lo), seg: 8 (over z_hi, core).
Axes of the slice: x: 4, y: 4, z: 8 (z_hi: 4, z_lo: 2; z = z_hi * 2 + z_lo), core: 2. Of those that a mesh axis runs over, the one named last changes fastest.
Arguments:
- spectra: bfloat16 [112, 2048, 2, 512], P('seg', 'blk'), as said below
- valid_flags: int32 [112, 2048], P('seg', 'blk'), may hold values 0 or 1
Outputs:
- correlations: bfloat16 [2, 2048, 64, 1024], P(None, ('blk', 'seg'))
Inputs may be any that keep to these rules, and one draw needn't show every extreme that they name: `spectra`: rough spectral values; their scale varies from bin to bin, channel to channel and window to window.
All inputs are finite; a program needn't handle non-finite values. No bound on the sum of `valid_flags` on one device may be relied on, other than what follows from the above.
Results may differ from a plain program's by a relative error of at most 0.015.
Values may be sent and summed in bfloat16 or wider, within the bound.
No kernel may reach another device: no remote copies, remote signals or barrier semaphores. Data moves between devices by JAX's collectives and lax.ppermute only.
A program may use at most 128 MiB of HBM per device.

v0:
```python
import functools
import math

import jax
import jax.numpy as jnp
from jax import lax
from jax.experimental import pallas as pl
from jax.experimental.pallas import tpu as pltpu
from jax.sharding import Mesh, PartitionSpec as P


LAG_COUNT = 1024
WIN_SAMPLES = 15000
BAND_START = 30
SMOOTH_HALF = 32
BINS = 512
WIN = 14
CH = 64
CHUNKS = 2
FC = 32 // CHUNKS
CBINS = BINS // CHUNKS
F32 = jnp.float32
BF16 = jnp.bfloat16

VM = pl.BlockSpec(memory_space=pltpu.VMEM)
SM = pl.BlockSpec(memory_space=pltpu.SMEM)
ANY = pl.BlockSpec(memory_space=pl.ANY)


def params():
    return pltpu.CompilerParams(vmem_limit_bytes=48 << 20)


def whiten_kernel(pos_ref, spec_ref, flags_ref, *refs):
    outs = refs[: 8 * CHUNKS]
    band, eye, invc, white = refs[8 * CHUNKS :]
    w = pl.program_id(0)
    z, c = pos_ref[0], pos_ref[1]

    @pl.when(w == 0)
    def _():
        rows = lax.broadcasted_iota(jnp.int32, (BINS, BINS), 0)
        cols = lax.broadcasted_iota(jnp.int32, (BINS, BINS), 1)
        band[...] = jnp.where(jnp.abs(rows - cols) <= SMOOTH_HALF, 1.0, 0.0).astype(BF16)
        r2 = lax.broadcasted_iota(jnp.int32, (256, 256), 0)
        c2 = lax.broadcasted_iota(jnp.int32, (256, 256), 1)
        eye[...] = jnp.where(r2 == c2, 1.0, 0.0).astype(BF16)
        f = lax.broadcasted_iota(jnp.int32, (BINS, 128), 0)
        count = jnp.minimum(f + SMOOTH_HALF, BINS - 1) - jnp.maximum(f - SMOOTH_HALF, 0) + 1
        invc[...] = 1.0 / count.astype(F32)

    re16, im16 = spec_ref[0, 0], spec_ref[1, 0]
    re, im = re16.astype(F32), im16.astype(F32)
    amp = jnp.sqrt(re * re + im * im).astype(BF16)
    amp2 = jnp.concatenate([amp, amp], axis=0)
    both = jnp.concatenate([re16, im16], axis=0)
    nt = (((1,), (1,)), ((), ()))
    summed = lax.dot_general(band[...], amp2, nt, preferred_element_type=F32)
    scale = flags_ref[0] / (summed * invc[...] + 1e-05)
    for h in range(2):
        half = lax.dot_general(
            eye[...], both[:, h * 256 : (h + 1) * 256], nt, preferred_element_type=F32
        )
        white[h * 256 : (h + 1) * 256] = (half * scale[h * 256 : (h + 1) * 256]).astype(BF16)
    for k in range(CHUNKS):
        for r in range(8):
            base = k * CBINS + ((z + r) & 7) * (2 * FC)
            for crel in range(2):
                start = pl.multiple_of(base + (c ^ crel) * FC, FC)
                outs[k * 8 + r][crel, w] = white[pl.ds(start, FC), :]


def whiten(spec, flags2, pos):
    shape = jax.ShapeDtypeStruct((2, WIN, FC, 128), BF16)
    full = pl.BlockSpec((2, WIN, FC, 128), lambda w, *_: (0, 0, 0, 0))
    return pl.pallas_call(
        whiten_kernel,
        out_shape=[shape] * (8 * CHUNKS),
        grid_spec=pltpu.PrefetchScalarGridSpec(
            num_scalar_prefetch=1,
            grid=(WIN,),
            in_specs=[
                pl.BlockSpec((2, 1, CH, BINS), lambda w, *_: (0, w, 0, 0)),
                pl.BlockSpec((1, 1, 128), lambda w, *_: (w, 0, 0)),
            ],
            out_specs=[full] * (8 * CHUNKS),
            scratch_shapes=[
                pltpu.VMEM((BINS, BINS), BF16),
                pltpu.VMEM((256, 256), BF16),
                pltpu.VMEM((BINS, 128), F32),
                pltpu.VMEM((BINS, 128), BF16),
            ],
        ),
        compiler_params=params(),
        cost_estimate=pl.CostEstimate(
            flops=3 * 512 * 512 * 128 * WIN, bytes_accessed=4 << 20, transcendentals=0
        ),
        name="whiten",
    )(pos, spec, flags2)


def merge_kernel(pos_ref, *refs):
    ins, (same, other, core) = refs[:8], refs[-3:]
    z = pos_ref[0]
    core[0] = pos_ref[1]
    for r in range(8):
        src = (z - r) & 7
        same[src & 1, src >> 1] = ins[r][0]
        other[src & 1, src >> 1] = ins[r][1]


def merge(pieces, pos, *after):
    shape = jax.ShapeDtypeStruct((2, 4, WIN, FC, 128), BF16)
    return pl.pallas_call(
        merge_kernel,
        out_shape=[shape] * 2 + [jax.ShapeDtypeStruct((1,), jnp.int32)],
        in_specs=[SM] + [VM] * 8 + [ANY] * len(after),
        out_specs=[VM] * 2 + [SM],
        compiler_params=params(),
        cost_estimate=pl.CostEstimate(
            flops=0, bytes_accessed=4 * 8 * WIN * FC * 256, transcendentals=0
        ),
        name="merge",
    )(pos, *pieces, *after)


def cross_kernel(pos_ref, own0, own1, prev0, prev1, *refs):
    outs, (wide, res) = refs[-10:-2], refs[-2:]
    z, c = pos_ref[0], pos_ref[1]
    rows = 4 * WIN * FC
    for n, (first, second) in enumerate(((own0, own1), (prev0, prev1))):
        for b in range(2):
            base = (n * 2 + b) * 2 * rows
            wide[base : base + rows] = first[b].reshape(rows, 128).astype(F32)
            wide[base + rows : base + 2 * rows] = second[b].reshape(rows, 128).astype(F32)
    sign = jnp.where(lax.broadcasted_iota(jnp.int32, (CH, 128), 1) < CH, 1.0, -1.0).astype(F32)
    tn = (((0,), (0,)), ((), ()))

    def one_bin(f, carry):
        x = [
            wide[pl.ds(n * 2 * rows + f, 8 * WIN, stride=FC), :].astype(BF16) for n in range(4)
        ]
        own_a, own_b, prev_a, prev_b = x
        for b, (left, rights) in enumerate(
            ((own_a, (prev_b, prev_a)), (own_b, (own_a, prev_b)))
        ):
            g = lax.dot_general(
                left, jnp.concatenate(rights, axis=1), tn, preferred_element_type=F32
            )
            for rnd in range(2):
                top = g[:CH, rnd * 128 : rnd * 128 + 128]
                bottom = pltpu.roll(g[CH:, rnd * 128 : rnd * 128 + 128], CH, 1)
                start = pl.multiple_of(((rnd * 2 + b) * FC + f) * CH, CH)
                res[pl.ds(start, CH), :] = bottom + sign * top
        return carry

    lax.fori_loop(0, FC, one_bin, 0, unroll=2)
    for r in range(8):
        dst = (z + r) & 7
        for crel in range(2):
            row = ((dst >> 1) * 2 + (c ^ crel)) * 8
            for rnd in range(2):
                base = (rnd * 2 + (dst & 1)) * FC * CH + row
                for i in range(8):
                    outs[r][crel, rnd, i] = res[pl.ds(base + i, FC, stride=CH), :].astype(BF16)


def cross(own0, own1, prev0, prev1, pos, *after):
    shape = jax.ShapeDtypeStruct((2, 2, 8, FC, 128), BF16)
    return pl.pallas_call(
        cross_kernel,
        out_shape=[shape] * 8,
        in_specs=[SM] + [VM] * 4 + [ANY] * len(after),
        out_specs=[VM] * 8,
        scratch_shapes=[
            pltpu.VMEM((32 * WIN * FC, 128), F32),
            pltpu.VMEM((4 * FC * CH, 128), F32),
        ],
        compiler_params=params(),
        cost_estimate=pl.CostEstimate(
            flops=4 * FC * 128 * 256 * 256, bytes_accessed=3 << 20, transcendentals=0
        ),
        name="cross",
    )(pos, own0, own1, prev0, prev1, *after)


def turn_kernel(pos_ref, *refs):
    ins, (same, other, buf) = refs[:8], refs[-3:]
    z = pos_ref[0]
    for crel, out in enumerate((same, other)):
        for rnd in range(2):
            for i in range(8):
                for r in range(8):
                    start = pl.multiple_of(((z - r) & 7) * FC, FC)
                    buf[pl.ds(start, FC), :] = ins[r][crel, rnd, i].astype(F32)
                out[rnd, i] = buf[...].T.astype(BF16)


def turn(pieces, pos, *after):
    shape = jax.ShapeDtypeStruct((2, 8, 128, 8 * FC), BF16)
    return pl.pallas_call(
        turn_kernel,
        out_shape=[shape] * 2,
        in_specs=[SM] + [VM] * 8 + [ANY] * len(after),
        out_specs=[VM] * 2,
        scratch_shapes=[pltpu.VMEM((8 * FC, 128), F32)],
        compiler_params=params(),
        cost_estimate=pl.CostEstimate(flops=0, bytes_accessed=4 << 20, transcendentals=0),
        name="turn",
    )(pos, *pieces, *after)


def invert_kernel(scaling, *refs):
    parts, (table, out) = refs[: 2 * CHUNKS], refs[2 * CHUNKS :]
    rows = []
    for i in range(4):
        cols = [p[0, i, k * CH : (k + 1) * CH] for k in range(2) for p in parts]
        rows.append(jnp.concatenate(cols, axis=1))
    left = jnp.concatenate(rows, axis=0)
    result = jnp.dot(left, table[...], preferred_element_type=F32) * scaling
    out[0] = result.reshape(4, CH, LAG_COUNT).astype(BF16)


def invert(parts, table, scaling):
    part = pl.BlockSpec((1, 4, 128, 8 * FC), lambda r, i: (r, i, 0, 0))
    return pl.pallas_call(
        functools.partial(invert_kernel, scaling),
        out_shape=jax.ShapeDtypeStruct((2, 8, CH, LAG_COUNT), BF16),
        grid=(2, 2),
        in_specs=[part] * (2 * CHUNKS) + [pl.BlockSpec((2 * BINS, LAG_COUNT), lambda r, i: (0, 0))],
        out_specs=pl.BlockSpec((1, 4, CH, LAG_COUNT), lambda r, i: (r, i, 0, 0)),
        compiler_params=params(),
        cost_estimate=pl.CostEstimate(
            flops=2 * 1024 * 1024 * 1024, bytes_accessed=6 << 20, transcendentals=0
        ),
        name="invert",
    )(*parts, table)


def lag_table(core):
    n = lax.broadcasted_iota(jnp.int32, (BINS, LAG_COUNT), 0)
    fine = n % FC
    z = (n // FC) % 8
    part = (n // (8 * FC)) % 2
    chunk = n // (16 * FC)
    freq_ids = chunk * CBINS + z * (2 * FC) + (part ^ core) * FC + fine + BAND_START
    delay_ids = lax.broadcasted_iota(jnp.int32, (BINS, LAG_COUNT), 1) - LAG_COUNT // 2
    angles = jnp.mod(freq_ids * delay_ids, WIN_SAMPLES).astype(F32) * (2.0 * math.pi / WIN_SAMPLES)
    return jnp.concatenate([jnp.cos(angles), -jnp.sin(angles)], axis=0).astype(BF16)


def place(z):
    return (z % 2) * 4 + z // 2


def ring(value, shift):
    return lax.ppermute(
        value, ("zl", "zh"), [(place(z), place((z + shift) % 8)) for z in range(8)]
    )


def other_core(value):
    return lax.ppermute(value, "c", [(0, 1), (1, 0)])


ORDER = (4, 3, 5, 2, 6, 1, 7)


def round_ring(pieces):
    got = {0: pieces[0]}
    for r in ORDER:
        got[r] = ring(pieces[r], r)
    return [got[r] for r in range(8)]


def shards(spectra, valid_flags):
    z = 2 * lax.axis_index("zh") + lax.axis_index("zl")
    pos = jnp.stack([z, lax.axis_index("c")]).astype(jnp.int32)
    windows = spectra.shape[0] * lax.axis_size(("zh", "c"))
    scaling = 1.0 / math.sqrt(windows * BINS)
    flags = valid_flags.astype(F32)
    flags2 = jnp.concatenate([flags, flags], axis=1)[:, None, :]
    white = whiten(jnp.transpose(spectra, (2, 0, 1, 3)), flags2, pos)
    up = [(i, (i + 1) % 16) for i in range(16)]
    swap = [(2 * i + k, 2 * j + 1 - k) for i, j in up for k in range(2)]
    parts = []
    table = None
    crossed, turned = (), ()
    for k in range(CHUNKS):
        got = round_ring(white[k * 8 : k * 8 + 8])
        same, other, core = merge(got, pos, *(() if table is None else (table,)))
        prev0 = lax.ppermute(same, ("x", "y"), up)
        prev1 = lax.ppermute(other, ("x", "y", "c"), swap)
        own1 = other_core(other)
        if k == 0:
            table = lag_table(core[0])
        out = cross(same, own1, prev0, prev1, pos, *crossed)
        crossed = (out[0],)
        same, other = turn(round_ring(out), pos, *turned)
        turned = (same,)
        parts += [same, other_core(other)]
    return invert(parts, table, scaling)


def solution(mesh):
    grid = mesh.devices.reshape(4, 4, 2, 4, 2)
    fine = Mesh(grid, ("x", "y", "zl", "zh", "c"))
    blk, seg = ("x", "y", "zl"), ("zh", "c")
    in_specs = (P(seg, blk, None, None), P(seg, blk))
    out_specs = P(None, blk + seg, None, None)


    return jax.shard_map(shards, mesh=fine, in_specs=in_specs, out_specs=out_specs, check_vma=False)
```

profile of v0, /device:TPU:1, one launch (start us, length us, event | category | flops | bytes accessed | tf_op | source)
XLA Modules:
  0.0 156.6 jit_solution(5821429357856777320)
XLA Ops:
  2.8 7.0 %whiten.1 = (bf16[2,14,16,128]{3,2,1,0:T(8,128)(2,1)S(1)}, bf16[2,14,16,128]{3,2,1,0:T(8,128)(2,1)S(1)}, bf16[2,14,16,128]{3,2,1,0:T(8,128)(2,1)S(1)}, bf16[2,14...) custom-call(s32[2]{0:T(128)S(1)} %pad_add_fusion.pos_ref, ...), custom_call_target="tpu_custom_call" | custom-call | flops 1409286144 | bytes 4194304 | tf_op jit(solution)/shard_map/whiten/pallas_call | solution.py:76
  12.3 3.0 %collective-permute-start.1 = (bf16[2,14,16,128]{3,2,1,0:T(8,128)(2,1)S(1)}, bf16[2,14,16,128]{3,2,1,0:T(8,128)(2,1)S(1)}, u32[]{:S(2)}, u32[]{:S(2)}) collective-permute-start(bf16[2,14,16,128]{3,2,1,0:T(8,128)(2,1)S(1)} %get-tuple-element.48), channel_id=1, source_target_pairs={{0,2},{8,10},{2,4},{10,12},{4,6},{12,14},{6,0},{14,8},{1,3},{9,11}... | collective-permute-start | bytes 344072 | tf_op jit(solution)/shard_map/ppermute | solution.py:257
  15.3 3.8 %collective-permute-start.2 = (bf16[2,14,16,128]{3,2,1,0:T(8,128)(2,1)S(1)}, bf16[2,14,16,128]{3,2,1,0:T(8,128)(2,1)S(1)}, u32[]{:S(2)}, u32[]{:S(2)}) collective-permute-start(bf16[2,14,16,128]{3,2,1,0:T(8,128)(2,1)S(1)} %get-tuple-element.49), channel_id=1, source_target_pairs={{0,10},{8,4},{2,12},{10,6},{4,14},{12,0},{6,8},{14,2},{1,11},{9,5}... | collective-permute-start | bytes 344072 | tf_op jit(solution)/shard_map/ppermute | solution.py:257
  19.5 4.5 %collective-permute-start.4 = (bf16[2,14,16,128]{3,2,1,0:T(8,128)(2,1)S(1)}, bf16[2,14,16,128]{3,2,1,0:T(8,128)(2,1)S(1)}, u32[]{:S(2)}, u32[]{:S(2)}) collective-permute-start(bf16[2,14,16,128]{3,2,1,0:T(8,128)(2,1)S(1)} %get-tuple-element.51), channel_id=1, source_target_pairs={{0,12},{8,6},{2,14},{10,0},{4,8},{12,2},{6,10},{14,4},{1,13},{9,7}... | collective-permute-start | bytes 344072 | tf_op jit(solution)/shard_map/ppermute | solution.py:257
  27.2 5.2 %collective-permute-done.2.refs_3_ = bf16[2,14,16,128]{3,2,1,0:T(8,128)(2,1)S(1)} collective-permute-done((bf16[2,14,16,128]{3,2,1,0:T(8,128)(2,1)S(1)}, bf16[2,14,16,128]{3,2,1,0:T(8,128)(2,1)S(1)}, u32[]{:S(2)}, u32[]{:S(2)}) %collective-permute-start.2) | collective-permute-done | bytes 114720 | tf_op jit(solution)/shard_map/ppermute | solution.py:257
  33.3 6.0 %collective-permute-start.19 = (bf16[2,14,16,128]{3,2,1,0:T(8,128)(2,1)S(1)}, bf16[2,14,16,128]{3,2,1,0:T(8,128)(2,1)S(1)}, u32[]{:S(2)}, u32[]{:S(2)}) collective-permute-start(bf16[2,14,16,128]{3,2,1,0:T(8,128)(2,1)S(1)} %get-tuple-element.68), channel_id=1, source_target_pairs={{0,2},{8,10},{2,4},{10,12},{4,6},{12,14},{6,0},{14,8},{1,3},{9,11}... | collective-permute-start | bytes 344072 | tf_op jit(solution)/shard_map/ppermute | solution.py:257
  47.8 10.9 %cosine_convert_fusion = (bf16[512,1024]{1,0:T(8,128)(2,1)S(1)}, bf16[512,1024]{1,0:T(8,128)(2,1)S(1)}) fusion(s32[1024]{0:T(1024)S(1)} %iota_add_fusion, s32[512]{0:T(512)S(1)} %get-tuple-element.90, s32[512]{0:T(512)S(1)} %get-tuple-element.93, pred[512]{0:T(512)(128)(4,1)S(1)} %get-tuple-element.97, s32[]{:T(128)} %bitcast.3, ...), kind=kLoop, calls=%fused_computation.26 | loop fusion | flops 24117248 | bytes 2119684 | tf_op jit(solution)/shard_map/convert
  58.8 3.0 %collective-permute-start.23 = (bf16[2,14,16,128]{3,2,1,0:T(8,128)(2,1)S(1)}, bf16[2,14,16,128]{3,2,1,0:T(8,128)(2,1)S(1)}, u32[]{:S(2)}, u32[]{:S(2)}) collective-permute-start(bf16[2,14,16,128]{3,2,1,0:T(8,128)(2,1)S(1)} %get-tuple-element.72), channel_id=1, source_target_pairs={{0,6},{8,14},{2,0},{10,8},{4,2},{12,10},{6,4},{14,12},{1,7},{9,15}... | collective-permute-start | bytes 344072 | tf_op jit(solution)/shard_map/ppermute | solution.py:257
  62.2 4.2 %collective-permute-start.9 = (bf16[2,4,14,16,128]{4,3,2,1,0:T(8,128)(2,1)S(1)}, bf16[2,4,14,16,128]{4,3,2,1,0:T(8,128)(2,1)S(1)}, u32[]{:S(2)}, u32[]{:S(2)}) collective-permute-start(bf16[2,4,14,16,128]{4,3,2,1,0:T(8,128)(2,1)S(1)} %get-tuple-element.55), channel_id=1, source_target_pairs={{0,17},{1,16},{16,33},{17,32},{32,49},{33,48},{48,65},{49,64},{64,... | collective-permute-start | bytes 1376264 | tf_op jit(solution)/shard_map/ppermute | solution.py:293
  68.8 6.6 %collective-permute-start.27 = (bf16[2,4,14,16,128]{4,3,2,1,0:T(8,128)(2,1)S(1)}, bf16[2,4,14,16,128]{4,3,2,1,0:T(8,128)(2,1)S(1)}, u32[]{:S(2)}, u32[]{:S(2)}) collective-permute-start(bf16[2,4,14,16,128]{4,3,2,1,0:T(8,128)(2,1)S(1)} %get-tuple-element.76), channel_id=1, source_target_pairs={{0,17},{1,16},{16,33},{17,32},{32,49},{33,48},{48,65},{49,64},{64,... | collective-permute-start | bytes 1376264 | tf_op jit(solution)/shard_map/ppermute | solution.py:293
  75.4 3.5 %collective-permute-done.9.prev1 = bf16[2,4,14,16,128]{4,3,2,1,0:T(8,128)(2,1)S(1)} collective-permute-done((bf16[2,4,14,16,128]{4,3,2,1,0:T(8,128)(2,1)S(1)}, bf16[2,4,14,16,128]{4,3,2,1,0:T(8,128)(2,1)S(1)}, u32[]{:S(2)}, u32[]{:S(2)}) %collective-permute-start.9) | collective-permute-done | bytes 458784 | tf_op jit(solution)/shard_map/ppermute | solution.py:293
  78.9 5.4 %cross.2 = (bf16[2,2,8,16,128]{4,3,2,1,0:T(8,128)(2,1)S(1)}, bf16[2,2,8,16,128]{4,3,2,1,0:T(8,128)(2,1)S(1)}, bf16[2,2,8,16,128]{4,3,2,1,0:T(8,128)(2,1)S(1)}, b...) custom-call(s32[2]{0:T(128)S(1)} %pad_add_fusion.pos_ref, ...), custom_call_target="tpu_custom_call" | custom-call | flops 536870912 | bytes 3145728 | tf_op jit(solution)/shard_map/cross/pallas_call | solution.py:170
  87.2 2.8 %collective-permute-done.26.prev0 = bf16[2,4,14,16,128]{4,3,2,1,0:T(8,128)(2,1)S(1)} collective-permute-done((bf16[2,4,14,16,128]{4,3,2,1,0:T(8,128)(2,1)S(1)}, bf16[2,4,14,16,128]{4,3,2,1,0:T(8,128)(2,1)S(1)}, u32[]{:S(2)}, u32[]{:S(2)}) %collective-permute-start.26) | collective-permute-done | bytes 458784 | tf_op jit(solution)/shard_map/ppermute | solution.py:292
  90.0 3.0 %collective-permute-start.12 = (bf16[2,2,8,16,128]{4,3,2,1,0:T(8,128)(2,1)S(1)}, bf16[2,2,8,16,128]{4,3,2,1,0:T(8,128)(2,1)S(1)}, u32[]{:S(2)}, u32[]{:S(2)}) collective-permute-start(bf16[2,2,8,16,128]{4,3,2,1,0:T(8,128)(2,1)S(1)} %get-tuple-element.59), channel_id=1, source_target_pairs={{0,10},{8,4},{2,12},{10,6},{4,14},{12,0},{6,8},{14,2},{1,11},{9,5}... | collective-permute-start | bytes 393224 | tf_op jit(solution)/shard_map/ppermute | solution.py:257
  93.0 6.1 %collective-permute-done.27.prev1 = bf16[2,4,14,16,128]{4,3,2,1,0:T(8,128)(2,1)S(1)} collective-permute-done((bf16[2,4,14,16,128]{4,3,2,1,0:T(8,128)(2,1)S(1)}, bf16[2,4,14,16,128]{4,3,2,1,0:T(8,128)(2,1)S(1)}, u32[]{:S(2)}, u32[]{:S(2)}) %collective-permute-start.27) | collective-permute-done | bytes 458784 | tf_op jit(solution)/shard_map/ppermute | solution.py:293
  99.1 2.8 %collective-permute-start.13 = (bf16[2,2,8,16,128]{4,3,2,1,0:T(8,128)(2,1)S(1)}, bf16[2,2,8,16,128]{4,3,2,1,0:T(8,128)(2,1)S(1)}, u32[]{:S(2)}, u32[]{:S(2)}) collective-permute-start(bf16[2,2,8,16,128]{4,3,2,1,0:T(8,128)(2,1)S(1)} %get-tuple-element.60), channel_id=1, source_target_pairs={{0,4},{8,12},{2,6},{10,14},{4,0},{12,8},{6,2},{14,10},{1,5},{9,13}... | collective-permute-start | bytes 393224 | tf_op jit(solution)/shard_map/ppermute | solution.py:257
  104.3 5.4 %cross.3 = (bf16[2,2,8,16,128]{4,3,2,1,0:T(8,128)(2,1)S(1)}, bf16[2,2,8,16,128]{4,3,2,1,0:T(8,128)(2,1)S(1)}, bf16[2,2,8,16,128]{4,3,2,1,0:T(8,128)(2,1)S(1)}, b...) custom-call(s32[2]{0:T(128)S(1)} %pad_add_fusion.pos_ref, ...), custom_call_target="tpu_custom_call" | custom-call | flops 536870912 | bytes 3145728 | tf_op jit(solution)/shard_map/cross/pallas_call | solution.py:170
  109.7 2.9 %collective-permute-start.15 = (bf16[2,2,8,16,128]{4,3,2,1,0:T(8,128)(2,1)S(1)}, bf16[2,2,8,16,128]{4,3,2,1,0:T(8,128)(2,1)S(1)}, u32[]{:S(2)}, u32[]{:S(2)}) collective-permute-start(bf16[2,2,8,16,128]{4,3,2,1,0:T(8,128)(2,1)S(1)} %get-tuple-element.62), channel_id=1, source_target_pairs={{0,6},{8,14},{2,0},{10,8},{4,2},{12,10},{6,4},{14,12},{1,7},{9,15}... | collective-permute-start | bytes 393224 | tf_op jit(solution)/shard_map/ppermute | solution.py:257
  114.1 2.8 %collective-permute-done.14.refs_5_ = bf16[2,2,8,16,128]{4,3,2,1,0:T(8,128)(2,1)S(1)} collective-permute-done((bf16[2,2,8,16,128]{4,3,2,1,0:T(8,128)(2,1)S(1)}, bf16[2,2,8,16,128]{4,3,2,1,0:T(8,128)(2,1)S(1)}, u32[]{:S(2)}, u32[]{:S(2)}) %collective-permute-start.14) | collective-permute-done | bytes 131104 | tf_op jit(solution)/shard_map/ppermute | solution.py:257
  116.9 5.5 %collective-permute-start.30 = (bf16[2,2,8,16,128]{4,3,2,1,0:T(8,128)(2,1)S(1)}, bf16[2,2,8,16,128]{4,3,2,1,0:T(8,128)(2,1)S(1)}, u32[]{:S(2)}, u32[]{:S(2)}) collective-permute-start(bf16[2,2,8,16,128]{4,3,2,1,0:T(8,128)(2,1)S(1)} %get-tuple-element.80), channel_id=1, source_target_pairs={{0,10},{8,4},{2,12},{10,6},{4,14},{12,0},{6,8},{14,2},{1,11},{9,5}... | collective-permute-start | bytes 393224 | tf_op jit(solution)/shard_map/ppermute | solution.py:257
  127.2 2.8 %collective-permute-start.32 = (bf16[2,2,8,16,128]{4,3,2,1,0:T(8,128)(2,1)S(1)}, bf16[2,2,8,16,128]{4,3,2,1,0:T(8,128)(2,1)S(1)}, u32[]{:S(2)}, u32[]{:S(2)}) collective-permute-start(bf16[2,2,8,16,128]{4,3,2,1,0:T(8,128)(2,1)S(1)} %get-tuple-element.82), channel_id=1, source_target_pairs={{0,12},{8,6},{2,14},{10,0},{4,8},{12,2},{6,10},{14,4},{1,13},{9,7}... | collective-permute-start | bytes 393224 | tf_op jit(solution)/shard_map/ppermute | solution.py:257
  136.0 4.4 %collective-permute-done.31.refs_4_ = bf16[2,2,8,16,128]{4,3,2,1,0:T(8,128)(2,1)S(1)} collective-permute-done((bf16[2,2,8,16,128]{4,3,2,1,0:T(8,128)(2,1)S(1)}, bf16[2,2,8,16,128]{4,3,2,1,0:T(8,128)(2,1)S(1)}, u32[]{:S(2)}, u32[]{:S(2)}) %collective-permute-start.31) | collective-permute-done | bytes 131104 | tf_op jit(solution)/shard_map/ppermute | solution.py:257
  140.4 7.6 %collective-permute-done.33.refs_6_ = bf16[2,2,8,16,128]{4,3,2,1,0:T(8,128)(2,1)S(1)} collective-permute-done((bf16[2,2,8,16,128]{4,3,2,1,0:T(8,128)(2,1)S(1)}, bf16[2,2,8,16,128]{4,3,2,1,0:T(8,128)(2,1)S(1)}, u32[]{:S(2)}, u32[]{:S(2)}) %collective-permute-start.33) | collective-permute-done | bytes 131104 | tf_op jit(solution)/shard_map/ppermute | solution.py:257
  152.8 3.7 %invert.1 = bf16[2,8,64,1024]{3,2,1,0:T(8,128)(2,1)} custom-call(bf16[2,8,128,128]{3,2,1,0:T(8,128)(2,1)S(1)} %get-tuple-element.64.refs_8_.refs_0_, bf16[2,8,128,128]{3,2,1,0:T(8,128)(2,1)S(1)} %collective-permute-done.17.refs_1_, bf16[2,8,128,128]{3,2,1,0:T(8,128)(2,1)S(1)} %get-tuple-element.85.refs_2_, ...), custom_call_target="tpu_custom_call" | custom-call | flops 2147483648 | bytes 6291456 | tf_op jit(solution)/shard_map/invert/pallas_call | solution.py:226
  (70 shorter events, 43.4 us)
Async XLA Ops:
  15.3 17.1 %collective-permute-start.2 = (bf16[2,14,16,128]{3,2,1,0:T(8,128)(2,1)S(1)}, bf16[2,14,16,128]{3,2,1,0:T(8,128)(2,1)S(1)}, u32[]{:S(2)}, u32[]{:S(2)}) collective-permute-start(bf16[2,14,16,128]{3,2,1,0:T(8,128)(2,1)S(1)} %get-tuple-element.49), channel_id=1, source_target_pairs={{0,10},{8,4},{2,12},{10,6},{4,14},{12,0},{6,8},{14,2},{1,11},{9,5}... | collective-permute-start | bytes 344072 | tf_op jit(solution)/shard_map/ppermute | solution.py:257
  19.5 19.8 %collective-permute-start.4 = (bf16[2,14,16,128]{3,2,1,0:T(8,128)(2,1)S(1)}, bf16[2,14,16,128]{3,2,1,0:T(8,128)(2,1)S(1)}, u32[]{:S(2)}, u32[]{:S(2)}) collective-permute-start(bf16[2,14,16,128]{3,2,1,0:T(8,128)(2,1)S(1)} %get-tuple-element.51), channel_id=1, source_target_pairs={{0,12},{8,6},{2,14},{10,0},{4,8},{12,2},{6,10},{14,4},{1,13},{9,7}... | collective-permute-start | bytes 344072 | tf_op jit(solution)/shard_map/ppermute | solution.py:257
  24.0 17.4 %collective-permute-start.5 = (bf16[2,14,16,128]{3,2,1,0:T(8,128)(2,1)S(1)}, bf16[2,14,16,128]{3,2,1,0:T(8,128)(2,1)S(1)}, u32[]{:S(2)}, u32[]{:S(2)}) collective-permute-start(bf16[2,14,16,128]{3,2,1,0:T(8,128)(2,1)S(1)} %get-tuple-element.52), channel_id=1, source_target_pairs={{0,6},{8,14},{2,0},{10,8},{4,2},{12,10},{6,4},{14,12},{1,7},{9,15}... | collective-permute-start | bytes 344072 | tf_op jit(solution)/shard_map/ppermute | solution.py:257
  26.5 17.2 %collective-permute-start.6 = (bf16[2,14,16,128]{3,2,1,0:T(8,128)(2,1)S(1)}, bf16[2,14,16,128]{3,2,1,0:T(8,128)(2,1)S(1)}, u32[]{:S(2)}, u32[]{:S(2)}) collective-permute-start(bf16[2,14,16,128]{3,2,1,0:T(8,128)(2,1)S(1)} %get-tuple-element.53), channel_id=1, source_target_pairs={{0,14},{8,0},{2,8},{10,2},{4,10},{12,4},{6,12},{14,6},{1,15},{9,1}... | collective-permute-start | bytes 344072 | tf_op jit(solution)/shard_map/ppermute | solution.py:257
  33.3 25.5 %collective-permute-start.19 = (bf16[2,14,16,128]{3,2,1,0:T(8,128)(2,1)S(1)}, bf16[2,14,16,128]{3,2,1,0:T(8,128)(2,1)S(1)}, u32[]{:S(2)}, u32[]{:S(2)}) collective-permute-start(bf16[2,14,16,128]{3,2,1,0:T(8,128)(2,1)S(1)} %get-tuple-element.68), channel_id=1, source_target_pairs={{0,2},{8,10},{2,4},{10,12},{4,6},{12,14},{6,0},{14,8},{1,3},{9,11}... | collective-permute-start | bytes 344072 | tf_op jit(solution)/shard_map/ppermute | solution.py:257
  39.3 22.5 %collective-permute-start.20 = (bf16[2,14,16,128]{3,2,1,0:T(8,128)(2,1)S(1)}, bf16[2,14,16,128]{3,2,1,0:T(8,128)(2,1)S(1)}, u32[]{:S(2)}, u32[]{:S(2)}) collective-permute-start(bf16[2,14,16,128]{3,2,1,0:T(8,128)(2,1)S(1)} %get-tuple-element.69), channel_id=1, source_target_pairs={{0,10},{8,4},{2,12},{10,6},{4,14},{12,0},{6,8},{14,2},{1,11},{9,5}... | collective-permute-start | bytes 344072 | tf_op jit(solution)/shard_map/ppermute | solution.py:257
  41.4 20.7 %collective-permute-start.21 = (bf16[2,14,16,128]{3,2,1,0:T(8,128)(2,1)S(1)}, bf16[2,14,16,128]{3,2,1,0:T(8,128)(2,1)S(1)}, u32[]{:S(2)}, u32[]{:S(2)}) collective-permute-start(bf16[2,14,16,128]{3,2,1,0:T(8,128)(2,1)S(1)} %get-tuple-element.70), channel_id=1, source_target_pairs={{0,4},{8,12},{2,6},{10,14},{4,0},{12,8},{6,2},{14,10},{1,5},{9,13}... | collective-permute-start | bytes 344072 | tf_op jit(solution)/shard_map/ppermute | solution.py:257
  43.7 22.7 %collective-permute-start.22 = (bf16[2,14,16,128]{3,2,1,0:T(8,128)(2,1)S(1)}, bf16[2,14,16,128]{3,2,1,0:T(8,128)(2,1)S(1)}, u32[]{:S(2)}, u32[]{:S(2)}) collective-permute-start(bf16[2,14,16,128]{3,2,1,0:T(8,128)(2,1)S(1)} %get-tuple-element.71), channel_id=1, source_target_pairs={{0,12},{8,6},{2,14},{10,0},{4,8},{12,2},{6,10},{14,4},{1,13},{9,7}... | collective-permute-start | bytes 344072 | tf_op jit(solution)/shard_map/ppermute | solution.py:257
  46.5 28.9 %collective-permute-start.8 = (bf16[2,4,14,16,128]{4,3,2,1,0:T(8,128)(2,1)S(1)}, bf16[2,4,14,16,128]{4,3,2,1,0:T(8,128)(2,1)S(1)}, u32[]{:S(2)}, u32[]{:S(2)}) collective-permute-start(bf16[2,4,14,16,128]{4,3,2,1,0:T(8,128)(2,1)S(1)} %get-tuple-element.54.own0), channel_id=1, source_target_pairs={{0,16},{16,32},{32,48},{48,64},{64,80},{80,96},{96,112},{112,128},... | collective-permute-start | bytes 1376264 | tf_op jit(solution)/shard_map/ppermute | solution.py:292
  62.2 16.8 %collective-permute-start.9 = (bf16[2,4,14,16,128]{4,3,2,1,0:T(8,128)(2,1)S(1)}, bf16[2,4,14,16,128]{4,3,2,1,0:T(8,128)(2,1)S(1)}, u32[]{:S(2)}, u32[]{:S(2)}) collective-permute-start(bf16[2,4,14,16,128]{4,3,2,1,0:T(8,128)(2,1)S(1)} %get-tuple-element.55), channel_id=1, source_target_pairs={{0,17},{1,16},{16,33},{17,32},{32,49},{33,48},{48,65},{49,64},{64,... | collective-permute-start | bytes 1376264 | tf_op jit(solution)/shard_map/ppermute | solution.py:293
  67.7 22.3 %collective-permute-start.26 = (bf16[2,4,14,16,128]{4,3,2,1,0:T(8,128)(2,1)S(1)}, bf16[2,4,14,16,128]{4,3,2,1,0:T(8,128)(2,1)S(1)}, u32[]{:S(2)}, u32[]{:S(2)}) collective-permute-start(bf16[2,4,14,16,128]{4,3,2,1,0:T(8,128)(2,1)S(1)} %get-tuple-element.75.own0), channel_id=1, source_target_pairs={{0,16},{16,32},{32,48},{48,64},{64,80},{80,96},{96,112},{112,128},... | collective-permute-start | bytes 1376264 | tf_op jit(solution)/shard_map/ppermute | solution.py:292
  68.8 30.3 %collective-permute-start.27 = (bf16[2,4,14,16,128]{4,3,2,1,0:T(8,128)(2,1)S(1)}, bf16[2,4,14,16,128]{4,3,2,1,0:T(8,128)(2,1)S(1)}, u32[]{:S(2)}, u32[]{:S(2)}) collective-permute-start(bf16[2,4,14,16,128]{4,3,2,1,0:T(8,128)(2,1)S(1)} %get-tuple-element.76), channel_id=1, source_target_pairs={{0,17},{1,16},{16,33},{17,32},{32,49},{33,48},{48,65},{49,64},{64,... | collective-permute-start | bytes 1376264 | tf_op jit(solution)/shard_map/ppermute | solution.py:293
  75.4 26.5 %collective-permute-start.25 = (bf16[2,4,14,16,128]{4,3,2,1,0:T(8,128)(2,1)S(1)}, bf16[2,4,14,16,128]{4,3,2,1,0:T(8,128)(2,1)S(1)}, u32[]{:S(2)}, u32[]{:S(2)}) collective-permute-start(bf16[2,4,14,16,128]{4,3,2,1,0:T(8,128)(2,1)S(1)} %get-tuple-element.76), channel_id=1, source_target_pairs={{0,1},{1,0},{2,3},{3,2},{4,5},{5,4},{6,7},{7,6},{8,9},{9,8},{10,11... | collective-permute-start | bytes 1376264 | tf_op jit(solution)/shard_map/ppermute | solution.py:263
  84.3 25.4 %collective-permute-start.10 = (bf16[2,2,8,16,128]{4,3,2,1,0:T(8,128)(2,1)S(1)}, bf16[2,2,8,16,128]{4,3,2,1,0:T(8,128)(2,1)S(1)}, u32[]{:S(2)}, u32[]{:S(2)}) collective-permute-start(bf16[2,2,8,16,128]{4,3,2,1,0:T(8,128)(2,1)S(1)} %get-tuple-element.57), channel_id=1, source_target_pairs={{0,8},{8,2},{2,10},{10,4},{4,12},{12,6},{6,14},{14,0},{1,9},{9,3},... | collective-permute-start | bytes 393224 | tf_op jit(solution)/shard_map/ppermute | solution.py:257
  85.9 26.7 %collective-permute-start.11 = (bf16[2,2,8,16,128]{4,3,2,1,0:T(8,128)(2,1)S(1)}, bf16[2,2,8,16,128]{4,3,2,1,0:T(8,128)(2,1)S(1)}, u32[]{:S(2)}, u32[]{:S(2)}) collective-permute-start(bf16[2,2,8,16,128]{4,3,2,1,0:T(8,128)(2,1)S(1)} %get-tuple-element.58), channel_id=1, source_target_pairs={{0,2},{8,10},{2,4},{10,12},{4,6},{12,14},{6,0},{14,8},{1,3},{9,11}... | collective-permute-start | bytes 393224 | tf_op jit(solution)/shard_map/ppermute | solution.py:257
  90.0 22.7 %collective-permute-start.12 = (bf16[2,2,8,16,128]{4,3,2,1,0:T(8,128)(2,1)S(1)}, bf16[2,2,8,16,128]{4,3,2,1,0:T(8,128)(2,1)S(1)}, u32[]{:S(2)}, u32[]{:S(2)}) collective-permute-start(bf16[2,2,8,16,128]{4,3,2,1,0:T(8,128)(2,1)S(1)} %get-tuple-element.59), channel_id=1, source_target_pairs={{0,10},{8,4},{2,12},{10,6},{4,14},{12,0},{6,8},{14,2},{1,11},{9,5}... | collective-permute-start | bytes 393224 | tf_op jit(solution)/shard_map/ppermute | solution.py:257
  109.7 15.5 %collective-permute-start.15 = (bf16[2,2,8,16,128]{4,3,2,1,0:T(8,128)(2,1)S(1)}, bf16[2,2,8,16,128]{4,3,2,1,0:T(8,128)(2,1)S(1)}, u32[]{:S(2)}, u32[]{:S(2)}) collective-permute-start(bf16[2,2,8,16,128]{4,3,2,1,0:T(8,128)(2,1)S(1)} %get-tuple-element.62), channel_id=1, source_target_pairs={{0,6},{8,14},{2,0},{10,8},{4,2},{12,10},{6,4},{14,12},{1,7},{9,15}... | collective-permute-start | bytes 393224 | tf_op jit(solution)/shard_map/ppermute | solution.py:257
  112.7 17.4 %collective-permute-start.28 = (bf16[2,2,8,16,128]{4,3,2,1,0:T(8,128)(2,1)S(1)}, bf16[2,2,8,16,128]{4,3,2,1,0:T(8,128)(2,1)S(1)}, u32[]{:S(2)}, u32[]{:S(2)}) collective-permute-start(bf16[2,2,8,16,128]{4,3,2,1,0:T(8,128)(2,1)S(1)} %get-tuple-element.78), channel_id=1, source_target_pairs={{0,8},{8,2},{2,10},{10,4},{4,12},{12,6},{6,14},{14,0},{1,9},{9,3},... | collective-permute-start | bytes 393224 | tf_op jit(solution)/shard_map/ppermute | solution.py:257
  114.1 17.4 %collective-permute-start.29 = (bf16[2,2,8,16,128]{4,3,2,1,0:T(8,128)(2,1)S(1)}, bf16[2,2,8,16,128]{4,3,2,1,0:T(8,128)(2,1)S(1)}, u32[]{:S(2)}, u32[]{:S(2)}) collective-permute-start(bf16[2,2,8,16,128]{4,3,2,1,0:T(8,128)(2,1)S(1)} %get-tuple-element.79), channel_id=1, source_target_pairs={{0,2},{8,10},{2,4},{10,12},{4,6},{12,14},{6,0},{14,8},{1,3},{9,11}... | collective-permute-start | bytes 393224 | tf_op jit(solution)/shard_map/ppermute | solution.py:257
  116.9 17.3 %collective-permute-start.30 = (bf16[2,2,8,16,128]{4,3,2,1,0:T(8,128)(2,1)S(1)}, bf16[2,2,8,16,128]{4,3,2,1,0:T(8,128)(2,1)S(1)}, u32[]{:S(2)}, u32[]{:S(2)}) collective-permute-start(bf16[2,2,8,16,128]{4,3,2,1,0:T(8,128)(2,1)S(1)} %get-tuple-element.80), channel_id=1, source_target_pairs={{0,10},{8,4},{2,12},{10,6},{4,14},{12,0},{6,8},{14,2},{1,11},{9,5}... | collective-permute-start | bytes 393224 | tf_op jit(solution)/shard_map/ppermute | solution.py:257
  125.2 15.3 %collective-permute-start.31 = (bf16[2,2,8,16,128]{4,3,2,1,0:T(8,128)(2,1)S(1)}, bf16[2,2,8,16,128]{4,3,2,1,0:T(8,128)(2,1)S(1)}, u32[]{:S(2)}, u32[]{:S(2)}) collective-permute-start(bf16[2,2,8,16,128]{4,3,2,1,0:T(8,128)(2,1)S(1)} %get-tuple-element.81), channel_id=1, source_target_pairs={{0,4},{8,12},{2,6},{10,14},{4,0},{12,8},{6,2},{14,10},{1,5},{9,13}... | collective-permute-start | bytes 393224 | tf_op jit(solution)/shard_map/ppermute | solution.py:257
  130.1 18.0 %collective-permute-start.33 = (bf16[2,2,8,16,128]{4,3,2,1,0:T(8,128)(2,1)S(1)}, bf16[2,2,8,16,128]{4,3,2,1,0:T(8,128)(2,1)S(1)}, u32[]{:S(2)}, u32[]{:S(2)}) collective-permute-start(bf16[2,2,8,16,128]{4,3,2,1,0:T(8,128)(2,1)S(1)} %get-tuple-element.83), channel_id=1, source_target_pairs={{0,6},{8,14},{2,0},{10,8},{4,2},{12,10},{6,4},{14,12},{1,7},{9,15}... | collective-permute-start | bytes 393224 | tf_op jit(solution)/shard_map/ppermute | solution.py:257
  131.5 18.0 %collective-permute-start.34 = (bf16[2,2,8,16,128]{4,3,2,1,0:T(8,128)(2,1)S(1)}, bf16[2,2,8,16,128]{4,3,2,1,0:T(8,128)(2,1)S(1)}, u32[]{:S(2)}, u32[]{:S(2)}) collective-permute-start(bf16[2,2,8,16,128]{4,3,2,1,0:T(8,128)(2,1)S(1)} %get-tuple-element.84), channel_id=1, source_target_pairs={{0,14},{8,0},{2,8},{10,2},{4,10},{12,4},{6,12},{14,6},{1,15},{9,1}... | collective-permute-start | bytes 393224 | tf_op jit(solution)/shard_map/ppermute | solution.py:257
  134.2 17.1 %collective-permute-start.17 = (bf16[2,8,128,128]{3,2,1,0:T(8,128)(2,1)S(1)}, bf16[2,8,128,128]{3,2,1,0:T(8,128)(2,1)S(1)}, u32[]{:S(2)}, u32[]{:S(2)}) collective-permute-start(bf16[2,8,128,128]{3,2,1,0:T(8,128)(2,1)S(1)} %get-tuple-element.65), channel_id=1, source_target_pairs={{0,1},{1,0},{2,3},{3,2},{4,5},{5,4},{6,7},{7,6},{8,9},{9,8},{10,11... | collective-permute-start | bytes 1572872 | tf_op jit(solution)/shard_map/ppermute | solution.py:263
  (12 other events, 141.8 us)
where the time goes:
time: 157 us
  starting transfers between devices  74.9 us (48%)
  waiting for transfers between devices  41.3 us (26%)
  Pallas kernels  26.3 us (17%)
  other arithmetic  12 us (8%)
  local copies, waits for them, and re-layouts  1.89 us (1%)
    ppermute x28, starting transfers between devices, ring(): lax.ppermute(value, ('zl', 'zh'), [(place(z), place((z + shift) % 8)) for...  59.3 us
    ppermute x28, waiting for transfers between devices, ring(): lax.ppermute(value, ('zl', 'zh'), [(place(z), place((z + shift) % 8)) for...  27.3 us
    another operation x1, other arithmetic  10.9 us
    ppermute x2, starting transfers between devices, shards(): prev1 = lax.ppermute(other, ('x', 'y', 'c'), swap)  10.9 us
    pallas_call x2, Pallas kernels, cross(): pl.pallas_call(cross_kernel, out_shape=[shape] * 8, in_specs=[SM] + [VM]...  10.8 us
    ppermute x2, waiting for transfers between devices, shards(): prev1 = lax.ppermute(other, ('x', 'y', 'c'), swap)  9.62 us
    pallas_call x1, Pallas kernels, whiten(): pl.pallas_call(whiten_kernel, out_shape=[shape] * (8 * CHUNKS), grid_spec...  6.99 us
    pallas_call x1, Pallas kernels, invert(): pl.pallas_call(functools.partial(invert_kernel, scaling), out_shape=jax.S...  3.73 us
  transfers between devices with their start and end apart: 36, of which 12 were waited for; matrix products, arithmetic and copies ran while one was open for 7% of the time, Pallas kernels for 10%

commit v1 on v0

--- a/solution.py
+++ b/solution.py
@@ -19,6 +19,7 @@
 CHUNKS = 2
 FC = 32 // CHUNKS
 CBINS = BINS // CHUNKS
+ORDER = (0, 4, 3, 5, 2, 6, 1, 7)
 F32 = jnp.float32
 BF16 = jnp.bfloat16
 
@@ -103,10 +104,10 @@
     ins, (same, other, core) = refs[:8], refs[-3:]
     z = pos_ref[0]
     core[0] = pos_ref[1]
-    for r in range(8):
+    for n, r in enumerate(ORDER):
         src = (z - r) & 7
-        same[src & 1, src >> 1] = ins[r][0]
-        other[src & 1, src >> 1] = ins[r][1]
+        same[src & 1, src >> 1] = ins[n][0]
+        other[src & 1, src >> 1] = ins[n][1]
 
 
 def merge(pieces, pos, *after):
@@ -190,9 +191,9 @@
     for crel, out in enumerate((same, other)):
         for rnd in range(2):
             for i in range(8):
-                for r in range(8):
+                for n, r in enumerate(ORDER):
                     start = pl.multiple_of(((z - r) & 7) * FC, FC)
-                    buf[pl.ds(start, FC), :] = ins[r][crel, rnd, i].astype(F32)
+                    buf[pl.ds(start, FC), :] = ins[n][crel, rnd, i].astype(F32)
                 out[rnd, i] = buf[...].T.astype(BF16)
 
 
@@ -263,14 +264,8 @@
     return lax.ppermute(value, "c", [(0, 1), (1, 0)])
 
 
-ORDER = (4, 3, 5, 2, 6, 1, 7)
-
-
 def round_ring(pieces):
-    got = {0: pieces[0]}
-    for r in ORDER:
-        got[r] = ring(pieces[r], r)
-    return [got[r] for r in range(8)]
+    return [ring(pieces[r], r) if r else pieces[0] for r in ORDER]
 
 
 def shards(spectra, valid_flags):

time: 157 us -> 146 us (0.930)
  waiting for transfers between devices: 41.3 us -> 26.5 us
  starting transfers between devices: 74.9 us -> 78.9 us
    ppermute x28, waiting for transfers between devices: 27.3 us -> 9.15 us  [ring(): lax.ppermute(value, ('zl', 'zh'), [(place(z), place((z + shift) % 8)) for...]
    ppermute x4, starting transfers between devices: 2.28 us -> 10 us  [other_core(): return lax.ppermute(value, 'c', [(0, 1), (1, 0)])]
    ppermute x2, waiting for transfers between devices: 9.62 us -> 14.5 us  [shards(): prev1 = lax.ppermute(other, ('x', 'y', 'c'), swap)]
    ppermute x28, starting transfers between devices: 59.3 us -> 56.8 us  [ring(): lax.ppermute(value, ('zl', 'zh'), [(place(z), place((z + shift) % 8)) for...]
  transfers between devices with their start and end apart: 36 -> 36, of which waited for: 12 -> 8; matrix products, arithmetic and copies ran while one was open for 7% -> 8% of each run, Pallas kernels for 10% -> 11%
where the time goes in v1:
time: 146 us
  starting transfers between devices  78.9 us (54%)
  waiting for transfers between devices  26.5 us (18%)
  Pallas kernels  26.3 us (18%)
  other arithmetic  12 us (8%)
  local copies, waits for them, and re-layouts  1.89 us (1%)
    ppermute x28, starting transfers between devices, ring(): lax.ppermute(value, ('zl', 'zh'), [(place(z), place((z + shift) % 8)) for...  56.8 us
    ppermute x2, waiting for transfers between devices, shards(): prev1 = lax.ppermute(other, ('x', 'y', 'c'), swap)  14.5 us
    another operation x1, other arithmetic  10.9 us
    pallas_call x2, Pallas kernels, cross(): pl.pallas_call(cross_kernel, out_shape=[shape] * 8, in_specs=[SM] + [VM]...  10.8 us
    ppermute x4, starting transfers between devices, other_core(): return lax.ppermute(value, 'c', [(0, 1), (1, 0)])  10 us
    ppermute x2, starting transfers between devices, shards(): prev1 = lax.ppermute(other, ('x', 'y', 'c'), swap)  9.73 us
    ppermute x28, waiting for transfers between devices, ring(): lax.ppermute(value, ('zl', 'zh'), [(place(z), place((z + shift) % 8)) for...  9.15 us
    pallas_call x1, Pallas kernels, whiten(): pl.pallas_call(whiten_kernel, out_shape=[shape] * (8 * CHUNKS), grid_spec...  6.99 us
  transfers between devices with their start and end apart: 36, of which 8 were waited for; matrix products, arithmetic and copies ran while one was open for 8% of the time, Pallas kernels for 11%

profile of v1, /device:TPU:1, one launch (start us, length us, event | category | flops | bytes accessed | tf_op | source)
XLA Modules:
  0.0 145.8 jit_solution(5432703736007338843)
XLA Ops:
  2.8 7.0 %whiten.1 = (bf16[2,14,16,128]{3,2,1,0:T(8,128)(2,1)S(1)}, bf16[2,14,16,128]{3,2,1,0:T(8,128)(2,1)S(1)}, bf16[2,14,16,128]{3,2,1,0:T(8,128)(2,1)S(1)}, bf16[2,14...) custom-call(s32[2]{0:T(128)S(1)} %pad_add_fusion.pos_ref, ...), custom_call_target="tpu_custom_call" | custom-call | flops 1409286144 | bytes 4194304 | tf_op jit(solution)/shard_map/whiten/pallas_call | solution.py:77
  9.8 7.8 %collective-permute-start = (bf16[2,14,16,128]{3,2,1,0:T(8,128)(2,1)S(1)}, bf16[2,14,16,128]{3,2,1,0:T(8,128)(2,1)S(1)}, u32[]{:S(2)}, u32[]{:S(2)}) collective-permute-start(bf16[2,14,16,128]{3,2,1,0:T(8,128)(2,1)S(1)} %get-tuple-element.47), channel_id=1, source_target_pairs={{0,4},{8,12},{2,6},{10,14},{4,0},{12,8},{6,2},{14,10},{1,5},{9,13}... | collective-permute-start | bytes 344072 | tf_op jit(solution)/shard_map/ppermute | solution.py:258
  19.2 2.8 %collective-permute-start.2 = (bf16[2,14,16,128]{3,2,1,0:T(8,128)(2,1)S(1)}, bf16[2,14,16,128]{3,2,1,0:T(8,128)(2,1)S(1)}, u32[]{:S(2)}, u32[]{:S(2)}) collective-permute-start(bf16[2,14,16,128]{3,2,1,0:T(8,128)(2,1)S(1)} %get-tuple-element.49), channel_id=1, source_target_pairs={{0,12},{8,6},{2,14},{10,0},{4,8},{12,2},{6,10},{14,4},{1,13},{9,7}... | collective-permute-start | bytes 344072 | tf_op jit(solution)/shard_map/ppermute | solution.py:258
  23.2 2.4 %collective-permute-start.4 = (bf16[2,14,16,128]{3,2,1,0:T(8,128)(2,1)S(1)}, bf16[2,14,16,128]{3,2,1,0:T(8,128)(2,1)S(1)}, u32[]{:S(2)}, u32[]{:S(2)}) collective-permute-start(bf16[2,14,16,128]{3,2,1,0:T(8,128)(2,1)S(1)} %get-tuple-element.51), channel_id=1, source_target_pairs={{0,6},{8,14},{2,0},{10,8},{4,2},{12,10},{6,4},{14,12},{1,7},{9,15}... | collective-permute-start | bytes 344072 | tf_op jit(solution)/shard_map/ppermute | solution.py:258
  26.5 6.0 %collective-permute-done.1.refs_2_ = bf16[2,14,16,128]{3,2,1,0:T(8,128)(2,1)S(1)} collective-permute-done((bf16[2,14,16,128]{3,2,1,0:T(8,128)(2,1)S(1)}, bf16[2,14,16,128]{3,2,1,0:T(8,128)(2,1)S(1)}, u32[]{:S(2)}, u32[]{:S(2)}) %collective-permute-start.1) | collective-permute-done | bytes 114720 | tf_op jit(solution)/shard_map/ppermute | solution.py:258
  34.4 3.8 %collective-permute-start.19 = (bf16[2,14,16,128]{3,2,1,0:T(8,128)(2,1)S(1)}, bf16[2,14,16,128]{3,2,1,0:T(8,128)(2,1)S(1)}, u32[]{:S(2)}, u32[]{:S(2)}) collective-permute-start(bf16[2,14,16,128]{3,2,1,0:T(8,128)(2,1)S(1)} %get-tuple-element.68), channel_id=1, source_target_pairs={{0,10},{8,4},{2,12},{10,6},{4,14},{12,0},{6,8},{14,2},{1,11},{9,5}... | collective-permute-start | bytes 344072 | tf_op jit(solution)/shard_map/ppermute | solution.py:258
  45.6 10.9 %cosine_convert_fusion = (bf16[512,1024]{1,0:T(8,128)(2,1)S(1)}, bf16[512,1024]{1,0:T(8,128)(2,1)S(1)}) fusion(s32[1024]{0:T(1024)S(1)} %iota_add_fusion, s32[512]{0:T(512)S(1)} %get-tuple-element.90, s32[512]{0:T(512)S(1)} %get-tuple-element.93, pred[512]{0:T(512)(128)(4,1)S(1)} %get-tuple-element.97, s32[]{:T(128)} %bitcast.3, ...), kind=kLoop, calls=%fused_computation.26 | loop fusion | flops 24117248 | bytes 2119684 | tf_op jit(solution)/shard_map/convert
  56.5 2.3 %collective-permute-start.23 = (bf16[2,14,16,128]{3,2,1,0:T(8,128)(2,1)S(1)}, bf16[2,14,16,128]{3,2,1,0:T(8,128)(2,1)S(1)}, u32[]{:S(2)}, u32[]{:S(2)}) collective-permute-start(bf16[2,14,16,128]{3,2,1,0:T(8,128)(2,1)S(1)} %get-tuple-element.72), channel_id=1, source_target_pairs={{0,8},{8,2},{2,10},{10,4},{4,12},{12,6},{6,14},{14,0},{1,9},{9,3},... | collective-permute-start | bytes 344072 | tf_op jit(solution)/shard_map/ppermute | solution.py:258
  59.5 7.0 %collective-permute-start.9 = (bf16[2,4,14,16,128]{4,3,2,1,0:T(8,128)(2,1)S(1)}, bf16[2,4,14,16,128]{4,3,2,1,0:T(8,128)(2,1)S(1)}, u32[]{:S(2)}, u32[]{:S(2)}) collective-permute-start(bf16[2,4,14,16,128]{4,3,2,1,0:T(8,128)(2,1)S(1)} %get-tuple-element.55), channel_id=1, source_target_pairs={{0,17},{1,16},{16,33},{17,32},{32,49},{33,48},{48,65},{49,64},{64,... | collective-permute-start | bytes 1376264 | tf_op jit(solution)/shard_map/ppermute | solution.py:288
  68.8 2.7 %collective-permute-start.27 = (bf16[2,4,14,16,128]{4,3,2,1,0:T(8,128)(2,1)S(1)}, bf16[2,4,14,16,128]{4,3,2,1,0:T(8,128)(2,1)S(1)}, u32[]{:S(2)}, u32[]{:S(2)}) collective-permute-start(bf16[2,4,14,16,128]{4,3,2,1,0:T(8,128)(2,1)S(1)} %get-tuple-element.76), channel_id=1, source_target_pairs={{0,17},{1,16},{16,33},{17,32},{32,49},{33,48},{48,65},{49,64},{64,... | collective-permute-start | bytes 1376264 | tf_op jit(solution)/shard_map/ppermute | solution.py:288
  71.6 7.5 %collective-permute-done.9.prev1 = bf16[2,4,14,16,128]{4,3,2,1,0:T(8,128)(2,1)S(1)} collective-permute-done((bf16[2,4,14,16,128]{4,3,2,1,0:T(8,128)(2,1)S(1)}, bf16[2,4,14,16,128]{4,3,2,1,0:T(8,128)(2,1)S(1)}, u32[]{:S(2)}, u32[]{:S(2)}) %collective-permute-start.9) | collective-permute-done | bytes 458784 | tf_op jit(solution)/shard_map/ppermute | solution.py:288
  79.1 5.4 %cross.2 = (bf16[2,2,8,16,128]{4,3,2,1,0:T(8,128)(2,1)S(1)}, bf16[2,2,8,16,128]{4,3,2,1,0:T(8,128)(2,1)S(1)}, bf16[2,2,8,16,128]{4,3,2,1,0:T(8,128)(2,1)S(1)}, b...) custom-call(s32[2]{0:T(128)S(1)} %pad_add_fusion.pos_ref, ...), custom_call_target="tpu_custom_call" | custom-call | flops 536870912 | bytes 3145728 | tf_op jit(solution)/shard_map/cross/pallas_call | solution.py:171
  84.5 2.8 %collective-permute-start.10 = (bf16[2,2,8,16,128]{4,3,2,1,0:T(8,128)(2,1)S(1)}, bf16[2,2,8,16,128]{4,3,2,1,0:T(8,128)(2,1)S(1)}, u32[]{:S(2)}, u32[]{:S(2)}) collective-permute-start(bf16[2,2,8,16,128]{4,3,2,1,0:T(8,128)(2,1)S(1)} %get-tuple-element.57), channel_id=1, source_target_pairs={{0,4},{8,12},{2,6},{10,14},{4,0},{12,8},{6,2},{14,10},{1,5},{9,13}... | collective-permute-start | bytes 393224 | tf_op jit(solution)/shard_map/ppermute | solution.py:258
  91.8 6.9 %collective-permute-done.27.prev1 = bf16[2,4,14,16,128]{4,3,2,1,0:T(8,128)(2,1)S(1)} collective-permute-done((bf16[2,4,14,16,128]{4,3,2,1,0:T(8,128)(2,1)S(1)}, bf16[2,4,14,16,128]{4,3,2,1,0:T(8,128)(2,1)S(1)}, u32[]{:S(2)}, u32[]{:S(2)}) %collective-permute-start.27) | collective-permute-done | bytes 458784 | tf_op jit(solution)/shard_map/ppermute | solution.py:288
  98.8 3.6 %collective-permute-start.14 = (bf16[2,2,8,16,128]{4,3,2,1,0:T(8,128)(2,1)S(1)}, bf16[2,2,8,16,128]{4,3,2,1,0:T(8,128)(2,1)S(1)}, u32[]{:S(2)}, u32[]{:S(2)}) collective-permute-start(bf16[2,2,8,16,128]{4,3,2,1,0:T(8,128)(2,1)S(1)} %get-tuple-element.61), channel_id=1, source_target_pairs={{0,6},{8,14},{2,0},{10,8},{4,2},{12,10},{6,4},{14,12},{1,7},{9,15}... | collective-permute-start | bytes 393224 | tf_op jit(solution)/shard_map/ppermute | solution.py:258
  102.3 5.4 %cross.3 = (bf16[2,2,8,16,128]{4,3,2,1,0:T(8,128)(2,1)S(1)}, bf16[2,2,8,16,128]{4,3,2,1,0:T(8,128)(2,1)S(1)}, bf16[2,2,8,16,128]{4,3,2,1,0:T(8,128)(2,1)S(1)}, b...) custom-call(s32[2]{0:T(128)S(1)} %pad_add_fusion.pos_ref, ...), custom_call_target="tpu_custom_call" | custom-call | flops 536870912 | bytes 3145728 | tf_op jit(solution)/shard_map/cross/pallas_call | solution.py:171
  108.1 2.7 %collective-permute-start.16 = (bf16[2,2,8,16,128]{4,3,2,1,0:T(8,128)(2,1)S(1)}, bf16[2,2,8,16,128]{4,3,2,1,0:T(8,128)(2,1)S(1)}, u32[]{:S(2)}, u32[]{:S(2)}) collective-permute-start(bf16[2,2,8,16,128]{4,3,2,1,0:T(8,128)(2,1)S(1)} %get-tuple-element.63), channel_id=1, source_target_pairs={{0,14},{8,0},{2,8},{10,2},{4,10},{12,4},{6,12},{14,6},{1,15},{9,1}... | collective-permute-start | bytes 393224 | tf_op jit(solution)/shard_map/ppermute | solution.py:258
  110.7 2.8 %collective-permute-start.28 = (bf16[2,2,8,16,128]{4,3,2,1,0:T(8,128)(2,1)S(1)}, bf16[2,2,8,16,128]{4,3,2,1,0:T(8,128)(2,1)S(1)}, u32[]{:S(2)}, u32[]{:S(2)}) collective-permute-start(bf16[2,2,8,16,128]{4,3,2,1,0:T(8,128)(2,1)S(1)} %get-tuple-element.78), channel_id=1, source_target_pairs={{0,4},{8,12},{2,6},{10,14},{4,0},{12,8},{6,2},{14,10},{1,5},{9,13}... | collective-permute-start | bytes 393224 | tf_op jit(solution)/shard_map/ppermute | solution.py:258
  113.8 4.2 %collective-permute-start.30 = (bf16[2,2,8,16,128]{4,3,2,1,0:T(8,128)(2,1)S(1)}, bf16[2,2,8,16,128]{4,3,2,1,0:T(8,128)(2,1)S(1)}, u32[]{:S(2)}, u32[]{:S(2)}) collective-permute-start(bf16[2,2,8,16,128]{4,3,2,1,0:T(8,128)(2,1)S(1)} %get-tuple-element.80), channel_id=1, source_target_pairs={{0,12},{8,6},{2,14},{10,0},{4,8},{12,2},{6,10},{14,4},{1,13},{9,7}... | collective-permute-start | bytes 393224 | tf_op jit(solution)/shard_map/ppermute | solution.py:258
  118.0 3.6 %collective-permute-start.32 = (bf16[2,2,8,16,128]{4,3,2,1,0:T(8,128)(2,1)S(1)}, bf16[2,2,8,16,128]{4,3,2,1,0:T(8,128)(2,1)S(1)}, u32[]{:S(2)}, u32[]{:S(2)}) collective-permute-start(bf16[2,2,8,16,128]{4,3,2,1,0:T(8,128)(2,1)S(1)} %get-tuple-element.82), channel_id=1, source_target_pairs={{0,6},{8,14},{2,0},{10,8},{4,2},{12,10},{6,4},{14,12},{1,7},{9,15}... | collective-permute-start | bytes 393224 | tf_op jit(solution)/shard_map/ppermute | solution.py:258
  123.2 3.2 %collective-permute-start.34 = (bf16[2,2,8,16,128]{4,3,2,1,0:T(8,128)(2,1)S(1)}, bf16[2,2,8,16,128]{4,3,2,1,0:T(8,128)(2,1)S(1)}, u32[]{:S(2)}, u32[]{:S(2)}) collective-permute-start(bf16[2,2,8,16,128]{4,3,2,1,0:T(8,128)(2,1)S(1)} %get-tuple-element.84), channel_id=1, source_target_pairs={{0,14},{8,0},{2,8},{10,2},{4,10},{12,4},{6,12},{14,6},{1,15},{9,1}... | collective-permute-start | bytes 393224 | tf_op jit(solution)/shard_map/ppermute | solution.py:258
  127.7 7.8 %collective-permute-start.17 = (bf16[2,8,128,128]{3,2,1,0:T(8,128)(2,1)S(1)}, bf16[2,8,128,128]{3,2,1,0:T(8,128)(2,1)S(1)}, u32[]{:S(2)}, u32[]{:S(2)}) collective-permute-start(bf16[2,8,128,128]{3,2,1,0:T(8,128)(2,1)S(1)} %get-tuple-element.65), channel_id=1, source_target_pairs={{0,1},{1,0},{2,3},{3,2},{4,5},{5,4},{6,7},{7,6},{8,9},{9,8},{10,11... | collective-permute-start | bytes 1572872 | tf_op jit(solution)/shard_map/ppermute | solution.py:264
  138.3 2.2 %collective-permute-start.35 = (bf16[2,8,128,128]{3,2,1,0:T(8,128)(2,1)S(1)}, bf16[2,8,128,128]{3,2,1,0:T(8,128)(2,1)S(1)}, u32[]{:S(2)}, u32[]{:S(2)}) collective-permute-start(bf16[2,8,128,128]{3,2,1,0:T(8,128)(2,1)S(1)} %get-tuple-element.86), channel_id=1, source_target_pairs={{0,1},{1,0},{2,3},{3,2},{4,5},{5,4},{6,7},{7,6},{8,9},{9,8},{10,11... | collective-permute-start | bytes 1572872 | tf_op jit(solution)/shard_map/ppermute | solution.py:264
  142.1 3.7 %invert.1 = bf16[2,8,64,1024]{3,2,1,0:T(8,128)(2,1)} custom-call(bf16[2,8,128,128]{3,2,1,0:T(8,128)(2,1)S(1)} %get-tuple-element.64.refs_8_.refs_0_, bf16[2,8,128,128]{3,2,1,0:T(8,128)(2,1)S(1)} %collective-permute-done.17.refs_1_, bf16[2,8,128,128]{3,2,1,0:T(8,128)(2,1)S(1)} %get-tuple-element.85.refs_2_, ...), custom_call_target="tpu_custom_call" | custom-call | flops 2147483648 | bytes 6291456 | tf_op jit(solution)/shard_map/invert/pallas_call | solution.py:227
  (70 shorter events, 31.1 us)
Async XLA Ops:
  9.8 15.9 %collective-permute-start = (bf16[2,14,16,128]{3,2,1,0:T(8,128)(2,1)S(1)}, bf16[2,14,16,128]{3,2,1,0:T(8,128)(2,1)S(1)}, u32[]{:S(2)}, u32[]{:S(2)}) collective-permute-start(bf16[2,14,16,128]{3,2,1,0:T(8,128)(2,1)S(1)} %get-tuple-element.47), channel_id=1, source_target_pairs={{0,4},{8,12},{2,6},{10,14},{4,0},{12,8},{6,2},{14,10},{1,5},{9,13}... | collective-permute-start | bytes 344072 | tf_op jit(solution)/shard_map/ppermute | solution.py:258
  17.6 14.9 %collective-permute-start.1 = (bf16[2,14,16,128]{3,2,1,0:T(8,128)(2,1)S(1)}, bf16[2,14,16,128]{3,2,1,0:T(8,128)(2,1)S(1)}, u32[]{:S(2)}, u32[]{:S(2)}) collective-permute-start(bf16[2,14,16,128]{3,2,1,0:T(8,128)(2,1)S(1)} %get-tuple-element.48), channel_id=1, source_target_pairs={{0,10},{8,4},{2,12},{10,6},{4,14},{12,0},{6,8},{14,2},{1,11},{9,5}... | collective-permute-start | bytes 344072 | tf_op jit(solution)/shard_map/ppermute | solution.py:258
  19.2 13.3 %collective-permute-start.2 = (bf16[2,14,16,128]{3,2,1,0:T(8,128)(2,1)S(1)}, bf16[2,14,16,128]{3,2,1,0:T(8,128)(2,1)S(1)}, u32[]{:S(2)}, u32[]{:S(2)}) collective-permute-start(bf16[2,14,16,128]{3,2,1,0:T(8,128)(2,1)S(1)} %get-tuple-element.49), channel_id=1, source_target_pairs={{0,12},{8,6},{2,14},{10,0},{4,8},{12,2},{6,10},{14,4},{1,13},{9,7}... | collective-permute-start | bytes 344072 | tf_op jit(solution)/shard_map/ppermute | solution.py:258
  23.2 15.0 %collective-permute-start.4 = (bf16[2,14,16,128]{3,2,1,0:T(8,128)(2,1)S(1)}, bf16[2,14,16,128]{3,2,1,0:T(8,128)(2,1)S(1)}, u32[]{:S(2)}, u32[]{:S(2)}) collective-permute-start(bf16[2,14,16,128]{3,2,1,0:T(8,128)(2,1)S(1)} %get-tuple-element.51), channel_id=1, source_target_pairs={{0,6},{8,14},{2,0},{10,8},{4,2},{12,10},{6,4},{14,12},{1,7},{9,15}... | collective-permute-start | bytes 344072 | tf_op jit(solution)/shard_map/ppermute | solution.py:258
  25.7 13.4 %collective-permute-start.5 = (bf16[2,14,16,128]{3,2,1,0:T(8,128)(2,1)S(1)}, bf16[2,14,16,128]{3,2,1,0:T(8,128)(2,1)S(1)}, u32[]{:S(2)}, u32[]{:S(2)}) collective-permute-start(bf16[2,14,16,128]{3,2,1,0:T(8,128)(2,1)S(1)} %get-tuple-element.52), channel_id=1, source_target_pairs={{0,8},{8,2},{2,10},{10,4},{4,12},{12,6},{6,14},{14,0},{1,9},{9,3},... | collective-permute-start | bytes 344072 | tf_op jit(solution)/shard_map/ppermute | solution.py:258
  34.4 22.1 %collective-permute-start.19 = (bf16[2,14,16,128]{3,2,1,0:T(8,128)(2,1)S(1)}, bf16[2,14,16,128]{3,2,1,0:T(8,128)(2,1)S(1)}, u32[]{:S(2)}, u32[]{:S(2)}) collective-permute-start(bf16[2,14,16,128]{3,2,1,0:T(8,128)(2,1)S(1)} %get-tuple-element.68), channel_id=1, source_target_pairs={{0,10},{8,4},{2,12},{10,6},{4,14},{12,0},{6,8},{14,2},{1,11},{9,5}... | collective-permute-start | bytes 344072 | tf_op jit(solution)/shard_map/ppermute | solution.py:258
  38.2 20.6 %collective-permute-start.20 = (bf16[2,14,16,128]{3,2,1,0:T(8,128)(2,1)S(1)}, bf16[2,14,16,128]{3,2,1,0:T(8,128)(2,1)S(1)}, u32[]{:S(2)}, u32[]{:S(2)}) collective-permute-start(bf16[2,14,16,128]{3,2,1,0:T(8,128)(2,1)S(1)} %get-tuple-element.69), channel_id=1, source_target_pairs={{0,12},{8,6},{2,14},{10,0},{4,8},{12,2},{6,10},{14,4},{1,13},{9,7}... | collective-permute-start | bytes 344072 | tf_op jit(solution)/shard_map/ppermute | solution.py:258
  39.1 20.4 %collective-permute-start.21 = (bf16[2,14,16,128]{3,2,1,0:T(8,128)(2,1)S(1)}, bf16[2,14,16,128]{3,2,1,0:T(8,128)(2,1)S(1)}, u32[]{:S(2)}, u32[]{:S(2)}) collective-permute-start(bf16[2,14,16,128]{3,2,1,0:T(8,128)(2,1)S(1)} %get-tuple-element.70), channel_id=1, source_target_pairs={{0,2},{8,10},{2,4},{10,12},{4,6},{12,14},{6,0},{14,8},{1,3},{9,11}... | collective-permute-start | bytes 344072 | tf_op jit(solution)/shard_map/ppermute | solution.py:258
  41.0 25.4 %collective-permute-start.22 = (bf16[2,14,16,128]{3,2,1,0:T(8,128)(2,1)S(1)}, bf16[2,14,16,128]{3,2,1,0:T(8,128)(2,1)S(1)}, u32[]{:S(2)}, u32[]{:S(2)}) collective-permute-start(bf16[2,14,16,128]{3,2,1,0:T(8,128)(2,1)S(1)} %get-tuple-element.71), channel_id=1, source_target_pairs={{0,6},{8,14},{2,0},{10,8},{4,2},{12,10},{6,4},{14,12},{1,7},{9,15}... | collective-permute-start | bytes 344072 | tf_op jit(solution)/shard_map/ppermute | solution.py:258
  44.2 27.3 %collective-permute-start.8 = (bf16[2,4,14,16,128]{4,3,2,1,0:T(8,128)(2,1)S(1)}, bf16[2,4,14,16,128]{4,3,2,1,0:T(8,128)(2,1)S(1)}, u32[]{:S(2)}, u32[]{:S(2)}) collective-permute-start(bf16[2,4,14,16,128]{4,3,2,1,0:T(8,128)(2,1)S(1)} %get-tuple-element.54.own0), channel_id=1, source_target_pairs={{0,16},{16,32},{32,48},{48,64},{64,80},{80,96},{96,112},{112,128},... | collective-permute-start | bytes 1376264 | tf_op jit(solution)/shard_map/ppermute | solution.py:287
  59.5 19.6 %collective-permute-start.9 = (bf16[2,4,14,16,128]{4,3,2,1,0:T(8,128)(2,1)S(1)}, bf16[2,4,14,16,128]{4,3,2,1,0:T(8,128)(2,1)S(1)}, u32[]{:S(2)}, u32[]{:S(2)}) collective-permute-start(bf16[2,4,14,16,128]{4,3,2,1,0:T(8,128)(2,1)S(1)} %get-tuple-element.55), channel_id=1, source_target_pairs={{0,17},{1,16},{16,33},{17,32},{32,49},{33,48},{48,65},{49,64},{64,... | collective-permute-start | bytes 1376264 | tf_op jit(solution)/shard_map/ppermute | solution.py:288
  67.7 22.8 %collective-permute-start.26 = (bf16[2,4,14,16,128]{4,3,2,1,0:T(8,128)(2,1)S(1)}, bf16[2,4,14,16,128]{4,3,2,1,0:T(8,128)(2,1)S(1)}, u32[]{:S(2)}, u32[]{:S(2)}) collective-permute-start(bf16[2,4,14,16,128]{4,3,2,1,0:T(8,128)(2,1)S(1)} %get-tuple-element.75.own0), channel_id=1, source_target_pairs={{0,16},{16,32},{32,48},{48,64},{64,80},{80,96},{96,112},{112,128},... | collective-permute-start | bytes 1376264 | tf_op jit(solution)/shard_map/ppermute | solution.py:287
  68.8 29.9 %collective-permute-start.27 = (bf16[2,4,14,16,128]{4,3,2,1,0:T(8,128)(2,1)S(1)}, bf16[2,4,14,16,128]{4,3,2,1,0:T(8,128)(2,1)S(1)}, u32[]{:S(2)}, u32[]{:S(2)}) collective-permute-start(bf16[2,4,14,16,128]{4,3,2,1,0:T(8,128)(2,1)S(1)} %get-tuple-element.76), channel_id=1, source_target_pairs={{0,17},{1,16},{16,33},{17,32},{32,49},{33,48},{48,65},{49,64},{64,... | collective-permute-start | bytes 1376264 | tf_op jit(solution)/shard_map/ppermute | solution.py:288
  71.6 27.2 %collective-permute-start.25 = (bf16[2,4,14,16,128]{4,3,2,1,0:T(8,128)(2,1)S(1)}, bf16[2,4,14,16,128]{4,3,2,1,0:T(8,128)(2,1)S(1)}, u32[]{:S(2)}, u32[]{:S(2)}) collective-permute-start(bf16[2,4,14,16,128]{4,3,2,1,0:T(8,128)(2,1)S(1)} %get-tuple-element.76), channel_id=1, source_target_pairs={{0,1},{1,0},{2,3},{3,2},{4,5},{5,4},{6,7},{7,6},{8,9},{9,8},{10,11... | collective-permute-start | bytes 1376264 | tf_op jit(solution)/shard_map/ppermute | solution.py:264
  84.5 23.2 %collective-permute-start.10 = (bf16[2,2,8,16,128]{4,3,2,1,0:T(8,128)(2,1)S(1)}, bf16[2,2,8,16,128]{4,3,2,1,0:T(8,128)(2,1)S(1)}, u32[]{:S(2)}, u32[]{:S(2)}) collective-permute-start(bf16[2,2,8,16,128]{4,3,2,1,0:T(8,128)(2,1)S(1)} %get-tuple-element.57), channel_id=1, source_target_pairs={{0,4},{8,12},{2,6},{10,14},{4,0},{12,8},{6,2},{14,10},{1,5},{9,13}... | collective-permute-start | bytes 393224 | tf_op jit(solution)/shard_map/ppermute | solution.py:258
  87.4 20.7 %collective-permute-start.11 = (bf16[2,2,8,16,128]{4,3,2,1,0:T(8,128)(2,1)S(1)}, bf16[2,2,8,16,128]{4,3,2,1,0:T(8,128)(2,1)S(1)}, u32[]{:S(2)}, u32[]{:S(2)}) collective-permute-start(bf16[2,2,8,16,128]{4,3,2,1,0:T(8,128)(2,1)S(1)} %get-tuple-element.58), channel_id=1, source_target_pairs={{0,10},{8,4},{2,12},{10,6},{4,14},{12,0},{6,8},{14,2},{1,11},{9,5}... | collective-permute-start | bytes 393224 | tf_op jit(solution)/shard_map/ppermute | solution.py:258
  90.5 20.2 %collective-permute-start.12 = (bf16[2,2,8,16,128]{4,3,2,1,0:T(8,128)(2,1)S(1)}, bf16[2,2,8,16,128]{4,3,2,1,0:T(8,128)(2,1)S(1)}, u32[]{:S(2)}, u32[]{:S(2)}) collective-permute-start(bf16[2,2,8,16,128]{4,3,2,1,0:T(8,128)(2,1)S(1)} %get-tuple-element.59), channel_id=1, source_target_pairs={{0,12},{8,6},{2,14},{10,0},{4,8},{12,2},{6,10},{14,4},{1,13},{9,7}... | collective-permute-start | bytes 393224 | tf_op jit(solution)/shard_map/ppermute | solution.py:258
  98.8 14.7 %collective-permute-start.13 = (bf16[2,2,8,16,128]{4,3,2,1,0:T(8,128)(2,1)S(1)}, bf16[2,2,8,16,128]{4,3,2,1,0:T(8,128)(2,1)S(1)}, u32[]{:S(2)}, u32[]{:S(2)}) collective-permute-start(bf16[2,2,8,16,128]{4,3,2,1,0:T(8,128)(2,1)S(1)} %get-tuple-element.60), channel_id=1, source_target_pairs={{0,2},{8,10},{2,4},{10,12},{4,6},{12,14},{6,0},{14,8},{1,3},{9,11}... | collective-permute-start | bytes 393224 | tf_op jit(solution)/shard_map/ppermute | solution.py:258
  98.8 15.0 %collective-permute-start.14 = (bf16[2,2,8,16,128]{4,3,2,1,0:T(8,128)(2,1)S(1)}, bf16[2,2,8,16,128]{4,3,2,1,0:T(8,128)(2,1)S(1)}, u32[]{:S(2)}, u32[]{:S(2)}) collective-permute-start(bf16[2,2,8,16,128]{4,3,2,1,0:T(8,128)(2,1)S(1)} %get-tuple-element.61), channel_id=1, source_target_pairs={{0,6},{8,14},{2,0},{10,8},{4,2},{12,10},{6,4},{14,12},{1,7},{9,15}... | collective-permute-start | bytes 393224 | tf_op jit(solution)/shard_map/ppermute | solution.py:258
  113.8 13.9 %collective-permute-start.30 = (bf16[2,2,8,16,128]{4,3,2,1,0:T(8,128)(2,1)S(1)}, bf16[2,2,8,16,128]{4,3,2,1,0:T(8,128)(2,1)S(1)}, u32[]{:S(2)}, u32[]{:S(2)}) collective-permute-start(bf16[2,2,8,16,128]{4,3,2,1,0:T(8,128)(2,1)S(1)} %get-tuple-element.80), channel_id=1, source_target_pairs={{0,12},{8,6},{2,14},{10,0},{4,8},{12,2},{6,10},{14,4},{1,13},{9,7}... | collective-permute-start | bytes 393224 | tf_op jit(solution)/shard_map/ppermute | solution.py:258
  118.0 17.6 %collective-permute-start.31 = (bf16[2,2,8,16,128]{4,3,2,1,0:T(8,128)(2,1)S(1)}, bf16[2,2,8,16,128]{4,3,2,1,0:T(8,128)(2,1)S(1)}, u32[]{:S(2)}, u32[]{:S(2)}) collective-permute-start(bf16[2,2,8,16,128]{4,3,2,1,0:T(8,128)(2,1)S(1)} %get-tuple-element.81), channel_id=1, source_target_pairs={{0,2},{8,10},{2,4},{10,12},{4,6},{12,14},{6,0},{14,8},{1,3},{9,11}... | collective-permute-start | bytes 393224 | tf_op jit(solution)/shard_map/ppermute | solution.py:258
  118.0 17.6 %collective-permute-start.32 = (bf16[2,2,8,16,128]{4,3,2,1,0:T(8,128)(2,1)S(1)}, bf16[2,2,8,16,128]{4,3,2,1,0:T(8,128)(2,1)S(1)}, u32[]{:S(2)}, u32[]{:S(2)}) collective-permute-start(bf16[2,2,8,16,128]{4,3,2,1,0:T(8,128)(2,1)S(1)} %get-tuple-element.82), channel_id=1, source_target_pairs={{0,6},{8,14},{2,0},{10,8},{4,2},{12,10},{6,4},{14,12},{1,7},{9,15}... | collective-permute-start | bytes 393224 | tf_op jit(solution)/shard_map/ppermute | solution.py:258
  122.9 14.1 %collective-permute-start.33 = (bf16[2,2,8,16,128]{4,3,2,1,0:T(8,128)(2,1)S(1)}, bf16[2,2,8,16,128]{4,3,2,1,0:T(8,128)(2,1)S(1)}, u32[]{:S(2)}, u32[]{:S(2)}) collective-permute-start(bf16[2,2,8,16,128]{4,3,2,1,0:T(8,128)(2,1)S(1)} %get-tuple-element.83), channel_id=1, source_target_pairs={{0,8},{8,2},{2,10},{10,4},{4,12},{12,6},{6,14},{14,0},{1,9},{9,3},... | collective-permute-start | bytes 393224 | tf_op jit(solution)/shard_map/ppermute | solution.py:258
  123.2 13.8 %collective-permute-start.34 = (bf16[2,2,8,16,128]{4,3,2,1,0:T(8,128)(2,1)S(1)}, bf16[2,2,8,16,128]{4,3,2,1,0:T(8,128)(2,1)S(1)}, u32[]{:S(2)}, u32[]{:S(2)}) collective-permute-start(bf16[2,2,8,16,128]{4,3,2,1,0:T(8,128)(2,1)S(1)} %get-tuple-element.84), channel_id=1, source_target_pairs={{0,14},{8,0},{2,8},{10,2},{4,10},{12,4},{6,12},{14,6},{1,15},{9,1}... | collective-permute-start | bytes 393224 | tf_op jit(solution)/shard_map/ppermute | solution.py:258
  (12 other events, 121.8 us)

commit v2 on v1

--- a/solution.py
+++ b/solution.py
@@ -57,7 +57,7 @@
     both = jnp.concatenate([re16, im16], axis=0)
     nt = (((1,), (1,)), ((), ()))
     summed = lax.dot_general(band[...], amp2, nt, preferred_element_type=F32)
-    scale = flags_ref[0] / (summed * invc[...] + 1e-05)
+    scale = flags_ref[0].astype(F32) / (summed * invc[...] + 1e-05)
     for h in range(2):
         half = lax.dot_general(
             eye[...], both[:, h * 256 : (h + 1) * 256], nt, preferred_element_type=F32
@@ -265,7 +265,10 @@
 
 
 def round_ring(pieces):
-    return [ring(pieces[r], r) if r else pieces[0] for r in ORDER]
+    got = []
+    for r in ORDER:
+        got.append(ring(pieces[r], r) if r else pieces[0])
+    return got
 
 
 def shards(spectra, valid_flags):
@@ -273,8 +276,7 @@
     pos = jnp.stack([z, lax.axis_index("c")]).astype(jnp.int32)
     windows = spectra.shape[0] * lax.axis_size(("zh", "c"))
     scaling = 1.0 / math.sqrt(windows * BINS)
-    flags = valid_flags.astype(F32)
-    flags2 = jnp.concatenate([flags, flags], axis=1)[:, None, :]
+    flags2 = jnp.concatenate([valid_flags, valid_flags], axis=1)[:, None, :]
     white = whiten(jnp.transpose(spectra, (2, 0, 1, 3)), flags2, pos)
     up = [(i, (i + 1) % 16) for i in range(16)]
     swap = [(2 * i + k, 2 * j + 1 - k) for i, j in up for k in range(2)]

time: 146 us -> 146 us (level)
  no operation moved by 1% of the time
where the time goes in v2:
time: 146 us
  starting transfers between devices  78.8 us (54%)
  waiting for transfers between devices  26.6 us (18%)
  Pallas kernels  26.3 us (18%)
  other arithmetic  12 us (8%)
  local copies, waits for them, and re-layouts  1.89 us (1%)
    ppermute x28, starting transfers between devices, ring(): lax.ppermute(value, ('zl', 'zh'), [(place(z), place((z + shift) % 8)) for...  56.6 us
    ppermute x2, waiting for transfers between devices, shards(): prev1 = lax.ppermute(other, ('x', 'y', 'c'), swap)  14.4 us
    another operation x1, other arithmetic  10.9 us
    pallas_call x2, Pallas kernels, cross(): pl.pallas_call(cross_kernel, out_shape=[shape] * 8, in_specs=[SM] + [VM]...  10.8 us
    ppermute x4, starting transfers between devices, other_core(): return lax.ppermute(value, 'c', [(0, 1), (1, 0)])  10 us
    ppermute x2, starting transfers between devices, shards(): prev1 = lax.ppermute(other, ('x', 'y', 'c'), swap)  9.71 us
    ppermute x28, waiting for transfers between devices, ring(): lax.ppermute(value, ('zl', 'zh'), [(place(z), place((z + shift) % 8)) for...  9.22 us
    pallas_call x1, Pallas kernels, whiten(): pl.pallas_call(whiten_kernel, out_shape=[shape] * (8 * CHUNKS), grid_spec...  6.98 us
  transfers between devices with their start and end apart: 36, of which 8 were waited for; matrix products, arithmetic and copies ran while one was open for 8% of the time, Pallas kernels for 11%

profile of v2, /device:TPU:1, one launch (start us, length us, event | category | flops | bytes accessed | tf_op | source)
XLA Modules:
  0.0 145.8 jit_solution(18279472730068457182)
XLA Ops:
  2.8 7.0 %whiten.1 = (bf16[2,14,16,128]{3,2,1,0:T(8,128)(2,1)S(1)}, bf16[2,14,16,128]{3,2,1,0:T(8,128)(2,1)S(1)}, bf16[2,14,16,128]{3,2,1,0:T(8,128)(2,1)S(1)}, bf16[2,14...) custom-call(s32[2]{0:T(128)S(1)} %pad_add_fusion.1.pos_ref, ...), custom_call_target="tpu_custom_call" | custom-call | flops 1409286144 | bytes 4194304 | tf_op jit(solution)/shard_map/whiten/pallas_call | solution.py:77
  9.8 7.8 %collective-permute-start = (bf16[2,14,16,128]{3,2,1,0:T(8,128)(2,1)S(1)}, bf16[2,14,16,128]{3,2,1,0:T(8,128)(2,1)S(1)}, u32[]{:S(2)}, u32[]{:S(2)}) collective-permute-start(bf16[2,14,16,128]{3,2,1,0:T(8,128)(2,1)S(1)} %get-tuple-element.47), channel_id=1, source_target_pairs={{0,4},{8,12},{2,6},{10,14},{4,0},{12,8},{6,2},{14,10},{1,5},{9,13}... | collective-permute-start | bytes 344072 | tf_op jit(solution)/shard_map/ppermute | solution.py:258
  19.3 2.8 %collective-permute-start.2 = (bf16[2,14,16,128]{3,2,1,0:T(8,128)(2,1)S(1)}, bf16[2,14,16,128]{3,2,1,0:T(8,128)(2,1)S(1)}, u32[]{:S(2)}, u32[]{:S(2)}) collective-permute-start(bf16[2,14,16,128]{3,2,1,0:T(8,128)(2,1)S(1)} %get-tuple-element.49), channel_id=1, source_target_pairs={{0,12},{8,6},{2,14},{10,0},{4,8},{12,2},{6,10},{14,4},{1,13},{9,7}... | collective-permute-start | bytes 344072 | tf_op jit(solution)/shard_map/ppermute | solution.py:258
  23.3 2.4 %collective-permute-start.4 = (bf16[2,14,16,128]{3,2,1,0:T(8,128)(2,1)S(1)}, bf16[2,14,16,128]{3,2,1,0:T(8,128)(2,1)S(1)}, u32[]{:S(2)}, u32[]{:S(2)}) collective-permute-start(bf16[2,14,16,128]{3,2,1,0:T(8,128)(2,1)S(1)} %get-tuple-element.51), channel_id=1, source_target_pairs={{0,6},{8,14},{2,0},{10,8},{4,2},{12,10},{6,4},{14,12},{1,7},{9,15}... | collective-permute-start | bytes 344072 | tf_op jit(solution)/shard_map/ppermute | solution.py:258
  26.6 6.0 %collective-permute-done.1.refs_2_ = bf16[2,14,16,128]{3,2,1,0:T(8,128)(2,1)S(1)} collective-permute-done((bf16[2,14,16,128]{3,2,1,0:T(8,128)(2,1)S(1)}, bf16[2,14,16,128]{3,2,1,0:T(8,128)(2,1)S(1)}, u32[]{:S(2)}, u32[]{:S(2)}) %collective-permute-start.1) | collective-permute-done | bytes 114720 | tf_op jit(solution)/shard_map/ppermute | solution.py:258
  34.5 3.7 %collective-permute-start.19 = (bf16[2,14,16,128]{3,2,1,0:T(8,128)(2,1)S(1)}, bf16[2,14,16,128]{3,2,1,0:T(8,128)(2,1)S(1)}, u32[]{:S(2)}, u32[]{:S(2)}) collective-permute-start(bf16[2,14,16,128]{3,2,1,0:T(8,128)(2,1)S(1)} %get-tuple-element.68), channel_id=1, source_target_pairs={{0,10},{8,4},{2,12},{10,6},{4,14},{12,0},{6,8},{14,2},{1,11},{9,5}... | collective-permute-start | bytes 344072 | tf_op jit(solution)/shard_map/ppermute | solution.py:258
  45.7 10.9 %cosine_convert_fusion = (bf16[512,1024]{1,0:T(8,128)(2,1)S(1)}, bf16[512,1024]{1,0:T(8,128)(2,1)S(1)}) fusion(s32[1024]{0:T(1024)S(1)} %iota_add_fusion, s32[512]{0:T(512)S(1)} %get-tuple-element.90, s32[512]{0:T(512)S(1)} %get-tuple-element.93, pred[512]{0:T(512)(128)(4,1)S(1)} %get-tuple-element.97, s32[]{:T(128)} %bitcast.3, ...), kind=kLoop, calls=%fused_computation.26 | loop fusion | flops 24117248 | bytes 2119684 | tf_op jit(solution)/shard_map/convert
  56.6 2.2 %collective-permute-start.23 = (bf16[2,14,16,128]{3,2,1,0:T(8,128)(2,1)S(1)}, bf16[2,14,16,128]{3,2,1,0:T(8,128)(2,1)S(1)}, u32[]{:S(2)}, u32[]{:S(2)}) collective-permute-start(bf16[2,14,16,128]{3,2,1,0:T(8,128)(2,1)S(1)} %get-tuple-element.72), channel_id=1, source_target_pairs={{0,8},{8,2},{2,10},{10,4},{4,12},{12,6},{6,14},{14,0},{1,9},{9,3},... | collective-permute-start | bytes 344072 | tf_op jit(solution)/shard_map/ppermute | solution.py:258
  59.6 7.0 %collective-permute-start.9 = (bf16[2,4,14,16,128]{4,3,2,1,0:T(8,128)(2,1)S(1)}, bf16[2,4,14,16,128]{4,3,2,1,0:T(8,128)(2,1)S(1)}, u32[]{:S(2)}, u32[]{:S(2)}) collective-permute-start(bf16[2,4,14,16,128]{4,3,2,1,0:T(8,128)(2,1)S(1)} %get-tuple-element.55), channel_id=1, source_target_pairs={{0,17},{1,16},{16,33},{17,32},{32,49},{33,48},{48,65},{49,64},{64,... | collective-permute-start | bytes 1376264 | tf_op jit(solution)/shard_map/ppermute | solution.py:290
  68.9 2.7 %collective-permute-start.27 = (bf16[2,4,14,16,128]{4,3,2,1,0:T(8,128)(2,1)S(1)}, bf16[2,4,14,16,128]{4,3,2,1,0:T(8,128)(2,1)S(1)}, u32[]{:S(2)}, u32[]{:S(2)}) collective-permute-start(bf16[2,4,14,16,128]{4,3,2,1,0:T(8,128)(2,1)S(1)} %get-tuple-element.76), channel_id=1, source_target_pairs={{0,17},{1,16},{16,33},{17,32},{32,49},{33,48},{48,65},{49,64},{64,... | collective-permute-start | bytes 1376264 | tf_op jit(solution)/shard_map/ppermute | solution.py:290
  71.7 7.5 %collective-permute-done.9.prev1 = bf16[2,4,14,16,128]{4,3,2,1,0:T(8,128)(2,1)S(1)} collective-permute-done((bf16[2,4,14,16,128]{4,3,2,1,0:T(8,128)(2,1)S(1)}, bf16[2,4,14,16,128]{4,3,2,1,0:T(8,128)(2,1)S(1)}, u32[]{:S(2)}, u32[]{:S(2)}) %collective-permute-start.9) | collective-permute-done | bytes 458784 | tf_op jit(solution)/shard_map/ppermute | solution.py:290
  79.2 5.4 %cross.2 = (bf16[2,2,8,16,128]{4,3,2,1,0:T(8,128)(2,1)S(1)}, bf16[2,2,8,16,128]{4,3,2,1,0:T(8,128)(2,1)S(1)}, bf16[2,2,8,16,128]{4,3,2,1,0:T(8,128)(2,1)S(1)}, b...) custom-call(s32[2]{0:T(128)S(1)} %pad_add_fusion.1.pos_ref, ...), custom_call_target="tpu_custom_call" | custom-call | flops 536870912 | bytes 3145728 | tf_op jit(solution)/shard_map/cross/pallas_call | solution.py:171
  84.6 2.9 %collective-permute-start.10 = (bf16[2,2,8,16,128]{4,3,2,1,0:T(8,128)(2,1)S(1)}, bf16[2,2,8,16,128]{4,3,2,1,0:T(8,128)(2,1)S(1)}, u32[]{:S(2)}, u32[]{:S(2)}) collective-permute-start(bf16[2,2,8,16,128]{4,3,2,1,0:T(8,128)(2,1)S(1)} %get-tuple-element.57), channel_id=1, source_target_pairs={{0,4},{8,12},{2,6},{10,14},{4,0},{12,8},{6,2},{14,10},{1,5},{9,13}... | collective-permute-start | bytes 393224 | tf_op jit(solution)/shard_map/ppermute | solution.py:258
  91.9 6.9 %collective-permute-done.27.prev1 = bf16[2,4,14,16,128]{4,3,2,1,0:T(8,128)(2,1)S(1)} collective-permute-done((bf16[2,4,14,16,128]{4,3,2,1,0:T(8,128)(2,1)S(1)}, bf16[2,4,14,16,128]{4,3,2,1,0:T(8,128)(2,1)S(1)}, u32[]{:S(2)}, u32[]{:S(2)}) %collective-permute-start.27) | collective-permute-done | bytes 458784 | tf_op jit(solution)/shard_map/ppermute | solution.py:290
  98.8 3.6 %collective-permute-start.14 = (bf16[2,2,8,16,128]{4,3,2,1,0:T(8,128)(2,1)S(1)}, bf16[2,2,8,16,128]{4,3,2,1,0:T(8,128)(2,1)S(1)}, u32[]{:S(2)}, u32[]{:S(2)}) collective-permute-start(bf16[2,2,8,16,128]{4,3,2,1,0:T(8,128)(2,1)S(1)} %get-tuple-element.61), channel_id=1, source_target_pairs={{0,6},{8,14},{2,0},{10,8},{4,2},{12,10},{6,4},{14,12},{1,7},{9,15}... | collective-permute-start | bytes 393224 | tf_op jit(solution)/shard_map/ppermute | solution.py:258
  102.4 5.4 %cross.3 = (bf16[2,2,8,16,128]{4,3,2,1,0:T(8,128)(2,1)S(1)}, bf16[2,2,8,16,128]{4,3,2,1,0:T(8,128)(2,1)S(1)}, bf16[2,2,8,16,128]{4,3,2,1,0:T(8,128)(2,1)S(1)}, b...) custom-call(s32[2]{0:T(128)S(1)} %pad_add_fusion.1.pos_ref, ...), custom_call_target="tpu_custom_call" | custom-call | flops 536870912 | bytes 3145728 | tf_op jit(solution)/shard_map/cross/pallas_call | solution.py:171
  108.1 2.7 %collective-permute-start.16 = (bf16[2,2,8,16,128]{4,3,2,1,0:T(8,128)(2,1)S(1)}, bf16[2,2,8,16,128]{4,3,2,1,0:T(8,128)(2,1)S(1)}, u32[]{:S(2)}, u32[]{:S(2)}) collective-permute-start(bf16[2,2,8,16,128]{4,3,2,1,0:T(8,128)(2,1)S(1)} %get-tuple-element.63), channel_id=1, source_target_pairs={{0,14},{8,0},{2,8},{10,2},{4,10},{12,4},{6,12},{14,6},{1,15},{9,1}... | collective-permute-start | bytes 393224 | tf_op jit(solution)/shard_map/ppermute | solution.py:258
  110.8 2.8 %collective-permute-start.28 = (bf16[2,2,8,16,128]{4,3,2,1,0:T(8,128)(2,1)S(1)}, bf16[2,2,8,16,128]{4,3,2,1,0:T(8,128)(2,1)S(1)}, u32[]{:S(2)}, u32[]{:S(2)}) collective-permute-start(bf16[2,2,8,16,128]{4,3,2,1,0:T(8,128)(2,1)S(1)} %get-tuple-element.78), channel_id=1, source_target_pairs={{0,4},{8,12},{2,6},{10,14},{4,0},{12,8},{6,2},{14,10},{1,5},{9,13}... | collective-permute-start | bytes 393224 | tf_op jit(solution)/shard_map/ppermute | solution.py:258
  113.9 4.2 %collective-permute-start.30 = (bf16[2,2,8,16,128]{4,3,2,1,0:T(8,128)(2,1)S(1)}, bf16[2,2,8,16,128]{4,3,2,1,0:T(8,128)(2,1)S(1)}, u32[]{:S(2)}, u32[]{:S(2)}) collective-permute-start(bf16[2,2,8,16,128]{4,3,2,1,0:T(8,128)(2,1)S(1)} %get-tuple-element.80), channel_id=1, source_target_pairs={{0,12},{8,6},{2,14},{10,0},{4,8},{12,2},{6,10},{14,4},{1,13},{9,7}... | collective-permute-start | bytes 393224 | tf_op jit(solution)/shard_map/ppermute | solution.py:258
  118.1 3.6 %collective-permute-start.32 = (bf16[2,2,8,16,128]{4,3,2,1,0:T(8,128)(2,1)S(1)}, bf16[2,2,8,16,128]{4,3,2,1,0:T(8,128)(2,1)S(1)}, u32[]{:S(2)}, u32[]{:S(2)}) collective-permute-start(bf16[2,2,8,16,128]{4,3,2,1,0:T(8,128)(2,1)S(1)} %get-tuple-element.82), channel_id=1, source_target_pairs={{0,6},{8,14},{2,0},{10,8},{4,2},{12,10},{6,4},{14,12},{1,7},{9,15}... | collective-permute-start | bytes 393224 | tf_op jit(solution)/shard_map/ppermute | solution.py:258
  123.3 3.1 %collective-permute-start.34 = (bf16[2,2,8,16,128]{4,3,2,1,0:T(8,128)(2,1)S(1)}, bf16[2,2,8,16,128]{4,3,2,1,0:T(8,128)(2,1)S(1)}, u32[]{:S(2)}, u32[]{:S(2)}) collective-permute-start(bf16[2,2,8,16,128]{4,3,2,1,0:T(8,128)(2,1)S(1)} %get-tuple-element.84), channel_id=1, source_target_pairs={{0,14},{8,0},{2,8},{10,2},{4,10},{12,4},{6,12},{14,6},{1,15},{9,1}... | collective-permute-start | bytes 393224 | tf_op jit(solution)/shard_map/ppermute | solution.py:258
  127.8 7.8 %collective-permute-start.17 = (bf16[2,8,128,128]{3,2,1,0:T(8,128)(2,1)S(1)}, bf16[2,8,128,128]{3,2,1,0:T(8,128)(2,1)S(1)}, u32[]{:S(2)}, u32[]{:S(2)}) collective-permute-start(bf16[2,8,128,128]{3,2,1,0:T(8,128)(2,1)S(1)} %get-tuple-element.65), channel_id=1, source_target_pairs={{0,1},{1,0},{2,3},{3,2},{4,5},{5,4},{6,7},{7,6},{8,9},{9,8},{10,11... | collective-permute-start | bytes 1572872 | tf_op jit(solution)/shard_map/ppermute | solution.py:264
  138.4 2.2 %collective-permute-start.35 = (bf16[2,8,128,128]{3,2,1,0:T(8,128)(2,1)S(1)}, bf16[2,8,128,128]{3,2,1,0:T(8,128)(2,1)S(1)}, u32[]{:S(2)}, u32[]{:S(2)}) collective-permute-start(bf16[2,8,128,128]{3,2,1,0:T(8,128)(2,1)S(1)} %get-tuple-element.86), channel_id=1, source_target_pairs={{0,1},{1,0},{2,3},{3,2},{4,5},{5,4},{6,7},{7,6},{8,9},{9,8},{10,11... | collective-permute-start | bytes 1572872 | tf_op jit(solution)/shard_map/ppermute | solution.py:264
  142.1 3.7 %invert.1 = bf16[2,8,64,1024]{3,2,1,0:T(8,128)(2,1)} custom-call(bf16[2,8,128,128]{3,2,1,0:T(8,128)(2,1)S(1)} %get-tuple-element.64.refs_8_.refs_0_, bf16[2,8,128,128]{3,2,1,0:T(8,128)(2,1)S(1)} %collective-permute-done.17.refs_1_, bf16[2,8,128,128]{3,2,1,0:T(8,128)(2,1)S(1)} %get-tuple-element.85.refs_2_, ...), custom_call_target="tpu_custom_call" | custom-call | flops 2147483648 | bytes 6291456 | tf_op jit(solution)/shard_map/invert/pallas_call | solution.py:227
  (69 shorter events, 31.3 us)
Async XLA Ops:
  9.8 15.9 %collective-permute-start = (bf16[2,14,16,128]{3,2,1,0:T(8,128)(2,1)S(1)}, bf16[2,14,16,128]{3,2,1,0:T(8,128)(2,1)S(1)}, u32[]{:S(2)}, u32[]{:S(2)}) collective-permute-start(bf16[2,14,16,128]{3,2,1,0:T(8,128)(2,1)S(1)} %get-tuple-element.47), channel_id=1, source_target_pairs={{0,4},{8,12},{2,6},{10,14},{4,0},{12,8},{6,2},{14,10},{1,5},{9,13}... | collective-permute-start | bytes 344072 | tf_op jit(solution)/shard_map/ppermute | solution.py:258
  17.6 15.0 %collective-permute-start.1 = (bf16[2,14,16,128]{3,2,1,0:T(8,128)(2,1)S(1)}, bf16[2,14,16,128]{3,2,1,0:T(8,128)(2,1)S(1)}, u32[]{:S(2)}, u32[]{:S(2)}) collective-permute-start(bf16[2,14,16,128]{3,2,1,0:T(8,128)(2,1)S(1)} %get-tuple-element.48), channel_id=1, source_target_pairs={{0,10},{8,4},{2,12},{10,6},{4,14},{12,0},{6,8},{14,2},{1,11},{9,5}... | collective-permute-start | bytes 344072 | tf_op jit(solution)/shard_map/ppermute | solution.py:258
  19.3 13.3 %collective-permute-start.2 = (bf16[2,14,16,128]{3,2,1,0:T(8,128)(2,1)S(1)}, bf16[2,14,16,128]{3,2,1,0:T(8,128)(2,1)S(1)}, u32[]{:S(2)}, u32[]{:S(2)}) collective-permute-start(bf16[2,14,16,128]{3,2,1,0:T(8,128)(2,1)S(1)} %get-tuple-element.49), channel_id=1, source_target_pairs={{0,12},{8,6},{2,14},{10,0},{4,8},{12,2},{6,10},{14,4},{1,13},{9,7}... | collective-permute-start | bytes 344072 | tf_op jit(solution)/shard_map/ppermute | solution.py:258
  23.3 15.0 %collective-permute-start.4 = (bf16[2,14,16,128]{3,2,1,0:T(8,128)(2,1)S(1)}, bf16[2,14,16,128]{3,2,1,0:T(8,128)(2,1)S(1)}, u32[]{:S(2)}, u32[]{:S(2)}) collective-permute-start(bf16[2,14,16,128]{3,2,1,0:T(8,128)(2,1)S(1)} %get-tuple-element.51), channel_id=1, source_target_pairs={{0,6},{8,14},{2,0},{10,8},{4,2},{12,10},{6,4},{14,12},{1,7},{9,15}... | collective-permute-start | bytes 344072 | tf_op jit(solution)/shard_map/ppermute | solution.py:258
  25.7 13.4 %collective-permute-start.5 = (bf16[2,14,16,128]{3,2,1,0:T(8,128)(2,1)S(1)}, bf16[2,14,16,128]{3,2,1,0:T(8,128)(2,1)S(1)}, u32[]{:S(2)}, u32[]{:S(2)}) collective-permute-start(bf16[2,14,16,128]{3,2,1,0:T(8,128)(2,1)S(1)} %get-tuple-element.52), channel_id=1, source_target_pairs={{0,8},{8,2},{2,10},{10,4},{4,12},{12,6},{6,14},{14,0},{1,9},{9,3},... | collective-permute-start | bytes 344072 | tf_op jit(solution)/shard_map/ppermute | solution.py:258
  34.5 22.1 %collective-permute-start.19 = (bf16[2,14,16,128]{3,2,1,0:T(8,128)(2,1)S(1)}, bf16[2,14,16,128]{3,2,1,0:T(8,128)(2,1)S(1)}, u32[]{:S(2)}, u32[]{:S(2)}) collective-permute-start(bf16[2,14,16,128]{3,2,1,0:T(8,128)(2,1)S(1)} %get-tuple-element.68), channel_id=1, source_target_pairs={{0,10},{8,4},{2,12},{10,6},{4,14},{12,0},{6,8},{14,2},{1,11},{9,5}... | collective-permute-start | bytes 344072 | tf_op jit(solution)/shard_map/ppermute | solution.py:258
  38.3 20.6 %collective-permute-start.20 = (bf16[2,14,16,128]{3,2,1,0:T(8,128)(2,1)S(1)}, bf16[2,14,16,128]{3,2,1,0:T(8,128)(2,1)S(1)}, u32[]{:S(2)}, u32[]{:S(2)}) collective-permute-start(bf16[2,14,16,128]{3,2,1,0:T(8,128)(2,1)S(1)} %get-tuple-element.69), channel_id=1, source_target_pairs={{0,12},{8,6},{2,14},{10,0},{4,8},{12,2},{6,10},{14,4},{1,13},{9,7}... | collective-permute-start | bytes 344072 | tf_op jit(solution)/shard_map/ppermute | solution.py:258
  39.2 20.4 %collective-permute-start.21 = (bf16[2,14,16,128]{3,2,1,0:T(8,128)(2,1)S(1)}, bf16[2,14,16,128]{3,2,1,0:T(8,128)(2,1)S(1)}, u32[]{:S(2)}, u32[]{:S(2)}) collective-permute-start(bf16[2,14,16,128]{3,2,1,0:T(8,128)(2,1)S(1)} %get-tuple-element.70), channel_id=1, source_target_pairs={{0,2},{8,10},{2,4},{10,12},{4,6},{12,14},{6,0},{14,8},{1,3},{9,11}... | collective-permute-start | bytes 344072 | tf_op jit(solution)/shard_map/ppermute | solution.py:258
  41.1 25.5 %collective-permute-start.22 = (bf16[2,14,16,128]{3,2,1,0:T(8,128)(2,1)S(1)}, bf16[2,14,16,128]{3,2,1,0:T(8,128)(2,1)S(1)}, u32[]{:S(2)}, u32[]{:S(2)}) collective-permute-start(bf16[2,14,16,128]{3,2,1,0:T(8,128)(2,1)S(1)} %get-tuple-element.71), channel_id=1, source_target_pairs={{0,6},{8,14},{2,0},{10,8},{4,2},{12,10},{6,4},{14,12},{1,7},{9,15}... | collective-permute-start | bytes 344072 | tf_op jit(solution)/shard_map/ppermute | solution.py:258
  44.3 27.4 %collective-permute-start.8 = (bf16[2,4,14,16,128]{4,3,2,1,0:T(8,128)(2,1)S(1)}, bf16[2,4,14,16,128]{4,3,2,1,0:T(8,128)(2,1)S(1)}, u32[]{:S(2)}, u32[]{:S(2)}) collective-permute-start(bf16[2,4,14,16,128]{4,3,2,1,0:T(8,128)(2,1)S(1)} %get-tuple-element.54.own0), channel_id=1, source_target_pairs={{0,16},{16,32},{32,48},{48,64},{64,80},{80,96},{96,112},{112,128},... | collective-permute-start | bytes 1376264 | tf_op jit(solution)/shard_map/ppermute | solution.py:289
  59.6 19.6 %collective-permute-start.9 = (bf16[2,4,14,16,128]{4,3,2,1,0:T(8,128)(2,1)S(1)}, bf16[2,4,14,16,128]{4,3,2,1,0:T(8,128)(2,1)S(1)}, u32[]{:S(2)}, u32[]{:S(2)}) collective-permute-start(bf16[2,4,14,16,128]{4,3,2,1,0:T(8,128)(2,1)S(1)} %get-tuple-element.55), channel_id=1, source_target_pairs={{0,17},{1,16},{16,33},{17,32},{32,49},{33,48},{48,65},{49,64},{64,... | collective-permute-start | bytes 1376264 | tf_op jit(solution)/shard_map/ppermute | solution.py:290
  67.8 22.8 %collective-permute-start.26 = (bf16[2,4,14,16,128]{4,3,2,1,0:T(8,128)(2,1)S(1)}, bf16[2,4,14,16,128]{4,3,2,1,0:T(8,128)(2,1)S(1)}, u32[]{:S(2)}, u32[]{:S(2)}) collective-permute-start(bf16[2,4,14,16,128]{4,3,2,1,0:T(8,128)(2,1)S(1)} %get-tuple-element.75.own0), channel_id=1, source_target_pairs={{0,16},{16,32},{32,48},{48,64},{64,80},{80,96},{96,112},{112,128},... | collective-permute-start | bytes 1376264 | tf_op jit(solution)/shard_map/ppermute | solution.py:289
  68.9 29.9 %collective-permute-start.27 = (bf16[2,4,14,16,128]{4,3,2,1,0:T(8,128)(2,1)S(1)}, bf16[2,4,14,16,128]{4,3,2,1,0:T(8,128)(2,1)S(1)}, u32[]{:S(2)}, u32[]{:S(2)}) collective-permute-start(bf16[2,4,14,16,128]{4,3,2,1,0:T(8,128)(2,1)S(1)} %get-tuple-element.76), channel_id=1, source_target_pairs={{0,17},{1,16},{16,33},{17,32},{32,49},{33,48},{48,65},{49,64},{64,... | collective-permute-start | bytes 1376264 | tf_op jit(solution)/shard_map/ppermute | solution.py:290
  71.7 27.2 %collective-permute-start.25 = (bf16[2,4,14,16,128]{4,3,2,1,0:T(8,128)(2,1)S(1)}, bf16[2,4,14,16,128]{4,3,2,1,0:T(8,128)(2,1)S(1)}, u32[]{:S(2)}, u32[]{:S(2)}) collective-permute-start(bf16[2,4,14,16,128]{4,3,2,1,0:T(8,128)(2,1)S(1)} %get-tuple-element.76), channel_id=1, source_target_pairs={{0,1},{1,0},{2,3},{3,2},{4,5},{5,4},{6,7},{7,6},{8,9},{9,8},{10,11... | collective-permute-start | bytes 1376264 | tf_op jit(solution)/shard_map/ppermute | solution.py:264
  84.6 23.2 %collective-permute-start.10 = (bf16[2,2,8,16,128]{4,3,2,1,0:T(8,128)(2,1)S(1)}, bf16[2,2,8,16,128]{4,3,2,1,0:T(8,128)(2,1)S(1)}, u32[]{:S(2)}, u32[]{:S(2)}) collective-permute-start(bf16[2,2,8,16,128]{4,3,2,1,0:T(8,128)(2,1)S(1)} %get-tuple-element.57), channel_id=1, source_target_pairs={{0,4},{8,12},{2,6},{10,14},{4,0},{12,8},{6,2},{14,10},{1,5},{9,13}... | collective-permute-start | bytes 393224 | tf_op jit(solution)/shard_map/ppermute | solution.py:258
  87.4 20.7 %collective-permute-start.11 = (bf16[2,2,8,16,128]{4,3,2,1,0:T(8,128)(2,1)S(1)}, bf16[2,2,8,16,128]{4,3,2,1,0:T(8,128)(2,1)S(1)}, u32[]{:S(2)}, u32[]{:S(2)}) collective-permute-start(bf16[2,2,8,16,128]{4,3,2,1,0:T(8,128)(2,1)S(1)} %get-tuple-element.58), channel_id=1, source_target_pairs={{0,10},{8,4},{2,12},{10,6},{4,14},{12,0},{6,8},{14,2},{1,11},{9,5}... | collective-permute-start | bytes 393224 | tf_op jit(solution)/shard_map/ppermute | solution.py:258
  90.7 20.1 %collective-permute-start.12 = (bf16[2,2,8,16,128]{4,3,2,1,0:T(8,128)(2,1)S(1)}, bf16[2,2,8,16,128]{4,3,2,1,0:T(8,128)(2,1)S(1)}, u32[]{:S(2)}, u32[]{:S(2)}) collective-permute-start(bf16[2,2,8,16,128]{4,3,2,1,0:T(8,128)(2,1)S(1)} %get-tuple-element.59), channel_id=1, source_target_pairs={{0,12},{8,6},{2,14},{10,0},{4,8},{12,2},{6,10},{14,4},{1,13},{9,7}... | collective-permute-start | bytes 393224 | tf_op jit(solution)/shard_map/ppermute | solution.py:258
  98.8 14.8 %collective-permute-start.13 = (bf16[2,2,8,16,128]{4,3,2,1,0:T(8,128)(2,1)S(1)}, bf16[2,2,8,16,128]{4,3,2,1,0:T(8,128)(2,1)S(1)}, u32[]{:S(2)}, u32[]{:S(2)}) collective-permute-start(bf16[2,2,8,16,128]{4,3,2,1,0:T(8,128)(2,1)S(1)} %get-tuple-element.60), channel_id=1, source_target_pairs={{0,2},{8,10},{2,4},{10,12},{4,6},{12,14},{6,0},{14,8},{1,3},{9,11}... | collective-permute-start | bytes 393224 | tf_op jit(solution)/shard_map/ppermute | solution.py:258
  98.8 15.0 %collective-permute-start.14 = (bf16[2,2,8,16,128]{4,3,2,1,0:T(8,128)(2,1)S(1)}, bf16[2,2,8,16,128]{4,3,2,1,0:T(8,128)(2,1)S(1)}, u32[]{:S(2)}, u32[]{:S(2)}) collective-permute-start(bf16[2,2,8,16,128]{4,3,2,1,0:T(8,128)(2,1)S(1)} %get-tuple-element.61), channel_id=1, source_target_pairs={{0,6},{8,14},{2,0},{10,8},{4,2},{12,10},{6,4},{14,12},{1,7},{9,15}... | collective-permute-start | bytes 393224 | tf_op jit(solution)/shard_map/ppermute | solution.py:258
  113.9 13.9 %collective-permute-start.30 = (bf16[2,2,8,16,128]{4,3,2,1,0:T(8,128)(2,1)S(1)}, bf16[2,2,8,16,128]{4,3,2,1,0:T(8,128)(2,1)S(1)}, u32[]{:S(2)}, u32[]{:S(2)}) collective-permute-start(bf16[2,2,8,16,128]{4,3,2,1,0:T(8,128)(2,1)S(1)} %get-tuple-element.80), channel_id=1, source_target_pairs={{0,12},{8,6},{2,14},{10,0},{4,8},{12,2},{6,10},{14,4},{1,13},{9,7}... | collective-permute-start | bytes 393224 | tf_op jit(solution)/shard_map/ppermute | solution.py:258
  118.1 17.5 %collective-permute-start.31 = (bf16[2,2,8,16,128]{4,3,2,1,0:T(8,128)(2,1)S(1)}, bf16[2,2,8,16,128]{4,3,2,1,0:T(8,128)(2,1)S(1)}, u32[]{:S(2)}, u32[]{:S(2)}) collective-permute-start(bf16[2,2,8,16,128]{4,3,2,1,0:T(8,128)(2,1)S(1)} %get-tuple-element.81), channel_id=1, source_target_pairs={{0,2},{8,10},{2,4},{10,12},{4,6},{12,14},{6,0},{14,8},{1,3},{9,11}... | collective-permute-start | bytes 393224 | tf_op jit(solution)/shard_map/ppermute | solution.py:258
  118.1 17.5 %collective-permute-start.32 = (bf16[2,2,8,16,128]{4,3,2,1,0:T(8,128)(2,1)S(1)}, bf16[2,2,8,16,128]{4,3,2,1,0:T(8,128)(2,1)S(1)}, u32[]{:S(2)}, u32[]{:S(2)}) collective-permute-start(bf16[2,2,8,16,128]{4,3,2,1,0:T(8,128)(2,1)S(1)} %get-tuple-element.82), channel_id=1, source_target_pairs={{0,6},{8,14},{2,0},{10,8},{4,2},{12,10},{6,4},{14,12},{1,7},{9,15}... | collective-permute-start | bytes 393224 | tf_op jit(solution)/shard_map/ppermute | solution.py:258
  122.9 14.1 %collective-permute-start.33 = (bf16[2,2,8,16,128]{4,3,2,1,0:T(8,128)(2,1)S(1)}, bf16[2,2,8,16,128]{4,3,2,1,0:T(8,128)(2,1)S(1)}, u32[]{:S(2)}, u32[]{:S(2)}) collective-permute-start(bf16[2,2,8,16,128]{4,3,2,1,0:T(8,128)(2,1)S(1)} %get-tuple-element.83), channel_id=1, source_target_pairs={{0,8},{8,2},{2,10},{10,4},{4,12},{12,6},{6,14},{14,0},{1,9},{9,3},... | collective-permute-start | bytes 393224 | tf_op jit(solution)/shard_map/ppermute | solution.py:258
  123.3 13.8 %collective-permute-start.34 = (bf16[2,2,8,16,128]{4,3,2,1,0:T(8,128)(2,1)S(1)}, bf16[2,2,8,16,128]{4,3,2,1,0:T(8,128)(2,1)S(1)}, u32[]{:S(2)}, u32[]{:S(2)}) collective-permute-start(bf16[2,2,8,16,128]{4,3,2,1,0:T(8,128)(2,1)S(1)} %get-tuple-element.84), channel_id=1, source_target_pairs={{0,14},{8,0},{2,8},{10,2},{4,10},{12,4},{6,12},{14,6},{1,15},{9,1}... | collective-permute-start | bytes 393224 | tf_op jit(solution)/shard_map/ppermute | solution.py:258
  (12 other events, 121.7 us)

commit v3 on v2

--- a/solution.py
+++ b/solution.py
@@ -23,6 +23,7 @@
 F32 = jnp.float32
 BF16 = jnp.bfloat16
 
+ALL = ("x", "y", "zl", "zh", "c")
 VM = pl.BlockSpec(memory_space=pltpu.VMEM)
 SM = pl.BlockSpec(memory_space=pltpu.SMEM)
 ANY = pl.BlockSpec(memory_space=pl.ANY)
@@ -131,9 +132,9 @@
     rows = 4 * WIN * FC
     for n, (first, second) in enumerate(((own0, own1), (prev0, prev1))):
         for b in range(2):
-            base = (n * 2 + b) * 2 * rows
-            wide[base : base + rows] = first[b].reshape(rows, 128).astype(F32)
-            wide[base + rows : base + 2 * rows] = second[b].reshape(rows, 128).astype(F32)
+            base = pl.multiple_of(((n ^ c) * 2 + b) * 2 * rows, rows)
+            wide[pl.ds(base, rows)] = first[b].reshape(rows, 128).astype(F32)
+            wide[pl.ds(base + rows, rows)] = second[b].reshape(rows, 128).astype(F32)
     sign = jnp.where(lax.broadcasted_iota(jnp.int32, (CH, 128), 1) < CH, 1.0, -1.0).astype(F32)
     tn = (((0,), (0,)), ((), ()))
 
@@ -254,21 +255,35 @@
     return (z % 2) * 4 + z // 2
 
 
-def ring(value, shift):
-    return lax.ppermute(
-        value, ("zl", "zh"), [(place(z), place((z + shift) % 8)) for z in range(8)]
-    )
+def ring(value, r):
+    pairs = [(place(z), place((z + r) % 8)) for z in range(8)]
+    return lax.ppermute(value, ("zl", "zh"), pairs)
+
+
+def device(m, z, c):
+    return (m % 16) * 16 + place(z % 8) * 2 + c
+
+
+EVERY = [(m, z, c) for m in range(16) for z in range(8) for c in range(2)]
+
+
+def ring_back(value, r):
+    pairs = [(device(m, z, c), device(m + c, z + r, c)) for m, z, c in EVERY]
+    return lax.ppermute(value, ALL, pairs)
+
+
+def round_ring(pieces, name):
+    got = []
+    for r in ORDER:
+        if name == "back":
+            got.append(ring_back(pieces[r], r))
+        else:
+            got.append(ring(pieces[r], r) if r else pieces[0])
+    return got
 
 
 def other_core(value):
     return lax.ppermute(value, "c", [(0, 1), (1, 0)])
-
-
-def round_ring(pieces):
-    got = []
-    for r in ORDER:
-        got.append(ring(pieces[r], r) if r else pieces[0])
-    return got
 
 
 def shards(spectra, valid_flags):
@@ -278,22 +293,22 @@
     scaling = 1.0 / math.sqrt(windows * BINS)
     flags2 = jnp.concatenate([valid_flags, valid_flags], axis=1)[:, None, :]
     white = whiten(jnp.transpose(spectra, (2, 0, 1, 3)), flags2, pos)
-    up = [(i, (i + 1) % 16) for i in range(16)]
-    swap = [(2 * i + k, 2 * j + 1 - k) for i, j in up for k in range(2)]
+    keep = [(device(m, z, c), device(m + 1 - 2 * c, z, c)) for m, z, c in EVERY]
+    swap = [(device(m, z, c), device(m - 1 + 2 * c, z, 1 - c)) for m, z, c in EVERY]
     parts = []
     table = None
     crossed, turned = (), ()
     for k in range(CHUNKS):
-        got = round_ring(white[k * 8 : k * 8 + 8])
+        got = round_ring(white[k * 8 : k * 8 + 8], "go")
         same, other, core = merge(got, pos, *(() if table is None else (table,)))
-        prev0 = lax.ppermute(same, ("x", "y"), up)
-        prev1 = lax.ppermute(other, ("x", "y", "c"), swap)
+        prev0 = lax.ppermute(same, ALL, keep)
+        prev1 = lax.ppermute(other, ALL, swap)
         own1 = other_core(other)
         if k == 0:
             table = lag_table(core[0])
         out = cross(same, own1, prev0, prev1, pos, *crossed)
         crossed = (out[0],)
-        same, other = turn(round_ring(out), pos, *turned)
+        same, other = turn(round_ring(out, "back"), pos, *turned)
         turned = (same,)
         parts += [same, other_core(other)]
     return invert(parts, table, scaling)

time: 146 us -> 156 us (1.068)
  the two profiles are of different devices: /device:TPU:1 before, /device:TPU:97 now
where the time goes in v3:
time: 156 us
  starting transfers between devices  81.2 us (52%)
  waiting for transfers between devices  34.2 us (22%)
  Pallas kernels  26.3 us (17%)
  other arithmetic  12 us (8%)
  local copies, waits for them, and re-layouts  1.89 us (1%)
    ppermute x16, starting transfers between devices, ring_back(): return lax.ppermute(value, ALL, pairs)  39.2 us
    ppermute x14, starting transfers between devices, ring(): return lax.ppermute(value, ('zl', 'zh'), pairs)  25.2 us
    ppermute x16, waiting for transfers between devices, ring_back(): return lax.ppermute(value, ALL, pairs)  22.7 us
    another operation x1, other arithmetic  10.9 us
    pallas_call x2, Pallas kernels, cross(): pl.pallas_call(cross_kernel, out_shape=[shape] * 8, in_specs=[SM] + [VM]...  10.8 us
    ppermute x14, waiting for transfers between devices, ring(): return lax.ppermute(value, ('zl', 'zh'), pairs)  9.61 us
    pallas_call x1, Pallas kernels, whiten(): pl.pallas_call(whiten_kernel, out_shape=[shape] * (8 * CHUNKS), grid_spec...  6.99 us
    ppermute x2, starting transfers between devices, shards(): prev1 = lax.ppermute(other, ALL, swap)  6.67 us
  transfers between devices with their start and end apart: 38, of which 11 were waited for; matrix products, arithmetic and copies ran while one was open for 7% of the time, Pallas kernels for 10%

profile of v3, /device:TPU:97, one launch (start us, length us, event | category | flops | bytes accessed | tf_op | source)
XLA Modules:
  0.0 155.9 jit_solution(3072250779793699256)
XLA Ops:
  2.8 7.0 %whiten.1 = (bf16[2,14,16,128]{3,2,1,0:T(8,128)(2,1)S(1)}, bf16[2,14,16,128]{3,2,1,0:T(8,128)(2,1)S(1)}, bf16[2,14,16,128]{3,2,1,0:T(8,128)(2,1)S(1)}, bf16[2,14...) custom-call(s32[2]{0:T(128)S(1)} %pad_add_fusion.1.pos_ref, ...), custom_call_target="tpu_custom_call" | custom-call | flops 1409286144 | bytes 4194304 | tf_op jit(solution)/shard_map/whiten/pallas_call | solution.py:78
  9.8 4.3 %collective-permute-start = (bf16[2,14,16,128]{3,2,1,0:T(8,128)(2,1)S(1)}, bf16[2,14,16,128]{3,2,1,0:T(8,128)(2,1)S(1)}, u32[]{:S(2)}, u32[]{:S(2)}) collective-permute-start(bf16[2,14,16,128]{3,2,1,0:T(8,128)(2,1)S(1)} %get-tuple-element.47), channel_id=1, source_target_pairs={{0,4},{8,12},{2,6},{10,14},{4,0},{12,8},{6,2},{14,10},{1,5},{9,13}... | collective-permute-start | bytes 344072 | tf_op jit(solution)/shard_map/ppermute | solution.py:260
  14.1 3.3 %collective-permute-start.2 = (bf16[2,14,16,128]{3,2,1,0:T(8,128)(2,1)S(1)}, bf16[2,14,16,128]{3,2,1,0:T(8,128)(2,1)S(1)}, u32[]{:S(2)}, u32[]{:S(2)}) collective-permute-start(bf16[2,14,16,128]{3,2,1,0:T(8,128)(2,1)S(1)} %get-tuple-element.49), channel_id=1, source_target_pairs={{0,12},{8,6},{2,14},{10,0},{4,8},{12,2},{6,10},{14,4},{1,13},{9,7}... | collective-permute-start | bytes 344072 | tf_op jit(solution)/shard_map/ppermute | solution.py:260
  21.9 5.1 %collective-permute-done.1.refs_2_ = bf16[2,14,16,128]{3,2,1,0:T(8,128)(2,1)S(1)} collective-permute-done((bf16[2,14,16,128]{3,2,1,0:T(8,128)(2,1)S(1)}, bf16[2,14,16,128]{3,2,1,0:T(8,128)(2,1)S(1)}, u32[]{:S(2)}, u32[]{:S(2)}) %collective-permute-start.1) | collective-permute-done | bytes 114720 | tf_op jit(solution)/shard_map/ppermute | solution.py:260
  26.9 4.3 %collective-permute-start.6 = (bf16[2,14,16,128]{3,2,1,0:T(8,128)(2,1)S(1)}, bf16[2,14,16,128]{3,2,1,0:T(8,128)(2,1)S(1)}, u32[]{:S(2)}, u32[]{:S(2)}) collective-permute-start(bf16[2,14,16,128]{3,2,1,0:T(8,128)(2,1)S(1)} %get-tuple-element.53), channel_id=1, source_target_pairs={{0,14},{8,0},{2,8},{10,2},{4,10},{12,4},{6,12},{14,6},{1,15},{9,1}... | collective-permute-start | bytes 344072 | tf_op jit(solution)/shard_map/ppermute | solution.py:260
  36.4 3.4 %collective-permute-start.22 = (bf16[2,14,16,128]{3,2,1,0:T(8,128)(2,1)S(1)}, bf16[2,14,16,128]{3,2,1,0:T(8,128)(2,1)S(1)}, u32[]{:S(2)}, u32[]{:S(2)}) collective-permute-start(bf16[2,14,16,128]{3,2,1,0:T(8,128)(2,1)S(1)} %get-tuple-element.70), channel_id=1, source_target_pairs={{0,2},{8,10},{2,4},{10,12},{4,6},{12,14},{6,0},{14,8},{1,3},{9,11}... | collective-permute-start | bytes 344072 | tf_op jit(solution)/shard_map/ppermute | solution.py:260
  40.9 6.2 %collective-permute-start.9 = (bf16[2,4,14,16,128]{4,3,2,1,0:T(8,128)(2,1)S(1)}, bf16[2,4,14,16,128]{4,3,2,1,0:T(8,128)(2,1)S(1)}, u32[]{:S(2)}, u32[]{:S(2)}) collective-permute-start(bf16[2,4,14,16,128]{4,3,2,1,0:T(8,128)(2,1)S(1)} %get-tuple-element.55), channel_id=1, source_target_pairs={{0,241},{1,16},{8,249},{9,24},{2,243},{3,18},{10,251},{11,26},{4,2... | collective-permute-start | bytes 1376264 | tf_op jit(solution)/shard_map/ppermute | solution.py:305
  47.1 4.0 %collective-permute-start.7 = (bf16[2,4,14,16,128]{4,3,2,1,0:T(8,128)(2,1)S(1)}, bf16[2,4,14,16,128]{4,3,2,1,0:T(8,128)(2,1)S(1)}, u32[]{:S(2)}, u32[]{:S(2)}) collective-permute-start(bf16[2,4,14,16,128]{4,3,2,1,0:T(8,128)(2,1)S(1)} %get-tuple-element.55), channel_id=1, source_target_pairs={{0,1},{1,0},{2,3},{3,2},{4,5},{5,4},{6,7},{7,6},{8,9},{9,8},{10,11... | collective-permute-start | bytes 1376264 | tf_op jit(solution)/shard_map/ppermute | solution.py:286
  51.1 5.0 %collective-permute-start.8 = (bf16[2,4,14,16,128]{4,3,2,1,0:T(8,128)(2,1)S(1)}, bf16[2,4,14,16,128]{4,3,2,1,0:T(8,128)(2,1)S(1)}, u32[]{:S(2)}, u32[]{:S(2)}) collective-permute-start(bf16[2,4,14,16,128]{4,3,2,1,0:T(8,128)(2,1)S(1)} %get-tuple-element.54.own0), channel_id=1, source_target_pairs={{0,16},{1,241},{8,24},{9,249},{2,18},{3,243},{10,26},{11,251},{4,2... | collective-permute-start | bytes 1376264 | tf_op jit(solution)/shard_map/ppermute | solution.py:304
  56.1 10.9 %cosine_convert_fusion = (bf16[512,1024]{1,0:T(8,128)(2,1)S(1)}, bf16[512,1024]{1,0:T(8,128)(2,1)S(1)}) fusion(s32[1024]{0:T(1024)S(1)} %iota_add_fusion, s32[512]{0:T(512)S(1)} %get-tuple-element.90, s32[512]{0:T(512)S(1)} %get-tuple-element.93, pred[512]{0:T(512)(128)(4,1)S(1)} %get-tuple-element.97, s32[]{:T(128)} %bitcast.3, ...), kind=kLoop, calls=%fused_computation.26 | loop fusion | flops 24117248 | bytes 2119684 | tf_op jit(solution)/shard_map/convert
  74.7 5.4 %cross.2 = (bf16[2,2,8,16,128]{4,3,2,1,0:T(8,128)(2,1)S(1)}, bf16[2,2,8,16,128]{4,3,2,1,0:T(8,128)(2,1)S(1)}, bf16[2,2,8,16,128]{4,3,2,1,0:T(8,128)(2,1)S(1)}, b...) custom-call(s32[2]{0:T(128)S(1)} %pad_add_fusion.1.pos_ref, ...), custom_call_target="tpu_custom_call" | custom-call | flops 536870912 | bytes 3145728 | tf_op jit(solution)/shard_map/cross/pallas_call | solution.py:172
  80.1 3.7 %collective-permute-start.11 = (bf16[2,2,8,16,128]{4,3,2,1,0:T(8,128)(2,1)S(1)}, bf16[2,2,8,16,128]{4,3,2,1,0:T(8,128)(2,1)S(1)}, u32[]{:S(2)}, u32[]{:S(2)}) collective-permute-start(bf16[2,2,8,16,128]{4,3,2,1,0:T(8,128)(2,1)S(1)} %get-tuple-element.57), channel_id=1, source_target_pairs={{0,4},{1,21},{8,12},{9,29},{2,6},{3,23},{10,14},{11,31},{4,0},{5,1... | collective-permute-start | bytes 393224 | tf_op jit(solution)/shard_map/ppermute | solution.py:272
  83.8 3.1 %collective-permute-start.12 = (bf16[2,2,8,16,128]{4,3,2,1,0:T(8,128)(2,1)S(1)}, bf16[2,2,8,16,128]{4,3,2,1,0:T(8,128)(2,1)S(1)}, u32[]{:S(2)}, u32[]{:S(2)}) collective-permute-start(bf16[2,2,8,16,128]{4,3,2,1,0:T(8,128)(2,1)S(1)} %get-tuple-element.58), channel_id=1, source_target_pairs={{0,10},{1,27},{8,4},{9,21},{2,12},{3,29},{10,6},{11,23},{4,14},{5,... | collective-permute-start | bytes 393224 | tf_op jit(solution)/shard_map/ppermute | solution.py:272
  89.1 2.7 %collective-permute-start.14 = (bf16[2,2,8,16,128]{4,3,2,1,0:T(8,128)(2,1)S(1)}, bf16[2,2,8,16,128]{4,3,2,1,0:T(8,128)(2,1)S(1)}, u32[]{:S(2)}, u32[]{:S(2)}) collective-permute-start(bf16[2,2,8,16,128]{4,3,2,1,0:T(8,128)(2,1)S(1)} %get-tuple-element.60), channel_id=1, source_target_pairs={{0,2},{1,19},{8,10},{9,27},{2,4},{3,21},{10,12},{11,29},{4,6},{5,2... | collective-permute-start | bytes 393224 | tf_op jit(solution)/shard_map/ppermute | solution.py:272
  92.8 3.7 %collective-permute-done.11.refs_1_ = bf16[2,2,8,16,128]{4,3,2,1,0:T(8,128)(2,1)S(1)} collective-permute-done((bf16[2,2,8,16,128]{4,3,2,1,0:T(8,128)(2,1)S(1)}, bf16[2,2,8,16,128]{4,3,2,1,0:T(8,128)(2,1)S(1)}, u32[]{:S(2)}, u32[]{:S(2)}) %collective-permute-start.11) | collective-permute-done | bytes 131104 | tf_op jit(solution)/shard_map/ppermute | solution.py:272
  100.0 3.4 %collective-permute-start.17 = (bf16[2,2,8,16,128]{4,3,2,1,0:T(8,128)(2,1)S(1)}, bf16[2,2,8,16,128]{4,3,2,1,0:T(8,128)(2,1)S(1)}, u32[]{:S(2)}, u32[]{:S(2)}) collective-permute-start(bf16[2,2,8,16,128]{4,3,2,1,0:T(8,128)(2,1)S(1)} %get-tuple-element.63), channel_id=1, source_target_pairs={{0,14},{1,31},{8,0},{9,17},{2,8},{3,25},{10,2},{11,19},{4,10},{5,2... | collective-permute-start | bytes 393224 | tf_op jit(solution)/shard_map/ppermute | solution.py:272
  103.4 5.4 %cross.3 = (bf16[2,2,8,16,128]{4,3,2,1,0:T(8,128)(2,1)S(1)}, bf16[2,2,8,16,128]{4,3,2,1,0:T(8,128)(2,1)S(1)}, bf16[2,2,8,16,128]{4,3,2,1,0:T(8,128)(2,1)S(1)}, b...) custom-call(s32[2]{0:T(128)S(1)} %pad_add_fusion.1.pos_ref, ...), custom_call_target="tpu_custom_call" | custom-call | flops 536870912 | bytes 3145728 | tf_op jit(solution)/shard_map/cross/pallas_call | solution.py:172
  108.9 3.8 %collective-permute-start.10 = (bf16[2,2,8,16,128]{4,3,2,1,0:T(8,128)(2,1)S(1)}, bf16[2,2,8,16,128]{4,3,2,1,0:T(8,128)(2,1)S(1)}, u32[]{:S(2)}, u32[]{:S(2)}) collective-permute-start(bf16[2,2,8,16,128]{4,3,2,1,0:T(8,128)(2,1)S(1)} %get-tuple-element.56.refs_0_), channel_id=1, source_target_pairs={{0,0},{1,17},{8,8},{9,25},{2,2},{3,19},{10,10},{11,27},{4,4},{5,21... | collective-permute-start | bytes 393224 | tf_op jit(solution)/shard_map/ppermute | solution.py:272
  117.5 5.2 %collective-permute-start.31 = (bf16[2,2,8,16,128]{4,3,2,1,0:T(8,128)(2,1)S(1)}, bf16[2,2,8,16,128]{4,3,2,1,0:T(8,128)(2,1)S(1)}, u32[]{:S(2)}, u32[]{:S(2)}) collective-permute-start(bf16[2,2,8,16,128]{4,3,2,1,0:T(8,128)(2,1)S(1)} %get-tuple-element.79), channel_id=1, source_target_pairs={{0,10},{1,27},{8,4},{9,21},{2,12},{3,29},{10,6},{11,23},{4,14},{5,... | collective-permute-start | bytes 393224 | tf_op jit(solution)/shard_map/ppermute | solution.py:272
  122.7 3.7 %collective-permute-start.33 = (bf16[2,2,8,16,128]{4,3,2,1,0:T(8,128)(2,1)S(1)}, bf16[2,2,8,16,128]{4,3,2,1,0:T(8,128)(2,1)S(1)}, u32[]{:S(2)}, u32[]{:S(2)}) collective-permute-start(bf16[2,2,8,16,128]{4,3,2,1,0:T(8,128)(2,1)S(1)} %get-tuple-element.81), channel_id=1, source_target_pairs={{0,2},{1,19},{8,10},{9,27},{2,4},{3,21},{10,12},{11,29},{4,6},{5,2... | collective-permute-start | bytes 393224 | tf_op jit(solution)/shard_map/ppermute | solution.py:272
  128.7 3.7 %collective-permute-start.35 = (bf16[2,2,8,16,128]{4,3,2,1,0:T(8,128)(2,1)S(1)}, bf16[2,2,8,16,128]{4,3,2,1,0:T(8,128)(2,1)S(1)}, u32[]{:S(2)}, u32[]{:S(2)}) collective-permute-start(bf16[2,2,8,16,128]{4,3,2,1,0:T(8,128)(2,1)S(1)} %get-tuple-element.83), channel_id=1, source_target_pairs={{0,8},{1,25},{8,2},{9,19},{2,10},{3,27},{10,4},{11,21},{4,12},{5,2... | collective-permute-start | bytes 393224 | tf_op jit(solution)/shard_map/ppermute | solution.py:272
  132.3 7.3 %collective-permute-done.31.refs_2_ = bf16[2,2,8,16,128]{4,3,2,1,0:T(8,128)(2,1)S(1)} collective-permute-done((bf16[2,2,8,16,128]{4,3,2,1,0:T(8,128)(2,1)S(1)}, bf16[2,2,8,16,128]{4,3,2,1,0:T(8,128)(2,1)S(1)}, u32[]{:S(2)}, u32[]{:S(2)}) %collective-permute-start.31) | collective-permute-done | bytes 131104 | tf_op jit(solution)/shard_map/ppermute | solution.py:272
  141.6 7.3 %collective-permute-done.36.refs_7_ = bf16[2,2,8,16,128]{4,3,2,1,0:T(8,128)(2,1)S(1)} collective-permute-done((bf16[2,2,8,16,128]{4,3,2,1,0:T(8,128)(2,1)S(1)}, bf16[2,2,8,16,128]{4,3,2,1,0:T(8,128)(2,1)S(1)}, u32[]{:S(2)}, u32[]{:S(2)}) %collective-permute-start.36) | collective-permute-done | bytes 131104 | tf_op jit(solution)/shard_map/ppermute | solution.py:272
  152.2 3.7 %invert.1 = bf16[2,8,64,1024]{3,2,1,0:T(8,128)(2,1)} custom-call(bf16[2,8,128,128]{3,2,1,0:T(8,128)(2,1)S(1)} %get-tuple-element.64.refs_8_.refs_0_, bf16[2,8,128,128]{3,2,1,0:T(8,128)(2,1)S(1)} %collective-permute-done.18.refs_1_, bf16[2,8,128,128]{3,2,1,0:T(8,128)(2,1)S(1)} %get-tuple-element.85.refs_2_, ...), custom_call_target="tpu_custom_call" | custom-call | flops 2147483648 | bytes 6291456 | tf_op jit(solution)/shard_map/invert/pallas_call | solution.py:228
  (73 shorter events, 40.2 us)
Async XLA Ops:
  14.1 17.1 %collective-permute-start.2 = (bf16[2,14,16,128]{3,2,1,0:T(8,128)(2,1)S(1)}, bf16[2,14,16,128]{3,2,1,0:T(8,128)(2,1)S(1)}, u32[]{:S(2)}, u32[]{:S(2)}) collective-permute-start(bf16[2,14,16,128]{3,2,1,0:T(8,128)(2,1)S(1)} %get-tuple-element.49), channel_id=1, source_target_pairs={{0,12},{8,6},{2,14},{10,0},{4,8},{12,2},{6,10},{14,4},{1,13},{9,7}... | collective-permute-start | bytes 344072 | tf_op jit(solution)/shard_map/ppermute | solution.py:260
  17.4 15.7 %collective-permute-start.3 = (bf16[2,14,16,128]{3,2,1,0:T(8,128)(2,1)S(1)}, bf16[2,14,16,128]{3,2,1,0:T(8,128)(2,1)S(1)}, u32[]{:S(2)}, u32[]{:S(2)}) collective-permute-start(bf16[2,14,16,128]{3,2,1,0:T(8,128)(2,1)S(1)} %get-tuple-element.50), channel_id=1, source_target_pairs={{0,2},{8,10},{2,4},{10,12},{4,6},{12,14},{6,0},{14,8},{1,3},{9,11}... | collective-permute-start | bytes 344072 | tf_op jit(solution)/shard_map/ppermute | solution.py:260
  18.1 17.3 %collective-permute-start.4 = (bf16[2,14,16,128]{3,2,1,0:T(8,128)(2,1)S(1)}, bf16[2,14,16,128]{3,2,1,0:T(8,128)(2,1)S(1)}, u32[]{:S(2)}, u32[]{:S(2)}) collective-permute-start(bf16[2,14,16,128]{3,2,1,0:T(8,128)(2,1)S(1)} %get-tuple-element.51), channel_id=1, source_target_pairs={{0,6},{8,14},{2,0},{10,8},{4,2},{12,10},{6,4},{14,12},{1,7},{9,15}... | collective-permute-start | bytes 344072 | tf_op jit(solution)/shard_map/ppermute | solution.py:260
  19.8 16.6 %collective-permute-start.5 = (bf16[2,14,16,128]{3,2,1,0:T(8,128)(2,1)S(1)}, bf16[2,14,16,128]{3,2,1,0:T(8,128)(2,1)S(1)}, u32[]{:S(2)}, u32[]{:S(2)}) collective-permute-start(bf16[2,14,16,128]{3,2,1,0:T(8,128)(2,1)S(1)} %get-tuple-element.52), channel_id=1, source_target_pairs={{0,8},{8,2},{2,10},{10,4},{4,12},{12,6},{6,14},{14,0},{1,9},{9,3},... | collective-permute-start | bytes 344072 | tf_op jit(solution)/shard_map/ppermute | solution.py:260
  33.1 14.0 %collective-permute-start.20 = (bf16[2,14,16,128]{3,2,1,0:T(8,128)(2,1)S(1)}, bf16[2,14,16,128]{3,2,1,0:T(8,128)(2,1)S(1)}, u32[]{:S(2)}, u32[]{:S(2)}) collective-permute-start(bf16[2,14,16,128]{3,2,1,0:T(8,128)(2,1)S(1)} %get-tuple-element.68), channel_id=1, source_target_pairs={{0,10},{8,4},{2,12},{10,6},{4,14},{12,0},{6,8},{14,2},{1,11},{9,5}... | collective-permute-start | bytes 344072 | tf_op jit(solution)/shard_map/ppermute | solution.py:260
  35.4 15.6 %collective-permute-start.21 = (bf16[2,14,16,128]{3,2,1,0:T(8,128)(2,1)S(1)}, bf16[2,14,16,128]{3,2,1,0:T(8,128)(2,1)S(1)}, u32[]{:S(2)}, u32[]{:S(2)}) collective-permute-start(bf16[2,14,16,128]{3,2,1,0:T(8,128)(2,1)S(1)} %get-tuple-element.69), channel_id=1, source_target_pairs={{0,12},{8,6},{2,14},{10,0},{4,8},{12,2},{6,10},{14,4},{1,13},{9,7}... | collective-permute-start | bytes 344072 | tf_op jit(solution)/shard_map/ppermute | solution.py:260
  36.4 30.6 %collective-permute-start.22 = (bf16[2,14,16,128]{3,2,1,0:T(8,128)(2,1)S(1)}, bf16[2,14,16,128]{3,2,1,0:T(8,128)(2,1)S(1)}, u32[]{:S(2)}, u32[]{:S(2)}) collective-permute-start(bf16[2,14,16,128]{3,2,1,0:T(8,128)(2,1)S(1)} %get-tuple-element.70), channel_id=1, source_target_pairs={{0,2},{8,10},{2,4},{10,12},{4,6},{12,14},{6,0},{14,8},{1,3},{9,11}... | collective-permute-start | bytes 344072 | tf_op jit(solution)/shard_map/ppermute | solution.py:260
  39.8 27.5 %collective-permute-start.23 = (bf16[2,14,16,128]{3,2,1,0:T(8,128)(2,1)S(1)}, bf16[2,14,16,128]{3,2,1,0:T(8,128)(2,1)S(1)}, u32[]{:S(2)}, u32[]{:S(2)}) collective-permute-start(bf16[2,14,16,128]{3,2,1,0:T(8,128)(2,1)S(1)} %get-tuple-element.71), channel_id=1, source_target_pairs={{0,6},{8,14},{2,0},{10,8},{4,2},{12,10},{6,4},{14,12},{1,7},{9,15}... | collective-permute-start | bytes 344072 | tf_op jit(solution)/shard_map/ppermute | solution.py:260
  40.9 33.8 %collective-permute-start.9 = (bf16[2,4,14,16,128]{4,3,2,1,0:T(8,128)(2,1)S(1)}, bf16[2,4,14,16,128]{4,3,2,1,0:T(8,128)(2,1)S(1)}, u32[]{:S(2)}, u32[]{:S(2)}) collective-permute-start(bf16[2,4,14,16,128]{4,3,2,1,0:T(8,128)(2,1)S(1)} %get-tuple-element.55), channel_id=1, source_target_pairs={{0,241},{1,16},{8,249},{9,24},{2,243},{3,18},{10,251},{11,26},{4,2... | collective-permute-start | bytes 1376264 | tf_op jit(solution)/shard_map/ppermute | solution.py:305
  47.1 27.6 %collective-permute-start.7 = (bf16[2,4,14,16,128]{4,3,2,1,0:T(8,128)(2,1)S(1)}, bf16[2,4,14,16,128]{4,3,2,1,0:T(8,128)(2,1)S(1)}, u32[]{:S(2)}, u32[]{:S(2)}) collective-permute-start(bf16[2,4,14,16,128]{4,3,2,1,0:T(8,128)(2,1)S(1)} %get-tuple-element.55), channel_id=1, source_target_pairs={{0,1},{1,0},{2,3},{3,2},{4,5},{5,4},{6,7},{7,6},{8,9},{9,8},{10,11... | collective-permute-start | bytes 1376264 | tf_op jit(solution)/shard_map/ppermute | solution.py:286
  51.1 23.5 %collective-permute-start.8 = (bf16[2,4,14,16,128]{4,3,2,1,0:T(8,128)(2,1)S(1)}, bf16[2,4,14,16,128]{4,3,2,1,0:T(8,128)(2,1)S(1)}, u32[]{:S(2)}, u32[]{:S(2)}) collective-permute-start(bf16[2,4,14,16,128]{4,3,2,1,0:T(8,128)(2,1)S(1)} %get-tuple-element.54.own0), channel_id=1, source_target_pairs={{0,16},{1,241},{8,24},{9,249},{2,18},{3,243},{10,26},{11,251},{4,2... | collective-permute-start | bytes 1376264 | tf_op jit(solution)/shard_map/ppermute | solution.py:304
  74.2 14.9 %collective-permute-start.28 = (bf16[2,4,14,16,128]{4,3,2,1,0:T(8,128)(2,1)S(1)}, bf16[2,4,14,16,128]{4,3,2,1,0:T(8,128)(2,1)S(1)}, u32[]{:S(2)}, u32[]{:S(2)}) collective-permute-start(bf16[2,4,14,16,128]{4,3,2,1,0:T(8,128)(2,1)S(1)} %get-tuple-element.76), channel_id=1, source_target_pairs={{0,241},{1,16},{8,249},{9,24},{2,243},{3,18},{10,251},{11,26},{4,2... | collective-permute-start | bytes 1376264 | tf_op jit(solution)/shard_map/ppermute | solution.py:305
  74.6 17.2 %collective-permute-start.26 = (bf16[2,4,14,16,128]{4,3,2,1,0:T(8,128)(2,1)S(1)}, bf16[2,4,14,16,128]{4,3,2,1,0:T(8,128)(2,1)S(1)}, u32[]{:S(2)}, u32[]{:S(2)}) collective-permute-start(bf16[2,4,14,16,128]{4,3,2,1,0:T(8,128)(2,1)S(1)} %get-tuple-element.76), channel_id=1, source_target_pairs={{0,1},{1,0},{2,3},{3,2},{4,5},{5,4},{6,7},{7,6},{8,9},{9,8},{10,11... | collective-permute-start | bytes 1376264 | tf_op jit(solution)/shard_map/ppermute | solution.py:286
  80.1 16.4 %collective-permute-start.11 = (bf16[2,2,8,16,128]{4,3,2,1,0:T(8,128)(2,1)S(1)}, bf16[2,2,8,16,128]{4,3,2,1,0:T(8,128)(2,1)S(1)}, u32[]{:S(2)}, u32[]{:S(2)}) collective-permute-start(bf16[2,2,8,16,128]{4,3,2,1,0:T(8,128)(2,1)S(1)} %get-tuple-element.57), channel_id=1, source_target_pairs={{0,4},{1,21},{8,12},{9,29},{2,6},{3,23},{10,14},{11,31},{4,0},{5,1... | collective-permute-start | bytes 393224 | tf_op jit(solution)/shard_map/ppermute | solution.py:272
  83.8 16.3 %collective-permute-start.12 = (bf16[2,2,8,16,128]{4,3,2,1,0:T(8,128)(2,1)S(1)}, bf16[2,2,8,16,128]{4,3,2,1,0:T(8,128)(2,1)S(1)}, u32[]{:S(2)}, u32[]{:S(2)}) collective-permute-start(bf16[2,2,8,16,128]{4,3,2,1,0:T(8,128)(2,1)S(1)} %get-tuple-element.58), channel_id=1, source_target_pairs={{0,10},{1,27},{8,4},{9,21},{2,12},{3,29},{10,6},{11,23},{4,14},{5,... | collective-permute-start | bytes 393224 | tf_op jit(solution)/shard_map/ppermute | solution.py:272
  86.8 22.0 %collective-permute-start.13 = (bf16[2,2,8,16,128]{4,3,2,1,0:T(8,128)(2,1)S(1)}, bf16[2,2,8,16,128]{4,3,2,1,0:T(8,128)(2,1)S(1)}, u32[]{:S(2)}, u32[]{:S(2)}) collective-permute-start(bf16[2,2,8,16,128]{4,3,2,1,0:T(8,128)(2,1)S(1)} %get-tuple-element.59), channel_id=1, source_target_pairs={{0,12},{1,29},{8,6},{9,23},{2,14},{3,31},{10,0},{11,17},{4,8},{5,2... | collective-permute-start | bytes 393224 | tf_op jit(solution)/shard_map/ppermute | solution.py:272
  89.1 23.5 %collective-permute-start.14 = (bf16[2,2,8,16,128]{4,3,2,1,0:T(8,128)(2,1)S(1)}, bf16[2,2,8,16,128]{4,3,2,1,0:T(8,128)(2,1)S(1)}, u32[]{:S(2)}, u32[]{:S(2)}) collective-permute-start(bf16[2,2,8,16,128]{4,3,2,1,0:T(8,128)(2,1)S(1)} %get-tuple-element.60), channel_id=1, source_target_pairs={{0,2},{1,19},{8,10},{9,27},{2,4},{3,21},{10,12},{11,29},{4,6},{5,2... | collective-permute-start | bytes 393224 | tf_op jit(solution)/shard_map/ppermute | solution.py:272
  91.8 23.5 %collective-permute-start.15 = (bf16[2,2,8,16,128]{4,3,2,1,0:T(8,128)(2,1)S(1)}, bf16[2,2,8,16,128]{4,3,2,1,0:T(8,128)(2,1)S(1)}, u32[]{:S(2)}, u32[]{:S(2)}) collective-permute-start(bf16[2,2,8,16,128]{4,3,2,1,0:T(8,128)(2,1)S(1)} %get-tuple-element.61), channel_id=1, source_target_pairs={{0,6},{1,23},{8,14},{9,31},{2,0},{3,17},{10,8},{11,25},{4,2},{5,19... | collective-permute-start | bytes 393224 | tf_op jit(solution)/shard_map/ppermute | solution.py:272
  96.5 21.0 %collective-permute-start.16 = (bf16[2,2,8,16,128]{4,3,2,1,0:T(8,128)(2,1)S(1)}, bf16[2,2,8,16,128]{4,3,2,1,0:T(8,128)(2,1)S(1)}, u32[]{:S(2)}, u32[]{:S(2)}) collective-permute-start(bf16[2,2,8,16,128]{4,3,2,1,0:T(8,128)(2,1)S(1)} %get-tuple-element.62), channel_id=1, source_target_pairs={{0,8},{1,25},{8,2},{9,19},{2,10},{3,27},{10,4},{11,21},{4,12},{5,2... | collective-permute-start | bytes 393224 | tf_op jit(solution)/shard_map/ppermute | solution.py:272
  100.0 22.7 %collective-permute-start.17 = (bf16[2,2,8,16,128]{4,3,2,1,0:T(8,128)(2,1)S(1)}, bf16[2,2,8,16,128]{4,3,2,1,0:T(8,128)(2,1)S(1)}, u32[]{:S(2)}, u32[]{:S(2)}) collective-permute-start(bf16[2,2,8,16,128]{4,3,2,1,0:T(8,128)(2,1)S(1)} %get-tuple-element.63), channel_id=1, source_target_pairs={{0,14},{1,31},{8,0},{9,17},{2,8},{3,25},{10,2},{11,19},{4,10},{5,2... | collective-permute-start | bytes 393224 | tf_op jit(solution)/shard_map/ppermute | solution.py:272
  117.5 22.1 %collective-permute-start.31 = (bf16[2,2,8,16,128]{4,3,2,1,0:T(8,128)(2,1)S(1)}, bf16[2,2,8,16,128]{4,3,2,1,0:T(8,128)(2,1)S(1)}, u32[]{:S(2)}, u32[]{:S(2)}) collective-permute-start(bf16[2,2,8,16,128]{4,3,2,1,0:T(8,128)(2,1)S(1)} %get-tuple-element.79), channel_id=1, source_target_pairs={{0,10},{1,27},{8,4},{9,21},{2,12},{3,29},{10,6},{11,23},{4,14},{5,... | collective-permute-start | bytes 393224 | tf_op jit(solution)/shard_map/ppermute | solution.py:272
  122.7 18.2 %collective-permute-start.32 = (bf16[2,2,8,16,128]{4,3,2,1,0:T(8,128)(2,1)S(1)}, bf16[2,2,8,16,128]{4,3,2,1,0:T(8,128)(2,1)S(1)}, u32[]{:S(2)}, u32[]{:S(2)}) collective-permute-start(bf16[2,2,8,16,128]{4,3,2,1,0:T(8,128)(2,1)S(1)} %get-tuple-element.80), channel_id=1, source_target_pairs={{0,12},{1,29},{8,6},{9,23},{2,14},{3,31},{10,0},{11,17},{4,8},{5,2... | collective-permute-start | bytes 393224 | tf_op jit(solution)/shard_map/ppermute | solution.py:272
  122.7 18.3 %collective-permute-start.33 = (bf16[2,2,8,16,128]{4,3,2,1,0:T(8,128)(2,1)S(1)}, bf16[2,2,8,16,128]{4,3,2,1,0:T(8,128)(2,1)S(1)}, u32[]{:S(2)}, u32[]{:S(2)}) collective-permute-start(bf16[2,2,8,16,128]{4,3,2,1,0:T(8,128)(2,1)S(1)} %get-tuple-element.81), channel_id=1, source_target_pairs={{0,2},{1,19},{8,10},{9,27},{2,4},{3,21},{10,12},{11,29},{4,6},{5,2... | collective-permute-start | bytes 393224 | tf_op jit(solution)/shard_map/ppermute | solution.py:272
  126.4 14.6 %collective-permute-start.34 = (bf16[2,2,8,16,128]{4,3,2,1,0:T(8,128)(2,1)S(1)}, bf16[2,2,8,16,128]{4,3,2,1,0:T(8,128)(2,1)S(1)}, u32[]{:S(2)}, u32[]{:S(2)}) collective-permute-start(bf16[2,2,8,16,128]{4,3,2,1,0:T(8,128)(2,1)S(1)} %get-tuple-element.82), channel_id=1, source_target_pairs={{0,6},{1,23},{8,14},{9,31},{2,0},{3,17},{10,8},{11,25},{4,2},{5,19... | collective-permute-start | bytes 393224 | tf_op jit(solution)/shard_map/ppermute | solution.py:272
  (14 other events, 141.9 us)

commit v4 on v3

--- a/solution.py
+++ b/solution.py
@@ -29,15 +29,17 @@
 ANY = pl.BlockSpec(memory_space=pl.ANY)
 
 
+def place(z):
+    return (z % 2) * 4 + z // 2
+
+
 def params():
     return pltpu.CompilerParams(vmem_limit_bytes=48 << 20)
 
 
 def whiten_kernel(pos_ref, spec_ref, flags_ref, *refs):
-    outs = refs[: 8 * CHUNKS]
-    band, eye, invc, white = refs[8 * CHUNKS :]
+    outs, core, (band, eye, invc, white) = refs[:CHUNKS], refs[CHUNKS], refs[CHUNKS + 1 :]
     w = pl.program_id(0)
-    z, c = pos_ref[0], pos_ref[1]
 
     @pl.when(w == 0)
     def _():
@@ -65,19 +67,19 @@
         )
         white[h * 256 : (h + 1) * 256] = (half * scale[h * 256 : (h + 1) * 256]).astype(BF16)
     for k in range(CHUNKS):
-        for r in range(8):
-            base = k * CBINS + ((z + r) & 7) * (2 * FC)
-            for crel in range(2):
-                start = pl.multiple_of(base + (c ^ crel) * FC, FC)
-                outs[k * 8 + r][crel, w] = white[pl.ds(start, FC), :]
+        for z in range(8):
+            for c in range(2):
+                start = k * CBINS + z * 2 * FC + c * FC
+                outs[k][place(z) * 2 + c, w] = white[start : start + FC]
+    core[0] = pos_ref[1]
 
 
 def whiten(spec, flags2, pos):
-    shape = jax.ShapeDtypeStruct((2, WIN, FC, 128), BF16)
-    full = pl.BlockSpec((2, WIN, FC, 128), lambda w, *_: (0, 0, 0, 0))
+    shape = jax.ShapeDtypeStruct((16, WIN, FC, 128), BF16)
+    full = pl.BlockSpec((16, WIN, FC, 128), lambda w, *_: (0, 0, 0, 0))
     return pl.pallas_call(
         whiten_kernel,
-        out_shape=[shape] * (8 * CHUNKS),
+        out_shape=[shape] * CHUNKS + [jax.ShapeDtypeStruct((1,), jnp.int32)],
         grid_spec=pltpu.PrefetchScalarGridSpec(
             num_scalar_prefetch=1,
             grid=(WIN,),
@@ -85,7 +87,7 @@
                 pl.BlockSpec((2, 1, CH, BINS), lambda w, *_: (0, w, 0, 0)),
                 pl.BlockSpec((1, 1, 128), lambda w, *_: (w, 0, 0)),
             ],
-            out_specs=[full] * (8 * CHUNKS),
+            out_specs=[full] * CHUNKS + [SM],
             scratch_shapes=[
                 pltpu.VMEM((BINS, BINS), BF16),
                 pltpu.VMEM((256, 256), BF16),
@@ -101,46 +103,20 @@
     )(pos, spec, flags2)
 
 
-def merge_kernel(pos_ref, *refs):
-    ins, (same, other, core) = refs[:8], refs[-3:]
-    z = pos_ref[0]
-    core[0] = pos_ref[1]
-    for n, r in enumerate(ORDER):
-        src = (z - r) & 7
-        same[src & 1, src >> 1] = ins[n][0]
-        other[src & 1, src >> 1] = ins[n][1]
-
-
-def merge(pieces, pos, *after):
-    shape = jax.ShapeDtypeStruct((2, 4, WIN, FC, 128), BF16)
-    return pl.pallas_call(
-        merge_kernel,
-        out_shape=[shape] * 2 + [jax.ShapeDtypeStruct((1,), jnp.int32)],
-        in_specs=[SM] + [VM] * 8 + [ANY] * len(after),
-        out_specs=[VM] * 2 + [SM],
-        compiler_params=params(),
-        cost_estimate=pl.CostEstimate(
-            flops=0, bytes_accessed=4 * 8 * WIN * FC * 256, transcendentals=0
-        ),
-        name="merge",
-    )(pos, *pieces, *after)
-
-
-def cross_kernel(pos_ref, own0, own1, prev0, prev1, *refs):
+def cross_kernel(pos_ref, here, there, *refs):
     outs, (wide, res) = refs[-10:-2], refs[-2:]
     z, c = pos_ref[0], pos_ref[1]
-    rows = 4 * WIN * FC
-    for n, (first, second) in enumerate(((own0, own1), (prev0, prev1))):
+    rows = 8 * WIN * FC
+    for n, ref in enumerate((here, there)):
         for b in range(2):
-            base = pl.multiple_of(((n ^ c) * 2 + b) * 2 * rows, rows)
-            wide[pl.ds(base, rows)] = first[b].reshape(rows, 128).astype(F32)
-            wide[pl.ds(base + rows, rows)] = second[b].reshape(rows, 128).astype(F32)
+            base = pl.multiple_of(((n ^ c) * 2 + b) * rows, rows)
+            wide[pl.ds(base, rows)] = ref[8 * b : 8 * b + 8].reshape(rows, 128).astype(F32)
     sign = jnp.where(lax.broadcasted_iota(jnp.int32, (CH, 128), 1) < CH, 1.0, -1.0).astype(F32)
     tn = (((0,), (0,)), ((), ()))
 
     def one_bin(f, carry):
         x = [
-            wide[pl.ds(n * 2 * rows + f, 8 * WIN, stride=FC), :].astype(BF16) for n in range(4)
+            wide[pl.ds(n * rows + f, 8 * WIN, stride=FC), :].astype(BF16) for n in range(4)
         ]
         own_a, own_b, prev_a, prev_b = x
         for b, (left, rights) in enumerate(
@@ -167,12 +143,12 @@
                     outs[r][crel, rnd, i] = res[pl.ds(base + i, FC, stride=CH), :].astype(BF16)
 
 
-def cross(own0, own1, prev0, prev1, pos, *after):
+def cross(here, there, pos, *after):
     shape = jax.ShapeDtypeStruct((2, 2, 8, FC, 128), BF16)
     return pl.pallas_call(
         cross_kernel,
         out_shape=[shape] * 8,
-        in_specs=[SM] + [VM] * 4 + [ANY] * len(after),
+        in_specs=[SM] + [VM] * 2 + [ANY] * len(after),
         out_specs=[VM] * 8,
         scratch_shapes=[
             pltpu.VMEM((32 * WIN * FC, 128), F32),
@@ -183,7 +159,7 @@
             flops=4 * FC * 128 * 256 * 256, bytes_accessed=3 << 20, transcendentals=0
         ),
         name="cross",
-    )(pos, own0, own1, prev0, prev1, *after)
+    )(pos, here, there, *after)
 
 
 def turn_kernel(pos_ref, *refs):
@@ -239,25 +215,42 @@
     )(*parts, table)
 
 
+def turns(freq_ids, delay_ids):
+    angles = jnp.mod(freq_ids * delay_ids, WIN_SAMPLES).astype(F32) * (2.0 * math.pi / WIN_SAMPLES)
+    return jnp.cos(angles), jnp.sin(angles)
+
+
 def lag_table(core):
-    n = lax.broadcasted_iota(jnp.int32, (BINS, LAG_COUNT), 0)
+    n = lax.broadcasted_iota(jnp.int32, (BINS, 1), 0)
     fine = n % FC
     z = (n // FC) % 8
     part = (n // (8 * FC)) % 2
     chunk = n // (16 * FC)
     freq_ids = chunk * CBINS + z * (2 * FC) + (part ^ core) * FC + fine + BAND_START
-    delay_ids = lax.broadcasted_iota(jnp.int32, (BINS, LAG_COUNT), 1) - LAG_COUNT // 2
-    angles = jnp.mod(freq_ids * delay_ids, WIN_SAMPLES).astype(F32) * (2.0 * math.pi / WIN_SAMPLES)
-    return jnp.concatenate([jnp.cos(angles), -jnp.sin(angles)], axis=0).astype(BF16)
-
-
-def place(z):
-    return (z % 2) * 4 + z // 2
-
-
-def ring(value, r):
-    pairs = [(place(z), place((z + r) % 8)) for z in range(8)]
-    return lax.ppermute(value, ("zl", "zh"), pairs)
+    lane = lax.broadcasted_iota(jnp.int32, (BINS, 128), 1)
+    coarse = lane % 8 * 128 - LAG_COUNT // 2
+    return *turns(freq_ids, lane), *turns(freq_ids, coarse)
+
+
+def table_kernel(cos_a, sin_a, cos_b, sin_b, *refs):
+    out = refs[-1]
+    ca, sa, cb, sb = cos_a[...], sin_a[...], cos_b[...], sin_b[...]
+    for n in range(LAG_COUNT // 128):
+        c, s = cb[:, n : n + 1], sb[:, n : n + 1]
+        out[:BINS, n * 128 : n * 128 + 128] = (ca * c - sa * s).astype(BF16)
+        out[BINS:, n * 128 : n * 128 + 128] = (-(sa * c + ca * s)).astype(BF16)
+
+
+def join_table(parts):
+    return pl.pallas_call(
+        table_kernel,
+        out_shape=jax.ShapeDtypeStruct((2 * BINS, LAG_COUNT), BF16),
+        in_specs=[VM] * 4,
+        out_specs=VM,
+        compiler_params=params(),
+        cost_estimate=pl.CostEstimate(flops=8 << 20, bytes_accessed=4 << 20, transcendentals=0),
+        name="table",
+    )(*parts)
 
 
 def device(m, z, c):
@@ -272,13 +265,10 @@
     return lax.ppermute(value, ALL, pairs)
 
 
-def round_ring(pieces, name):
+def round_ring(pieces):
     got = []
     for r in ORDER:
-        if name == "back":
-            got.append(ring_back(pieces[r], r))
-        else:
-            got.append(ring(pieces[r], r) if r else pieces[0])
+        got.append(ring_back(pieces[r], r))
     return got
 
 
@@ -292,23 +282,17 @@
     windows = spectra.shape[0] * lax.axis_size(("zh", "c"))
     scaling = 1.0 / math.sqrt(windows * BINS)
     flags2 = jnp.concatenate([valid_flags, valid_flags], axis=1)[:, None, :]
-    white = whiten(jnp.transpose(spectra, (2, 0, 1, 3)), flags2, pos)
-    keep = [(device(m, z, c), device(m + 1 - 2 * c, z, c)) for m, z, c in EVERY]
-    swap = [(device(m, z, c), device(m - 1 + 2 * c, z, 1 - c)) for m, z, c in EVERY]
+    *white, core = whiten(jnp.transpose(spectra, (2, 0, 1, 3)), flags2, pos)
+    shift = [(device(m, z, c), device(m + 1 - 2 * c, z, c)) for m, z, c in EVERY]
+    table = join_table(lag_table(core[0]))
     parts = []
-    table = None
-    crossed, turned = (), ()
+    crossed, turned = (table,), ()
     for k in range(CHUNKS):
-        got = round_ring(white[k * 8 : k * 8 + 8], "go")
-        same, other, core = merge(got, pos, *(() if table is None else (table,)))
-        prev0 = lax.ppermute(same, ALL, keep)
-        prev1 = lax.ppermute(other, ALL, swap)
-        own1 = other_core(other)
-        if k == 0:
-            table = lag_table(core[0])
-        out = cross(same, own1, prev0, prev1, pos, *crossed)
+        here = lax.all_to_all(white[k], ("zl", "zh", "c"), 0, 0, tiled=True)
+        there = lax.ppermute(here, ALL, shift)
+        out = cross(here, there, pos, *crossed)
         crossed = (out[0],)
-        same, other = turn(round_ring(out, "back"), pos, *turned)
+        same, other = turn(round_ring(out), pos, *turned)
         turned = (same,)
         parts += [same, other_core(other)]
     return invert(parts, table, scaling)

time: 156 us -> 165 us (1.058)
  the two profiles are of different devices: /device:TPU:97 before, /device:TPU:1 now
where the time goes in v4:
time: 165 us
  waiting for transfers between devices  54.2 us (33%)
  starting transfers between devices  43.1 us (26%)
  blocking collectives  35.6 us (22%)
  Pallas kernels  27 us (16%)
  other arithmetic  2.98 us (2%)
  local copies, waits for them, and re-layouts  1.9 us (1%)
    all_to_all x1, blocking collectives, shards(): here = lax.all_to_all(white[k], ('zl', 'zh', 'c'), 0, 0, tiled=True)  35.6 us
    ppermute x16, waiting for transfers between devices, ring_back(): return lax.ppermute(value, ALL, pairs)  32.9 us
    ppermute x16, starting transfers between devices, ring_back(): return lax.ppermute(value, ALL, pairs)  29 us
    all_to_all x1, waiting for transfers between devices, shards(): here = lax.all_to_all(white[k], ('zl', 'zh', 'c'), 0, 0, tiled=True)  18.4 us
    pallas_call x2, Pallas kernels, cross(): pl.pallas_call(cross_kernel, out_shape=[shape] * 8, in_specs=[SM] + [VM]...  10.8 us
    ppermute x2, starting transfers between devices, shards(): there = lax.ppermute(here, ALL, shift)  9.94 us
    pallas_call x1, Pallas kernels, whiten(): pl.pallas_call(whiten_kernel, out_shape=[shape] * CHUNKS + [jax.ShapeDtyp...  8.49 us
    pallas_call x1, Pallas kernels, invert(): pl.pallas_call(functools.partial(invert_kernel, scaling), out_shape=jax.S...  3.74 us
  transfers between devices with their start and end apart: 21, of which 11 were waited for; matrix products, arithmetic and copies ran while one was open for 2% of the time, Pallas kernels for 5%

profile of v4, /device:TPU:1, one launch (start us, length us, event | category | flops | bytes accessed | tf_op | source)
XLA Modules:
  0.0 164.8 jit_solution(17101707467038586990)
XLA Ops:
  2.1 8.5 %whiten.1 = (bf16[16,14,16,128]{3,2,1,0:T(8,128)(2,1)S(1)}, bf16[16,14,16,128]{3,2,1,0:T(8,128)(2,1)}, s32[1]{0:T(128)}) custom-call(s32[2]{0:T(128)S(1)} %pad_add_fusion.1.pos_ref, bf16[2,14,64,512]{3,2,1,0:T(8,128)(2,1)S(1)} %bitcast.6, s32[14,1,128]{2,1,0:T(1,128)S(1)} %broadcast_in_dim.3.flags_ref), custom_call_target="tpu_custom_call" | custom-call | flops 1409286144 | bytes 4194304 | tf_op jit(solution)/shard_map/whiten/pallas_call | solution.py:80
  10.6 35.6 %all_to_all.10.here = bf16[16,14,16,128]{3,2,1,0:T(8,128)(2,1)S(1)} all-to-all(bf16[16,14,16,128]{3,2,1,0:T(8,128)(2,1)S(1)} %get-tuple-element.28), channel_id=1, replica_groups=mesh['x'=4,'y'=4,'zl'=2,'zh'=4,'c'=2] {'zl','zh','c'}, dimensions={0} | all-to-all | bytes 1835008 | tf_op jit(solution)/shard_map/all_to_all | solution.py:291
  46.1 3.5 %all-to-all-start.1 = ((bf16[16,14,16,128]{3,2,1,0:T(8,128)(2,1)}), bf16[16,14,16,128]{3,2,1,0:T(8,128)(2,1)S(1)}, u32[]{:S(2)}, u32[]{:S(2)}) async-start(bf16[16,14,16,128]{3,2,1,0:T(8,128)(2,1)} %get-tuple-element.40), calls=%async_computation.1 | async-start | bytes 1835008 | tf_op jit(solution)/shard_map/all_to_all | solution.py:291
  49.7 5.0 %collective-permute-start = (bf16[16,14,16,128]{3,2,1,0:T(8,128)(2,1)S(1)}, bf16[16,14,16,128]{3,2,1,0:T(8,128)(2,1)S(1)}, u32[]{:S(2)}, u32[]{:S(2)}) collective-permute-start(bf16[16,14,16,128]{3,2,1,0:T(8,128)(2,1)S(1)} %all_to_all.10.here), channel_id=1, source_target_pairs={{0,16},{1,241},{8,24},{9,249},{2,18},{3,243},{10,26},{11,251},{4,2... | collective-permute-start | bytes 2752520 | tf_op jit(solution)/shard_map/ppermute | solution.py:292
  54.7 18.4 %all-to-all-done.1.here = bf16[16,14,16,128]{3,2,1,0:T(8,128)(2,1)S(1)} async-done(((bf16[16,14,16,128]{3,2,1,0:T(8,128)(2,1)}), bf16[16,14,16,128]{3,2,1,0:T(8,128)(2,1)S(1)}, u32[]{:S(2)}, u32[]{:S(2)}) %all-to-all-start.1) | async-done | bytes 917536 | tf_op jit(solution)/shard_map/all_to_all | solution.py:291
  73.1 4.9 %collective-permute-start.10 = (bf16[16,14,16,128]{3,2,1,0:T(8,128)(2,1)S(1)}, bf16[16,14,16,128]{3,2,1,0:T(8,128)(2,1)S(1)}, u32[]{:S(2)}, u32[]{:S(2)}) collective-permute-start(bf16[16,14,16,128]{3,2,1,0:T(8,128)(2,1)S(1)} %all-to-all-done.1.here), channel_id=1, source_target_pairs={{0,16},{1,241},{8,24},{9,249},{2,18},{3,243},{10,26},{11,251},{4,2... | collective-permute-start | bytes 2752520 | tf_op jit(solution)/shard_map/ppermute | solution.py:292
  78.6 2.2 %fusion.12 = (f32[512,128]{1,0:T(8,128)S(1)}, f32[512,128]{1,0:T(8,128)S(1)}, f32[512,128]{1,0:T(8,128)S(1)}, f32[512,128]{1,0:T(8,128)S(1)}) fusion(s32[128]{0:T(128)S(1)} %get-tuple-element.55, s32[128]{0:T(128)S(1)} %get-tuple-element.56, pred[128]{0:T(512)(128)(4,1)S(1)} %compare_and_fusion, s32[512]{0:T(512)S(1)} %fusion.22), kind=kLoop, calls=%fused_computation.17 | loop fusion | flops 1376256 | bytes 1051776 | tf_op jit(solution)/shard_map/sin | solution.py:220
  82.2 5.4 %cross.2 = (bf16[2,2,8,16,128]{4,3,2,1,0:T(8,128)(2,1)S(1)}, bf16[2,2,8,16,128]{4,3,2,1,0:T(8,128)(2,1)S(1)}, bf16[2,2,8,16,128]{4,3,2,1,0:T(8,128)(2,1)S(1)}, b...) custom-call(s32[2]{0:T(128)S(1)} %pad_add_fusion.1.pos_ref, ...), custom_call_target="tpu_custom_call" | custom-call | flops 536870912 | bytes 3145728 | tf_op jit(solution)/shard_map/cross/pallas_call | solution.py:148
  88.3 5.4 %cross.3 = (bf16[2,2,8,16,128]{4,3,2,1,0:T(8,128)(2,1)S(1)}, bf16[2,2,8,16,128]{4,3,2,1,0:T(8,128)(2,1)S(1)}, bf16[2,2,8,16,128]{4,3,2,1,0:T(8,128)(2,1)S(1)}, b...) custom-call(s32[2]{0:T(128)S(1)} %pad_add_fusion.1.pos_ref, ...), custom_call_target="tpu_custom_call" | custom-call | flops 536870912 | bytes 3145728 | tf_op jit(solution)/shard_map/cross/pallas_call | solution.py:148
  93.7 1.9 %collective-permute-start.11 = (bf16[2,2,8,16,128]{4,3,2,1,0:T(8,128)(2,1)S(1)}, bf16[2,2,8,16,128]{4,3,2,1,0:T(8,128)(2,1)S(1)}, u32[]{:S(2)}, u32[]{:S(2)}) collective-permute-start(bf16[2,2,8,16,128]{4,3,2,1,0:T(8,128)(2,1)S(1)} %get-tuple-element.41), channel_id=1, source_target_pairs={{0,0},{1,17},{8,8},{9,25},{2,2},{3,19},{10,10},{11,27},{4,4},{5,21... | collective-permute-start | bytes 393224 | tf_op jit(solution)/shard_map/ppermute | solution.py:265
  95.7 2.2 %collective-permute-start.12 = (bf16[2,2,8,16,128]{4,3,2,1,0:T(8,128)(2,1)S(1)}, bf16[2,2,8,16,128]{4,3,2,1,0:T(8,128)(2,1)S(1)}, u32[]{:S(2)}, u32[]{:S(2)}) collective-permute-start(bf16[2,2,8,16,128]{4,3,2,1,0:T(8,128)(2,1)S(1)} %get-tuple-element.42), channel_id=1, source_target_pairs={{0,4},{1,21},{8,12},{9,29},{2,6},{3,23},{10,14},{11,31},{4,0},{5,1... | collective-permute-start | bytes 393224 | tf_op jit(solution)/shard_map/ppermute | solution.py:265
  97.8 2.5 %collective-permute-start.13 = (bf16[2,2,8,16,128]{4,3,2,1,0:T(8,128)(2,1)S(1)}, bf16[2,2,8,16,128]{4,3,2,1,0:T(8,128)(2,1)S(1)}, u32[]{:S(2)}, u32[]{:S(2)}) collective-permute-start(bf16[2,2,8,16,128]{4,3,2,1,0:T(8,128)(2,1)S(1)} %get-tuple-element.43), channel_id=1, source_target_pairs={{0,10},{1,27},{8,4},{9,21},{2,12},{3,29},{10,6},{11,23},{4,14},{5,... | collective-permute-start | bytes 393224 | tf_op jit(solution)/shard_map/ppermute | solution.py:265
  100.4 2.2 %collective-permute-start.1 = (bf16[2,2,8,16,128]{4,3,2,1,0:T(8,128)(2,1)S(1)}, bf16[2,2,8,16,128]{4,3,2,1,0:T(8,128)(2,1)S(1)}, u32[]{:S(2)}, u32[]{:S(2)}) collective-permute-start(bf16[2,2,8,16,128]{4,3,2,1,0:T(8,128)(2,1)S(1)} %get-tuple-element.30.refs_0_), channel_id=1, source_target_pairs={{0,0},{1,17},{8,8},{9,25},{2,2},{3,19},{10,10},{11,27},{4,4},{5,21... | collective-permute-start | bytes 393224 | tf_op jit(solution)/shard_map/ppermute | solution.py:265
  102.6 4.5 %collective-permute-start.2 = (bf16[2,2,8,16,128]{4,3,2,1,0:T(8,128)(2,1)S(1)}, bf16[2,2,8,16,128]{4,3,2,1,0:T(8,128)(2,1)S(1)}, u32[]{:S(2)}, u32[]{:S(2)}) collective-permute-start(bf16[2,2,8,16,128]{4,3,2,1,0:T(8,128)(2,1)S(1)} %get-tuple-element.31), channel_id=1, source_target_pairs={{0,4},{1,21},{8,12},{9,29},{2,6},{3,23},{10,14},{11,31},{4,0},{5,1... | collective-permute-start | bytes 393224 | tf_op jit(solution)/shard_map/ppermute | solution.py:265
  107.1 3.5 %collective-permute-start.3 = (bf16[2,2,8,16,128]{4,3,2,1,0:T(8,128)(2,1)S(1)}, bf16[2,2,8,16,128]{4,3,2,1,0:T(8,128)(2,1)S(1)}, u32[]{:S(2)}, u32[]{:S(2)}) collective-permute-start(bf16[2,2,8,16,128]{4,3,2,1,0:T(8,128)(2,1)S(1)} %get-tuple-element.32), channel_id=1, source_target_pairs={{0,10},{1,27},{8,4},{9,21},{2,12},{3,29},{10,6},{11,23},{4,14},{5,... | collective-permute-start | bytes 393224 | tf_op jit(solution)/shard_map/ppermute | solution.py:265
  110.6 4.5 %collective-permute-start.4 = (bf16[2,2,8,16,128]{4,3,2,1,0:T(8,128)(2,1)S(1)}, bf16[2,2,8,16,128]{4,3,2,1,0:T(8,128)(2,1)S(1)}, u32[]{:S(2)}, u32[]{:S(2)}) collective-permute-start(bf16[2,2,8,16,128]{4,3,2,1,0:T(8,128)(2,1)S(1)} %get-tuple-element.33), channel_id=1, source_target_pairs={{0,12},{1,29},{8,6},{9,23},{2,14},{3,31},{10,0},{11,17},{4,8},{5,2... | collective-permute-start | bytes 393224 | tf_op jit(solution)/shard_map/ppermute | solution.py:265
  115.1 13.1 %collective-permute-done.13.refs_2_ = bf16[2,2,8,16,128]{4,3,2,1,0:T(8,128)(2,1)S(1)} collective-permute-done((bf16[2,2,8,16,128]{4,3,2,1,0:T(8,128)(2,1)S(1)}, bf16[2,2,8,16,128]{4,3,2,1,0:T(8,128)(2,1)S(1)}, u32[]{:S(2)}, u32[]{:S(2)}) %collective-permute-start.13) | collective-permute-done | bytes 131104 | tf_op jit(solution)/shard_map/ppermute | solution.py:265
  128.8 4.9 %collective-permute-done.3.refs_2_ = bf16[2,2,8,16,128]{4,3,2,1,0:T(8,128)(2,1)S(1)} collective-permute-done((bf16[2,2,8,16,128]{4,3,2,1,0:T(8,128)(2,1)S(1)}, bf16[2,2,8,16,128]{4,3,2,1,0:T(8,128)(2,1)S(1)}, u32[]{:S(2)}, u32[]{:S(2)}) %collective-permute-start.3) | collective-permute-done | bytes 131104 | tf_op jit(solution)/shard_map/ppermute | solution.py:265
  135.2 4.8 %collective-permute-done.5.refs_4_ = bf16[2,2,8,16,128]{4,3,2,1,0:T(8,128)(2,1)S(1)} collective-permute-done((bf16[2,2,8,16,128]{4,3,2,1,0:T(8,128)(2,1)S(1)}, bf16[2,2,8,16,128]{4,3,2,1,0:T(8,128)(2,1)S(1)}, u32[]{:S(2)}, u32[]{:S(2)}) %collective-permute-start.5) | collective-permute-done | bytes 131104 | tf_op jit(solution)/shard_map/ppermute | solution.py:265
  140.0 2.0 %collective-permute-start.16 = (bf16[2,2,8,16,128]{4,3,2,1,0:T(8,128)(2,1)S(1)}, bf16[2,2,8,16,128]{4,3,2,1,0:T(8,128)(2,1)S(1)}, u32[]{:S(2)}, u32[]{:S(2)}) collective-permute-start(bf16[2,2,8,16,128]{4,3,2,1,0:T(8,128)(2,1)S(1)} %get-tuple-element.46), channel_id=1, source_target_pairs={{0,6},{1,23},{8,14},{9,31},{2,0},{3,17},{10,8},{11,25},{4,2},{5,19... | collective-permute-start | bytes 393224 | tf_op jit(solution)/shard_map/ppermute | solution.py:265
  144.2 2.3 %collective-permute-start.18 = (bf16[2,2,8,16,128]{4,3,2,1,0:T(8,128)(2,1)S(1)}, bf16[2,2,8,16,128]{4,3,2,1,0:T(8,128)(2,1)S(1)}, u32[]{:S(2)}, u32[]{:S(2)}) collective-permute-start(bf16[2,2,8,16,128]{4,3,2,1,0:T(8,128)(2,1)S(1)} %get-tuple-element.48), channel_id=1, source_target_pairs={{0,14},{1,31},{8,0},{9,17},{2,8},{3,25},{10,2},{11,19},{4,10},{5,2... | collective-permute-start | bytes 393224 | tf_op jit(solution)/shard_map/ppermute | solution.py:265
  147.7 5.1 %collective-permute-done.14.refs_3_ = bf16[2,2,8,16,128]{4,3,2,1,0:T(8,128)(2,1)S(1)} collective-permute-done((bf16[2,2,8,16,128]{4,3,2,1,0:T(8,128)(2,1)S(1)}, bf16[2,2,8,16,128]{4,3,2,1,0:T(8,128)(2,1)S(1)}, u32[]{:S(2)}, u32[]{:S(2)}) %collective-permute-start.14) | collective-permute-done | bytes 131104 | tf_op jit(solution)/shard_map/ppermute | solution.py:265
  152.9 3.2 %collective-permute-done.16.refs_5_ = bf16[2,2,8,16,128]{4,3,2,1,0:T(8,128)(2,1)S(1)} collective-permute-done((bf16[2,2,8,16,128]{4,3,2,1,0:T(8,128)(2,1)S(1)}, bf16[2,2,8,16,128]{4,3,2,1,0:T(8,128)(2,1)S(1)}, u32[]{:S(2)}, u32[]{:S(2)}) %collective-permute-start.16) | collective-permute-done | bytes 131104 | tf_op jit(solution)/shard_map/ppermute | solution.py:265
  161.1 3.7 %invert.1 = bf16[2,8,64,1024]{3,2,1,0:T(8,128)(2,1)} custom-call(bf16[2,8,128,128]{3,2,1,0:T(8,128)(2,1)S(1)} %get-tuple-element.38.refs_8_.refs_0_, bf16[2,8,128,128]{3,2,1,0:T(8,128)(2,1)S(1)} %collective-permute-done.9.refs_1_, bf16[2,8,128,128]{3,2,1,0:T(8,128)(2,1)S(1)} %get-tuple-element.49.refs_2_, ...), custom_call_target="tpu_custom_call" | custom-call | flops 2147483648 | bytes 6291456 | tf_op jit(solution)/shard_map/invert/pallas_call | solution.py:204
  (36 shorter events, 15.3 us)
Async XLA Ops:
  0.0 1.9 %copy-start = (s32[14,64]{1,0:T(8,128)S(1)}, s32[14,64]{1,0:T(8,128)}, u32[]{:S(2)}) copy-start(s32[14,64]{1,0:T(8,128)} %param.3) | copy-start | bytes 10756
  46.1 26.9 %all-to-all-start.1 = ((bf16[16,14,16,128]{3,2,1,0:T(8,128)(2,1)}), bf16[16,14,16,128]{3,2,1,0:T(8,128)(2,1)S(1)}, u32[]{:S(2)}, u32[]{:S(2)}) async-start(bf16[16,14,16,128]{3,2,1,0:T(8,128)(2,1)} %get-tuple-element.40), calls=%async_computation.1 | async-start | bytes 1835008 | tf_op jit(solution)/shard_map/all_to_all | solution.py:291
  49.7 32.5 %collective-permute-start = (bf16[16,14,16,128]{3,2,1,0:T(8,128)(2,1)S(1)}, bf16[16,14,16,128]{3,2,1,0:T(8,128)(2,1)S(1)}, u32[]{:S(2)}, u32[]{:S(2)}) collective-permute-start(bf16[16,14,16,128]{3,2,1,0:T(8,128)(2,1)S(1)} %all_to_all.10.here), channel_id=1, source_target_pairs={{0,16},{1,241},{8,24},{9,249},{2,18},{3,243},{10,26},{11,251},{4,2... | collective-permute-start | bytes 2752520 | tf_op jit(solution)/shard_map/ppermute | solution.py:292
  73.1 15.3 %collective-permute-start.10 = (bf16[16,14,16,128]{3,2,1,0:T(8,128)(2,1)S(1)}, bf16[16,14,16,128]{3,2,1,0:T(8,128)(2,1)S(1)}, u32[]{:S(2)}, u32[]{:S(2)}) collective-permute-start(bf16[16,14,16,128]{3,2,1,0:T(8,128)(2,1)S(1)} %all-to-all-done.1.here), channel_id=1, source_target_pairs={{0,16},{1,241},{8,24},{9,249},{2,18},{3,243},{10,26},{11,251},{4,2... | collective-permute-start | bytes 2752520 | tf_op jit(solution)/shard_map/ppermute | solution.py:292
  93.7 13.4 %collective-permute-start.11 = (bf16[2,2,8,16,128]{4,3,2,1,0:T(8,128)(2,1)S(1)}, bf16[2,2,8,16,128]{4,3,2,1,0:T(8,128)(2,1)S(1)}, u32[]{:S(2)}, u32[]{:S(2)}) collective-permute-start(bf16[2,2,8,16,128]{4,3,2,1,0:T(8,128)(2,1)S(1)} %get-tuple-element.41), channel_id=1, source_target_pairs={{0,0},{1,17},{8,8},{9,25},{2,2},{3,19},{10,10},{11,27},{4,4},{5,21... | collective-permute-start | bytes 393224 | tf_op jit(solution)/shard_map/ppermute | solution.py:265
  95.7 14.9 %collective-permute-start.12 = (bf16[2,2,8,16,128]{4,3,2,1,0:T(8,128)(2,1)S(1)}, bf16[2,2,8,16,128]{4,3,2,1,0:T(8,128)(2,1)S(1)}, u32[]{:S(2)}, u32[]{:S(2)}) collective-permute-start(bf16[2,2,8,16,128]{4,3,2,1,0:T(8,128)(2,1)S(1)} %get-tuple-element.42), channel_id=1, source_target_pairs={{0,4},{1,21},{8,12},{9,29},{2,6},{3,23},{10,14},{11,31},{4,0},{5,1... | collective-permute-start | bytes 393224 | tf_op jit(solution)/shard_map/ppermute | solution.py:265
  97.8 30.4 %collective-permute-start.13 = (bf16[2,2,8,16,128]{4,3,2,1,0:T(8,128)(2,1)S(1)}, bf16[2,2,8,16,128]{4,3,2,1,0:T(8,128)(2,1)S(1)}, u32[]{:S(2)}, u32[]{:S(2)}) collective-permute-start(bf16[2,2,8,16,128]{4,3,2,1,0:T(8,128)(2,1)S(1)} %get-tuple-element.43), channel_id=1, source_target_pairs={{0,10},{1,27},{8,4},{9,21},{2,12},{3,29},{10,6},{11,23},{4,14},{5,... | collective-permute-start | bytes 393224 | tf_op jit(solution)/shard_map/ppermute | solution.py:265
  100.4 27.9 %collective-permute-start.1 = (bf16[2,2,8,16,128]{4,3,2,1,0:T(8,128)(2,1)S(1)}, bf16[2,2,8,16,128]{4,3,2,1,0:T(8,128)(2,1)S(1)}, u32[]{:S(2)}, u32[]{:S(2)}) collective-permute-start(bf16[2,2,8,16,128]{4,3,2,1,0:T(8,128)(2,1)S(1)} %get-tuple-element.30.refs_0_), channel_id=1, source_target_pairs={{0,0},{1,17},{8,8},{9,25},{2,2},{3,19},{10,10},{11,27},{4,4},{5,21... | collective-permute-start | bytes 393224 | tf_op jit(solution)/shard_map/ppermute | solution.py:265
  102.6 26.2 %collective-permute-start.2 = (bf16[2,2,8,16,128]{4,3,2,1,0:T(8,128)(2,1)S(1)}, bf16[2,2,8,16,128]{4,3,2,1,0:T(8,128)(2,1)S(1)}, u32[]{:S(2)}, u32[]{:S(2)}) collective-permute-start(bf16[2,2,8,16,128]{4,3,2,1,0:T(8,128)(2,1)S(1)} %get-tuple-element.31), channel_id=1, source_target_pairs={{0,4},{1,21},{8,12},{9,29},{2,6},{3,23},{10,14},{11,31},{4,0},{5,1... | collective-permute-start | bytes 393224 | tf_op jit(solution)/shard_map/ppermute | solution.py:265
  107.1 26.6 %collective-permute-start.3 = (bf16[2,2,8,16,128]{4,3,2,1,0:T(8,128)(2,1)S(1)}, bf16[2,2,8,16,128]{4,3,2,1,0:T(8,128)(2,1)S(1)}, u32[]{:S(2)}, u32[]{:S(2)}) collective-permute-start(bf16[2,2,8,16,128]{4,3,2,1,0:T(8,128)(2,1)S(1)} %get-tuple-element.32), channel_id=1, source_target_pairs={{0,10},{1,27},{8,4},{9,21},{2,12},{3,29},{10,6},{11,23},{4,14},{5,... | collective-permute-start | bytes 393224 | tf_op jit(solution)/shard_map/ppermute | solution.py:265
  110.6 24.6 %collective-permute-start.4 = (bf16[2,2,8,16,128]{4,3,2,1,0:T(8,128)(2,1)S(1)}, bf16[2,2,8,16,128]{4,3,2,1,0:T(8,128)(2,1)S(1)}, u32[]{:S(2)}, u32[]{:S(2)}) collective-permute-start(bf16[2,2,8,16,128]{4,3,2,1,0:T(8,128)(2,1)S(1)} %get-tuple-element.33), channel_id=1, source_target_pairs={{0,12},{1,29},{8,6},{9,23},{2,14},{3,31},{10,0},{11,17},{4,8},{5,2... | collective-permute-start | bytes 393224 | tf_op jit(solution)/shard_map/ppermute | solution.py:265
  128.2 11.8 %collective-permute-start.5 = (bf16[2,2,8,16,128]{4,3,2,1,0:T(8,128)(2,1)S(1)}, bf16[2,2,8,16,128]{4,3,2,1,0:T(8,128)(2,1)S(1)}, u32[]{:S(2)}, u32[]{:S(2)}) collective-permute-start(bf16[2,2,8,16,128]{4,3,2,1,0:T(8,128)(2,1)S(1)} %get-tuple-element.34), channel_id=1, source_target_pairs={{0,2},{1,19},{8,10},{9,27},{2,4},{3,21},{10,12},{11,29},{4,6},{5,2... | collective-permute-start | bytes 393224 | tf_op jit(solution)/shard_map/ppermute | solution.py:265
  128.2 11.8 %collective-permute-start.6 = (bf16[2,2,8,16,128]{4,3,2,1,0:T(8,128)(2,1)S(1)}, bf16[2,2,8,16,128]{4,3,2,1,0:T(8,128)(2,1)S(1)}, u32[]{:S(2)}, u32[]{:S(2)}) collective-permute-start(bf16[2,2,8,16,128]{4,3,2,1,0:T(8,128)(2,1)S(1)} %get-tuple-element.35), channel_id=1, source_target_pairs={{0,6},{1,23},{8,14},{9,31},{2,0},{3,17},{10,8},{11,25},{4,2},{5,19... | collective-permute-start | bytes 393224 | tf_op jit(solution)/shard_map/ppermute | solution.py:265
  128.8 13.2 %collective-permute-start.7 = (bf16[2,2,8,16,128]{4,3,2,1,0:T(8,128)(2,1)S(1)}, bf16[2,2,8,16,128]{4,3,2,1,0:T(8,128)(2,1)S(1)}, u32[]{:S(2)}, u32[]{:S(2)}) collective-permute-start(bf16[2,2,8,16,128]{4,3,2,1,0:T(8,128)(2,1)S(1)} %get-tuple-element.36), channel_id=1, source_target_pairs={{0,8},{1,25},{8,2},{9,19},{2,10},{3,27},{10,4},{11,21},{4,12},{5,2... | collective-permute-start | bytes 393224 | tf_op jit(solution)/shard_map/ppermute | solution.py:265
  133.7 10.5 %collective-permute-start.8 = (bf16[2,2,8,16,128]{4,3,2,1,0:T(8,128)(2,1)S(1)}, bf16[2,2,8,16,128]{4,3,2,1,0:T(8,128)(2,1)S(1)}, u32[]{:S(2)}, u32[]{:S(2)}) collective-permute-start(bf16[2,2,8,16,128]{4,3,2,1,0:T(8,128)(2,1)S(1)} %get-tuple-element.37), channel_id=1, source_target_pairs={{0,14},{1,31},{8,0},{9,17},{2,8},{3,25},{10,2},{11,19},{4,10},{5,2... | collective-permute-start | bytes 393224 | tf_op jit(solution)/shard_map/ppermute | solution.py:265
  135.2 17.7 %collective-permute-start.14 = (bf16[2,2,8,16,128]{4,3,2,1,0:T(8,128)(2,1)S(1)}, bf16[2,2,8,16,128]{4,3,2,1,0:T(8,128)(2,1)S(1)}, u32[]{:S(2)}, u32[]{:S(2)}) collective-permute-start(bf16[2,2,8,16,128]{4,3,2,1,0:T(8,128)(2,1)S(1)} %get-tuple-element.44), channel_id=1, source_target_pairs={{0,12},{1,29},{8,6},{9,23},{2,14},{3,31},{10,0},{11,17},{4,8},{5,2... | collective-permute-start | bytes 393224 | tf_op jit(solution)/shard_map/ppermute | solution.py:265
  140.0 12.9 %collective-permute-start.15 = (bf16[2,2,8,16,128]{4,3,2,1,0:T(8,128)(2,1)S(1)}, bf16[2,2,8,16,128]{4,3,2,1,0:T(8,128)(2,1)S(1)}, u32[]{:S(2)}, u32[]{:S(2)}) collective-permute-start(bf16[2,2,8,16,128]{4,3,2,1,0:T(8,128)(2,1)S(1)} %get-tuple-element.45), channel_id=1, source_target_pairs={{0,2},{1,19},{8,10},{9,27},{2,4},{3,21},{10,12},{11,29},{4,6},{5,2... | collective-permute-start | bytes 393224 | tf_op jit(solution)/shard_map/ppermute | solution.py:265
  140.0 16.1 %collective-permute-start.16 = (bf16[2,2,8,16,128]{4,3,2,1,0:T(8,128)(2,1)S(1)}, bf16[2,2,8,16,128]{4,3,2,1,0:T(8,128)(2,1)S(1)}, u32[]{:S(2)}, u32[]{:S(2)}) collective-permute-start(bf16[2,2,8,16,128]{4,3,2,1,0:T(8,128)(2,1)S(1)} %get-tuple-element.46), channel_id=1, source_target_pairs={{0,6},{1,23},{8,14},{9,31},{2,0},{3,17},{10,8},{11,25},{4,2},{5,19... | collective-permute-start | bytes 393224 | tf_op jit(solution)/shard_map/ppermute | solution.py:265
  142.0 14.1 %collective-permute-start.17 = (bf16[2,2,8,16,128]{4,3,2,1,0:T(8,128)(2,1)S(1)}, bf16[2,2,8,16,128]{4,3,2,1,0:T(8,128)(2,1)S(1)}, u32[]{:S(2)}, u32[]{:S(2)}) collective-permute-start(bf16[2,2,8,16,128]{4,3,2,1,0:T(8,128)(2,1)S(1)} %get-tuple-element.47), channel_id=1, source_target_pairs={{0,8},{1,25},{8,2},{9,19},{2,10},{3,27},{10,4},{11,21},{4,12},{5,2... | collective-permute-start | bytes 393224 | tf_op jit(solution)/shard_map/ppermute | solution.py:265
  144.2 12.9 %collective-permute-start.18 = (bf16[2,2,8,16,128]{4,3,2,1,0:T(8,128)(2,1)S(1)}, bf16[2,2,8,16,128]{4,3,2,1,0:T(8,128)(2,1)S(1)}, u32[]{:S(2)}, u32[]{:S(2)}) collective-permute-start(bf16[2,2,8,16,128]{4,3,2,1,0:T(8,128)(2,1)S(1)} %get-tuple-element.48), channel_id=1, source_target_pairs={{0,14},{1,31},{8,0},{9,17},{2,8},{3,25},{10,2},{11,19},{4,10},{5,2... | collective-permute-start | bytes 393224 | tf_op jit(solution)/shard_map/ppermute | solution.py:265
  158.3 2.0 %collective-permute-start.19 = (bf16[2,8,128,128]{3,2,1,0:T(8,128)(2,1)S(1)}, bf16[2,8,128,128]{3,2,1,0:T(8,128)(2,1)S(1)}, u32[]{:S(2)}, u32[]{:S(2)}) collective-permute-start(bf16[2,8,128,128]{3,2,1,0:T(8,128)(2,1)S(1)} %get-tuple-element.50), channel_id=1, source_target_pairs={{0,1},{1,0},{2,3},{3,2},{4,5},{5,4},{6,7},{7,6},{8,9},{9,8},{10,11... | collective-permute-start | bytes 1572872 | tf_op jit(solution)/shard_map/ppermute | solution.py:276
  158.4 2.6 %collective-permute-start.9 = (bf16[2,8,128,128]{3,2,1,0:T(8,128)(2,1)S(1)}, bf16[2,8,128,128]{3,2,1,0:T(8,128)(2,1)S(1)}, u32[]{:S(2)}, u32[]{:S(2)}) collective-permute-start(bf16[2,8,128,128]{3,2,1,0:T(8,128)(2,1)S(1)} %get-tuple-element.39), channel_id=1, source_target_pairs={{0,1},{1,0},{2,3},{3,2},{4,5},{5,4},{6,7},{7,6},{8,9},{9,8},{10,11... | collective-permute-start | bytes 1572872 | tf_op jit(solution)/shard_map/ppermute | solution.py:276

commit v5 on v4

--- a/solution.py
+++ b/solution.py
@@ -16,6 +16,7 @@
 BINS = 512
 WIN = 14
 CH = 64
+STEP = 2
 CHUNKS = 2
 FC = 32 // CHUNKS
 CBINS = BINS // CHUNKS
@@ -38,7 +39,7 @@
 
 
 def whiten_kernel(pos_ref, spec_ref, flags_ref, *refs):
-    outs, core, (band, eye, invc, white) = refs[:CHUNKS], refs[CHUNKS], refs[CHUNKS + 1 :]
+    outs, core, (band, eye, invc) = refs[:CHUNKS], refs[CHUNKS], refs[CHUNKS + 1 :]
     w = pl.program_id(0)
 
     @pl.when(w == 0)
@@ -53,46 +54,44 @@
         count = jnp.minimum(f + SMOOTH_HALF, BINS - 1) - jnp.maximum(f - SMOOTH_HALF, 0) + 1
         invc[...] = 1.0 / count.astype(F32)
 
-    re16, im16 = spec_ref[0, 0], spec_ref[1, 0]
-    re, im = re16.astype(F32), im16.astype(F32)
-    amp = jnp.sqrt(re * re + im * im).astype(BF16)
-    amp2 = jnp.concatenate([amp, amp], axis=0)
-    both = jnp.concatenate([re16, im16], axis=0)
     nt = (((1,), (1,)), ((), ()))
-    summed = lax.dot_general(band[...], amp2, nt, preferred_element_type=F32)
-    scale = flags_ref[0].astype(F32) / (summed * invc[...] + 1e-05)
-    for h in range(2):
-        half = lax.dot_general(
-            eye[...], both[:, h * 256 : (h + 1) * 256], nt, preferred_element_type=F32
-        )
-        white[h * 256 : (h + 1) * 256] = (half * scale[h * 256 : (h + 1) * 256]).astype(BF16)
-    for k in range(CHUNKS):
-        for z in range(8):
-            for c in range(2):
-                start = k * CBINS + z * 2 * FC + c * FC
-                outs[k][place(z) * 2 + c, w] = white[start : start + FC]
+    for v in range(STEP):
+        re16, im16 = spec_ref[0, v], spec_ref[1, v]
+        re, im = re16.astype(F32), im16.astype(F32)
+        amp = jnp.sqrt(re * re + im * im).astype(BF16)
+        amp2 = jnp.concatenate([amp, amp], axis=0)
+        both = jnp.concatenate([re16, im16], axis=0)
+        summed = lax.dot_general(band[...], amp2, nt, preferred_element_type=F32)
+        scale = flags_ref[v].astype(F32) / (summed * invc[...] + 1e-05)
+        for h in range(2):
+            half = lax.dot_general(
+                eye[...], both[:, h * 256 : (h + 1) * 256], nt, preferred_element_type=F32
+            )
+            white = (half * scale[h * 256 : (h + 1) * 256]).astype(BF16)
+            for n in range(256 // FC):
+                k, d = divmod(h * 256 // FC + n, 16)
+                outs[k][place(d // 2) * 2 + d % 2, w * STEP + v] = white[n * FC : (n + 1) * FC]
     core[0] = pos_ref[1]
 
 
 def whiten(spec, flags2, pos):
-    shape = jax.ShapeDtypeStruct((16, WIN, FC, 128), BF16)
+    shape = pltpu.HBM((16, WIN, FC, 128), BF16)
     full = pl.BlockSpec((16, WIN, FC, 128), lambda w, *_: (0, 0, 0, 0))
     return pl.pallas_call(
         whiten_kernel,
         out_shape=[shape] * CHUNKS + [jax.ShapeDtypeStruct((1,), jnp.int32)],
         grid_spec=pltpu.PrefetchScalarGridSpec(
             num_scalar_prefetch=1,
-            grid=(WIN,),
+            grid=(WIN // STEP,),
             in_specs=[
-                pl.BlockSpec((2, 1, CH, BINS), lambda w, *_: (0, w, 0, 0)),
-                pl.BlockSpec((1, 1, 128), lambda w, *_: (w, 0, 0)),
+                pl.BlockSpec((2, STEP, CH, BINS), lambda w, *_: (0, w, 0, 0)),
+                pl.BlockSpec((STEP, 1, 128), lambda w, *_: (w, 0, 0)),
             ],
             out_specs=[full] * CHUNKS + [SM],
             scratch_shapes=[
                 pltpu.VMEM((BINS, BINS), BF16),
                 pltpu.VMEM((256, 256), BF16),
                 pltpu.VMEM((BINS, 128), F32),
-                pltpu.VMEM((BINS, 128), BF16),
             ],
         ),
         compiler_params=params(),
@@ -103,13 +102,13 @@
     )(pos, spec, flags2)
 
 
-def cross_kernel(pos_ref, here, there, *refs):
+def cross_kernel(turned, pos_ref, here, there, *refs):
     outs, (wide, res) = refs[-10:-2], refs[-2:]
     z, c = pos_ref[0], pos_ref[1]
     rows = 8 * WIN * FC
     for n, ref in enumerate((here, there)):
         for b in range(2):
-            base = pl.multiple_of(((n ^ c) * 2 + b) * rows, rows)
+            base = pl.multiple_of(((n ^ c if turned else n) * 2 + b) * rows, rows)
             wide[pl.ds(base, rows)] = ref[8 * b : 8 * b + 8].reshape(rows, 128).astype(F32)
     sign = jnp.where(lax.broadcasted_iota(jnp.int32, (CH, 128), 1) < CH, 1.0, -1.0).astype(F32)
     tn = (((0,), (0,)), ((), ()))
@@ -143,10 +142,10 @@
                     outs[r][crel, rnd, i] = res[pl.ds(base + i, FC, stride=CH), :].astype(BF16)
 
 
-def cross(here, there, pos, *after):
+def cross(turned, here, there, pos, *after):
     shape = jax.ShapeDtypeStruct((2, 2, 8, FC, 128), BF16)
     return pl.pallas_call(
-        cross_kernel,
+        functools.partial(cross_kernel, turned),
         out_shape=[shape] * 8,
         in_specs=[SM] + [VM] * 2 + [ANY] * len(after),
         out_specs=[VM] * 8,
@@ -260,15 +259,11 @@
 EVERY = [(m, z, c) for m in range(16) for z in range(8) for c in range(2)]
 
 
-def ring_back(value, r):
-    pairs = [(device(m, z, c), device(m + c, z + r, c)) for m, z, c in EVERY]
-    return lax.ppermute(value, ALL, pairs)
-
-
-def round_ring(pieces):
+def round_ring(pieces, turned):
     got = []
     for r in ORDER:
-        got.append(ring_back(pieces[r], r))
+        pairs = [(device(m, z, c), device(m + c * turned, z + r, c)) for m, z, c in EVERY]
+        got.append(lax.ppermute(pieces[r], ALL, pairs) if r or turned else pieces[r])
     return got
 
 
@@ -283,16 +278,19 @@
     scaling = 1.0 / math.sqrt(windows * BINS)
     flags2 = jnp.concatenate([valid_flags, valid_flags], axis=1)[:, None, :]
     *white, core = whiten(jnp.transpose(spectra, (2, 0, 1, 3)), flags2, pos)
-    shift = [(device(m, z, c), device(m + 1 - 2 * c, z, c)) for m, z, c in EVERY]
     table = join_table(lag_table(core[0]))
     parts = []
     crossed, turned = (table,), ()
     for k in range(CHUNKS):
+        turned_round = int(k == CHUNKS - 1)
+        shift = [
+            (device(m, z, c), device(m + 1 - 2 * c * turned_round, z, c)) for m, z, c in EVERY
+        ]
         here = lax.all_to_all(white[k], ("zl", "zh", "c"), 0, 0, tiled=True)
         there = lax.ppermute(here, ALL, shift)
-        out = cross(here, there, pos, *crossed)
+        out = cross(turned_round, here, there, pos, *crossed)
         crossed = (out[0],)
-        same, other = turn(round_ring(out), pos, *turned)
+        same, other = turn(round_ring(out, turned_round), pos, *turned)
         turned = (same,)
         parts += [same, other_core(other)]
     return invert(parts, table, scaling)

time: 165 us -> 162 us (0.982)
  Pallas kernels: 27 us -> 24.9 us
  starting transfers between devices: 43.1 us -> 41.3 us
    all_to_all x1, waiting for transfers between devices: 18.4 us -> 22 us  [shards(): here = lax.all_to_all(white[k], ('zl', 'zh', 'c'), 0, 0, tiled=True)]
    ppermute x2, starting transfers between devices: 9.94 us -> 6.31 us  [shards(): there = lax.ppermute(here, ALL, shift)]
    ppermute x16 -> x15, waiting for transfers between devices: 32.9 us -> 30 us  [round_ring(): lax.ppermute(pieces[r], ALL, pairs)]
    pallas_call x1, Pallas kernels: 8.49 us -> 6.34 us  [whiten(): pl.pallas_call(whiten_kernel, out_shape=[shape] * CHUNKS + [jax.ShapeDtyp...]
    ppermute x16 -> x15, starting transfers between devices: 29 us -> 30.8 us  [round_ring(): lax.ppermute(pieces[r], ALL, pairs)]
  transfers between devices with their start and end apart: 21 -> 20, of which waited for: 11 -> 11; matrix products, arithmetic and copies ran while one was open for 2% -> 2% of each run, Pallas kernels for 5% -> 5%
where the time goes in v5:
time: 162 us
  waiting for transfers between devices  54.9 us (34%)
  starting transfers between devices  41.3 us (25%)
  blocking collectives  35.8 us (22%)
  Pallas kernels  24.9 us (15%)
  other arithmetic  2.98 us (2%)
  local copies, waits for them, and re-layouts  1.91 us (1%)
    all_to_all x1, blocking collectives, shards(): here = lax.all_to_all(white[k], ('zl', 'zh', 'c'), 0, 0, tiled=True)  35.8 us
    ppermute x15, starting transfers between devices, round_ring(): lax.ppermute(pieces[r], ALL, pairs)  30.8 us
    ppermute x15, waiting for transfers between devices, round_ring(): lax.ppermute(pieces[r], ALL, pairs)  30 us
    all_to_all x1, waiting for transfers between devices, shards(): here = lax.all_to_all(white[k], ('zl', 'zh', 'c'), 0, 0, tiled=True)  22 us
    pallas_call x2, Pallas kernels, cross(): pl.pallas_call(functools.partial(cross_kernel, turned), out_shape=[shape]...  10.8 us
    pallas_call x1, Pallas kernels, whiten(): pl.pallas_call(whiten_kernel, out_shape=[shape] * CHUNKS + [jax.ShapeDtyp...  6.34 us
    ppermute x2, starting transfers between devices, shards(): there = lax.ppermute(here, ALL, shift)  6.31 us
    pallas_call x1, Pallas kernels, invert(): pl.pallas_call(functools.partial(invert_kernel, scaling), out_shape=jax.S...  3.73 us
  transfers between devices with their start and end apart: 20, of which 11 were waited for; matrix products, arithmetic and copies ran while one was open for 2% of the time, Pallas kernels for 5%

profile of v5, /device:TPU:1, one launch (start us, length us, event | category | flops | bytes accessed | tf_op | source)
XLA Modules:
  0.0 161.8 jit_solution(10003479450750061018)
XLA Ops:
  0.0 1.9 %copy.5 = bf16[14,64,2,512]{3,1,0,2:T(8,128)(2,1)S(1)} copy(bf16[14,64,2,512]{3,2,1,0:T(2,128)(2,1)} %param.2) | data formatting | bytes 3670016 | tf_op args[0]
  2.1 6.3 %whiten.1 = (bf16[16,14,16,128]{3,2,1,0:T(8,128)(2,1)}, bf16[16,14,16,128]{3,2,1,0:T(8,128)(2,1)}, s32[1]{0:T(128)}) custom-call(s32[2]{0:T(128)S(1)} %pad_add_fusion.1.pos_ref, bf16[2,14,64,512]{3,2,1,0:T(8,128)(2,1)S(1)} %bitcast.6, s32[14,1,128]{2,1,0:T(1,128)S(1)} %broadcast_in_dim.3.flags_ref), custom_call_target="tpu_custom_call" | custom-call | flops 1409286144 | bytes 4194304 | tf_op jit(solution)/shard_map/whiten/pallas_call | solution.py:80
  8.4 35.8 %all_to_all.10.here = bf16[16,14,16,128]{3,2,1,0:T(8,128)(2,1)S(1)} all-to-all(bf16[16,14,16,128]{3,2,1,0:T(8,128)(2,1)} %get-tuple-element.28), channel_id=1, replica_groups=mesh['x'=4,'y'=4,'zl'=2,'zh'=4,'c'=2] {'zl','zh','c'}, dimensions={0} | all-to-all | bytes 1835008 | tf_op jit(solution)/shard_map/all_to_all | solution.py:289
  44.2 3.5 %all-to-all-start.1 = ((bf16[16,14,16,128]{3,2,1,0:T(8,128)(2,1)}), bf16[16,14,16,128]{3,2,1,0:T(8,128)(2,1)S(1)}, u32[]{:S(2)}, u32[]{:S(2)}) async-start(bf16[16,14,16,128]{3,2,1,0:T(8,128)(2,1)} %get-tuple-element.40), calls=%async_computation.1 | async-start | bytes 1835008 | tf_op jit(solution)/shard_map/all_to_all | solution.py:289
  49.1 22.0 %all-to-all-done.1.here = bf16[16,14,16,128]{3,2,1,0:T(8,128)(2,1)S(1)} async-done(((bf16[16,14,16,128]{3,2,1,0:T(8,128)(2,1)}), bf16[16,14,16,128]{3,2,1,0:T(8,128)(2,1)S(1)}, u32[]{:S(2)}, u32[]{:S(2)}) %all-to-all-start.1) | async-done | bytes 917536 | tf_op jit(solution)/shard_map/all_to_all | solution.py:289
  71.1 4.9 %collective-permute-start.9 = (bf16[16,14,16,128]{3,2,1,0:T(8,128)(2,1)S(1)}, bf16[16,14,16,128]{3,2,1,0:T(8,128)(2,1)S(1)}, u32[]{:S(2)}, u32[]{:S(2)}) collective-permute-start(bf16[16,14,16,128]{3,2,1,0:T(8,128)(2,1)S(1)} %all-to-all-done.1.here), channel_id=1, source_target_pairs={{0,16},{1,241},{8,24},{9,249},{2,18},{3,243},{10,26},{11,251},{4,2... | collective-permute-start | bytes 2752520 | tf_op jit(solution)/shard_map/ppermute | solution.py:290
  76.7 2.2 %fusion.12 = (f32[512,128]{1,0:T(8,128)S(1)}, f32[512,128]{1,0:T(8,128)S(1)}, f32[512,128]{1,0:T(8,128)S(1)}, f32[512,128]{1,0:T(8,128)S(1)}) fusion(s32[128]{0:T(128)S(1)} %get-tuple-element.55, s32[128]{0:T(128)S(1)} %get-tuple-element.56, pred[128]{0:T(512)(128)(4,1)S(1)} %compare_and_fusion, s32[512]{0:T(512)S(1)} %fusion.22), kind=kLoop, calls=%fused_computation.17 | loop fusion | flops 1376256 | bytes 1051776 | tf_op jit(solution)/shard_map/sin | solution.py:219
  80.3 5.4 %cross.2 = (bf16[2,2,8,16,128]{4,3,2,1,0:T(8,128)(2,1)S(1)}, bf16[2,2,8,16,128]{4,3,2,1,0:T(8,128)(2,1)S(1)}, bf16[2,2,8,16,128]{4,3,2,1,0:T(8,128)(2,1)S(1)}, b...) custom-call(s32[2]{0:T(128)S(1)} %pad_add_fusion.1.pos_ref, ...), custom_call_target="tpu_custom_call" | custom-call | flops 536870912 | bytes 3145728 | tf_op jit(solution)/shard_map/cross/pallas_call | solution.py:147
  86.4 5.4 %cross.3 = (bf16[2,2,8,16,128]{4,3,2,1,0:T(8,128)(2,1)S(1)}, bf16[2,2,8,16,128]{4,3,2,1,0:T(8,128)(2,1)S(1)}, bf16[2,2,8,16,128]{4,3,2,1,0:T(8,128)(2,1)S(1)}, b...) custom-call(s32[2]{0:T(128)S(1)} %pad_add_fusion.1.pos_ref, ...), custom_call_target="tpu_custom_call" | custom-call | flops 536870912 | bytes 3145728 | tf_op jit(solution)/shard_map/cross/pallas_call | solution.py:147
  91.8 1.9 %collective-permute-start.10 = (bf16[2,2,8,16,128]{4,3,2,1,0:T(8,128)(2,1)S(1)}, bf16[2,2,8,16,128]{4,3,2,1,0:T(8,128)(2,1)S(1)}, u32[]{:S(2)}, u32[]{:S(2)}) collective-permute-start(bf16[2,2,8,16,128]{4,3,2,1,0:T(8,128)(2,1)S(1)} %get-tuple-element.41), channel_id=1, source_target_pairs={{0,0},{1,17},{8,8},{9,25},{2,2},{3,19},{10,10},{11,27},{4,4},{5,21... | collective-permute-start | bytes 393224 | tf_op jit(solution)/shard_map/ppermute | solution.py:266
  93.7 2.2 %collective-permute-start.11 = (bf16[2,2,8,16,128]{4,3,2,1,0:T(8,128)(2,1)S(1)}, bf16[2,2,8,16,128]{4,3,2,1,0:T(8,128)(2,1)S(1)}, u32[]{:S(2)}, u32[]{:S(2)}) collective-permute-start(bf16[2,2,8,16,128]{4,3,2,1,0:T(8,128)(2,1)S(1)} %get-tuple-element.42), channel_id=1, source_target_pairs={{0,4},{1,21},{8,12},{9,29},{2,6},{3,23},{10,14},{11,31},{4,0},{5,1... | collective-permute-start | bytes 393224 | tf_op jit(solution)/shard_map/ppermute | solution.py:266
  95.9 2.5 %collective-permute-start.12 = (bf16[2,2,8,16,128]{4,3,2,1,0:T(8,128)(2,1)S(1)}, bf16[2,2,8,16,128]{4,3,2,1,0:T(8,128)(2,1)S(1)}, u32[]{:S(2)}, u32[]{:S(2)}) collective-permute-start(bf16[2,2,8,16,128]{4,3,2,1,0:T(8,128)(2,1)S(1)} %get-tuple-element.43), channel_id=1, source_target_pairs={{0,10},{1,27},{8,4},{9,21},{2,12},{3,29},{10,6},{11,23},{4,14},{5,... | collective-permute-start | bytes 393224 | tf_op jit(solution)/shard_map/ppermute | solution.py:266
  98.4 4.5 %collective-permute-start.1 = (bf16[2,2,8,16,128]{4,3,2,1,0:T(8,128)(2,1)S(1)}, bf16[2,2,8,16,128]{4,3,2,1,0:T(8,128)(2,1)S(1)}, u32[]{:S(2)}, u32[]{:S(2)}) collective-permute-start(bf16[2,2,8,16,128]{4,3,2,1,0:T(8,128)(2,1)S(1)} %get-tuple-element.31), channel_id=1, source_target_pairs={{0,4},{1,5},{8,12},{9,13},{2,6},{3,7},{10,14},{11,15},{4,0},{5,1},... | collective-permute-start | bytes 393224 | tf_op jit(solution)/shard_map/ppermute | solution.py:266
  102.9 2.5 %collective-permute-start.2 = (bf16[2,2,8,16,128]{4,3,2,1,0:T(8,128)(2,1)S(1)}, bf16[2,2,8,16,128]{4,3,2,1,0:T(8,128)(2,1)S(1)}, u32[]{:S(2)}, u32[]{:S(2)}) collective-permute-start(bf16[2,2,8,16,128]{4,3,2,1,0:T(8,128)(2,1)S(1)} %get-tuple-element.32), channel_id=1, source_target_pairs={{0,10},{1,11},{8,4},{9,5},{2,12},{3,13},{10,6},{11,7},{4,14},{5,15... | collective-permute-start | bytes 393224 | tf_op jit(solution)/shard_map/ppermute | solution.py:266
  105.4 2.0 %collective-permute-start.3 = (bf16[2,2,8,16,128]{4,3,2,1,0:T(8,128)(2,1)S(1)}, bf16[2,2,8,16,128]{4,3,2,1,0:T(8,128)(2,1)S(1)}, u32[]{:S(2)}, u32[]{:S(2)}) collective-permute-start(bf16[2,2,8,16,128]{4,3,2,1,0:T(8,128)(2,1)S(1)} %get-tuple-element.33), channel_id=1, source_target_pairs={{0,12},{1,13},{8,6},{9,7},{2,14},{3,15},{10,0},{11,1},{4,8},{5,9},... | collective-permute-start | bytes 393224 | tf_op jit(solution)/shard_map/ppermute | solution.py:266
  107.4 5.7 %collective-permute-start.4 = (bf16[2,2,8,16,128]{4,3,2,1,0:T(8,128)(2,1)S(1)}, bf16[2,2,8,16,128]{4,3,2,1,0:T(8,128)(2,1)S(1)}, u32[]{:S(2)}, u32[]{:S(2)}) collective-permute-start(bf16[2,2,8,16,128]{4,3,2,1,0:T(8,128)(2,1)S(1)} %get-tuple-element.34), channel_id=1, source_target_pairs={{0,2},{1,3},{8,10},{9,11},{2,4},{3,5},{10,12},{11,13},{4,6},{5,7},... | collective-permute-start | bytes 393224 | tf_op jit(solution)/shard_map/ppermute | solution.py:266
  113.1 13.0 %collective-permute-done.12.refs_2_ = bf16[2,2,8,16,128]{4,3,2,1,0:T(8,128)(2,1)S(1)} collective-permute-done((bf16[2,2,8,16,128]{4,3,2,1,0:T(8,128)(2,1)S(1)}, bf16[2,2,8,16,128]{4,3,2,1,0:T(8,128)(2,1)S(1)}, u32[]{:S(2)}, u32[]{:S(2)}) %collective-permute-start.12) | collective-permute-done | bytes 131104 | tf_op jit(solution)/shard_map/ppermute | solution.py:266
  126.1 3.5 %collective-permute-done.2.refs_2_ = bf16[2,2,8,16,128]{4,3,2,1,0:T(8,128)(2,1)S(1)} collective-permute-done((bf16[2,2,8,16,128]{4,3,2,1,0:T(8,128)(2,1)S(1)}, bf16[2,2,8,16,128]{4,3,2,1,0:T(8,128)(2,1)S(1)}, u32[]{:S(2)}, u32[]{:S(2)}) %collective-permute-start.2) | collective-permute-done | bytes 131104 | tf_op jit(solution)/shard_map/ppermute | solution.py:266
  130.3 3.0 %collective-permute-done.4.refs_4_ = bf16[2,2,8,16,128]{4,3,2,1,0:T(8,128)(2,1)S(1)} collective-permute-done((bf16[2,2,8,16,128]{4,3,2,1,0:T(8,128)(2,1)S(1)}, bf16[2,2,8,16,128]{4,3,2,1,0:T(8,128)(2,1)S(1)}, u32[]{:S(2)}, u32[]{:S(2)}) %collective-permute-start.4) | collective-permute-done | bytes 131104 | tf_op jit(solution)/shard_map/ppermute | solution.py:266
  135.0 2.2 %collective-permute-start.15 = (bf16[2,2,8,16,128]{4,3,2,1,0:T(8,128)(2,1)S(1)}, bf16[2,2,8,16,128]{4,3,2,1,0:T(8,128)(2,1)S(1)}, u32[]{:S(2)}, u32[]{:S(2)}) collective-permute-start(bf16[2,2,8,16,128]{4,3,2,1,0:T(8,128)(2,1)S(1)} %get-tuple-element.46), channel_id=1, source_target_pairs={{0,6},{1,23},{8,14},{9,31},{2,0},{3,17},{10,8},{11,25},{4,2},{5,19... | collective-permute-start | bytes 393224 | tf_op jit(solution)/shard_map/ppermute | solution.py:266
  137.2 4.6 %collective-permute-start.16 = (bf16[2,2,8,16,128]{4,3,2,1,0:T(8,128)(2,1)S(1)}, bf16[2,2,8,16,128]{4,3,2,1,0:T(8,128)(2,1)S(1)}, u32[]{:S(2)}, u32[]{:S(2)}) collective-permute-start(bf16[2,2,8,16,128]{4,3,2,1,0:T(8,128)(2,1)S(1)} %get-tuple-element.47), channel_id=1, source_target_pairs={{0,8},{1,25},{8,2},{9,19},{2,10},{3,27},{10,4},{11,21},{4,12},{5,2... | collective-permute-start | bytes 393224 | tf_op jit(solution)/shard_map/ppermute | solution.py:266
  144.6 2.0 %collective-permute-done.14.refs_4_ = bf16[2,2,8,16,128]{4,3,2,1,0:T(8,128)(2,1)S(1)} collective-permute-done((bf16[2,2,8,16,128]{4,3,2,1,0:T(8,128)(2,1)S(1)}, bf16[2,2,8,16,128]{4,3,2,1,0:T(8,128)(2,1)S(1)}, u32[]{:S(2)}, u32[]{:S(2)}) %collective-permute-start.14) | collective-permute-done | bytes 131104 | tf_op jit(solution)/shard_map/ppermute | solution.py:266
  146.6 6.4 %collective-permute-done.15.refs_5_ = bf16[2,2,8,16,128]{4,3,2,1,0:T(8,128)(2,1)S(1)} collective-permute-done((bf16[2,2,8,16,128]{4,3,2,1,0:T(8,128)(2,1)S(1)}, bf16[2,2,8,16,128]{4,3,2,1,0:T(8,128)(2,1)S(1)}, u32[]{:S(2)}, u32[]{:S(2)}) %collective-permute-start.15) | collective-permute-done | bytes 131104 | tf_op jit(solution)/shard_map/ppermute | solution.py:266
  158.1 3.7 %invert.1 = bf16[2,8,64,1024]{3,2,1,0:T(8,128)(2,1)} custom-call(bf16[2,8,128,128]{3,2,1,0:T(8,128)(2,1)S(1)} %get-tuple-element.38.refs_8_.refs_0_, bf16[2,8,128,128]{3,2,1,0:T(8,128)(2,1)S(1)} %collective-permute-done.8.refs_1_, bf16[2,8,128,128]{3,2,1,0:T(8,128)(2,1)S(1)} %get-tuple-element.49.refs_2_, ...), custom_call_target="tpu_custom_call" | custom-call | flops 2147483648 | bytes 6291456 | tf_op jit(solution)/shard_map/invert/pallas_call | solution.py:203
  (34 shorter events, 14.4 us)
Async XLA Ops:
  0.0 1.9 %copy-start = (s32[14,64]{1,0:T(8,128)S(1)}, s32[14,64]{1,0:T(8,128)}, u32[]{:S(2)}) copy-start(s32[14,64]{1,0:T(8,128)} %param.3) | copy-start | bytes 10756
  44.2 26.9 %all-to-all-start.1 = ((bf16[16,14,16,128]{3,2,1,0:T(8,128)(2,1)}), bf16[16,14,16,128]{3,2,1,0:T(8,128)(2,1)S(1)}, u32[]{:S(2)}, u32[]{:S(2)}) async-start(bf16[16,14,16,128]{3,2,1,0:T(8,128)(2,1)} %get-tuple-element.40), calls=%async_computation.1 | async-start | bytes 1835008 | tf_op jit(solution)/shard_map/all_to_all | solution.py:289
  47.8 32.5 %collective-permute-start = (bf16[16,14,16,128]{3,2,1,0:T(8,128)(2,1)S(1)}, bf16[16,14,16,128]{3,2,1,0:T(8,128)(2,1)S(1)}, u32[]{:S(2)}, u32[]{:S(2)}) collective-permute-start(bf16[16,14,16,128]{3,2,1,0:T(8,128)(2,1)S(1)} %all_to_all.10.here), channel_id=1, source_target_pairs={{0,16},{1,17},{8,24},{9,25},{2,18},{3,19},{10,26},{11,27},{4,20},{... | collective-permute-start | bytes 2752520 | tf_op jit(solution)/shard_map/ppermute | solution.py:290
  71.1 15.3 %collective-permute-start.9 = (bf16[16,14,16,128]{3,2,1,0:T(8,128)(2,1)S(1)}, bf16[16,14,16,128]{3,2,1,0:T(8,128)(2,1)S(1)}, u32[]{:S(2)}, u32[]{:S(2)}) collective-permute-start(bf16[16,14,16,128]{3,2,1,0:T(8,128)(2,1)S(1)} %all-to-all-done.1.here), channel_id=1, source_target_pairs={{0,16},{1,241},{8,24},{9,249},{2,18},{3,243},{10,26},{11,251},{4,2... | collective-permute-start | bytes 2752520 | tf_op jit(solution)/shard_map/ppermute | solution.py:290
  91.8 13.6 %collective-permute-start.10 = (bf16[2,2,8,16,128]{4,3,2,1,0:T(8,128)(2,1)S(1)}, bf16[2,2,8,16,128]{4,3,2,1,0:T(8,128)(2,1)S(1)}, u32[]{:S(2)}, u32[]{:S(2)}) collective-permute-start(bf16[2,2,8,16,128]{4,3,2,1,0:T(8,128)(2,1)S(1)} %get-tuple-element.41), channel_id=1, source_target_pairs={{0,0},{1,17},{8,8},{9,25},{2,2},{3,19},{10,10},{11,27},{4,4},{5,21... | collective-permute-start | bytes 393224 | tf_op jit(solution)/shard_map/ppermute | solution.py:266
  93.7 13.7 %collective-permute-start.11 = (bf16[2,2,8,16,128]{4,3,2,1,0:T(8,128)(2,1)S(1)}, bf16[2,2,8,16,128]{4,3,2,1,0:T(8,128)(2,1)S(1)}, u32[]{:S(2)}, u32[]{:S(2)}) collective-permute-start(bf16[2,2,8,16,128]{4,3,2,1,0:T(8,128)(2,1)S(1)} %get-tuple-element.42), channel_id=1, source_target_pairs={{0,4},{1,21},{8,12},{9,29},{2,6},{3,23},{10,14},{11,31},{4,0},{5,1... | collective-permute-start | bytes 393224 | tf_op jit(solution)/shard_map/ppermute | solution.py:266
  95.9 30.1 %collective-permute-start.12 = (bf16[2,2,8,16,128]{4,3,2,1,0:T(8,128)(2,1)S(1)}, bf16[2,2,8,16,128]{4,3,2,1,0:T(8,128)(2,1)S(1)}, u32[]{:S(2)}, u32[]{:S(2)}) collective-permute-start(bf16[2,2,8,16,128]{4,3,2,1,0:T(8,128)(2,1)S(1)} %get-tuple-element.43), channel_id=1, source_target_pairs={{0,10},{1,27},{8,4},{9,21},{2,12},{3,29},{10,6},{11,23},{4,14},{5,... | collective-permute-start | bytes 393224 | tf_op jit(solution)/shard_map/ppermute | solution.py:266
  98.4 27.6 %collective-permute-start.1 = (bf16[2,2,8,16,128]{4,3,2,1,0:T(8,128)(2,1)S(1)}, bf16[2,2,8,16,128]{4,3,2,1,0:T(8,128)(2,1)S(1)}, u32[]{:S(2)}, u32[]{:S(2)}) collective-permute-start(bf16[2,2,8,16,128]{4,3,2,1,0:T(8,128)(2,1)S(1)} %get-tuple-element.31), channel_id=1, source_target_pairs={{0,4},{1,5},{8,12},{9,13},{2,6},{3,7},{10,14},{11,15},{4,0},{5,1},... | collective-permute-start | bytes 393224 | tf_op jit(solution)/shard_map/ppermute | solution.py:266
  102.9 26.6 %collective-permute-start.2 = (bf16[2,2,8,16,128]{4,3,2,1,0:T(8,128)(2,1)S(1)}, bf16[2,2,8,16,128]{4,3,2,1,0:T(8,128)(2,1)S(1)}, u32[]{:S(2)}, u32[]{:S(2)}) collective-permute-start(bf16[2,2,8,16,128]{4,3,2,1,0:T(8,128)(2,1)S(1)} %get-tuple-element.32), channel_id=1, source_target_pairs={{0,10},{1,11},{8,4},{9,5},{2,12},{3,13},{10,6},{11,7},{4,14},{5,15... | collective-permute-start | bytes 393224 | tf_op jit(solution)/shard_map/ppermute | solution.py:266
  105.4 24.1 %collective-permute-start.3 = (bf16[2,2,8,16,128]{4,3,2,1,0:T(8,128)(2,1)S(1)}, bf16[2,2,8,16,128]{4,3,2,1,0:T(8,128)(2,1)S(1)}, u32[]{:S(2)}, u32[]{:S(2)}) collective-permute-start(bf16[2,2,8,16,128]{4,3,2,1,0:T(8,128)(2,1)S(1)} %get-tuple-element.33), channel_id=1, source_target_pairs={{0,12},{1,13},{8,6},{9,7},{2,14},{3,15},{10,0},{11,1},{4,8},{5,9},... | collective-permute-start | bytes 393224 | tf_op jit(solution)/shard_map/ppermute | solution.py:266
  107.4 25.9 %collective-permute-start.4 = (bf16[2,2,8,16,128]{4,3,2,1,0:T(8,128)(2,1)S(1)}, bf16[2,2,8,16,128]{4,3,2,1,0:T(8,128)(2,1)S(1)}, u32[]{:S(2)}, u32[]{:S(2)}) collective-permute-start(bf16[2,2,8,16,128]{4,3,2,1,0:T(8,128)(2,1)S(1)} %get-tuple-element.34), channel_id=1, source_target_pairs={{0,2},{1,3},{8,10},{9,11},{2,4},{3,5},{10,12},{11,13},{4,6},{5,7},... | collective-permute-start | bytes 393224 | tf_op jit(solution)/shard_map/ppermute | solution.py:266
  126.1 8.9 %collective-permute-start.5 = (bf16[2,2,8,16,128]{4,3,2,1,0:T(8,128)(2,1)S(1)}, bf16[2,2,8,16,128]{4,3,2,1,0:T(8,128)(2,1)S(1)}, u32[]{:S(2)}, u32[]{:S(2)}) collective-permute-start(bf16[2,2,8,16,128]{4,3,2,1,0:T(8,128)(2,1)S(1)} %get-tuple-element.35), channel_id=1, source_target_pairs={{0,6},{1,7},{8,14},{9,15},{2,0},{3,1},{10,8},{11,9},{4,2},{5,3},{1... | collective-permute-start | bytes 393224 | tf_op jit(solution)/shard_map/ppermute | solution.py:266
  126.1 11.1 %collective-permute-start.6 = (bf16[2,2,8,16,128]{4,3,2,1,0:T(8,128)(2,1)S(1)}, bf16[2,2,8,16,128]{4,3,2,1,0:T(8,128)(2,1)S(1)}, u32[]{:S(2)}, u32[]{:S(2)}) collective-permute-start(bf16[2,2,8,16,128]{4,3,2,1,0:T(8,128)(2,1)S(1)} %get-tuple-element.36), channel_id=1, source_target_pairs={{0,8},{1,9},{8,2},{9,3},{2,10},{3,11},{10,4},{11,5},{4,12},{5,13},... | collective-permute-start | bytes 393224 | tf_op jit(solution)/shard_map/ppermute | solution.py:266
  129.6 12.2 %collective-permute-start.7 = (bf16[2,2,8,16,128]{4,3,2,1,0:T(8,128)(2,1)S(1)}, bf16[2,2,8,16,128]{4,3,2,1,0:T(8,128)(2,1)S(1)}, u32[]{:S(2)}, u32[]{:S(2)}) collective-permute-start(bf16[2,2,8,16,128]{4,3,2,1,0:T(8,128)(2,1)S(1)} %get-tuple-element.37), channel_id=1, source_target_pairs={{0,14},{1,15},{8,0},{9,1},{2,8},{3,9},{10,2},{11,3},{4,10},{5,11},... | collective-permute-start | bytes 393224 | tf_op jit(solution)/shard_map/ppermute | solution.py:266
  129.6 15.0 %collective-permute-start.13 = (bf16[2,2,8,16,128]{4,3,2,1,0:T(8,128)(2,1)S(1)}, bf16[2,2,8,16,128]{4,3,2,1,0:T(8,128)(2,1)S(1)}, u32[]{:S(2)}, u32[]{:S(2)}) collective-permute-start(bf16[2,2,8,16,128]{4,3,2,1,0:T(8,128)(2,1)S(1)} %get-tuple-element.44), channel_id=1, source_target_pairs={{0,12},{1,29},{8,6},{9,23},{2,14},{3,31},{10,0},{11,17},{4,8},{5,2... | collective-permute-start | bytes 393224 | tf_op jit(solution)/shard_map/ppermute | solution.py:266
  133.3 13.3 %collective-permute-start.14 = (bf16[2,2,8,16,128]{4,3,2,1,0:T(8,128)(2,1)S(1)}, bf16[2,2,8,16,128]{4,3,2,1,0:T(8,128)(2,1)S(1)}, u32[]{:S(2)}, u32[]{:S(2)}) collective-permute-start(bf16[2,2,8,16,128]{4,3,2,1,0:T(8,128)(2,1)S(1)} %get-tuple-element.45), channel_id=1, source_target_pairs={{0,2},{1,19},{8,10},{9,27},{2,4},{3,21},{10,12},{11,29},{4,6},{5,2... | collective-permute-start | bytes 393224 | tf_op jit(solution)/shard_map/ppermute | solution.py:266
  135.0 18.1 %collective-permute-start.15 = (bf16[2,2,8,16,128]{4,3,2,1,0:T(8,128)(2,1)S(1)}, bf16[2,2,8,16,128]{4,3,2,1,0:T(8,128)(2,1)S(1)}, u32[]{:S(2)}, u32[]{:S(2)}) collective-permute-start(bf16[2,2,8,16,128]{4,3,2,1,0:T(8,128)(2,1)S(1)} %get-tuple-element.46), channel_id=1, source_target_pairs={{0,6},{1,23},{8,14},{9,31},{2,0},{3,17},{10,8},{11,25},{4,2},{5,19... | collective-permute-start | bytes 393224 | tf_op jit(solution)/shard_map/ppermute | solution.py:266
  137.2 15.8 %collective-permute-start.16 = (bf16[2,2,8,16,128]{4,3,2,1,0:T(8,128)(2,1)S(1)}, bf16[2,2,8,16,128]{4,3,2,1,0:T(8,128)(2,1)S(1)}, u32[]{:S(2)}, u32[]{:S(2)}) collective-permute-start(bf16[2,2,8,16,128]{4,3,2,1,0:T(8,128)(2,1)S(1)} %get-tuple-element.47), channel_id=1, source_target_pairs={{0,8},{1,25},{8,2},{9,19},{2,10},{3,27},{10,4},{11,21},{4,12},{5,2... | collective-permute-start | bytes 393224 | tf_op jit(solution)/shard_map/ppermute | solution.py:266
  141.8 12.2 %collective-permute-start.17 = (bf16[2,2,8,16,128]{4,3,2,1,0:T(8,128)(2,1)S(1)}, bf16[2,2,8,16,128]{4,3,2,1,0:T(8,128)(2,1)S(1)}, u32[]{:S(2)}, u32[]{:S(2)}) collective-permute-start(bf16[2,2,8,16,128]{4,3,2,1,0:T(8,128)(2,1)S(1)} %get-tuple-element.48), channel_id=1, source_target_pairs={{0,14},{1,31},{8,0},{9,17},{2,8},{3,25},{10,2},{11,19},{4,10},{5,2... | collective-permute-start | bytes 393224 | tf_op jit(solution)/shard_map/ppermute | solution.py:266
  155.3 2.0 %collective-permute-start.18 = (bf16[2,8,128,128]{3,2,1,0:T(8,128)(2,1)S(1)}, bf16[2,8,128,128]{3,2,1,0:T(8,128)(2,1)S(1)}, u32[]{:S(2)}, u32[]{:S(2)}) collective-permute-start(bf16[2,8,128,128]{3,2,1,0:T(8,128)(2,1)S(1)} %get-tuple-element.50), channel_id=1, source_target_pairs={{0,1},{1,0},{2,3},{3,2},{4,5},{5,4},{6,7},{7,6},{8,9},{9,8},{10,11... | collective-permute-start | bytes 1572872 | tf_op jit(solution)/shard_map/ppermute | solution.py:271
  155.4 2.6 %collective-permute-start.8 = (bf16[2,8,128,128]{3,2,1,0:T(8,128)(2,1)S(1)}, bf16[2,8,128,128]{3,2,1,0:T(8,128)(2,1)S(1)}, u32[]{:S(2)}, u32[]{:S(2)}) collective-permute-start(bf16[2,8,128,128]{3,2,1,0:T(8,128)(2,1)S(1)} %get-tuple-element.39), channel_id=1, source_target_pairs={{0,1},{1,0},{2,3},{3,2},{4,5},{5,4},{6,7},{7,6},{8,9},{9,8},{10,11... | collective-permute-start | bytes 1572872 | tf_op jit(solution)/shard_map/ppermute | solution.py:271

commit v6 on v5

--- a/solution.py
+++ b/solution.py
@@ -30,17 +30,15 @@
 ANY = pl.BlockSpec(memory_space=pl.ANY)
 
 
-def place(z):
-    return (z % 2) * 4 + z // 2
-
-
 def params():
-    return pltpu.CompilerParams(vmem_limit_bytes=48 << 20)
+    return pltpu.CompilerParams(vmem_limit_bytes=24 << 20)
 
 
 def whiten_kernel(pos_ref, spec_ref, flags_ref, *refs):
-    outs, core, (band, eye, invc) = refs[:CHUNKS], refs[CHUNKS], refs[CHUNKS + 1 :]
+    outs, core = refs[: 8 * CHUNKS], refs[8 * CHUNKS]
+    band, eye, invc, white = refs[8 * CHUNKS + 1 :]
     w = pl.program_id(0)
+    z, c = pos_ref[0], pos_ref[1]
 
     @pl.when(w == 0)
     def _():
@@ -67,19 +65,24 @@
             half = lax.dot_general(
                 eye[...], both[:, h * 256 : (h + 1) * 256], nt, preferred_element_type=F32
             )
-            white = (half * scale[h * 256 : (h + 1) * 256]).astype(BF16)
-            for n in range(256 // FC):
-                k, d = divmod(h * 256 // FC + n, 16)
-                outs[k][place(d // 2) * 2 + d % 2, w * STEP + v] = white[n * FC : (n + 1) * FC]
-    core[0] = pos_ref[1]
+            part = half * scale[h * 256 : (h + 1) * 256]
+            white[v, h * 256 : (h + 1) * 256] = part.astype(BF16)
+    for k in range(CHUNKS):
+        for r in range(8):
+            base = k * CBINS + ((z + r) & 7) * (2 * FC)
+            for crel in range(2):
+                start = pl.multiple_of(base + (c ^ crel) * FC, FC)
+                for v in range(STEP):
+                    outs[k * 8 + r][crel, w * STEP + v] = white[v, pl.ds(start, FC), :]
+    core[0] = c
 
 
 def whiten(spec, flags2, pos):
-    shape = pltpu.HBM((16, WIN, FC, 128), BF16)
-    full = pl.BlockSpec((16, WIN, FC, 128), lambda w, *_: (0, 0, 0, 0))
+    shape = jax.ShapeDtypeStruct((2, WIN, FC, 128), BF16)
+    full = pl.BlockSpec((2, WIN, FC, 128), lambda w, *_: (0, 0, 0, 0))
     return pl.pallas_call(
         whiten_kernel,
-        out_shape=[shape] * CHUNKS + [jax.ShapeDtypeStruct((1,), jnp.int32)],
+        out_shape=[shape] * (8 * CHUNKS) + [jax.ShapeDtypeStruct((1,), jnp.int32)],
         grid_spec=pltpu.PrefetchScalarGridSpec(
             num_scalar_prefetch=1,
             grid=(WIN // STEP,),
@@ -87,11 +90,12 @@
                 pl.BlockSpec((2, STEP, CH, BINS), lambda w, *_: (0, w, 0, 0)),
                 pl.BlockSpec((STEP, 1, 128), lambda w, *_: (w, 0, 0)),
             ],
-            out_specs=[full] * CHUNKS + [SM],
+            out_specs=[full] * (8 * CHUNKS) + [SM],
             scratch_shapes=[
                 pltpu.VMEM((BINS, BINS), BF16),
                 pltpu.VMEM((256, 256), BF16),
                 pltpu.VMEM((BINS, 128), F32),
+                pltpu.VMEM((STEP, BINS, 128), BF16),
             ],
         ),
         compiler_params=params(),
@@ -102,20 +106,45 @@
     )(pos, spec, flags2)
 
 
-def cross_kernel(turned, pos_ref, here, there, *refs):
+def merge_kernel(pos_ref, *refs):
+    ins, (same, other) = refs[:8], refs[-2:]
+    z = pos_ref[0]
+    for n, r in enumerate(ORDER):
+        src = (z - r) & 7
+        same[src & 1, src >> 1] = ins[n][0]
+        other[src & 1, src >> 1] = ins[n][1]
+
+
+def merge(pieces, pos, *after):
+    shape = jax.ShapeDtypeStruct((2, 4, WIN, FC, 128), BF16)
+    return pl.pallas_call(
+        merge_kernel,
+        out_shape=[shape] * 2,
+        in_specs=[SM] + [VM] * 8 + [ANY] * len(after),
+        out_specs=[VM] * 2,
+        compiler_params=params(),
+        cost_estimate=pl.CostEstimate(
+            flops=0, bytes_accessed=4 * 8 * WIN * FC * 256, transcendentals=0
+        ),
+        name="merge",
+    )(pos, *pieces, *after)
+
+
+def cross_kernel(turned, pos_ref, own0, own1, prev0, prev1, *refs):
     outs, (wide, res) = refs[-10:-2], refs[-2:]
     z, c = pos_ref[0], pos_ref[1]
-    rows = 8 * WIN * FC
-    for n, ref in enumerate((here, there)):
+    rows = 4 * WIN * FC
+    for n, (first, second) in enumerate(((own0, own1), (prev0, prev1))):
         for b in range(2):
-            base = pl.multiple_of(((n ^ c if turned else n) * 2 + b) * rows, rows)
-            wide[pl.ds(base, rows)] = ref[8 * b : 8 * b + 8].reshape(rows, 128).astype(F32)
+            base = pl.multiple_of(((n ^ c if turned else n) * 2 + b) * 2 * rows, rows)
+            wide[pl.ds(base, rows)] = first[b].reshape(rows, 128).astype(F32)
+            wide[pl.ds(base + rows, rows)] = second[b].reshape(rows, 128).astype(F32)
     sign = jnp.where(lax.broadcasted_iota(jnp.int32, (CH, 128), 1) < CH, 1.0, -1.0).astype(F32)
     tn = (((0,), (0,)), ((), ()))
 
     def one_bin(f, carry):
         x = [
-            wide[pl.ds(n * rows + f, 8 * WIN, stride=FC), :].astype(BF16) for n in range(4)
+            wide[pl.ds(n * 2 * rows + f, 8 * WIN, stride=FC), :].astype(BF16) for n in range(4)
         ]
         own_a, own_b, prev_a, prev_b = x
         for b, (left, rights) in enumerate(
@@ -142,12 +171,12 @@
                     outs[r][crel, rnd, i] = res[pl.ds(base + i, FC, stride=CH), :].astype(BF16)
 
 
-def cross(turned, here, there, pos, *after):
+def cross(turned, own0, own1, prev0, prev1, pos, *after):
     shape = jax.ShapeDtypeStruct((2, 2, 8, FC, 128), BF16)
     return pl.pallas_call(
         functools.partial(cross_kernel, turned),
         out_shape=[shape] * 8,
-        in_specs=[SM] + [VM] * 2 + [ANY] * len(after),
+        in_specs=[SM] + [VM] * 4 + [ANY] * len(after),
         out_specs=[VM] * 8,
         scratch_shapes=[
             pltpu.VMEM((32 * WIN * FC, 128), F32),
@@ -158,7 +187,7 @@
             flops=4 * FC * 128 * 256 * 256, bytes_accessed=3 << 20, transcendentals=0
         ),
         name="cross",
-    )(pos, here, there, *after)
+    )(pos, own0, own1, prev0, prev1, *after)
 
 
 def turn_kernel(pos_ref, *refs):
@@ -252,6 +281,10 @@
     )(*parts)
 
 
+def place(z):
+    return (z % 2) * 4 + z // 2
+
+
 def device(m, z, c):
     return (m % 16) * 16 + place(z % 8) * 2 + c
 
@@ -259,16 +292,22 @@
 EVERY = [(m, z, c) for m in range(16) for z in range(8) for c in range(2)]
 
 
-def round_ring(pieces, turned):
+def send(value, target):
+    return lax.ppermute(value, ALL, [(device(*d), device(*target(*d))) for d in EVERY])
+
+
+def round_ring(pieces, turned=0):
     got = []
     for r in ORDER:
-        pairs = [(device(m, z, c), device(m + c * turned, z + r, c)) for m, z, c in EVERY]
-        got.append(lax.ppermute(pieces[r], ALL, pairs) if r or turned else pieces[r])
+        if r or turned:
+            got.append(send(pieces[r], lambda m, z, c: (m + c * turned, z + r, c)))
+        else:
+            got.append(pieces[r])
     return got
 
 
 def other_core(value):
-    return lax.ppermute(value, "c", [(0, 1), (1, 0)])
+    return send(value, lambda m, z, c: (m, z, 1 - c))
 
 
 def shards(spectra, valid_flags):
@@ -280,17 +319,18 @@
     *white, core = whiten(jnp.transpose(spectra, (2, 0, 1, 3)), flags2, pos)
     table = join_table(lag_table(core[0]))
     parts = []
-    crossed, turned = (table,), ()
+    merged, crossed, turned = (table,), (), ()
     for k in range(CHUNKS):
-        turned_round = int(k == CHUNKS - 1)
-        shift = [
-            (device(m, z, c), device(m + 1 - 2 * c * turned_round, z, c)) for m, z, c in EVERY
-        ]
-        here = lax.all_to_all(white[k], ("zl", "zh", "c"), 0, 0, tiled=True)
-        there = lax.ppermute(here, ALL, shift)
-        out = cross(turned_round, here, there, pos, *crossed)
+        back = int(k == CHUNKS - 1)
+        got = round_ring(white[k * 8 : k * 8 + 8])
+        same, other = merge(got, pos, *merged)
+        merged = (same,)
+        prev0 = send(same, lambda m, z, c: (m + 1 - 2 * c * back, z, c))
+        prev1 = send(other, lambda m, z, c: (m + 1 - 2 * (1 - c) * back, z, 1 - c))
+        own1 = other_core(other)
+        out = cross(back, same, own1, prev0, prev1, pos, *crossed)
         crossed = (out[0],)
-        same, other = turn(round_ring(out, turned_round), pos, *turned)
+        same, other = turn(round_ring(out, back), pos, *turned)
         turned = (same,)
         parts += [same, other_core(other)]
     return invert(parts, table, scaling)

time: 162 us -> 156 us (0.963)
  blocking collectives: 35.8 us -> 0 us
  starting transfers between devices: 41.3 us -> 68.1 us
  waiting for transfers between devices: 54.9 us -> 57.4 us
    all_to_all x1 -> x0, blocking collectives: 35.8 us -> none  [shards(): here = lax.all_to_all(white[k], ('zl', 'zh', 'c'), 0, 0, tiled=True)]
    ppermute x19 -> x37, starting transfers between devices: 37.7 us -> 68.1 us  [send(): lax.ppermute(value, ALL, [(device(*d), device(*target(*d))) for d in EVERY])]
    ppermute x19 -> x37, waiting for transfers between devices: 32.9 us -> 57.4 us  [send(): lax.ppermute(value, ALL, [(device(*d), device(*target(*d))) for d in EVERY])]
    all_to_all x1 -> x0, waiting for transfers between devices: 22 us -> none  [shards(): here = lax.all_to_all(white[k], ('zl', 'zh', 'c'), 0, 0, tiled=True)]
    all_to_all x1 -> x0, starting transfers between devices: 3.53 us -> none  [shards(): here = lax.all_to_all(white[k], ('zl', 'zh', 'c'), 0, 0, tiled=True)]
    pallas_call x1 -> x3, Pallas kernels: 6.34 us -> 7.01 us  [the longest x1 5.79 us: whiten(): pl.pallas_call(whiten_kernel, out_shape=[shape] * (8 * CHUNKS) + [jax.Sha...]
  transfers between devices with their start and end apart: 20 -> 37, of which waited for: 11 -> 15; matrix products, arithmetic and copies ran while one was open for 2% -> 2% of each run, Pallas kernels for 5% -> 10%
where the time goes in v6:
time: 156 us
  starting transfers between devices  68.1 us (44%)
  waiting for transfers between devices  57.4 us (37%)
  Pallas kernels  25.6 us (16%)
  other arithmetic  2.99 us (2%)
  local copies, waits for them, and re-layouts  1.91 us (1%)
    ppermute x37, starting transfers between devices, send(): lax.ppermute(value, ALL, [(device(*d), device(*target(*d))) for d in EVERY])  68.1 us
    ppermute x37, waiting for transfers between devices, send(): lax.ppermute(value, ALL, [(device(*d), device(*target(*d))) for d in EVERY])  57.4 us
    pallas_call x2, Pallas kernels, cross(): pl.pallas_call(functools.partial(cross_kernel, turned), out_shape=[shape]...  10.8 us
    pallas_call x1, Pallas kernels, whiten(): pl.pallas_call(whiten_kernel, out_shape=[shape] * (8 * CHUNKS) + [jax.Sha...  5.79 us
    pallas_call x1, Pallas kernels, invert(): pl.pallas_call(functools.partial(invert_kernel, scaling), out_shape=jax.S...  3.73 us
  transfers between devices with their start and end apart: 37, of which 15 were waited for; matrix products, arithmetic and copies ran while one was open for 2% of the time, Pallas kernels for 10%

profile of v6, /device:TPU:1, one launch (start us, length us, event | category | flops | bytes accessed | tf_op | source)
XLA Modules:
  0.0 156.2 jit_solution(17374898024735301461)
XLA Ops:
  2.1 5.8 %whiten.1 = (bf16[2,14,16,128]{3,2,1,0:T(8,128)(2,1)S(1)}, bf16[2,14,16,128]{3,2,1,0:T(8,128)(2,1)S(1)}, bf16[2,14,16,128]{3,2,1,0:T(8,128)(2,1)S(1)}, bf16[2,14...) custom-call(s32[2]{0:T(128)S(1)} %pad_add_fusion.1.pos_ref, ...), custom_call_target="tpu_custom_call" | custom-call | flops 1409286144 | bytes 4194304 | tf_op jit(solution)/shard_map/whiten/pallas_call | solution.py:83
  7.9 7.8 %collective-permute-start = (bf16[2,14,16,128]{3,2,1,0:T(8,128)(2,1)S(1)}, bf16[2,14,16,128]{3,2,1,0:T(8,128)(2,1)S(1)}, u32[]{:S(2)}, u32[]{:S(2)}) collective-permute-start(bf16[2,14,16,128]{3,2,1,0:T(8,128)(2,1)S(1)} %get-tuple-element.47), channel_id=1, source_target_pairs={{0,4},{1,5},{8,12},{9,13},{2,6},{3,7},{10,14},{11,15},{4,0},{5,1},... | collective-permute-start | bytes 344072 | tf_op jit(solution)/shard_map/ppermute | solution.py:296
  17.3 2.8 %collective-permute-start.2 = (bf16[2,14,16,128]{3,2,1,0:T(8,128)(2,1)S(1)}, bf16[2,14,16,128]{3,2,1,0:T(8,128)(2,1)S(1)}, u32[]{:S(2)}, u32[]{:S(2)}) collective-permute-start(bf16[2,14,16,128]{3,2,1,0:T(8,128)(2,1)S(1)} %get-tuple-element.49), channel_id=1, source_target_pairs={{0,12},{1,13},{8,6},{9,7},{2,14},{3,15},{10,0},{11,1},{4,8},{5,9},... | collective-permute-start | bytes 344072 | tf_op jit(solution)/shard_map/ppermute | solution.py:296
  21.4 2.4 %collective-permute-start.4 = (bf16[2,14,16,128]{3,2,1,0:T(8,128)(2,1)S(1)}, bf16[2,14,16,128]{3,2,1,0:T(8,128)(2,1)S(1)}, u32[]{:S(2)}, u32[]{:S(2)}) collective-permute-start(bf16[2,14,16,128]{3,2,1,0:T(8,128)(2,1)S(1)} %get-tuple-element.51), channel_id=1, source_target_pairs={{0,6},{1,7},{8,14},{9,15},{2,0},{3,1},{10,8},{11,9},{4,2},{5,3},{1... | collective-permute-start | bytes 344072 | tf_op jit(solution)/shard_map/ppermute | solution.py:296
  25.2 5.4 %collective-permute-done.1.refs_2_ = bf16[2,14,16,128]{3,2,1,0:T(8,128)(2,1)S(1)} collective-permute-done((bf16[2,14,16,128]{3,2,1,0:T(8,128)(2,1)S(1)}, bf16[2,14,16,128]{3,2,1,0:T(8,128)(2,1)S(1)}, u32[]{:S(2)}, u32[]{:S(2)}) %collective-permute-start.1) | collective-permute-done | bytes 114720 | tf_op jit(solution)/shard_map/ppermute | solution.py:296
  38.7 3.1 %collective-permute-start.18 = (bf16[2,14,16,128]{3,2,1,0:T(8,128)(2,1)S(1)}, bf16[2,14,16,128]{3,2,1,0:T(8,128)(2,1)S(1)}, u32[]{:S(2)}, u32[]{:S(2)}) collective-permute-start(bf16[2,14,16,128]{3,2,1,0:T(8,128)(2,1)S(1)} %get-tuple-element.68), channel_id=1, source_target_pairs={{0,4},{1,5},{8,12},{9,13},{2,6},{3,7},{10,14},{11,15},{4,0},{5,1},... | collective-permute-start | bytes 344072 | tf_op jit(solution)/shard_map/ppermute | solution.py:296
  43.8 2.4 %collective-permute-start.20 = (bf16[2,14,16,128]{3,2,1,0:T(8,128)(2,1)S(1)}, bf16[2,14,16,128]{3,2,1,0:T(8,128)(2,1)S(1)}, u32[]{:S(2)}, u32[]{:S(2)}) collective-permute-start(bf16[2,14,16,128]{3,2,1,0:T(8,128)(2,1)S(1)} %get-tuple-element.70), channel_id=1, source_target_pairs={{0,12},{1,13},{8,6},{9,7},{2,14},{3,15},{10,0},{11,1},{4,8},{5,9},... | collective-permute-start | bytes 344072 | tf_op jit(solution)/shard_map/ppermute | solution.py:296
  50.5 7.5 %collective-permute-done.19.refs_2_ = bf16[2,14,16,128]{3,2,1,0:T(8,128)(2,1)S(1)} collective-permute-done((bf16[2,14,16,128]{3,2,1,0:T(8,128)(2,1)S(1)}, bf16[2,14,16,128]{3,2,1,0:T(8,128)(2,1)S(1)}, u32[]{:S(2)}, u32[]{:S(2)}) %collective-permute-start.19) | collective-permute-done | bytes 114720 | tf_op jit(solution)/shard_map/ppermute | solution.py:296
  57.9 3.2 %collective-permute-start.24 = (bf16[2,14,16,128]{3,2,1,0:T(8,128)(2,1)S(1)}, bf16[2,14,16,128]{3,2,1,0:T(8,128)(2,1)S(1)}, u32[]{:S(2)}, u32[]{:S(2)}) collective-permute-start(bf16[2,14,16,128]{3,2,1,0:T(8,128)(2,1)S(1)} %get-tuple-element.74), channel_id=1, source_target_pairs={{0,14},{1,15},{8,0},{9,1},{2,8},{3,9},{10,2},{11,3},{4,10},{5,11},... | collective-permute-start | bytes 344072 | tf_op jit(solution)/shard_map/ppermute | solution.py:296
  62.4 4.2 %collective-permute-start.9 = (bf16[2,4,14,16,128]{4,3,2,1,0:T(8,128)(2,1)S(1)}, bf16[2,4,14,16,128]{4,3,2,1,0:T(8,128)(2,1)S(1)}, u32[]{:S(2)}, u32[]{:S(2)}) collective-permute-start(bf16[2,4,14,16,128]{4,3,2,1,0:T(8,128)(2,1)S(1)} %get-tuple-element.56), channel_id=1, source_target_pairs={{0,17},{1,16},{8,25},{9,24},{2,19},{3,18},{10,27},{11,26},{4,21},{... | collective-permute-start | bytes 1376264 | tf_op jit(solution)/shard_map/ppermute | solution.py:296
  67.2 4.9 %collective-permute-start.26 = (bf16[2,4,14,16,128]{4,3,2,1,0:T(8,128)(2,1)S(1)}, bf16[2,4,14,16,128]{4,3,2,1,0:T(8,128)(2,1)S(1)}, u32[]{:S(2)}, u32[]{:S(2)}) collective-permute-start(bf16[2,4,14,16,128]{4,3,2,1,0:T(8,128)(2,1)S(1)} %get-tuple-element.75.own0), channel_id=1, source_target_pairs={{0,16},{1,241},{8,24},{9,249},{2,18},{3,243},{10,26},{11,251},{4,2... | collective-permute-start | bytes 1376264 | tf_op jit(solution)/shard_map/ppermute | solution.py:296
  74.0 15.9 %collective-permute-done.9.prev1 = bf16[2,4,14,16,128]{4,3,2,1,0:T(8,128)(2,1)S(1)} collective-permute-done((bf16[2,4,14,16,128]{4,3,2,1,0:T(8,128)(2,1)S(1)}, bf16[2,4,14,16,128]{4,3,2,1,0:T(8,128)(2,1)S(1)}, u32[]{:S(2)}, u32[]{:S(2)}) %collective-permute-start.9) | collective-permute-done | bytes 458784 | tf_op jit(solution)/shard_map/ppermute | solution.py:296
  89.9 5.4 %cross.2 = (bf16[2,2,8,16,128]{4,3,2,1,0:T(8,128)(2,1)S(1)}, bf16[2,2,8,16,128]{4,3,2,1,0:T(8,128)(2,1)S(1)}, bf16[2,2,8,16,128]{4,3,2,1,0:T(8,128)(2,1)S(1)}, b...) custom-call(s32[2]{0:T(128)S(1)} %pad_add_fusion.1.pos_ref, ...), custom_call_target="tpu_custom_call" | custom-call | flops 536870912 | bytes 3145728 | tf_op jit(solution)/shard_map/cross/pallas_call | solution.py:176
  98.2 3.9 %collective-permute-start.12 = (bf16[2,2,8,16,128]{4,3,2,1,0:T(8,128)(2,1)S(1)}, bf16[2,2,8,16,128]{4,3,2,1,0:T(8,128)(2,1)S(1)}, u32[]{:S(2)}, u32[]{:S(2)}) collective-permute-start(bf16[2,2,8,16,128]{4,3,2,1,0:T(8,128)(2,1)S(1)} %get-tuple-element.60), channel_id=1, source_target_pairs={{0,12},{1,13},{8,6},{9,7},{2,14},{3,15},{10,0},{11,1},{4,8},{5,9},... | collective-permute-start | bytes 393224 | tf_op jit(solution)/shard_map/ppermute | solution.py:296
  102.3 3.4 %collective-permute-start.14 = (bf16[2,2,8,16,128]{4,3,2,1,0:T(8,128)(2,1)S(1)}, bf16[2,2,8,16,128]{4,3,2,1,0:T(8,128)(2,1)S(1)}, u32[]{:S(2)}, u32[]{:S(2)}) collective-permute-start(bf16[2,2,8,16,128]{4,3,2,1,0:T(8,128)(2,1)S(1)} %get-tuple-element.62), channel_id=1, source_target_pairs={{0,6},{1,7},{8,14},{9,15},{2,0},{3,1},{10,8},{11,9},{4,2},{5,3},{1... | collective-permute-start | bytes 393224 | tf_op jit(solution)/shard_map/ppermute | solution.py:296
  105.7 5.4 %cross.3 = (bf16[2,2,8,16,128]{4,3,2,1,0:T(8,128)(2,1)S(1)}, bf16[2,2,8,16,128]{4,3,2,1,0:T(8,128)(2,1)S(1)}, bf16[2,2,8,16,128]{4,3,2,1,0:T(8,128)(2,1)S(1)}, b...) custom-call(s32[2]{0:T(128)S(1)} %pad_add_fusion.1.pos_ref, ...), custom_call_target="tpu_custom_call" | custom-call | flops 536870912 | bytes 3145728 | tf_op jit(solution)/shard_map/cross/pallas_call | solution.py:176
  119.4 4.0 %collective-permute-start.30 = (bf16[2,2,8,16,128]{4,3,2,1,0:T(8,128)(2,1)S(1)}, bf16[2,2,8,16,128]{4,3,2,1,0:T(8,128)(2,1)S(1)}, u32[]{:S(2)}, u32[]{:S(2)}) collective-permute-start(bf16[2,2,8,16,128]{4,3,2,1,0:T(8,128)(2,1)S(1)} %get-tuple-element.79), channel_id=1, source_target_pairs={{0,10},{1,27},{8,4},{9,21},{2,12},{3,29},{10,6},{11,23},{4,14},{5,... | collective-permute-start | bytes 393224 | tf_op jit(solution)/shard_map/ppermute | solution.py:296
  123.3 3.0 %collective-permute-start.31 = (bf16[2,2,8,16,128]{4,3,2,1,0:T(8,128)(2,1)S(1)}, bf16[2,2,8,16,128]{4,3,2,1,0:T(8,128)(2,1)S(1)}, u32[]{:S(2)}, u32[]{:S(2)}) collective-permute-start(bf16[2,2,8,16,128]{4,3,2,1,0:T(8,128)(2,1)S(1)} %get-tuple-element.80), channel_id=1, source_target_pairs={{0,12},{1,29},{8,6},{9,23},{2,14},{3,31},{10,0},{11,17},{4,8},{5,2... | collective-permute-start | bytes 393224 | tf_op jit(solution)/shard_map/ppermute | solution.py:296
  128.2 2.6 %collective-permute-start.33 = (bf16[2,2,8,16,128]{4,3,2,1,0:T(8,128)(2,1)S(1)}, bf16[2,2,8,16,128]{4,3,2,1,0:T(8,128)(2,1)S(1)}, u32[]{:S(2)}, u32[]{:S(2)}) collective-permute-start(bf16[2,2,8,16,128]{4,3,2,1,0:T(8,128)(2,1)S(1)} %get-tuple-element.82), channel_id=1, source_target_pairs={{0,6},{1,23},{8,14},{9,31},{2,0},{3,17},{10,8},{11,25},{4,2},{5,19... | collective-permute-start | bytes 393224 | tf_op jit(solution)/shard_map/ppermute | solution.py:296
  130.8 3.1 %collective-permute-done.29.refs_1_ = bf16[2,2,8,16,128]{4,3,2,1,0:T(8,128)(2,1)S(1)} collective-permute-done((bf16[2,2,8,16,128]{4,3,2,1,0:T(8,128)(2,1)S(1)}, bf16[2,2,8,16,128]{4,3,2,1,0:T(8,128)(2,1)S(1)}, u32[]{:S(2)}, u32[]{:S(2)}) %collective-permute-start.29) | collective-permute-done | bytes 131104 | tf_op jit(solution)/shard_map/ppermute | solution.py:296
  134.5 6.6 %collective-permute-done.30.refs_2_ = bf16[2,2,8,16,128]{4,3,2,1,0:T(8,128)(2,1)S(1)} collective-permute-done((bf16[2,2,8,16,128]{4,3,2,1,0:T(8,128)(2,1)S(1)}, bf16[2,2,8,16,128]{4,3,2,1,0:T(8,128)(2,1)S(1)}, u32[]{:S(2)}, u32[]{:S(2)}) %collective-permute-start.30) | collective-permute-done | bytes 131104 | tf_op jit(solution)/shard_map/ppermute | solution.py:296
  143.1 3.3 %collective-permute-done.33.refs_5_ = bf16[2,2,8,16,128]{4,3,2,1,0:T(8,128)(2,1)S(1)} collective-permute-done((bf16[2,2,8,16,128]{4,3,2,1,0:T(8,128)(2,1)S(1)}, bf16[2,2,8,16,128]{4,3,2,1,0:T(8,128)(2,1)S(1)}, u32[]{:S(2)}, u32[]{:S(2)}) %collective-permute-start.33) | collective-permute-done | bytes 131104 | tf_op jit(solution)/shard_map/ppermute | solution.py:296
  146.3 2.8 %collective-permute-done.35.refs_7_ = bf16[2,2,8,16,128]{4,3,2,1,0:T(8,128)(2,1)S(1)} collective-permute-done((bf16[2,2,8,16,128]{4,3,2,1,0:T(8,128)(2,1)S(1)}, bf16[2,2,8,16,128]{4,3,2,1,0:T(8,128)(2,1)S(1)}, u32[]{:S(2)}, u32[]{:S(2)}) %collective-permute-start.35) | collective-permute-done | bytes 131104 | tf_op jit(solution)/shard_map/ppermute | solution.py:296
  152.4 3.7 %invert.1 = bf16[2,8,64,1024]{3,2,1,0:T(8,128)(2,1)} custom-call(bf16[2,8,128,128]{3,2,1,0:T(8,128)(2,1)S(1)} %get-tuple-element.65.refs_8_.refs_0_, bf16[2,8,128,128]{3,2,1,0:T(8,128)(2,1)S(1)} %collective-permute-done.17.refs_1_, bf16[2,8,128,128]{3,2,1,0:T(8,128)(2,1)S(1)} %get-tuple-element.85.refs_2_, ...), custom_call_target="tpu_custom_call" | custom-call | flops 2147483648 | bytes 6291456 | tf_op jit(solution)/shard_map/invert/pallas_call | solution.py:232
  (69 shorter events, 43.6 us)
Async XLA Ops:
  7.9 16.5 %collective-permute-start = (bf16[2,14,16,128]{3,2,1,0:T(8,128)(2,1)S(1)}, bf16[2,14,16,128]{3,2,1,0:T(8,128)(2,1)S(1)}, u32[]{:S(2)}, u32[]{:S(2)}) collective-permute-start(bf16[2,14,16,128]{3,2,1,0:T(8,128)(2,1)S(1)} %get-tuple-element.47), channel_id=1, source_target_pairs={{0,4},{1,5},{8,12},{9,13},{2,6},{3,7},{10,14},{11,15},{4,0},{5,1},... | collective-permute-start | bytes 344072 | tf_op jit(solution)/shard_map/ppermute | solution.py:296
  15.7 14.9 %collective-permute-start.1 = (bf16[2,14,16,128]{3,2,1,0:T(8,128)(2,1)S(1)}, bf16[2,14,16,128]{3,2,1,0:T(8,128)(2,1)S(1)}, u32[]{:S(2)}, u32[]{:S(2)}) collective-permute-start(bf16[2,14,16,128]{3,2,1,0:T(8,128)(2,1)S(1)} %get-tuple-element.48), channel_id=1, source_target_pairs={{0,10},{1,11},{8,4},{9,5},{2,12},{3,13},{10,6},{11,7},{4,14},{5,15... | collective-permute-start | bytes 344072 | tf_op jit(solution)/shard_map/ppermute | solution.py:296
  17.3 16.9 %collective-permute-start.2 = (bf16[2,14,16,128]{3,2,1,0:T(8,128)(2,1)S(1)}, bf16[2,14,16,128]{3,2,1,0:T(8,128)(2,1)S(1)}, u32[]{:S(2)}, u32[]{:S(2)}) collective-permute-start(bf16[2,14,16,128]{3,2,1,0:T(8,128)(2,1)S(1)} %get-tuple-element.49), channel_id=1, source_target_pairs={{0,12},{1,13},{8,6},{9,7},{2,14},{3,15},{10,0},{11,1},{4,8},{5,9},... | collective-permute-start | bytes 344072 | tf_op jit(solution)/shard_map/ppermute | solution.py:296
  20.2 14.1 %collective-permute-start.3 = (bf16[2,14,16,128]{3,2,1,0:T(8,128)(2,1)S(1)}, bf16[2,14,16,128]{3,2,1,0:T(8,128)(2,1)S(1)}, u32[]{:S(2)}, u32[]{:S(2)}) collective-permute-start(bf16[2,14,16,128]{3,2,1,0:T(8,128)(2,1)S(1)} %get-tuple-element.50), channel_id=1, source_target_pairs={{0,2},{1,3},{8,10},{9,11},{2,4},{3,5},{10,12},{11,13},{4,6},{5,7},... | collective-permute-start | bytes 344072 | tf_op jit(solution)/shard_map/ppermute | solution.py:296
  38.1 34.1 %collective-permute-start.7 = (bf16[2,4,14,16,128]{4,3,2,1,0:T(8,128)(2,1)S(1)}, bf16[2,4,14,16,128]{4,3,2,1,0:T(8,128)(2,1)S(1)}, u32[]{:S(2)}, u32[]{:S(2)}) collective-permute-start(bf16[2,4,14,16,128]{4,3,2,1,0:T(8,128)(2,1)S(1)} %get-tuple-element.56), channel_id=1, source_target_pairs={{0,1},{1,0},{8,9},{9,8},{2,3},{3,2},{10,11},{11,10},{4,5},{5,4},{1... | collective-permute-start | bytes 1376264 | tf_op jit(solution)/shard_map/ppermute | solution.py:296
  41.7 16.2 %collective-permute-start.19 = (bf16[2,14,16,128]{3,2,1,0:T(8,128)(2,1)S(1)}, bf16[2,14,16,128]{3,2,1,0:T(8,128)(2,1)S(1)}, u32[]{:S(2)}, u32[]{:S(2)}) collective-permute-start(bf16[2,14,16,128]{3,2,1,0:T(8,128)(2,1)S(1)} %get-tuple-element.69), channel_id=1, source_target_pairs={{0,10},{1,11},{8,4},{9,5},{2,12},{3,13},{10,6},{11,7},{4,14},{5,15... | collective-permute-start | bytes 344072 | tf_op jit(solution)/shard_map/ppermute | solution.py:296
  43.8 14.1 %collective-permute-start.20 = (bf16[2,14,16,128]{3,2,1,0:T(8,128)(2,1)S(1)}, bf16[2,14,16,128]{3,2,1,0:T(8,128)(2,1)S(1)}, u32[]{:S(2)}, u32[]{:S(2)}) collective-permute-start(bf16[2,14,16,128]{3,2,1,0:T(8,128)(2,1)S(1)} %get-tuple-element.70), channel_id=1, source_target_pairs={{0,12},{1,13},{8,6},{9,7},{2,14},{3,15},{10,0},{11,1},{4,8},{5,9},... | collective-permute-start | bytes 344072 | tf_op jit(solution)/shard_map/ppermute | solution.py:296
  46.2 14.9 %collective-permute-start.21 = (bf16[2,14,16,128]{3,2,1,0:T(8,128)(2,1)S(1)}, bf16[2,14,16,128]{3,2,1,0:T(8,128)(2,1)S(1)}, u32[]{:S(2)}, u32[]{:S(2)}) collective-permute-start(bf16[2,14,16,128]{3,2,1,0:T(8,128)(2,1)S(1)} %get-tuple-element.71), channel_id=1, source_target_pairs={{0,2},{1,3},{8,10},{9,11},{2,4},{3,5},{10,12},{11,13},{4,6},{5,7},... | collective-permute-start | bytes 344072 | tf_op jit(solution)/shard_map/ppermute | solution.py:296
  48.5 13.9 %collective-permute-start.22 = (bf16[2,14,16,128]{3,2,1,0:T(8,128)(2,1)S(1)}, bf16[2,14,16,128]{3,2,1,0:T(8,128)(2,1)S(1)}, u32[]{:S(2)}, u32[]{:S(2)}) collective-permute-start(bf16[2,14,16,128]{3,2,1,0:T(8,128)(2,1)S(1)} %get-tuple-element.72), channel_id=1, source_target_pairs={{0,6},{1,7},{8,14},{9,15},{2,0},{3,1},{10,8},{11,9},{4,2},{5,3},{1... | collective-permute-start | bytes 344072 | tf_op jit(solution)/shard_map/ppermute | solution.py:296
  62.4 27.5 %collective-permute-start.9 = (bf16[2,4,14,16,128]{4,3,2,1,0:T(8,128)(2,1)S(1)}, bf16[2,4,14,16,128]{4,3,2,1,0:T(8,128)(2,1)S(1)}, u32[]{:S(2)}, u32[]{:S(2)}) collective-permute-start(bf16[2,4,14,16,128]{4,3,2,1,0:T(8,128)(2,1)S(1)} %get-tuple-element.56), channel_id=1, source_target_pairs={{0,17},{1,16},{8,25},{9,24},{2,19},{3,18},{10,27},{11,26},{4,21},{... | collective-permute-start | bytes 1376264 | tf_op jit(solution)/shard_map/ppermute | solution.py:296
  67.1 31.0 %collective-permute-start.25 = (bf16[2,4,14,16,128]{4,3,2,1,0:T(8,128)(2,1)S(1)}, bf16[2,4,14,16,128]{4,3,2,1,0:T(8,128)(2,1)S(1)}, u32[]{:S(2)}, u32[]{:S(2)}) collective-permute-start(bf16[2,4,14,16,128]{4,3,2,1,0:T(8,128)(2,1)S(1)} %get-tuple-element.76), channel_id=1, source_target_pairs={{0,1},{1,0},{8,9},{9,8},{2,3},{3,2},{10,11},{11,10},{4,5},{5,4},{1... | collective-permute-start | bytes 1376264 | tf_op jit(solution)/shard_map/ppermute | solution.py:296
  67.2 34.9 %collective-permute-start.26 = (bf16[2,4,14,16,128]{4,3,2,1,0:T(8,128)(2,1)S(1)}, bf16[2,4,14,16,128]{4,3,2,1,0:T(8,128)(2,1)S(1)}, u32[]{:S(2)}, u32[]{:S(2)}) collective-permute-start(bf16[2,4,14,16,128]{4,3,2,1,0:T(8,128)(2,1)S(1)} %get-tuple-element.75.own0), channel_id=1, source_target_pairs={{0,16},{1,241},{8,24},{9,249},{2,18},{3,243},{10,26},{11,251},{4,2... | collective-permute-start | bytes 1376264 | tf_op jit(solution)/shard_map/ppermute | solution.py:296
  72.2 30.2 %collective-permute-start.27 = (bf16[2,4,14,16,128]{4,3,2,1,0:T(8,128)(2,1)S(1)}, bf16[2,4,14,16,128]{4,3,2,1,0:T(8,128)(2,1)S(1)}, u32[]{:S(2)}, u32[]{:S(2)}) collective-permute-start(bf16[2,4,14,16,128]{4,3,2,1,0:T(8,128)(2,1)S(1)} %get-tuple-element.76), channel_id=1, source_target_pairs={{0,241},{1,16},{8,249},{9,24},{2,243},{3,18},{10,251},{11,26},{4,2... | collective-permute-start | bytes 1376264 | tf_op jit(solution)/shard_map/ppermute | solution.py:296
  95.3 15.8 %collective-permute-start.10 = (bf16[2,2,8,16,128]{4,3,2,1,0:T(8,128)(2,1)S(1)}, bf16[2,2,8,16,128]{4,3,2,1,0:T(8,128)(2,1)S(1)}, u32[]{:S(2)}, u32[]{:S(2)}) collective-permute-start(bf16[2,2,8,16,128]{4,3,2,1,0:T(8,128)(2,1)S(1)} %get-tuple-element.58), channel_id=1, source_target_pairs={{0,4},{1,5},{8,12},{9,13},{2,6},{3,7},{10,14},{11,15},{4,0},{5,1},... | collective-permute-start | bytes 393224 | tf_op jit(solution)/shard_map/ppermute | solution.py:296
  97.6 15.1 %collective-permute-start.11 = (bf16[2,2,8,16,128]{4,3,2,1,0:T(8,128)(2,1)S(1)}, bf16[2,2,8,16,128]{4,3,2,1,0:T(8,128)(2,1)S(1)}, u32[]{:S(2)}, u32[]{:S(2)}) collective-permute-start(bf16[2,2,8,16,128]{4,3,2,1,0:T(8,128)(2,1)S(1)} %get-tuple-element.59), channel_id=1, source_target_pairs={{0,10},{1,11},{8,4},{9,5},{2,12},{3,13},{10,6},{11,7},{4,14},{5,15... | collective-permute-start | bytes 393224 | tf_op jit(solution)/shard_map/ppermute | solution.py:296
  98.2 15.7 %collective-permute-start.12 = (bf16[2,2,8,16,128]{4,3,2,1,0:T(8,128)(2,1)S(1)}, bf16[2,2,8,16,128]{4,3,2,1,0:T(8,128)(2,1)S(1)}, u32[]{:S(2)}, u32[]{:S(2)}) collective-permute-start(bf16[2,2,8,16,128]{4,3,2,1,0:T(8,128)(2,1)S(1)} %get-tuple-element.60), channel_id=1, source_target_pairs={{0,12},{1,13},{8,6},{9,7},{2,14},{3,15},{10,0},{11,1},{4,8},{5,9},... | collective-permute-start | bytes 393224 | tf_op jit(solution)/shard_map/ppermute | solution.py:296
  102.1 16.0 %collective-permute-start.13 = (bf16[2,2,8,16,128]{4,3,2,1,0:T(8,128)(2,1)S(1)}, bf16[2,2,8,16,128]{4,3,2,1,0:T(8,128)(2,1)S(1)}, u32[]{:S(2)}, u32[]{:S(2)}) collective-permute-start(bf16[2,2,8,16,128]{4,3,2,1,0:T(8,128)(2,1)S(1)} %get-tuple-element.61), channel_id=1, source_target_pairs={{0,2},{1,3},{8,10},{9,11},{2,4},{3,5},{10,12},{11,13},{4,6},{5,7},... | collective-permute-start | bytes 393224 | tf_op jit(solution)/shard_map/ppermute | solution.py:296
  102.3 17.0 %collective-permute-start.14 = (bf16[2,2,8,16,128]{4,3,2,1,0:T(8,128)(2,1)S(1)}, bf16[2,2,8,16,128]{4,3,2,1,0:T(8,128)(2,1)S(1)}, u32[]{:S(2)}, u32[]{:S(2)}) collective-permute-start(bf16[2,2,8,16,128]{4,3,2,1,0:T(8,128)(2,1)S(1)} %get-tuple-element.62), channel_id=1, source_target_pairs={{0,6},{1,7},{8,14},{9,15},{2,0},{3,1},{10,8},{11,9},{4,2},{5,3},{1... | collective-permute-start | bytes 393224 | tf_op jit(solution)/shard_map/ppermute | solution.py:296
  113.9 14.3 %collective-permute-start.28 = (bf16[2,2,8,16,128]{4,3,2,1,0:T(8,128)(2,1)S(1)}, bf16[2,2,8,16,128]{4,3,2,1,0:T(8,128)(2,1)S(1)}, u32[]{:S(2)}, u32[]{:S(2)}) collective-permute-start(bf16[2,2,8,16,128]{4,3,2,1,0:T(8,128)(2,1)S(1)} %get-tuple-element.77), channel_id=1, source_target_pairs={{0,0},{1,17},{8,8},{9,25},{2,2},{3,19},{10,10},{11,27},{4,4},{5,21... | collective-permute-start | bytes 393224 | tf_op jit(solution)/shard_map/ppermute | solution.py:296
  118.1 15.7 %collective-permute-start.29 = (bf16[2,2,8,16,128]{4,3,2,1,0:T(8,128)(2,1)S(1)}, bf16[2,2,8,16,128]{4,3,2,1,0:T(8,128)(2,1)S(1)}, u32[]{:S(2)}, u32[]{:S(2)}) collective-permute-start(bf16[2,2,8,16,128]{4,3,2,1,0:T(8,128)(2,1)S(1)} %get-tuple-element.78), channel_id=1, source_target_pairs={{0,4},{1,21},{8,12},{9,29},{2,6},{3,23},{10,14},{11,31},{4,0},{5,1... | collective-permute-start | bytes 393224 | tf_op jit(solution)/shard_map/ppermute | solution.py:296
  119.4 21.7 %collective-permute-start.30 = (bf16[2,2,8,16,128]{4,3,2,1,0:T(8,128)(2,1)S(1)}, bf16[2,2,8,16,128]{4,3,2,1,0:T(8,128)(2,1)S(1)}, u32[]{:S(2)}, u32[]{:S(2)}) collective-permute-start(bf16[2,2,8,16,128]{4,3,2,1,0:T(8,128)(2,1)S(1)} %get-tuple-element.79), channel_id=1, source_target_pairs={{0,10},{1,27},{8,4},{9,21},{2,12},{3,29},{10,6},{11,23},{4,14},{5,... | collective-permute-start | bytes 393224 | tf_op jit(solution)/shard_map/ppermute | solution.py:296
  123.3 19.1 %collective-permute-start.31 = (bf16[2,2,8,16,128]{4,3,2,1,0:T(8,128)(2,1)S(1)}, bf16[2,2,8,16,128]{4,3,2,1,0:T(8,128)(2,1)S(1)}, u32[]{:S(2)}, u32[]{:S(2)}) collective-permute-start(bf16[2,2,8,16,128]{4,3,2,1,0:T(8,128)(2,1)S(1)} %get-tuple-element.80), channel_id=1, source_target_pairs={{0,12},{1,29},{8,6},{9,23},{2,14},{3,31},{10,0},{11,17},{4,8},{5,2... | collective-permute-start | bytes 393224 | tf_op jit(solution)/shard_map/ppermute | solution.py:296
  126.4 16.7 %collective-permute-start.32 = (bf16[2,2,8,16,128]{4,3,2,1,0:T(8,128)(2,1)S(1)}, bf16[2,2,8,16,128]{4,3,2,1,0:T(8,128)(2,1)S(1)}, u32[]{:S(2)}, u32[]{:S(2)}) collective-permute-start(bf16[2,2,8,16,128]{4,3,2,1,0:T(8,128)(2,1)S(1)} %get-tuple-element.81), channel_id=1, source_target_pairs={{0,2},{1,19},{8,10},{9,27},{2,4},{3,21},{10,12},{11,29},{4,6},{5,2... | collective-permute-start | bytes 393224 | tf_op jit(solution)/shard_map/ppermute | solution.py:296
  128.2 18.1 %collective-permute-start.33 = (bf16[2,2,8,16,128]{4,3,2,1,0:T(8,128)(2,1)S(1)}, bf16[2,2,8,16,128]{4,3,2,1,0:T(8,128)(2,1)S(1)}, u32[]{:S(2)}, u32[]{:S(2)}) collective-permute-start(bf16[2,2,8,16,128]{4,3,2,1,0:T(8,128)(2,1)S(1)} %get-tuple-element.82), channel_id=1, source_target_pairs={{0,6},{1,23},{8,14},{9,31},{2,0},{3,17},{10,8},{11,25},{4,2},{5,19... | collective-permute-start | bytes 393224 | tf_op jit(solution)/shard_map/ppermute | solution.py:296
  (14 other events, 130.2 us)

commit v7 on v6

--- a/solution.py
+++ b/solution.py
@@ -130,13 +130,13 @@
     )(pos, *pieces, *after)
 
 
-def cross_kernel(turned, pos_ref, own0, own1, prev0, prev1, *refs):
+def cross_kernel(pos_ref, own0, own1, prev0, prev1, *refs):
     outs, (wide, res) = refs[-10:-2], refs[-2:]
     z, c = pos_ref[0], pos_ref[1]
     rows = 4 * WIN * FC
     for n, (first, second) in enumerate(((own0, own1), (prev0, prev1))):
         for b in range(2):
-            base = pl.multiple_of(((n ^ c if turned else n) * 2 + b) * 2 * rows, rows)
+            base = pl.multiple_of(((n ^ c) * 2 + b) * 2 * rows, rows)
             wide[pl.ds(base, rows)] = first[b].reshape(rows, 128).astype(F32)
             wide[pl.ds(base + rows, rows)] = second[b].reshape(rows, 128).astype(F32)
     sign = jnp.where(lax.broadcasted_iota(jnp.int32, (CH, 128), 1) < CH, 1.0, -1.0).astype(F32)
@@ -167,14 +167,16 @@
             row = ((dst >> 1) * 2 + (c ^ crel)) * 8
             for rnd in range(2):
                 base = (rnd * 2 + (dst & 1)) * FC * CH + row
-                for i in range(8):
+
+                @pl.loop(0, 8, unroll=2)
+                def _(i, r=r, crel=crel, rnd=rnd, base=base):
                     outs[r][crel, rnd, i] = res[pl.ds(base + i, FC, stride=CH), :].astype(BF16)
 
 
-def cross(turned, own0, own1, prev0, prev1, pos, *after):
+def cross(own0, own1, prev0, prev1, pos, *after):
     shape = jax.ShapeDtypeStruct((2, 2, 8, FC, 128), BF16)
     return pl.pallas_call(
-        functools.partial(cross_kernel, turned),
+        cross_kernel,
         out_shape=[shape] * 8,
         in_specs=[SM] + [VM] * 4 + [ANY] * len(after),
         out_specs=[VM] * 8,
@@ -191,56 +193,75 @@
 
 
 def turn_kernel(pos_ref, *refs):
-    ins, (same, other, buf) = refs[:8], refs[-3:]
+    ins, (out, buf) = refs[:8], refs[-2:]
     z = pos_ref[0]
-    for crel, out in enumerate((same, other)):
-        for rnd in range(2):
-            for i in range(8):
-                for n, r in enumerate(ORDER):
-                    start = pl.multiple_of(((z - r) & 7) * FC, FC)
-                    buf[pl.ds(start, FC), :] = ins[n][crel, rnd, i].astype(F32)
-                out[rnd, i] = buf[...].T.astype(BF16)
-
-
-def turn(pieces, pos, *after):
-    shape = jax.ShapeDtypeStruct((2, 8, 128, 8 * FC), BF16)
+    for rnd in range(2):
+
+        @pl.loop(0, 8, unroll=2)
+        def _(i, rnd=rnd):
+            slot = i & 1
+            for n, r in enumerate(ORDER):
+                start = pl.multiple_of(((z - r) & 7) * FC, FC)
+                buf[slot, pl.ds(start, FC), :] = ins[n][0, rnd, i].astype(F32)
+            out[rnd, i] = buf[slot].T.astype(BF16)
+
+
+def turn(crel, pieces, pos, *after):
+    half = pl.BlockSpec((1, 2, 8, FC, 128), lambda n: (crel, 0, 0, 0, 0))
+    whole = pl.BlockSpec((2, 8, 128, 8 * FC), lambda n: (0, 0, 0, 0))
     return pl.pallas_call(
         turn_kernel,
-        out_shape=[shape] * 2,
-        in_specs=[SM] + [VM] * 8 + [ANY] * len(after),
-        out_specs=[VM] * 2,
-        scratch_shapes=[pltpu.VMEM((8 * FC, 128), F32)],
-        compiler_params=params(),
-        cost_estimate=pl.CostEstimate(flops=0, bytes_accessed=4 << 20, transcendentals=0),
+        out_shape=jax.ShapeDtypeStruct((2, 8, 128, 8 * FC), BF16),
+        grid=(1,),
+        in_specs=[SM] + [half] * 8 + [ANY] * len(after),
+        out_specs=whole,
+        scratch_shapes=[pltpu.VMEM((2, 8 * FC, 128), F32)],
+        compiler_params=params(),
+        cost_estimate=pl.CostEstimate(flops=0, bytes_accessed=2 << 20, transcendentals=0),
         name="turn",
     )(pos, *pieces, *after)
 
 
-def invert_kernel(scaling, *refs):
-    parts, (table, out) = refs[: 2 * CHUNKS], refs[2 * CHUNKS :]
-    rows = []
-    for i in range(4):
-        cols = [p[0, i, k * CH : (k + 1) * CH] for k in range(2) for p in parts]
-        rows.append(jnp.concatenate(cols, axis=1))
-    left = jnp.concatenate(rows, axis=0)
-    result = jnp.dot(left, table[...], preferred_element_type=F32) * scaling
-    out[0] = result.reshape(4, CH, LAG_COUNT).astype(BF16)
-
-
-def invert(parts, table, scaling):
+def invert_kernel(scaling, chunk, *refs):
+    parts, table, sums, out = refs[:2], refs[2], refs[3:-1], refs[-1]
+    total = 0.0
+    for k in range(2):
+        rows = []
+        for i in range(4):
+            cols = [p[0, i, k * CH : (k + 1) * CH] for p in parts]
+            rows.append(jnp.concatenate(cols, axis=1))
+        start = k * BINS + chunk * CBINS
+        total += jnp.dot(
+            jnp.concatenate(rows, axis=0),
+            table[start : start + CBINS],
+            preferred_element_type=F32,
+        )
+    total = total.reshape(4, CH, LAG_COUNT)
+    for ref in sums:
+        total += ref[0]
+    if chunk == CHUNKS - 1:
+        total = total * scaling
+    out[0] = total.astype(out.dtype)
+
+
+def invert(chunk, parts, table, sums, scaling):
     part = pl.BlockSpec((1, 4, 128, 8 * FC), lambda r, i: (r, i, 0, 0))
-    return pl.pallas_call(
-        functools.partial(invert_kernel, scaling),
-        out_shape=jax.ShapeDtypeStruct((2, 8, CH, LAG_COUNT), BF16),
+    block = pl.BlockSpec((1, 4, CH, LAG_COUNT), lambda r, i: (r, i, 0, 0))
+    dtype = BF16 if chunk == CHUNKS - 1 else F32
+    return pl.pallas_call(
+        functools.partial(invert_kernel, scaling, chunk),
+        out_shape=jax.ShapeDtypeStruct((2, 8, CH, LAG_COUNT), dtype),
         grid=(2, 2),
-        in_specs=[part] * (2 * CHUNKS) + [pl.BlockSpec((2 * BINS, LAG_COUNT), lambda r, i: (0, 0))],
-        out_specs=pl.BlockSpec((1, 4, CH, LAG_COUNT), lambda r, i: (r, i, 0, 0)),
+        in_specs=[part] * 2
+        + [pl.BlockSpec((2 * BINS, LAG_COUNT), lambda r, i: (0, 0))]
+        + [block] * len(sums),
+        out_specs=block,
         compiler_params=params(),
         cost_estimate=pl.CostEstimate(
-            flops=2 * 1024 * 1024 * 1024, bytes_accessed=6 << 20, transcendentals=0
+            flops=1024 * 1024 * 1024, bytes_accessed=6 << 20, transcendentals=0
         ),
         name="invert",
-    )(*parts, table)
+    )(*parts, table, *sums)
 
 
 def turns(freq_ids, delay_ids):
@@ -296,13 +317,17 @@
     return lax.ppermute(value, ALL, [(device(*d), device(*target(*d))) for d in EVERY])
 
 
-def round_ring(pieces, turned=0):
+def go_round(pieces):
     got = []
     for r in ORDER:
-        if r or turned:
-            got.append(send(pieces[r], lambda m, z, c: (m + c * turned, z + r, c)))
-        else:
-            got.append(pieces[r])
+        got.append(send(pieces[r], lambda m, z, c: (m, z + r, c)) if r else pieces[r])
+    return got
+
+
+def back_round(pieces):
+    got = []
+    for r in ORDER:
+        got.append(send(pieces[r], lambda m, z, c: (m + c, z + r, c)))
     return got
 
 
@@ -318,22 +343,22 @@
     flags2 = jnp.concatenate([valid_flags, valid_flags], axis=1)[:, None, :]
     *white, core = whiten(jnp.transpose(spectra, (2, 0, 1, 3)), flags2, pos)
     table = join_table(lag_table(core[0]))
-    parts = []
-    merged, crossed, turned = (table,), (), ()
+    sums = ()
+    merged, crossed = (table,), ()
     for k in range(CHUNKS):
-        back = int(k == CHUNKS - 1)
-        got = round_ring(white[k * 8 : k * 8 + 8])
+        got = go_round(white[k * 8 : k * 8 + 8])
         same, other = merge(got, pos, *merged)
-        merged = (same,)
-        prev0 = send(same, lambda m, z, c: (m + 1 - 2 * c * back, z, c))
-        prev1 = send(other, lambda m, z, c: (m + 1 - 2 * (1 - c) * back, z, 1 - c))
+        prev0 = send(same, lambda m, z, c: (m + 1 - 2 * c, z, c))
+        prev1 = send(other, lambda m, z, c: (m - 1 + 2 * c, z, 1 - c))
         own1 = other_core(other)
-        out = cross(back, same, own1, prev0, prev1, pos, *crossed)
-        crossed = (out[0],)
-        same, other = turn(round_ring(out, back), pos, *turned)
-        turned = (same,)
-        parts += [same, other_core(other)]
-    return invert(parts, table, scaling)
+        out = cross(same, own1, prev0, prev1, pos, *crossed)
+        crossed = merged = (out[0],)
+        got = back_round(out)
+        other = turn(1, got, pos, *sums)
+        received = other_core(other)
+        same = turn(0, got, pos, other)
+        sums = (invert(k, [same, received], table, sums, scaling),)
+    return sums[0]
 
 
 def solution(mesh):

time: 156 us -> 161 us (1.032)
  waiting for transfers between devices: 57.4 us -> 42.2 us
  starting transfers between devices: 68.1 us -> 81.1 us
  Pallas kernels: 25.6 us -> 31.8 us
    ppermute x37 -> x38, waiting for transfers between devices: 57.4 us -> 42.2 us  [send(): lax.ppermute(value, ALL, [(device(*d), device(*target(*d))) for d in EVERY])]
    ppermute x37 -> x38, starting transfers between devices: 68.1 us -> 81.1 us  [send(): lax.ppermute(value, ALL, [(device(*d), device(*target(*d))) for d in EVERY])]
    pallas_call x5 -> x8, Pallas kernels: 17.1 us -> 23.4 us  [the longest x2 12.4 us: cross(): pl.pallas_call(cross_kernel, out_shape=[shape] * 8, in_specs=[SM] + [VM]...]
  transfers between devices with their start and end apart: 37 -> 38, of which waited for: 15 -> 15; matrix products, arithmetic and copies ran while one was open for 2% -> 2% of each run, Pallas kernels for 10% -> 13%
where the time goes in v7:
time: 161 us
  starting transfers between devices  81.1 us (50%)
  waiting for transfers between devices  42.2 us (26%)
  Pallas kernels  31.8 us (20%)
  other arithmetic  3.77 us (2%)
  local copies, waits for them, and re-layouts  1.89 us (1%)
    ppermute x38, starting transfers between devices, send(): lax.ppermute(value, ALL, [(device(*d), device(*target(*d))) for d in EVERY])  81.1 us
    ppermute x38, waiting for transfers between devices, send(): lax.ppermute(value, ALL, [(device(*d), device(*target(*d))) for d in EVERY])  42.2 us
    pallas_call x2, Pallas kernels, cross(): pl.pallas_call(cross_kernel, out_shape=[shape] * 8, in_specs=[SM] + [VM]...  12.4 us
    pallas_call x4, Pallas kernels, turn(): pl.pallas_call(turn_kernel, out_shape=jax.ShapeDtypeStruct((2, 8, 128, 8...  6.29 us
    pallas_call x1, Pallas kernels, whiten(): pl.pallas_call(whiten_kernel, out_shape=[shape] * (8 * CHUNKS) + [jax.Sha...  5.79 us
    pallas_call x2, Pallas kernels, invert(): pl.pallas_call(functools.partial(invert_kernel, scaling, chunk), out_shap...  4.71 us
  transfers between devices with their start and end apart: 38, of which 15 were waited for; matrix products, arithmetic and copies ran while one was open for 2% of the time, Pallas kernels for 13%

profile of v7, /device:TPU:1, one launch (start us, length us, event | category | flops | bytes accessed | tf_op | source)
XLA Modules:
  0.0 161.0 jit_solution(12991891395761422452)
XLA Ops:
  2.8 5.8 %whiten.1 = (bf16[2,14,16,128]{3,2,1,0:T(8,128)(2,1)S(1)}, bf16[2,14,16,128]{3,2,1,0:T(8,128)(2,1)S(1)}, bf16[2,14,16,128]{3,2,1,0:T(8,128)(2,1)S(1)}, bf16[2,14...) custom-call(s32[2]{0:T(128)S(1)} %pad_add_fusion.1.pos_ref, ...), custom_call_target="tpu_custom_call" | custom-call | flops 1409286144 | bytes 4194304 | tf_op jit(solution)/shard_map/whiten/pallas_call | solution.py:83
  8.6 7.8 %collective-permute-start.7 = (bf16[2,14,16,128]{3,2,1,0:T(8,128)(2,1)S(1)}, bf16[2,14,16,128]{3,2,1,0:T(8,128)(2,1)S(1)}, u32[]{:S(2)}, u32[]{:S(2)}) collective-permute-start(bf16[2,14,16,128]{3,2,1,0:T(8,128)(2,1)S(1)} %get-tuple-element.51), channel_id=1, source_target_pairs={{0,4},{1,5},{8,12},{9,13},{2,6},{3,7},{10,14},{11,15},{4,0},{5,1},... | collective-permute-start | bytes 344072 | tf_op jit(solution)/shard_map/ppermute | solution.py:317
  18.1 2.8 %collective-permute-start.9 = (bf16[2,14,16,128]{3,2,1,0:T(8,128)(2,1)S(1)}, bf16[2,14,16,128]{3,2,1,0:T(8,128)(2,1)S(1)}, u32[]{:S(2)}, u32[]{:S(2)}) collective-permute-start(bf16[2,14,16,128]{3,2,1,0:T(8,128)(2,1)S(1)} %get-tuple-element.53), channel_id=1, source_target_pairs={{0,12},{1,13},{8,6},{9,7},{2,14},{3,15},{10,0},{11,1},{4,8},{5,9},... | collective-permute-start | bytes 344072 | tf_op jit(solution)/shard_map/ppermute | solution.py:317
  26.0 5.4 %collective-permute-done.8.refs_2_ = bf16[2,14,16,128]{3,2,1,0:T(8,128)(2,1)S(1)} collective-permute-done((bf16[2,14,16,128]{3,2,1,0:T(8,128)(2,1)S(1)}, bf16[2,14,16,128]{3,2,1,0:T(8,128)(2,1)S(1)}, u32[]{:S(2)}, u32[]{:S(2)}) %collective-permute-start.8) | collective-permute-done | bytes 114720 | tf_op jit(solution)/shard_map/ppermute | solution.py:317
  38.8 5.0 %collective-permute-start.15 = (bf16[2,4,14,16,128]{4,3,2,1,0:T(8,128)(2,1)S(1)}, bf16[2,4,14,16,128]{4,3,2,1,0:T(8,128)(2,1)S(1)}, u32[]{:S(2)}, u32[]{:S(2)}) collective-permute-start(bf16[2,4,14,16,128]{4,3,2,1,0:T(8,128)(2,1)S(1)} %get-tuple-element.59.own0), channel_id=1, source_target_pairs={{0,16},{1,241},{8,24},{9,249},{2,18},{3,243},{10,26},{11,251},{4,2... | collective-permute-start | bytes 1376264 | tf_op jit(solution)/shard_map/ppermute | solution.py:317
  44.7 2.7 %collective-permute-start = (bf16[2,14,16,128]{3,2,1,0:T(8,128)(2,1)S(1)}, bf16[2,14,16,128]{3,2,1,0:T(8,128)(2,1)S(1)}, u32[]{:S(2)}, u32[]{:S(2)}) collective-permute-start(bf16[2,14,16,128]{3,2,1,0:T(8,128)(2,1)S(1)} %get-tuple-element.43), channel_id=1, source_target_pairs={{0,4},{1,5},{8,12},{9,13},{2,6},{3,7},{10,14},{11,15},{4,0},{5,1},... | collective-permute-start | bytes 344072 | tf_op jit(solution)/shard_map/ppermute | solution.py:317
  47.3 2.5 %collective-permute-start.1 = (bf16[2,14,16,128]{3,2,1,0:T(8,128)(2,1)S(1)}, bf16[2,14,16,128]{3,2,1,0:T(8,128)(2,1)S(1)}, u32[]{:S(2)}, u32[]{:S(2)}) collective-permute-start(bf16[2,14,16,128]{3,2,1,0:T(8,128)(2,1)S(1)} %get-tuple-element.44), channel_id=1, source_target_pairs={{0,10},{1,11},{8,4},{9,5},{2,12},{3,13},{10,6},{11,7},{4,14},{5,15... | collective-permute-start | bytes 344072 | tf_op jit(solution)/shard_map/ppermute | solution.py:317
  49.8 3.3 %collective-permute-done.15.prev0 = bf16[2,4,14,16,128]{4,3,2,1,0:T(8,128)(2,1)S(1)} collective-permute-done((bf16[2,4,14,16,128]{4,3,2,1,0:T(8,128)(2,1)S(1)}, bf16[2,4,14,16,128]{4,3,2,1,0:T(8,128)(2,1)S(1)}, u32[]{:S(2)}, u32[]{:S(2)}) %collective-permute-start.15) | collective-permute-done | bytes 458784 | tf_op jit(solution)/shard_map/ppermute | solution.py:317
  53.5 6.2 %cross.2 = (bf16[2,2,8,16,128]{4,3,2,1,0:T(8,128)(2,1)S(1)}, bf16[2,2,8,16,128]{4,3,2,1,0:T(8,128)(2,1)S(1)}, bf16[2,2,8,16,128]{4,3,2,1,0:T(8,128)(2,1)S(1)}, b...) custom-call(s32[2]{0:T(128)S(1)} %pad_add_fusion.1.pos_ref, ...), custom_call_target="tpu_custom_call" | custom-call | flops 536870912 | bytes 3145728 | tf_op jit(solution)/shard_map/cross/pallas_call | solution.py:178
  65.5 2.7 %collective-permute-start.6 = (bf16[2,14,16,128]{3,2,1,0:T(8,128)(2,1)S(1)}, bf16[2,14,16,128]{3,2,1,0:T(8,128)(2,1)S(1)}, u32[]{:S(2)}, u32[]{:S(2)}) collective-permute-start(bf16[2,14,16,128]{3,2,1,0:T(8,128)(2,1)S(1)} %get-tuple-element.49), channel_id=1, source_target_pairs={{0,14},{1,15},{8,0},{9,1},{2,8},{3,9},{10,2},{11,3},{4,10},{5,11},... | collective-permute-start | bytes 344072 | tf_op jit(solution)/shard_map/ppermute | solution.py:317
  70.4 7.1 %collective-permute-start.30 = (bf16[2,2,8,16,128]{4,3,2,1,0:T(8,128)(2,1)S(1)}, bf16[2,2,8,16,128]{4,3,2,1,0:T(8,128)(2,1)S(1)}, u32[]{:S(2)}, u32[]{:S(2)}) collective-permute-start(bf16[2,2,8,16,128]{4,3,2,1,0:T(8,128)(2,1)S(1)} %get-tuple-element.73), channel_id=1, source_target_pairs={{0,10},{1,27},{8,4},{9,21},{2,12},{3,29},{10,6},{11,23},{4,14},{5,... | collective-permute-start | bytes 393224 | tf_op jit(solution)/shard_map/ppermute | solution.py:317
  77.5 6.4 %collective-permute-start.31 = (bf16[2,2,8,16,128]{4,3,2,1,0:T(8,128)(2,1)S(1)}, bf16[2,2,8,16,128]{4,3,2,1,0:T(8,128)(2,1)S(1)}, u32[]{:S(2)}, u32[]{:S(2)}) collective-permute-start(bf16[2,2,8,16,128]{4,3,2,1,0:T(8,128)(2,1)S(1)} %get-tuple-element.74), channel_id=1, source_target_pairs={{0,12},{1,29},{8,6},{9,23},{2,14},{3,31},{10,0},{11,17},{4,8},{5,2... | collective-permute-start | bytes 393224 | tf_op jit(solution)/shard_map/ppermute | solution.py:317
  85.7 2.8 %collective-permute-start.34 = (bf16[2,2,8,16,128]{4,3,2,1,0:T(8,128)(2,1)S(1)}, bf16[2,2,8,16,128]{4,3,2,1,0:T(8,128)(2,1)S(1)}, u32[]{:S(2)}, u32[]{:S(2)}) collective-permute-start(bf16[2,2,8,16,128]{4,3,2,1,0:T(8,128)(2,1)S(1)} %get-tuple-element.77), channel_id=1, source_target_pairs={{0,8},{1,25},{8,2},{9,19},{2,10},{3,27},{10,4},{11,21},{4,12},{5,2... | collective-permute-start | bytes 393224 | tf_op jit(solution)/shard_map/ppermute | solution.py:317
  88.7 4.8 %collective-permute-start.35 = (bf16[2,2,8,16,128]{4,3,2,1,0:T(8,128)(2,1)S(1)}, bf16[2,2,8,16,128]{4,3,2,1,0:T(8,128)(2,1)S(1)}, u32[]{:S(2)}, u32[]{:S(2)}) collective-permute-start(bf16[2,2,8,16,128]{4,3,2,1,0:T(8,128)(2,1)S(1)} %get-tuple-element.78), channel_id=1, source_target_pairs={{0,14},{1,31},{8,0},{9,17},{2,8},{3,25},{10,2},{11,19},{4,10},{5,2... | collective-permute-start | bytes 393224 | tf_op jit(solution)/shard_map/ppermute | solution.py:317
  96.2 2.6 %collective-permute-done.32.refs_4_ = bf16[2,2,8,16,128]{4,3,2,1,0:T(8,128)(2,1)S(1)} collective-permute-done((bf16[2,2,8,16,128]{4,3,2,1,0:T(8,128)(2,1)S(1)}, bf16[2,2,8,16,128]{4,3,2,1,0:T(8,128)(2,1)S(1)}, u32[]{:S(2)}, u32[]{:S(2)}) %collective-permute-start.32) | collective-permute-done | bytes 131104 | tf_op jit(solution)/shard_map/ppermute | solution.py:317
  106.1 2.6 %collective-permute-done.18.prev0 = bf16[2,4,14,16,128]{4,3,2,1,0:T(8,128)(2,1)S(1)} collective-permute-done((bf16[2,4,14,16,128]{4,3,2,1,0:T(8,128)(2,1)S(1)}, bf16[2,4,14,16,128]{4,3,2,1,0:T(8,128)(2,1)S(1)}, u32[]{:S(2)}, u32[]{:S(2)}) %collective-permute-start.18) | collective-permute-done | bytes 458784 | tf_op jit(solution)/shard_map/ppermute | solution.py:317
  108.6 2.7 %collective-permute-done.19.prev1 = bf16[2,4,14,16,128]{4,3,2,1,0:T(8,128)(2,1)S(1)} collective-permute-done((bf16[2,4,14,16,128]{4,3,2,1,0:T(8,128)(2,1)S(1)}, bf16[2,4,14,16,128]{4,3,2,1,0:T(8,128)(2,1)S(1)}, u32[]{:S(2)}, u32[]{:S(2)}) %collective-permute-start.19) | collective-permute-done | bytes 458784 | tf_op jit(solution)/shard_map/ppermute | solution.py:317
  111.3 6.2 %cross.3 = (bf16[2,2,8,16,128]{4,3,2,1,0:T(8,128)(2,1)S(1)}, bf16[2,2,8,16,128]{4,3,2,1,0:T(8,128)(2,1)S(1)}, bf16[2,2,8,16,128]{4,3,2,1,0:T(8,128)(2,1)S(1)}, b...) custom-call(s32[2]{0:T(128)S(1)} %pad_add_fusion.1.pos_ref, ...), custom_call_target="tpu_custom_call" | custom-call | flops 536870912 | bytes 3145728 | tf_op jit(solution)/shard_map/cross/pallas_call | solution.py:178
  119.5 3.0 %collective-permute-start.21 = (bf16[2,2,8,16,128]{4,3,2,1,0:T(8,128)(2,1)S(1)}, bf16[2,2,8,16,128]{4,3,2,1,0:T(8,128)(2,1)S(1)}, u32[]{:S(2)}, u32[]{:S(2)}) collective-permute-start(bf16[2,2,8,16,128]{4,3,2,1,0:T(8,128)(2,1)S(1)} %get-tuple-element.65), channel_id=1, source_target_pairs={{0,4},{1,21},{8,12},{9,29},{2,6},{3,23},{10,14},{11,31},{4,0},{5,1... | collective-permute-start | bytes 393224 | tf_op jit(solution)/shard_map/ppermute | solution.py:317
  123.0 5.1 %collective-permute-start.23 = (bf16[2,2,8,16,128]{4,3,2,1,0:T(8,128)(2,1)S(1)}, bf16[2,2,8,16,128]{4,3,2,1,0:T(8,128)(2,1)S(1)}, u32[]{:S(2)}, u32[]{:S(2)}) collective-permute-start(bf16[2,2,8,16,128]{4,3,2,1,0:T(8,128)(2,1)S(1)} %get-tuple-element.67), channel_id=1, source_target_pairs={{0,12},{1,29},{8,6},{9,23},{2,14},{3,31},{10,0},{11,17},{4,8},{5,2... | collective-permute-start | bytes 393224 | tf_op jit(solution)/shard_map/ppermute | solution.py:317
  130.3 4.6 %collective-permute-done.21.refs_1_ = bf16[2,2,8,16,128]{4,3,2,1,0:T(8,128)(2,1)S(1)} collective-permute-done((bf16[2,2,8,16,128]{4,3,2,1,0:T(8,128)(2,1)S(1)}, bf16[2,2,8,16,128]{4,3,2,1,0:T(8,128)(2,1)S(1)}, u32[]{:S(2)}, u32[]{:S(2)}) %collective-permute-start.21) | collective-permute-done | bytes 131104 | tf_op jit(solution)/shard_map/ppermute | solution.py:317
  137.2 7.9 %collective-permute-done.22.refs_2_ = bf16[2,2,8,16,128]{4,3,2,1,0:T(8,128)(2,1)S(1)} collective-permute-done((bf16[2,2,8,16,128]{4,3,2,1,0:T(8,128)(2,1)S(1)}, bf16[2,2,8,16,128]{4,3,2,1,0:T(8,128)(2,1)S(1)}, u32[]{:S(2)}, u32[]{:S(2)}) %collective-permute-start.22) | collective-permute-done | bytes 131104 | tf_op jit(solution)/shard_map/ppermute | solution.py:317
  148.5 6.0 %collective-permute-done.26.refs_6_ = bf16[2,2,8,16,128]{4,3,2,1,0:T(8,128)(2,1)S(1)} collective-permute-done((bf16[2,2,8,16,128]{4,3,2,1,0:T(8,128)(2,1)S(1)}, bf16[2,2,8,16,128]{4,3,2,1,0:T(8,128)(2,1)S(1)}, u32[]{:S(2)}, u32[]{:S(2)}) %collective-permute-start.26) | collective-permute-done | bytes 131104 | tf_op jit(solution)/shard_map/ppermute | solution.py:317
  158.1 2.9 %invert.3 = bf16[2,8,64,1024]{3,2,1,0:T(8,128)(2,1)} custom-call(bf16[2,8,128,128]{3,2,1,0:T(8,128)(2,1)S(1)} %turn.7.refs_0_, bf16[2,8,128,128]{3,2,1,0:T(8,128)(2,1)S(1)} %collective-permute-done.37.refs_1_, bf16[1024,1024]{1,0:T(8,128)(2,1)S(1)} %table.1.refs_8_.refs_2_, f32[2,8,64,1024]{3,2,1,0:T(8,128)S(1)} %invert.2.refs_8_.refs_3_), custom_call_target="tpu_custom_call" | custom-call | flops 1073741824 | bytes 6291456 | tf_op jit(solution)/shard_map/invert/pallas_call | solution.py:251
  (72 shorter events, 51.9 us)
Async XLA Ops:
  8.6 16.5 %collective-permute-start.7 = (bf16[2,14,16,128]{3,2,1,0:T(8,128)(2,1)S(1)}, bf16[2,14,16,128]{3,2,1,0:T(8,128)(2,1)S(1)}, u32[]{:S(2)}, u32[]{:S(2)}) collective-permute-start(bf16[2,14,16,128]{3,2,1,0:T(8,128)(2,1)S(1)} %get-tuple-element.51), channel_id=1, source_target_pairs={{0,4},{1,5},{8,12},{9,13},{2,6},{3,7},{10,14},{11,15},{4,0},{5,1},... | collective-permute-start | bytes 344072 | tf_op jit(solution)/shard_map/ppermute | solution.py:317
  16.4 14.9 %collective-permute-start.8 = (bf16[2,14,16,128]{3,2,1,0:T(8,128)(2,1)S(1)}, bf16[2,14,16,128]{3,2,1,0:T(8,128)(2,1)S(1)}, u32[]{:S(2)}, u32[]{:S(2)}) collective-permute-start(bf16[2,14,16,128]{3,2,1,0:T(8,128)(2,1)S(1)} %get-tuple-element.52), channel_id=1, source_target_pairs={{0,10},{1,11},{8,4},{9,5},{2,12},{3,13},{10,6},{11,7},{4,14},{5,15... | collective-permute-start | bytes 344072 | tf_op jit(solution)/shard_map/ppermute | solution.py:317
  18.1 16.9 %collective-permute-start.9 = (bf16[2,14,16,128]{3,2,1,0:T(8,128)(2,1)S(1)}, bf16[2,14,16,128]{3,2,1,0:T(8,128)(2,1)S(1)}, u32[]{:S(2)}, u32[]{:S(2)}) collective-permute-start(bf16[2,14,16,128]{3,2,1,0:T(8,128)(2,1)S(1)} %get-tuple-element.53), channel_id=1, source_target_pairs={{0,12},{1,13},{8,6},{9,7},{2,14},{3,15},{10,0},{11,1},{4,8},{5,9},... | collective-permute-start | bytes 344072 | tf_op jit(solution)/shard_map/ppermute | solution.py:317
  20.9 14.1 %collective-permute-start.10 = (bf16[2,14,16,128]{3,2,1,0:T(8,128)(2,1)S(1)}, bf16[2,14,16,128]{3,2,1,0:T(8,128)(2,1)S(1)}, u32[]{:S(2)}, u32[]{:S(2)}) collective-permute-start(bf16[2,14,16,128]{3,2,1,0:T(8,128)(2,1)S(1)} %get-tuple-element.54), channel_id=1, source_target_pairs={{0,2},{1,3},{8,10},{9,11},{2,4},{3,5},{10,12},{11,13},{4,6},{5,7},... | collective-permute-start | bytes 344072 | tf_op jit(solution)/shard_map/ppermute | solution.py:317
  22.1 13.0 %collective-permute-start.11 = (bf16[2,14,16,128]{3,2,1,0:T(8,128)(2,1)S(1)}, bf16[2,14,16,128]{3,2,1,0:T(8,128)(2,1)S(1)}, u32[]{:S(2)}, u32[]{:S(2)}) collective-permute-start(bf16[2,14,16,128]{3,2,1,0:T(8,128)(2,1)S(1)} %get-tuple-element.55), channel_id=1, source_target_pairs={{0,6},{1,7},{8,14},{9,15},{2,0},{3,1},{10,8},{11,9},{4,2},{5,3},{1... | collective-permute-start | bytes 344072 | tf_op jit(solution)/shard_map/ppermute | solution.py:317
  38.8 14.3 %collective-permute-start.15 = (bf16[2,4,14,16,128]{4,3,2,1,0:T(8,128)(2,1)S(1)}, bf16[2,4,14,16,128]{4,3,2,1,0:T(8,128)(2,1)S(1)}, u32[]{:S(2)}, u32[]{:S(2)}) collective-permute-start(bf16[2,4,14,16,128]{4,3,2,1,0:T(8,128)(2,1)S(1)} %get-tuple-element.59.own0), channel_id=1, source_target_pairs={{0,16},{1,241},{8,24},{9,249},{2,18},{3,243},{10,26},{11,251},{4,2... | collective-permute-start | bytes 1376264 | tf_op jit(solution)/shard_map/ppermute | solution.py:317
  44.7 19.1 %collective-permute-start = (bf16[2,14,16,128]{3,2,1,0:T(8,128)(2,1)S(1)}, bf16[2,14,16,128]{3,2,1,0:T(8,128)(2,1)S(1)}, u32[]{:S(2)}, u32[]{:S(2)}) collective-permute-start(bf16[2,14,16,128]{3,2,1,0:T(8,128)(2,1)S(1)} %get-tuple-element.43), channel_id=1, source_target_pairs={{0,4},{1,5},{8,12},{9,13},{2,6},{3,7},{10,14},{11,15},{4,0},{5,1},... | collective-permute-start | bytes 344072 | tf_op jit(solution)/shard_map/ppermute | solution.py:317
  47.3 18.1 %collective-permute-start.1 = (bf16[2,14,16,128]{3,2,1,0:T(8,128)(2,1)S(1)}, bf16[2,14,16,128]{3,2,1,0:T(8,128)(2,1)S(1)}, u32[]{:S(2)}, u32[]{:S(2)}) collective-permute-start(bf16[2,14,16,128]{3,2,1,0:T(8,128)(2,1)S(1)} %get-tuple-element.44), channel_id=1, source_target_pairs={{0,10},{1,11},{8,4},{9,5},{2,12},{3,13},{10,6},{11,7},{4,14},{5,15... | collective-permute-start | bytes 344072 | tf_op jit(solution)/shard_map/ppermute | solution.py:317
  59.7 25.9 %collective-permute-start.29 = (bf16[2,2,8,16,128]{4,3,2,1,0:T(8,128)(2,1)S(1)}, bf16[2,2,8,16,128]{4,3,2,1,0:T(8,128)(2,1)S(1)}, u32[]{:S(2)}, u32[]{:S(2)}) collective-permute-start(bf16[2,2,8,16,128]{4,3,2,1,0:T(8,128)(2,1)S(1)} %get-tuple-element.72), channel_id=1, source_target_pairs={{0,4},{1,21},{8,12},{9,29},{2,6},{3,23},{10,14},{11,31},{4,0},{5,1... | collective-permute-start | bytes 393224 | tf_op jit(solution)/shard_map/ppermute | solution.py:317
  63.7 13.8 %collective-permute-start.4 = (bf16[2,14,16,128]{3,2,1,0:T(8,128)(2,1)S(1)}, bf16[2,14,16,128]{3,2,1,0:T(8,128)(2,1)S(1)}, u32[]{:S(2)}, u32[]{:S(2)}) collective-permute-start(bf16[2,14,16,128]{3,2,1,0:T(8,128)(2,1)S(1)} %get-tuple-element.47), channel_id=1, source_target_pairs={{0,6},{1,7},{8,14},{9,15},{2,0},{3,1},{10,8},{11,9},{4,2},{5,3},{1... | collective-permute-start | bytes 344072 | tf_op jit(solution)/shard_map/ppermute | solution.py:317
  65.4 18.5 %collective-permute-start.5 = (bf16[2,14,16,128]{3,2,1,0:T(8,128)(2,1)S(1)}, bf16[2,14,16,128]{3,2,1,0:T(8,128)(2,1)S(1)}, u32[]{:S(2)}, u32[]{:S(2)}) collective-permute-start(bf16[2,14,16,128]{3,2,1,0:T(8,128)(2,1)S(1)} %get-tuple-element.48), channel_id=1, source_target_pairs={{0,8},{1,9},{8,2},{9,3},{2,10},{3,11},{10,4},{11,5},{4,12},{5,13},... | collective-permute-start | bytes 344072 | tf_op jit(solution)/shard_map/ppermute | solution.py:317
  65.5 18.5 %collective-permute-start.6 = (bf16[2,14,16,128]{3,2,1,0:T(8,128)(2,1)S(1)}, bf16[2,14,16,128]{3,2,1,0:T(8,128)(2,1)S(1)}, u32[]{:S(2)}, u32[]{:S(2)}) collective-permute-start(bf16[2,14,16,128]{3,2,1,0:T(8,128)(2,1)S(1)} %get-tuple-element.49), channel_id=1, source_target_pairs={{0,14},{1,15},{8,0},{9,1},{2,8},{3,9},{10,2},{11,3},{4,10},{5,11},... | collective-permute-start | bytes 344072 | tf_op jit(solution)/shard_map/ppermute | solution.py:317
  70.4 18.3 %collective-permute-start.30 = (bf16[2,2,8,16,128]{4,3,2,1,0:T(8,128)(2,1)S(1)}, bf16[2,2,8,16,128]{4,3,2,1,0:T(8,128)(2,1)S(1)}, u32[]{:S(2)}, u32[]{:S(2)}) collective-permute-start(bf16[2,2,8,16,128]{4,3,2,1,0:T(8,128)(2,1)S(1)} %get-tuple-element.73), channel_id=1, source_target_pairs={{0,10},{1,27},{8,4},{9,21},{2,12},{3,29},{10,6},{11,23},{4,14},{5,... | collective-permute-start | bytes 393224 | tf_op jit(solution)/shard_map/ppermute | solution.py:317
  77.5 16.0 %collective-permute-start.31 = (bf16[2,2,8,16,128]{4,3,2,1,0:T(8,128)(2,1)S(1)}, bf16[2,2,8,16,128]{4,3,2,1,0:T(8,128)(2,1)S(1)}, u32[]{:S(2)}, u32[]{:S(2)}) collective-permute-start(bf16[2,2,8,16,128]{4,3,2,1,0:T(8,128)(2,1)S(1)} %get-tuple-element.74), channel_id=1, source_target_pairs={{0,12},{1,29},{8,6},{9,23},{2,14},{3,31},{10,0},{11,17},{4,8},{5,2... | collective-permute-start | bytes 393224 | tf_op jit(solution)/shard_map/ppermute | solution.py:317
  83.9 14.9 %collective-permute-start.32 = (bf16[2,2,8,16,128]{4,3,2,1,0:T(8,128)(2,1)S(1)}, bf16[2,2,8,16,128]{4,3,2,1,0:T(8,128)(2,1)S(1)}, u32[]{:S(2)}, u32[]{:S(2)}) collective-permute-start(bf16[2,2,8,16,128]{4,3,2,1,0:T(8,128)(2,1)S(1)} %get-tuple-element.75), channel_id=1, source_target_pairs={{0,2},{1,19},{8,10},{9,27},{2,4},{3,21},{10,12},{11,29},{4,6},{5,2... | collective-permute-start | bytes 393224 | tf_op jit(solution)/shard_map/ppermute | solution.py:317
  83.9 17.0 %collective-permute-start.33 = (bf16[2,2,8,16,128]{4,3,2,1,0:T(8,128)(2,1)S(1)}, bf16[2,2,8,16,128]{4,3,2,1,0:T(8,128)(2,1)S(1)}, u32[]{:S(2)}, u32[]{:S(2)}) collective-permute-start(bf16[2,2,8,16,128]{4,3,2,1,0:T(8,128)(2,1)S(1)} %get-tuple-element.76), channel_id=1, source_target_pairs={{0,6},{1,23},{8,14},{9,31},{2,0},{3,17},{10,8},{11,25},{4,2},{5,19... | collective-permute-start | bytes 393224 | tf_op jit(solution)/shard_map/ppermute | solution.py:317
  85.7 15.5 %collective-permute-start.34 = (bf16[2,2,8,16,128]{4,3,2,1,0:T(8,128)(2,1)S(1)}, bf16[2,2,8,16,128]{4,3,2,1,0:T(8,128)(2,1)S(1)}, u32[]{:S(2)}, u32[]{:S(2)}) collective-permute-start(bf16[2,2,8,16,128]{4,3,2,1,0:T(8,128)(2,1)S(1)} %get-tuple-element.77), channel_id=1, source_target_pairs={{0,8},{1,25},{8,2},{9,19},{2,10},{3,27},{10,4},{11,21},{4,12},{5,2... | collective-permute-start | bytes 393224 | tf_op jit(solution)/shard_map/ppermute | solution.py:317
  88.7 14.8 %collective-permute-start.35 = (bf16[2,2,8,16,128]{4,3,2,1,0:T(8,128)(2,1)S(1)}, bf16[2,2,8,16,128]{4,3,2,1,0:T(8,128)(2,1)S(1)}, u32[]{:S(2)}, u32[]{:S(2)}) collective-permute-start(bf16[2,2,8,16,128]{4,3,2,1,0:T(8,128)(2,1)S(1)} %get-tuple-element.78), channel_id=1, source_target_pairs={{0,14},{1,31},{8,0},{9,17},{2,8},{3,25},{10,2},{11,19},{4,10},{5,2... | collective-permute-start | bytes 393224 | tf_op jit(solution)/shard_map/ppermute | solution.py:317
  106.0 39.1 %collective-permute-start.36 = (bf16[2,8,128,128]{3,2,1,0:T(8,128)(2,1)S(1)}, bf16[2,8,128,128]{3,2,1,0:T(8,128)(2,1)S(1)}, u32[]{:S(2)}, u32[]{:S(2)}) collective-permute-start(bf16[2,8,128,128]{3,2,1,0:T(8,128)(2,1)S(1)} %turn.4.refs_8_), channel_id=1, source_target_pairs={{0,1},{1,0},{8,9},{9,8},{2,3},{3,2},{10,11},{11,10},{4,5},{5,4},{1... | collective-permute-start | bytes 1572872 | tf_op jit(solution)/shard_map/ppermute | solution.py:317
  119.5 15.4 %collective-permute-start.21 = (bf16[2,2,8,16,128]{4,3,2,1,0:T(8,128)(2,1)S(1)}, bf16[2,2,8,16,128]{4,3,2,1,0:T(8,128)(2,1)S(1)}, u32[]{:S(2)}, u32[]{:S(2)}) collective-permute-start(bf16[2,2,8,16,128]{4,3,2,1,0:T(8,128)(2,1)S(1)} %get-tuple-element.65), channel_id=1, source_target_pairs={{0,4},{1,21},{8,12},{9,29},{2,6},{3,23},{10,14},{11,31},{4,0},{5,1... | collective-permute-start | bytes 393224 | tf_op jit(solution)/shard_map/ppermute | solution.py:317
  122.5 22.6 %collective-permute-start.22 = (bf16[2,2,8,16,128]{4,3,2,1,0:T(8,128)(2,1)S(1)}, bf16[2,2,8,16,128]{4,3,2,1,0:T(8,128)(2,1)S(1)}, u32[]{:S(2)}, u32[]{:S(2)}) collective-permute-start(bf16[2,2,8,16,128]{4,3,2,1,0:T(8,128)(2,1)S(1)} %get-tuple-element.66), channel_id=1, source_target_pairs={{0,10},{1,27},{8,4},{9,21},{2,12},{3,29},{10,6},{11,23},{4,14},{5,... | collective-permute-start | bytes 393224 | tf_op jit(solution)/shard_map/ppermute | solution.py:317
  123.0 25.4 %collective-permute-start.23 = (bf16[2,2,8,16,128]{4,3,2,1,0:T(8,128)(2,1)S(1)}, bf16[2,2,8,16,128]{4,3,2,1,0:T(8,128)(2,1)S(1)}, u32[]{:S(2)}, u32[]{:S(2)}) collective-permute-start(bf16[2,2,8,16,128]{4,3,2,1,0:T(8,128)(2,1)S(1)} %get-tuple-element.67), channel_id=1, source_target_pairs={{0,12},{1,29},{8,6},{9,23},{2,14},{3,31},{10,0},{11,17},{4,8},{5,2... | collective-permute-start | bytes 393224 | tf_op jit(solution)/shard_map/ppermute | solution.py:317
  128.1 20.3 %collective-permute-start.24 = (bf16[2,2,8,16,128]{4,3,2,1,0:T(8,128)(2,1)S(1)}, bf16[2,2,8,16,128]{4,3,2,1,0:T(8,128)(2,1)S(1)}, u32[]{:S(2)}, u32[]{:S(2)}) collective-permute-start(bf16[2,2,8,16,128]{4,3,2,1,0:T(8,128)(2,1)S(1)} %get-tuple-element.68), channel_id=1, source_target_pairs={{0,2},{1,19},{8,10},{9,27},{2,4},{3,21},{10,12},{11,29},{4,6},{5,2... | collective-permute-start | bytes 393224 | tf_op jit(solution)/shard_map/ppermute | solution.py:317
  134.8 13.6 %collective-permute-start.25 = (bf16[2,2,8,16,128]{4,3,2,1,0:T(8,128)(2,1)S(1)}, bf16[2,2,8,16,128]{4,3,2,1,0:T(8,128)(2,1)S(1)}, u32[]{:S(2)}, u32[]{:S(2)}) collective-permute-start(bf16[2,2,8,16,128]{4,3,2,1,0:T(8,128)(2,1)S(1)} %get-tuple-element.69), channel_id=1, source_target_pairs={{0,6},{1,23},{8,14},{9,31},{2,0},{3,17},{10,8},{11,25},{4,2},{5,19... | collective-permute-start | bytes 393224 | tf_op jit(solution)/shard_map/ppermute | solution.py:317
  (14 other events, 131.9 us)

commit v8 on v7

--- a/solution.py
+++ b/solution.py
@@ -20,7 +20,7 @@
 CHUNKS = 2
 FC = 32 // CHUNKS
 CBINS = BINS // CHUNKS
-ORDER = (0, 4, 3, 5, 2, 6, 1, 7)
+ORDER = (0, 1, 7, 4, 3, 5, 2, 6)
 F32 = jnp.float32
 BF16 = jnp.bfloat16
 
@@ -136,9 +136,9 @@
     rows = 4 * WIN * FC
     for n, (first, second) in enumerate(((own0, own1), (prev0, prev1))):
         for b in range(2):
-            base = pl.multiple_of(((n ^ c) * 2 + b) * 2 * rows, rows)
-            wide[pl.ds(base, rows)] = first[b].reshape(rows, 128).astype(F32)
-            wide[pl.ds(base + rows, rows)] = second[b].reshape(rows, 128).astype(F32)
+            base = (n * 2 + b) * 2 * rows
+            wide[base : base + rows] = first[b].reshape(rows, 128).astype(F32)
+            wide[base + rows : base + 2 * rows] = second[b].reshape(rows, 128).astype(F32)
     sign = jnp.where(lax.broadcasted_iota(jnp.int32, (CH, 128), 1) < CH, 1.0, -1.0).astype(F32)
     tn = (((0,), (0,)), ((), ()))
 
@@ -167,9 +167,7 @@
             row = ((dst >> 1) * 2 + (c ^ crel)) * 8
             for rnd in range(2):
                 base = (rnd * 2 + (dst & 1)) * FC * CH + row
-
-                @pl.loop(0, 8, unroll=2)
-                def _(i, r=r, crel=crel, rnd=rnd, base=base):
+                for i in range(8):
                     outs[r][crel, rnd, i] = res[pl.ds(base + i, FC, stride=CH), :].astype(BF16)
 
 
@@ -196,9 +194,7 @@
     ins, (out, buf) = refs[:8], refs[-2:]
     z = pos_ref[0]
     for rnd in range(2):
-
-        @pl.loop(0, 8, unroll=2)
-        def _(i, rnd=rnd):
+        for i in range(8):
             slot = i & 1
             for n, r in enumerate(ORDER):
                 start = pl.multiple_of(((z - r) & 7) * FC, FC)
@@ -317,17 +313,10 @@
     return lax.ppermute(value, ALL, [(device(*d), device(*target(*d))) for d in EVERY])
 
 
-def go_round(pieces):
+def round_ring(pieces):
     got = []
     for r in ORDER:
         got.append(send(pieces[r], lambda m, z, c: (m, z + r, c)) if r else pieces[r])
-    return got
-
-
-def back_round(pieces):
-    got = []
-    for r in ORDER:
-        got.append(send(pieces[r], lambda m, z, c: (m + c, z + r, c)))
     return got
 
 
@@ -346,14 +335,15 @@
     sums = ()
     merged, crossed = (table,), ()
     for k in range(CHUNKS):
-        got = go_round(white[k * 8 : k * 8 + 8])
+        got = round_ring(white[k * 8 : k * 8 + 8])
         same, other = merge(got, pos, *merged)
-        prev0 = send(same, lambda m, z, c: (m + 1 - 2 * c, z, c))
-        prev1 = send(other, lambda m, z, c: (m - 1 + 2 * c, z, 1 - c))
+        merged = (same,)
+        prev0 = send(same, lambda m, z, c: (m + 1, z, c))
+        prev1 = send(other, lambda m, z, c: (m + 1, z, 1 - c))
         own1 = other_core(other)
         out = cross(same, own1, prev0, prev1, pos, *crossed)
-        crossed = merged = (out[0],)
-        got = back_round(out)
+        crossed = (out[0],)
+        got = round_ring(out)
         other = turn(1, got, pos, *sums)
         received = other_core(other)
         same = turn(0, got, pos, other)

time: 161 us -> 157 us (0.975)
  starting transfers between devices: 81.1 us -> 71 us
  waiting for transfers between devices: 42.2 us -> 52.1 us
  Pallas kernels: 31.8 us -> 27.7 us
    ppermute x38 -> x36, starting transfers between devices: 81.1 us -> 71 us  [send(): lax.ppermute(value, ALL, [(device(*d), device(*target(*d))) for d in EVERY])]
    ppermute x38 -> x36, waiting for transfers between devices: 42.2 us -> 52.1 us  [send(): lax.ppermute(value, ALL, [(device(*d), device(*target(*d))) for d in EVERY])]
    pallas_call x4, Pallas kernels: 6.29 us -> 3.75 us  [turn(): pl.pallas_call(turn_kernel, out_shape=jax.ShapeDtypeStruct((2, 8, 128, 8...]
  transfers between devices with their start and end apart: 38 -> 36, of which waited for: 15 -> 13; matrix products, arithmetic and copies ran while one was open for 2% -> 2% of each run, Pallas kernels for 13% -> 11%
where the time goes in v8:
time: 157 us
  starting transfers between devices  71 us (45%)
  waiting for transfers between devices  52.1 us (33%)
  Pallas kernels  27.7 us (18%)
  other arithmetic  3.77 us (2%)
  local copies, waits for them, and re-layouts  1.89 us (1%)
    ppermute x36, starting transfers between devices, send(): lax.ppermute(value, ALL, [(device(*d), device(*target(*d))) for d in EVERY])  71 us
    ppermute x36, waiting for transfers between devices, send(): lax.ppermute(value, ALL, [(device(*d), device(*target(*d))) for d in EVERY])  52.1 us
    pallas_call x2, Pallas kernels, cross(): pl.pallas_call(cross_kernel, out_shape=[shape] * 8, in_specs=[SM] + [VM]...  10.8 us
    pallas_call x1, Pallas kernels, whiten(): pl.pallas_call(whiten_kernel, out_shape=[shape] * (8 * CHUNKS) + [jax.Sha...  5.79 us
    pallas_call x2, Pallas kernels, invert(): pl.pallas_call(functools.partial(invert_kernel, scaling, chunk), out_shap...  4.71 us
    pallas_call x4, Pallas kernels, turn(): pl.pallas_call(turn_kernel, out_shape=jax.ShapeDtypeStruct((2, 8, 128, 8...  3.75 us
  transfers between devices with their start and end apart: 36, of which 13 were waited for; matrix products, arithmetic and copies ran while one was open for 2% of the time, Pallas kernels for 11%

profile of v8, /device:TPU:1, one launch (start us, length us, event | category | flops | bytes accessed | tf_op | source)
XLA Modules:
  0.0 156.7 jit_solution(4496124553112103709)
XLA Ops:
  2.8 5.8 %whiten.1 = (bf16[2,14,16,128]{3,2,1,0:T(8,128)(2,1)S(1)}, bf16[2,14,16,128]{3,2,1,0:T(8,128)(2,1)S(1)}, bf16[2,14,16,128]{3,2,1,0:T(8,128)(2,1)S(1)}, bf16[2,14...) custom-call(s32[2]{0:T(128)S(1)} %pad_add_fusion.1.pos_ref, ...), custom_call_target="tpu_custom_call" | custom-call | flops 1409286144 | bytes 4194304 | tf_op jit(solution)/shard_map/whiten/pallas_call | solution.py:83
  11.2 4.0 %collective-permute-start.8 = (bf16[2,14,16,128]{3,2,1,0:T(8,128)(2,1)S(1)}, bf16[2,14,16,128]{3,2,1,0:T(8,128)(2,1)S(1)}, u32[]{:S(2)}, u32[]{:S(2)}) collective-permute-start(bf16[2,14,16,128]{3,2,1,0:T(8,128)(2,1)S(1)} %get-tuple-element.52), channel_id=1, source_target_pairs={{0,14},{1,15},{8,0},{9,1},{2,8},{3,9},{10,2},{11,3},{4,10},{5,11},... | collective-permute-start | bytes 344072 | tf_op jit(solution)/shard_map/ppermute | solution.py:313
  15.2 3.9 %collective-permute-start.9 = (bf16[2,14,16,128]{3,2,1,0:T(8,128)(2,1)S(1)}, bf16[2,14,16,128]{3,2,1,0:T(8,128)(2,1)S(1)}, u32[]{:S(2)}, u32[]{:S(2)}) collective-permute-start(bf16[2,14,16,128]{3,2,1,0:T(8,128)(2,1)S(1)} %get-tuple-element.53), channel_id=1, source_target_pairs={{0,4},{1,5},{8,12},{9,13},{2,6},{3,7},{10,14},{11,15},{4,0},{5,1},... | collective-permute-start | bytes 344072 | tf_op jit(solution)/shard_map/ppermute | solution.py:313
  19.6 4.0 %collective-permute-start.11 = (bf16[2,14,16,128]{3,2,1,0:T(8,128)(2,1)S(1)}, bf16[2,14,16,128]{3,2,1,0:T(8,128)(2,1)S(1)}, u32[]{:S(2)}, u32[]{:S(2)}) collective-permute-start(bf16[2,14,16,128]{3,2,1,0:T(8,128)(2,1)S(1)} %get-tuple-element.55), channel_id=1, source_target_pairs={{0,12},{1,13},{8,6},{9,7},{2,14},{3,15},{10,0},{11,1},{4,8},{5,9},... | collective-permute-start | bytes 344072 | tf_op jit(solution)/shard_map/ppermute | solution.py:313
  24.4 3.6 %collective-permute-start.13 = (bf16[2,14,16,128]{3,2,1,0:T(8,128)(2,1)S(1)}, bf16[2,14,16,128]{3,2,1,0:T(8,128)(2,1)S(1)}, u32[]{:S(2)}, u32[]{:S(2)}) collective-permute-start(bf16[2,14,16,128]{3,2,1,0:T(8,128)(2,1)S(1)} %get-tuple-element.57), channel_id=1, source_target_pairs={{0,6},{1,7},{8,14},{9,15},{2,0},{3,1},{10,8},{11,9},{4,2},{5,3},{1... | collective-permute-start | bytes 344072 | tf_op jit(solution)/shard_map/ppermute | solution.py:313
  32.8 4.2 %collective-permute-done.13.refs_7_ = bf16[2,14,16,128]{3,2,1,0:T(8,128)(2,1)S(1)} collective-permute-done((bf16[2,14,16,128]{3,2,1,0:T(8,128)(2,1)S(1)}, bf16[2,14,16,128]{3,2,1,0:T(8,128)(2,1)S(1)}, u32[]{:S(2)}, u32[]{:S(2)}) %collective-permute-start.13) | collective-permute-done | bytes 114720 | tf_op jit(solution)/shard_map/ppermute | solution.py:313
  46.4 2.8 %collective-permute-start.2 = (bf16[2,14,16,128]{3,2,1,0:T(8,128)(2,1)S(1)}, bf16[2,14,16,128]{3,2,1,0:T(8,128)(2,1)S(1)}, u32[]{:S(2)}, u32[]{:S(2)}) collective-permute-start(bf16[2,14,16,128]{3,2,1,0:T(8,128)(2,1)S(1)} %get-tuple-element.45), channel_id=1, source_target_pairs={{0,4},{1,5},{8,12},{9,13},{2,6},{3,7},{10,14},{11,15},{4,0},{5,1},... | collective-permute-start | bytes 344072 | tf_op jit(solution)/shard_map/ppermute | solution.py:313
  50.6 4.1 %collective-permute-done.19.prev1 = bf16[2,4,14,16,128]{4,3,2,1,0:T(8,128)(2,1)S(1)} collective-permute-done((bf16[2,4,14,16,128]{4,3,2,1,0:T(8,128)(2,1)S(1)}, bf16[2,4,14,16,128]{4,3,2,1,0:T(8,128)(2,1)S(1)}, u32[]{:S(2)}, u32[]{:S(2)}) %collective-permute-start.19) | collective-permute-done | bytes 458784 | tf_op jit(solution)/shard_map/ppermute | solution.py:313
  54.7 3.0 %collective-permute-start.4 = (bf16[2,14,16,128]{3,2,1,0:T(8,128)(2,1)S(1)}, bf16[2,14,16,128]{3,2,1,0:T(8,128)(2,1)S(1)}, u32[]{:S(2)}, u32[]{:S(2)}) collective-permute-start(bf16[2,14,16,128]{3,2,1,0:T(8,128)(2,1)S(1)} %get-tuple-element.47), channel_id=1, source_target_pairs={{0,12},{1,13},{8,6},{9,7},{2,14},{3,15},{10,0},{11,1},{4,8},{5,9},... | collective-permute-start | bytes 344072 | tf_op jit(solution)/shard_map/ppermute | solution.py:313
  58.7 5.2 %collective-permute-done.18.prev0 = bf16[2,4,14,16,128]{4,3,2,1,0:T(8,128)(2,1)S(1)} collective-permute-done((bf16[2,4,14,16,128]{4,3,2,1,0:T(8,128)(2,1)S(1)}, bf16[2,4,14,16,128]{4,3,2,1,0:T(8,128)(2,1)S(1)}, u32[]{:S(2)}, u32[]{:S(2)}) %collective-permute-start.18) | collective-permute-done | bytes 458784 | tf_op jit(solution)/shard_map/ppermute | solution.py:313
  63.9 3.3 %collective-permute-start.6 = (bf16[2,14,16,128]{3,2,1,0:T(8,128)(2,1)S(1)}, bf16[2,14,16,128]{3,2,1,0:T(8,128)(2,1)S(1)}, u32[]{:S(2)}, u32[]{:S(2)}) collective-permute-start(bf16[2,14,16,128]{3,2,1,0:T(8,128)(2,1)S(1)} %get-tuple-element.49), channel_id=1, source_target_pairs={{0,6},{1,7},{8,14},{9,15},{2,0},{3,1},{10,8},{11,9},{4,2},{5,3},{1... | collective-permute-start | bytes 344072 | tf_op jit(solution)/shard_map/ppermute | solution.py:313
  67.2 5.4 %cross.2 = (bf16[2,2,8,16,128]{4,3,2,1,0:T(8,128)(2,1)S(1)}, bf16[2,2,8,16,128]{4,3,2,1,0:T(8,128)(2,1)S(1)}, bf16[2,2,8,16,128]{4,3,2,1,0:T(8,128)(2,1)S(1)}, b...) custom-call(s32[2]{0:T(128)S(1)} %pad_add_fusion.1.pos_ref, ...), custom_call_target="tpu_custom_call" | custom-call | flops 536870912 | bytes 3145728 | tf_op jit(solution)/shard_map/cross/pallas_call | solution.py:176
  72.7 2.7 %collective-permute-start.28 = (bf16[2,2,8,16,128]{4,3,2,1,0:T(8,128)(2,1)S(1)}, bf16[2,2,8,16,128]{4,3,2,1,0:T(8,128)(2,1)S(1)}, u32[]{:S(2)}, u32[]{:S(2)}) collective-permute-start(bf16[2,2,8,16,128]{4,3,2,1,0:T(8,128)(2,1)S(1)} %get-tuple-element.73), channel_id=1, source_target_pairs={{0,14},{1,15},{8,0},{9,1},{2,8},{3,9},{10,2},{11,3},{4,10},{5,11},... | collective-permute-start | bytes 393224 | tf_op jit(solution)/shard_map/ppermute | solution.py:313
  75.4 2.6 %collective-permute-start.29 = (bf16[2,2,8,16,128]{4,3,2,1,0:T(8,128)(2,1)S(1)}, bf16[2,2,8,16,128]{4,3,2,1,0:T(8,128)(2,1)S(1)}, u32[]{:S(2)}, u32[]{:S(2)}) collective-permute-start(bf16[2,2,8,16,128]{4,3,2,1,0:T(8,128)(2,1)S(1)} %get-tuple-element.74), channel_id=1, source_target_pairs={{0,4},{1,5},{8,12},{9,13},{2,6},{3,7},{10,14},{11,15},{4,0},{5,1},... | collective-permute-start | bytes 393224 | tf_op jit(solution)/shard_map/ppermute | solution.py:313
  78.4 4.0 %collective-permute-start.31 = (bf16[2,2,8,16,128]{4,3,2,1,0:T(8,128)(2,1)S(1)}, bf16[2,2,8,16,128]{4,3,2,1,0:T(8,128)(2,1)S(1)}, u32[]{:S(2)}, u32[]{:S(2)}) collective-permute-start(bf16[2,2,8,16,128]{4,3,2,1,0:T(8,128)(2,1)S(1)} %get-tuple-element.76), channel_id=1, source_target_pairs={{0,12},{1,13},{8,6},{9,7},{2,14},{3,15},{10,0},{11,1},{4,8},{5,9},... | collective-permute-start | bytes 393224 | tf_op jit(solution)/shard_map/ppermute | solution.py:313
  82.5 3.6 %collective-permute-start.33 = (bf16[2,2,8,16,128]{4,3,2,1,0:T(8,128)(2,1)S(1)}, bf16[2,2,8,16,128]{4,3,2,1,0:T(8,128)(2,1)S(1)}, u32[]{:S(2)}, u32[]{:S(2)}) collective-permute-start(bf16[2,2,8,16,128]{4,3,2,1,0:T(8,128)(2,1)S(1)} %get-tuple-element.78), channel_id=1, source_target_pairs={{0,6},{1,7},{8,14},{9,15},{2,0},{3,1},{10,8},{11,9},{4,2},{5,3},{1... | collective-permute-start | bytes 393224 | tf_op jit(solution)/shard_map/ppermute | solution.py:313
  88.2 8.7 %collective-permute-start.16 = (bf16[2,4,14,16,128]{4,3,2,1,0:T(8,128)(2,1)S(1)}, bf16[2,4,14,16,128]{4,3,2,1,0:T(8,128)(2,1)S(1)}, u32[]{:S(2)}, u32[]{:S(2)}) collective-permute-start(bf16[2,4,14,16,128]{4,3,2,1,0:T(8,128)(2,1)S(1)} %get-tuple-element.61), channel_id=1, source_target_pairs={{0,17},{1,16},{8,25},{9,24},{2,19},{3,18},{10,27},{11,26},{4,21},{... | collective-permute-start | bytes 1376264 | tf_op jit(solution)/shard_map/ppermute | solution.py:313
  100.5 15.6 %collective-permute-done.16.prev1 = bf16[2,4,14,16,128]{4,3,2,1,0:T(8,128)(2,1)S(1)} collective-permute-done((bf16[2,4,14,16,128]{4,3,2,1,0:T(8,128)(2,1)S(1)}, bf16[2,4,14,16,128]{4,3,2,1,0:T(8,128)(2,1)S(1)}, u32[]{:S(2)}, u32[]{:S(2)}) %collective-permute-start.16) | collective-permute-done | bytes 458784 | tf_op jit(solution)/shard_map/ppermute | solution.py:313
  116.2 5.4 %cross.3 = (bf16[2,2,8,16,128]{4,3,2,1,0:T(8,128)(2,1)S(1)}, bf16[2,2,8,16,128]{4,3,2,1,0:T(8,128)(2,1)S(1)}, bf16[2,2,8,16,128]{4,3,2,1,0:T(8,128)(2,1)S(1)}, b...) custom-call(s32[2]{0:T(128)S(1)} %pad_add_fusion.1.pos_ref, ...), custom_call_target="tpu_custom_call" | custom-call | flops 536870912 | bytes 3145728 | tf_op jit(solution)/shard_map/cross/pallas_call | solution.py:176
  127.3 9.3 %collective-permute-done.20.refs_1_ = bf16[2,2,8,16,128]{4,3,2,1,0:T(8,128)(2,1)S(1)} collective-permute-done((bf16[2,2,8,16,128]{4,3,2,1,0:T(8,128)(2,1)S(1)}, bf16[2,2,8,16,128]{4,3,2,1,0:T(8,128)(2,1)S(1)}, u32[]{:S(2)}, u32[]{:S(2)}) %collective-permute-start.20) | collective-permute-done | bytes 131104 | tf_op jit(solution)/shard_map/ppermute | solution.py:313
  137.9 2.8 %collective-permute-start.26 = (bf16[2,2,8,16,128]{4,3,2,1,0:T(8,128)(2,1)S(1)}, bf16[2,2,8,16,128]{4,3,2,1,0:T(8,128)(2,1)S(1)}, u32[]{:S(2)}, u32[]{:S(2)}) collective-permute-start(bf16[2,2,8,16,128]{4,3,2,1,0:T(8,128)(2,1)S(1)} %get-tuple-element.71), channel_id=1, source_target_pairs={{0,6},{1,7},{8,14},{9,15},{2,0},{3,1},{10,8},{11,9},{4,2},{5,3},{1... | collective-permute-start | bytes 393224 | tf_op jit(solution)/shard_map/ppermute | solution.py:313
  143.5 2.9 %collective-permute-done.24.refs_5_ = bf16[2,2,8,16,128]{4,3,2,1,0:T(8,128)(2,1)S(1)} collective-permute-done((bf16[2,2,8,16,128]{4,3,2,1,0:T(8,128)(2,1)S(1)}, bf16[2,2,8,16,128]{4,3,2,1,0:T(8,128)(2,1)S(1)}, u32[]{:S(2)}, u32[]{:S(2)}) %collective-permute-start.24) | collective-permute-done | bytes 131104 | tf_op jit(solution)/shard_map/ppermute | solution.py:313
  146.4 4.3 %collective-permute-done.26.refs_7_ = bf16[2,2,8,16,128]{4,3,2,1,0:T(8,128)(2,1)S(1)} collective-permute-done((bf16[2,2,8,16,128]{4,3,2,1,0:T(8,128)(2,1)S(1)}, bf16[2,2,8,16,128]{4,3,2,1,0:T(8,128)(2,1)S(1)}, u32[]{:S(2)}, u32[]{:S(2)}) %collective-permute-start.26) | collective-permute-done | bytes 131104 | tf_op jit(solution)/shard_map/ppermute | solution.py:313
  153.8 2.9 %invert.3 = bf16[2,8,64,1024]{3,2,1,0:T(8,128)(2,1)} custom-call(bf16[2,8,128,128]{3,2,1,0:T(8,128)(2,1)S(1)} %turn.7.refs_0_, bf16[2,8,128,128]{3,2,1,0:T(8,128)(2,1)S(1)} %collective-permute-done.35.refs_1_, bf16[1024,1024]{1,0:T(8,128)(2,1)S(1)} %table.1.refs_8_.refs_2_, f32[2,8,64,1024]{3,2,1,0:T(8,128)S(1)} %invert.2.refs_8_.refs_3_), custom_call_target="tpu_custom_call" | custom-call | flops 1073741824 | bytes 6291456 | tf_op jit(solution)/shard_map/invert/pallas_call | solution.py:247
  (68 shorter events, 42.2 us)
Async XLA Ops:
  8.6 15.6 %collective-permute-start.7 = (bf16[2,14,16,128]{3,2,1,0:T(8,128)(2,1)S(1)}, bf16[2,14,16,128]{3,2,1,0:T(8,128)(2,1)S(1)}, u32[]{:S(2)}, u32[]{:S(2)}) collective-permute-start(bf16[2,14,16,128]{3,2,1,0:T(8,128)(2,1)S(1)} %get-tuple-element.51), channel_id=1, source_target_pairs={{0,8},{1,9},{8,2},{9,3},{2,10},{3,11},{10,4},{11,5},{4,12},{5,13},... | collective-permute-start | bytes 344072 | tf_op jit(solution)/shard_map/ppermute | solution.py:313
  11.2 13.2 %collective-permute-start.8 = (bf16[2,14,16,128]{3,2,1,0:T(8,128)(2,1)S(1)}, bf16[2,14,16,128]{3,2,1,0:T(8,128)(2,1)S(1)}, u32[]{:S(2)}, u32[]{:S(2)}) collective-permute-start(bf16[2,14,16,128]{3,2,1,0:T(8,128)(2,1)S(1)} %get-tuple-element.52), channel_id=1, source_target_pairs={{0,14},{1,15},{8,0},{9,1},{2,8},{3,9},{10,2},{11,3},{4,10},{5,11},... | collective-permute-start | bytes 344072 | tf_op jit(solution)/shard_map/ppermute | solution.py:313
  15.2 16.3 %collective-permute-start.9 = (bf16[2,14,16,128]{3,2,1,0:T(8,128)(2,1)S(1)}, bf16[2,14,16,128]{3,2,1,0:T(8,128)(2,1)S(1)}, u32[]{:S(2)}, u32[]{:S(2)}) collective-permute-start(bf16[2,14,16,128]{3,2,1,0:T(8,128)(2,1)S(1)} %get-tuple-element.53), channel_id=1, source_target_pairs={{0,4},{1,5},{8,12},{9,13},{2,6},{3,7},{10,14},{11,15},{4,0},{5,1},... | collective-permute-start | bytes 344072 | tf_op jit(solution)/shard_map/ppermute | solution.py:313
  19.1 13.4 %collective-permute-start.10 = (bf16[2,14,16,128]{3,2,1,0:T(8,128)(2,1)S(1)}, bf16[2,14,16,128]{3,2,1,0:T(8,128)(2,1)S(1)}, u32[]{:S(2)}, u32[]{:S(2)}) collective-permute-start(bf16[2,14,16,128]{3,2,1,0:T(8,128)(2,1)S(1)} %get-tuple-element.54), channel_id=1, source_target_pairs={{0,10},{1,11},{8,4},{9,5},{2,12},{3,13},{10,6},{11,7},{4,14},{5,15... | collective-permute-start | bytes 344072 | tf_op jit(solution)/shard_map/ppermute | solution.py:313
  19.6 13.0 %collective-permute-start.11 = (bf16[2,14,16,128]{3,2,1,0:T(8,128)(2,1)S(1)}, bf16[2,14,16,128]{3,2,1,0:T(8,128)(2,1)S(1)}, u32[]{:S(2)}, u32[]{:S(2)}) collective-permute-start(bf16[2,14,16,128]{3,2,1,0:T(8,128)(2,1)S(1)} %get-tuple-element.55), channel_id=1, source_target_pairs={{0,12},{1,13},{8,6},{9,7},{2,14},{3,15},{10,0},{11,1},{4,8},{5,9},... | collective-permute-start | bytes 344072 | tf_op jit(solution)/shard_map/ppermute | solution.py:313
  37.7 17.0 %collective-permute-start.19 = (bf16[2,4,14,16,128]{4,3,2,1,0:T(8,128)(2,1)S(1)}, bf16[2,4,14,16,128]{4,3,2,1,0:T(8,128)(2,1)S(1)}, u32[]{:S(2)}, u32[]{:S(2)}) collective-permute-start(bf16[2,4,14,16,128]{4,3,2,1,0:T(8,128)(2,1)S(1)} %get-tuple-element.62), channel_id=1, source_target_pairs={{0,17},{1,16},{8,25},{9,24},{2,19},{3,18},{10,27},{11,26},{4,21},{... | collective-permute-start | bytes 1376264 | tf_op jit(solution)/shard_map/ppermute | solution.py:313
  39.9 17.7 %collective-permute-start.17 = (bf16[2,4,14,16,128]{4,3,2,1,0:T(8,128)(2,1)S(1)}, bf16[2,4,14,16,128]{4,3,2,1,0:T(8,128)(2,1)S(1)}, u32[]{:S(2)}, u32[]{:S(2)}) collective-permute-start(bf16[2,4,14,16,128]{4,3,2,1,0:T(8,128)(2,1)S(1)} %get-tuple-element.62), channel_id=1, source_target_pairs={{0,1},{1,0},{8,9},{9,8},{2,3},{3,2},{10,11},{11,10},{4,5},{5,4},{1... | collective-permute-start | bytes 1376264 | tf_op jit(solution)/shard_map/ppermute | solution.py:313
  39.9 24.0 %collective-permute-start.18 = (bf16[2,4,14,16,128]{4,3,2,1,0:T(8,128)(2,1)S(1)}, bf16[2,4,14,16,128]{4,3,2,1,0:T(8,128)(2,1)S(1)}, u32[]{:S(2)}, u32[]{:S(2)}) collective-permute-start(bf16[2,4,14,16,128]{4,3,2,1,0:T(8,128)(2,1)S(1)} %get-tuple-element.59.refs_8_.own0), channel_id=1, source_target_pairs={{0,16},{1,17},{8,24},{9,25},{2,18},{3,19},{10,26},{11,27},{4,20},{... | collective-permute-start | bytes 1376264 | tf_op jit(solution)/shard_map/ppermute | solution.py:313
  46.4 26.2 %collective-permute-start.2 = (bf16[2,14,16,128]{3,2,1,0:T(8,128)(2,1)S(1)}, bf16[2,14,16,128]{3,2,1,0:T(8,128)(2,1)S(1)}, u32[]{:S(2)}, u32[]{:S(2)}) collective-permute-start(bf16[2,14,16,128]{3,2,1,0:T(8,128)(2,1)S(1)} %get-tuple-element.45), channel_id=1, source_target_pairs={{0,4},{1,5},{8,12},{9,13},{2,6},{3,7},{10,14},{11,15},{4,0},{5,1},... | collective-permute-start | bytes 344072 | tf_op jit(solution)/shard_map/ppermute | solution.py:313
  49.2 23.5 %collective-permute-start.3 = (bf16[2,14,16,128]{3,2,1,0:T(8,128)(2,1)S(1)}, bf16[2,14,16,128]{3,2,1,0:T(8,128)(2,1)S(1)}, u32[]{:S(2)}, u32[]{:S(2)}) collective-permute-start(bf16[2,14,16,128]{3,2,1,0:T(8,128)(2,1)S(1)} %get-tuple-element.46), channel_id=1, source_target_pairs={{0,10},{1,11},{8,4},{9,5},{2,12},{3,13},{10,6},{11,7},{4,14},{5,15... | collective-permute-start | bytes 344072 | tf_op jit(solution)/shard_map/ppermute | solution.py:313
  54.7 20.7 %collective-permute-start.4 = (bf16[2,14,16,128]{3,2,1,0:T(8,128)(2,1)S(1)}, bf16[2,14,16,128]{3,2,1,0:T(8,128)(2,1)S(1)}, u32[]{:S(2)}, u32[]{:S(2)}) collective-permute-start(bf16[2,14,16,128]{3,2,1,0:T(8,128)(2,1)S(1)} %get-tuple-element.47), channel_id=1, source_target_pairs={{0,12},{1,13},{8,6},{9,7},{2,14},{3,15},{10,0},{11,1},{4,8},{5,9},... | collective-permute-start | bytes 344072 | tf_op jit(solution)/shard_map/ppermute | solution.py:313
  57.7 20.3 %collective-permute-start.5 = (bf16[2,14,16,128]{3,2,1,0:T(8,128)(2,1)S(1)}, bf16[2,14,16,128]{3,2,1,0:T(8,128)(2,1)S(1)}, u32[]{:S(2)}, u32[]{:S(2)}) collective-permute-start(bf16[2,14,16,128]{3,2,1,0:T(8,128)(2,1)S(1)} %get-tuple-element.48), channel_id=1, source_target_pairs={{0,2},{1,3},{8,10},{9,11},{2,4},{3,5},{10,12},{11,13},{4,6},{5,7},... | collective-permute-start | bytes 344072 | tf_op jit(solution)/shard_map/ppermute | solution.py:313
  63.9 14.5 %collective-permute-start.6 = (bf16[2,14,16,128]{3,2,1,0:T(8,128)(2,1)S(1)}, bf16[2,14,16,128]{3,2,1,0:T(8,128)(2,1)S(1)}, u32[]{:S(2)}, u32[]{:S(2)}) collective-permute-start(bf16[2,14,16,128]{3,2,1,0:T(8,128)(2,1)S(1)} %get-tuple-element.49), channel_id=1, source_target_pairs={{0,6},{1,7},{8,14},{9,15},{2,0},{3,1},{10,8},{11,9},{4,2},{5,3},{1... | collective-permute-start | bytes 344072 | tf_op jit(solution)/shard_map/ppermute | solution.py:313
  78.4 18.4 %collective-permute-start.31 = (bf16[2,2,8,16,128]{4,3,2,1,0:T(8,128)(2,1)S(1)}, bf16[2,2,8,16,128]{4,3,2,1,0:T(8,128)(2,1)S(1)}, u32[]{:S(2)}, u32[]{:S(2)}) collective-permute-start(bf16[2,2,8,16,128]{4,3,2,1,0:T(8,128)(2,1)S(1)} %get-tuple-element.76), channel_id=1, source_target_pairs={{0,12},{1,13},{8,6},{9,7},{2,14},{3,15},{10,0},{11,1},{4,8},{5,9},... | collective-permute-start | bytes 393224 | tf_op jit(solution)/shard_map/ppermute | solution.py:313
  82.5 17.0 %collective-permute-start.32 = (bf16[2,2,8,16,128]{4,3,2,1,0:T(8,128)(2,1)S(1)}, bf16[2,2,8,16,128]{4,3,2,1,0:T(8,128)(2,1)S(1)}, u32[]{:S(2)}, u32[]{:S(2)}) collective-permute-start(bf16[2,2,8,16,128]{4,3,2,1,0:T(8,128)(2,1)S(1)} %get-tuple-element.77), channel_id=1, source_target_pairs={{0,2},{1,3},{8,10},{9,11},{2,4},{3,5},{10,12},{11,13},{4,6},{5,7},... | collective-permute-start | bytes 393224 | tf_op jit(solution)/shard_map/ppermute | solution.py:313
  82.5 17.0 %collective-permute-start.33 = (bf16[2,2,8,16,128]{4,3,2,1,0:T(8,128)(2,1)S(1)}, bf16[2,2,8,16,128]{4,3,2,1,0:T(8,128)(2,1)S(1)}, u32[]{:S(2)}, u32[]{:S(2)}) collective-permute-start(bf16[2,2,8,16,128]{4,3,2,1,0:T(8,128)(2,1)S(1)} %get-tuple-element.78), channel_id=1, source_target_pairs={{0,6},{1,7},{8,14},{9,15},{2,0},{3,1},{10,8},{11,9},{4,2},{5,3},{1... | collective-permute-start | bytes 393224 | tf_op jit(solution)/shard_map/ppermute | solution.py:313
  88.2 28.0 %collective-permute-start.16 = (bf16[2,4,14,16,128]{4,3,2,1,0:T(8,128)(2,1)S(1)}, bf16[2,4,14,16,128]{4,3,2,1,0:T(8,128)(2,1)S(1)}, u32[]{:S(2)}, u32[]{:S(2)}) collective-permute-start(bf16[2,4,14,16,128]{4,3,2,1,0:T(8,128)(2,1)S(1)} %get-tuple-element.61), channel_id=1, source_target_pairs={{0,17},{1,16},{8,25},{9,24},{2,19},{3,18},{10,27},{11,26},{4,21},{... | collective-permute-start | bytes 1376264 | tf_op jit(solution)/shard_map/ppermute | solution.py:313
  96.9 19.3 %collective-permute-start.14 = (bf16[2,4,14,16,128]{4,3,2,1,0:T(8,128)(2,1)S(1)}, bf16[2,4,14,16,128]{4,3,2,1,0:T(8,128)(2,1)S(1)}, u32[]{:S(2)}, u32[]{:S(2)}) collective-permute-start(bf16[2,4,14,16,128]{4,3,2,1,0:T(8,128)(2,1)S(1)} %get-tuple-element.61), channel_id=1, source_target_pairs={{0,1},{1,0},{8,9},{9,8},{2,3},{3,2},{10,11},{11,10},{4,5},{5,4},{1... | collective-permute-start | bytes 1376264 | tf_op jit(solution)/shard_map/ppermute | solution.py:313
  100.4 37.5 %collective-permute-start.34 = (bf16[2,8,128,128]{3,2,1,0:T(8,128)(2,1)S(1)}, bf16[2,8,128,128]{3,2,1,0:T(8,128)(2,1)S(1)}, u32[]{:S(2)}, u32[]{:S(2)}) collective-permute-start(bf16[2,8,128,128]{3,2,1,0:T(8,128)(2,1)S(1)} %turn.4.refs_8_), channel_id=1, source_target_pairs={{0,1},{1,0},{8,9},{9,8},{2,3},{3,2},{10,11},{11,10},{4,5},{5,4},{1... | collective-permute-start | bytes 1572872 | tf_op jit(solution)/shard_map/ppermute | solution.py:313
  121.6 15.1 %collective-permute-start.20 = (bf16[2,2,8,16,128]{4,3,2,1,0:T(8,128)(2,1)S(1)}, bf16[2,2,8,16,128]{4,3,2,1,0:T(8,128)(2,1)S(1)}, u32[]{:S(2)}, u32[]{:S(2)}) collective-permute-start(bf16[2,2,8,16,128]{4,3,2,1,0:T(8,128)(2,1)S(1)} %get-tuple-element.65), channel_id=1, source_target_pairs={{0,8},{1,9},{8,2},{9,3},{2,10},{3,11},{10,4},{11,5},{4,12},{5,13},... | collective-permute-start | bytes 393224 | tf_op jit(solution)/shard_map/ppermute | solution.py:313
  122.0 15.2 %collective-permute-start.21 = (bf16[2,2,8,16,128]{4,3,2,1,0:T(8,128)(2,1)S(1)}, bf16[2,2,8,16,128]{4,3,2,1,0:T(8,128)(2,1)S(1)}, u32[]{:S(2)}, u32[]{:S(2)}) collective-permute-start(bf16[2,2,8,16,128]{4,3,2,1,0:T(8,128)(2,1)S(1)} %get-tuple-element.66), channel_id=1, source_target_pairs={{0,14},{1,15},{8,0},{9,1},{2,8},{3,9},{10,2},{11,3},{4,10},{5,11},... | collective-permute-start | bytes 393224 | tf_op jit(solution)/shard_map/ppermute | solution.py:313
  124.3 19.2 %collective-permute-start.22 = (bf16[2,2,8,16,128]{4,3,2,1,0:T(8,128)(2,1)S(1)}, bf16[2,2,8,16,128]{4,3,2,1,0:T(8,128)(2,1)S(1)}, u32[]{:S(2)}, u32[]{:S(2)}) collective-permute-start(bf16[2,2,8,16,128]{4,3,2,1,0:T(8,128)(2,1)S(1)} %get-tuple-element.67), channel_id=1, source_target_pairs={{0,4},{1,5},{8,12},{9,13},{2,6},{3,7},{10,14},{11,15},{4,0},{5,1},... | collective-permute-start | bytes 393224 | tf_op jit(solution)/shard_map/ppermute | solution.py:313
  126.9 16.5 %collective-permute-start.23 = (bf16[2,2,8,16,128]{4,3,2,1,0:T(8,128)(2,1)S(1)}, bf16[2,2,8,16,128]{4,3,2,1,0:T(8,128)(2,1)S(1)}, u32[]{:S(2)}, u32[]{:S(2)}) collective-permute-start(bf16[2,2,8,16,128]{4,3,2,1,0:T(8,128)(2,1)S(1)} %get-tuple-element.68), channel_id=1, source_target_pairs={{0,10},{1,11},{8,4},{9,5},{2,12},{3,13},{10,6},{11,7},{4,14},{5,15... | collective-permute-start | bytes 393224 | tf_op jit(solution)/shard_map/ppermute | solution.py:313
  137.9 12.8 %collective-permute-start.26 = (bf16[2,2,8,16,128]{4,3,2,1,0:T(8,128)(2,1)S(1)}, bf16[2,2,8,16,128]{4,3,2,1,0:T(8,128)(2,1)S(1)}, u32[]{:S(2)}, u32[]{:S(2)}) collective-permute-start(bf16[2,2,8,16,128]{4,3,2,1,0:T(8,128)(2,1)S(1)} %get-tuple-element.71), channel_id=1, source_target_pairs={{0,6},{1,7},{8,14},{9,15},{2,0},{3,1},{10,8},{11,9},{4,2},{5,3},{1... | collective-permute-start | bytes 393224 | tf_op jit(solution)/shard_map/ppermute | solution.py:313
  (12 other events, 109.5 us)

commit v9 on v8

--- a/solution.py
+++ b/solution.py
@@ -60,7 +60,9 @@
         amp2 = jnp.concatenate([amp, amp], axis=0)
         both = jnp.concatenate([re16, im16], axis=0)
         summed = lax.dot_general(band[...], amp2, nt, preferred_element_type=F32)
-        scale = flags_ref[v].astype(F32) / (summed * invc[...] + 1e-05)
+        flags = flags_ref[pl.ds(w * STEP + v, 1), :].astype(F32)
+        flags = jnp.concatenate([flags, flags], axis=1)
+        scale = flags / (summed * invc[...] + 1e-05)
         for h in range(2):
             half = lax.dot_general(
                 eye[...], both[:, h * 256 : (h + 1) * 256], nt, preferred_element_type=F32
@@ -77,7 +79,7 @@
     core[0] = c
 
 
-def whiten(spec, flags2, pos):
+def whiten(spec, valid_flags, pos):
     shape = jax.ShapeDtypeStruct((2, WIN, FC, 128), BF16)
     full = pl.BlockSpec((2, WIN, FC, 128), lambda w, *_: (0, 0, 0, 0))
     return pl.pallas_call(
@@ -88,7 +90,7 @@
             grid=(WIN // STEP,),
             in_specs=[
                 pl.BlockSpec((2, STEP, CH, BINS), lambda w, *_: (0, w, 0, 0)),
-                pl.BlockSpec((STEP, 1, 128), lambda w, *_: (w, 0, 0)),
+                pl.BlockSpec((WIN, CH), lambda w, *_: (0, 0)),
             ],
             out_specs=[full] * (8 * CHUNKS) + [SM],
             scratch_shapes=[
@@ -103,7 +105,7 @@
             flops=3 * 512 * 512 * 128 * WIN, bytes_accessed=4 << 20, transcendentals=0
         ),
         name="whiten",
-    )(pos, spec, flags2)
+    )(pos, spec, valid_flags)
 
 
 def merge_kernel(pos_ref, *refs):
@@ -329,15 +331,14 @@
     pos = jnp.stack([z, lax.axis_index("c")]).astype(jnp.int32)
     windows = spectra.shape[0] * lax.axis_size(("zh", "c"))
     scaling = 1.0 / math.sqrt(windows * BINS)
-    flags2 = jnp.concatenate([valid_flags, valid_flags], axis=1)[:, None, :]
-    *white, core = whiten(jnp.transpose(spectra, (2, 0, 1, 3)), flags2, pos)
+    *white, core = whiten(jnp.transpose(spectra, (2, 0, 1, 3)), valid_flags, pos)
     table = join_table(lag_table(core[0]))
     sums = ()
-    merged, crossed = (table,), ()
+    merged, crossed = (), ()
     for k in range(CHUNKS):
         got = round_ring(white[k * 8 : k * 8 + 8])
         same, other = merge(got, pos, *merged)
-        merged = (same,)
+        merged = (same, table)
         prev0 = send(same, lambda m, z, c: (m + 1, z, c))
         prev1 = send(other, lambda m, z, c: (m + 1, z, 1 - c))
         own1 = other_core(other)

time: 157 us -> 167 us (1.064)
  the two profiles are of different devices: /device:TPU:1 before, /device:TPU:5 now
where the time goes in v9:
time: 167 us; the launch traced here: 166 us
  waiting for transfers between devices  73.7 us (44%)
  starting transfers between devices  60.1 us (36%)
  Pallas kernels  27.6 us (17%)
  other arithmetic  2.92 us (2%)
  local copies, waits for them, and re-layouts  1.9 us (1%)
    ppermute x36, waiting for transfers between devices, send(): lax.ppermute(value, ALL, [(device(*d), device(*target(*d))) for d in EVERY])  73.7 us
    ppermute x36, starting transfers between devices, send(): lax.ppermute(value, ALL, [(device(*d), device(*target(*d))) for d in EVERY])  60.1 us
    pallas_call x2, Pallas kernels, cross(): pl.pallas_call(cross_kernel, out_shape=[shape] * 8, in_specs=[SM] + [VM]...  10.8 us
    pallas_call x1, Pallas kernels, whiten(): pl.pallas_call(whiten_kernel, out_shape=[shape] * (8 * CHUNKS) + [jax.Sha...  5.71 us
    pallas_call x2, Pallas kernels, invert(): pl.pallas_call(functools.partial(invert_kernel, scaling, chunk), out_shap...  4.71 us
    pallas_call x4, Pallas kernels, turn(): pl.pallas_call(turn_kernel, out_shape=jax.ShapeDtypeStruct((2, 8, 128, 8...  3.75 us
  transfers between devices with their start and end apart: 36, of which 13 were waited for; matrix products, arithmetic and copies ran while one was open for 2% of the time, Pallas kernels for 10%

profile of v9, /device:TPU:5, one launch (start us, length us, event | category | flops | bytes accessed | tf_op | source)
XLA Modules:
  0.0 166.5 jit_solution(16167118162174841561)
XLA Ops:
  2.0 5.7 %whiten.1 = (bf16[2,14,16,128]{3,2,1,0:T(8,128)(2,1)S(1)}, bf16[2,14,16,128]{3,2,1,0:T(8,128)(2,1)S(1)}, bf16[2,14,16,128]{3,2,1,0:T(8,128)(2,1)S(1)}, bf16[2,14...) custom-call(s32[2]{0:T(128)S(1)} %pad_add_fusion.pos_ref, ...), custom_call_target="tpu_custom_call" | custom-call | flops 1409286144 | bytes 4194304 | tf_op jit(solution)/shard_map/whiten/pallas_call | solution.py:85
  9.4 4.0 %collective-permute-start.8 = (bf16[2,14,16,128]{3,2,1,0:T(8,128)(2,1)S(1)}, bf16[2,14,16,128]{3,2,1,0:T(8,128)(2,1)S(1)}, u32[]{:S(2)}, u32[]{:S(2)}) collective-permute-start(bf16[2,14,16,128]{3,2,1,0:T(8,128)(2,1)S(1)} %get-tuple-element.52), channel_id=1, source_target_pairs={{0,14},{1,15},{8,0},{9,1},{2,8},{3,9},{10,2},{11,3},{4,10},{5,11},... | collective-permute-start | bytes 344072 | tf_op jit(solution)/shard_map/ppermute | solution.py:315
  13.5 3.9 %collective-permute-start.9 = (bf16[2,14,16,128]{3,2,1,0:T(8,128)(2,1)S(1)}, bf16[2,14,16,128]{3,2,1,0:T(8,128)(2,1)S(1)}, u32[]{:S(2)}, u32[]{:S(2)}) collective-permute-start(bf16[2,14,16,128]{3,2,1,0:T(8,128)(2,1)S(1)} %get-tuple-element.53), channel_id=1, source_target_pairs={{0,4},{1,5},{8,12},{9,13},{2,6},{3,7},{10,14},{11,15},{4,0},{5,1},... | collective-permute-start | bytes 344072 | tf_op jit(solution)/shard_map/ppermute | solution.py:315
  17.8 4.0 %collective-permute-start.11 = (bf16[2,14,16,128]{3,2,1,0:T(8,128)(2,1)S(1)}, bf16[2,14,16,128]{3,2,1,0:T(8,128)(2,1)S(1)}, u32[]{:S(2)}, u32[]{:S(2)}) collective-permute-start(bf16[2,14,16,128]{3,2,1,0:T(8,128)(2,1)S(1)} %get-tuple-element.55), channel_id=1, source_target_pairs={{0,12},{1,13},{8,6},{9,7},{2,14},{3,15},{10,0},{11,1},{4,8},{5,9},... | collective-permute-start | bytes 344072 | tf_op jit(solution)/shard_map/ppermute | solution.py:315
  21.9 3.6 %collective-permute-start.13 = (bf16[2,14,16,128]{3,2,1,0:T(8,128)(2,1)S(1)}, bf16[2,14,16,128]{3,2,1,0:T(8,128)(2,1)S(1)}, u32[]{:S(2)}, u32[]{:S(2)}) collective-permute-start(bf16[2,14,16,128]{3,2,1,0:T(8,128)(2,1)S(1)} %get-tuple-element.57), channel_id=1, source_target_pairs={{0,6},{1,7},{8,14},{9,15},{2,0},{3,1},{10,8},{11,9},{4,2},{5,3},{1... | collective-permute-start | bytes 344072 | tf_op jit(solution)/shard_map/ppermute | solution.py:315
  25.4 5.4 %collective-permute-done.10.refs_4_ = bf16[2,14,16,128]{3,2,1,0:T(8,128)(2,1)S(1)} collective-permute-done((bf16[2,14,16,128]{3,2,1,0:T(8,128)(2,1)S(1)}, bf16[2,14,16,128]{3,2,1,0:T(8,128)(2,1)S(1)}, u32[]{:S(2)}, u32[]{:S(2)}) %collective-permute-start.10) | collective-permute-done | bytes 114720 | tf_op jit(solution)/shard_map/ppermute | solution.py:315
  31.4 3.9 %collective-permute-done.13.refs_7_ = bf16[2,14,16,128]{3,2,1,0:T(8,128)(2,1)S(1)} collective-permute-done((bf16[2,14,16,128]{3,2,1,0:T(8,128)(2,1)S(1)}, bf16[2,14,16,128]{3,2,1,0:T(8,128)(2,1)S(1)}, u32[]{:S(2)}, u32[]{:S(2)}) %collective-permute-start.13) | collective-permute-done | bytes 114720 | tf_op jit(solution)/shard_map/ppermute | solution.py:315
  42.2 8.7 %collective-permute-done.19.prev1 = bf16[2,4,14,16,128]{4,3,2,1,0:T(8,128)(2,1)S(1)} collective-permute-done((bf16[2,4,14,16,128]{4,3,2,1,0:T(8,128)(2,1)S(1)}, bf16[2,4,14,16,128]{4,3,2,1,0:T(8,128)(2,1)S(1)}, u32[]{:S(2)}, u32[]{:S(2)}) %collective-permute-start.19) | collective-permute-done | bytes 458784 | tf_op jit(solution)/shard_map/ppermute | solution.py:315
  50.9 3.4 %collective-permute-start.2 = (bf16[2,14,16,128]{3,2,1,0:T(8,128)(2,1)S(1)}, bf16[2,14,16,128]{3,2,1,0:T(8,128)(2,1)S(1)}, u32[]{:S(2)}, u32[]{:S(2)}) collective-permute-start(bf16[2,14,16,128]{3,2,1,0:T(8,128)(2,1)S(1)} %get-tuple-element.45), channel_id=1, source_target_pairs={{0,4},{1,5},{8,12},{9,13},{2,6},{3,7},{10,14},{11,15},{4,0},{5,1},... | collective-permute-start | bytes 344072 | tf_op jit(solution)/shard_map/ppermute | solution.py:315
  55.1 5.7 %collective-permute-done.18.prev0 = bf16[2,4,14,16,128]{4,3,2,1,0:T(8,128)(2,1)S(1)} collective-permute-done((bf16[2,4,14,16,128]{4,3,2,1,0:T(8,128)(2,1)S(1)}, bf16[2,4,14,16,128]{4,3,2,1,0:T(8,128)(2,1)S(1)}, u32[]{:S(2)}, u32[]{:S(2)}) %collective-permute-start.18) | collective-permute-done | bytes 458784 | tf_op jit(solution)/shard_map/ppermute | solution.py:315
  60.8 3.1 %collective-permute-start.4 = (bf16[2,14,16,128]{3,2,1,0:T(8,128)(2,1)S(1)}, bf16[2,14,16,128]{3,2,1,0:T(8,128)(2,1)S(1)}, u32[]{:S(2)}, u32[]{:S(2)}) collective-permute-start(bf16[2,14,16,128]{3,2,1,0:T(8,128)(2,1)S(1)} %get-tuple-element.47), channel_id=1, source_target_pairs={{0,12},{1,13},{8,6},{9,7},{2,14},{3,15},{10,0},{11,1},{4,8},{5,9},... | collective-permute-start | bytes 344072 | tf_op jit(solution)/shard_map/ppermute | solution.py:315
  63.9 5.4 %cross.2 = (bf16[2,2,8,16,128]{4,3,2,1,0:T(8,128)(2,1)S(1)}, bf16[2,2,8,16,128]{4,3,2,1,0:T(8,128)(2,1)S(1)}, bf16[2,2,8,16,128]{4,3,2,1,0:T(8,128)(2,1)S(1)}, b...) custom-call(s32[2]{0:T(128)S(1)} %pad_add_fusion.pos_ref, ...), custom_call_target="tpu_custom_call" | custom-call | flops 536870912 | bytes 3145728 | tf_op jit(solution)/shard_map/cross/pallas_call | solution.py:178
  70.1 2.9 %collective-permute-start.6 = (bf16[2,14,16,128]{3,2,1,0:T(8,128)(2,1)S(1)}, bf16[2,14,16,128]{3,2,1,0:T(8,128)(2,1)S(1)}, u32[]{:S(2)}, u32[]{:S(2)}) collective-permute-start(bf16[2,14,16,128]{3,2,1,0:T(8,128)(2,1)S(1)} %get-tuple-element.49), channel_id=1, source_target_pairs={{0,6},{1,7},{8,14},{9,15},{2,0},{3,1},{10,8},{11,9},{4,2},{5,3},{1... | collective-permute-start | bytes 344072 | tf_op jit(solution)/shard_map/ppermute | solution.py:315
  79.4 3.8 %collective-permute-start.31 = (bf16[2,2,8,16,128]{4,3,2,1,0:T(8,128)(2,1)S(1)}, bf16[2,2,8,16,128]{4,3,2,1,0:T(8,128)(2,1)S(1)}, u32[]{:S(2)}, u32[]{:S(2)}) collective-permute-start(bf16[2,2,8,16,128]{4,3,2,1,0:T(8,128)(2,1)S(1)} %get-tuple-element.76), channel_id=1, source_target_pairs={{0,12},{1,13},{8,6},{9,7},{2,14},{3,15},{10,0},{11,1},{4,8},{5,9},... | collective-permute-start | bytes 393224 | tf_op jit(solution)/shard_map/ppermute | solution.py:315
  83.2 8.3 %collective-permute-done.27.refs_1_ = bf16[2,2,8,16,128]{4,3,2,1,0:T(8,128)(2,1)S(1)} collective-permute-done((bf16[2,2,8,16,128]{4,3,2,1,0:T(8,128)(2,1)S(1)}, bf16[2,2,8,16,128]{4,3,2,1,0:T(8,128)(2,1)S(1)}, u32[]{:S(2)}, u32[]{:S(2)}) %collective-permute-start.27) | collective-permute-done | bytes 131104 | tf_op jit(solution)/shard_map/ppermute | solution.py:315
  91.4 3.6 %collective-permute-start.33 = (bf16[2,2,8,16,128]{4,3,2,1,0:T(8,128)(2,1)S(1)}, bf16[2,2,8,16,128]{4,3,2,1,0:T(8,128)(2,1)S(1)}, u32[]{:S(2)}, u32[]{:S(2)}) collective-permute-start(bf16[2,2,8,16,128]{4,3,2,1,0:T(8,128)(2,1)S(1)} %get-tuple-element.78), channel_id=1, source_target_pairs={{0,6},{1,7},{8,14},{9,15},{2,0},{3,1},{10,8},{11,9},{4,2},{5,3},{1... | collective-permute-start | bytes 393224 | tf_op jit(solution)/shard_map/ppermute | solution.py:315
  103.9 8.6 %collective-permute-done.15.prev0 = bf16[2,4,14,16,128]{4,3,2,1,0:T(8,128)(2,1)S(1)} collective-permute-done((bf16[2,4,14,16,128]{4,3,2,1,0:T(8,128)(2,1)S(1)}, bf16[2,4,14,16,128]{4,3,2,1,0:T(8,128)(2,1)S(1)}, u32[]{:S(2)}, u32[]{:S(2)}) %collective-permute-start.15) | collective-permute-done | bytes 458784 | tf_op jit(solution)/shard_map/ppermute | solution.py:315
  112.5 11.3 %collective-permute-done.16.prev1 = bf16[2,4,14,16,128]{4,3,2,1,0:T(8,128)(2,1)S(1)} collective-permute-done((bf16[2,4,14,16,128]{4,3,2,1,0:T(8,128)(2,1)S(1)}, bf16[2,4,14,16,128]{4,3,2,1,0:T(8,128)(2,1)S(1)}, u32[]{:S(2)}, u32[]{:S(2)}) %collective-permute-start.16) | collective-permute-done | bytes 458784 | tf_op jit(solution)/shard_map/ppermute | solution.py:315
  123.7 5.4 %cross.3 = (bf16[2,2,8,16,128]{4,3,2,1,0:T(8,128)(2,1)S(1)}, bf16[2,2,8,16,128]{4,3,2,1,0:T(8,128)(2,1)S(1)}, bf16[2,2,8,16,128]{4,3,2,1,0:T(8,128)(2,1)S(1)}, b...) custom-call(s32[2]{0:T(128)S(1)} %pad_add_fusion.pos_ref, ...), custom_call_target="tpu_custom_call" | custom-call | flops 536870912 | bytes 3145728 | tf_op jit(solution)/shard_map/cross/pallas_call | solution.py:178
  129.2 2.7 %collective-permute-start.21 = (bf16[2,2,8,16,128]{4,3,2,1,0:T(8,128)(2,1)S(1)}, bf16[2,2,8,16,128]{4,3,2,1,0:T(8,128)(2,1)S(1)}, u32[]{:S(2)}, u32[]{:S(2)}) collective-permute-start(bf16[2,2,8,16,128]{4,3,2,1,0:T(8,128)(2,1)S(1)} %get-tuple-element.66), channel_id=1, source_target_pairs={{0,14},{1,15},{8,0},{9,1},{2,8},{3,9},{10,2},{11,3},{4,10},{5,11},... | collective-permute-start | bytes 393224 | tf_op jit(solution)/shard_map/ppermute | solution.py:315
  134.9 11.7 %collective-permute-done.20.refs_1_ = bf16[2,2,8,16,128]{4,3,2,1,0:T(8,128)(2,1)S(1)} collective-permute-done((bf16[2,2,8,16,128]{4,3,2,1,0:T(8,128)(2,1)S(1)}, bf16[2,2,8,16,128]{4,3,2,1,0:T(8,128)(2,1)S(1)}, u32[]{:S(2)}, u32[]{:S(2)}) %collective-permute-start.20) | collective-permute-done | bytes 131104 | tf_op jit(solution)/shard_map/ppermute | solution.py:315
  152.9 4.4 %collective-permute-done.24.refs_5_ = bf16[2,2,8,16,128]{4,3,2,1,0:T(8,128)(2,1)S(1)} collective-permute-done((bf16[2,2,8,16,128]{4,3,2,1,0:T(8,128)(2,1)S(1)}, bf16[2,2,8,16,128]{4,3,2,1,0:T(8,128)(2,1)S(1)}, u32[]{:S(2)}, u32[]{:S(2)}) %collective-permute-start.24) | collective-permute-done | bytes 131104 | tf_op jit(solution)/shard_map/ppermute | solution.py:315
  157.3 3.3 %collective-permute-done.26.refs_7_ = bf16[2,2,8,16,128]{4,3,2,1,0:T(8,128)(2,1)S(1)} collective-permute-done((bf16[2,2,8,16,128]{4,3,2,1,0:T(8,128)(2,1)S(1)}, bf16[2,2,8,16,128]{4,3,2,1,0:T(8,128)(2,1)S(1)}, u32[]{:S(2)}, u32[]{:S(2)}) %collective-permute-start.26) | collective-permute-done | bytes 131104 | tf_op jit(solution)/shard_map/ppermute | solution.py:315
  163.6 2.9 %invert.3 = bf16[2,8,64,1024]{3,2,1,0:T(8,128)(2,1)} custom-call(bf16[2,8,128,128]{3,2,1,0:T(8,128)(2,1)S(1)} %turn.7.refs_0_, bf16[2,8,128,128]{3,2,1,0:T(8,128)(2,1)S(1)} %collective-permute-done.35.refs_1_, bf16[1024,1024]{1,0:T(8,128)(2,1)S(1)} %table.1.refs_9_.refs_2_, f32[2,8,64,1024]{3,2,1,0:T(8,128)S(1)} %invert.2.refs_8_.refs_3_), custom_call_target="tpu_custom_call" | custom-call | flops 1073741824 | bytes 6291456 | tf_op jit(solution)/shard_map/invert/pallas_call | solution.py:249
  (68 shorter events, 40.8 us)
Async XLA Ops:
  7.7 14.1 %collective-permute-start.7 = (bf16[2,14,16,128]{3,2,1,0:T(8,128)(2,1)S(1)}, bf16[2,14,16,128]{3,2,1,0:T(8,128)(2,1)S(1)}, u32[]{:S(2)}, u32[]{:S(2)}) collective-permute-start(bf16[2,14,16,128]{3,2,1,0:T(8,128)(2,1)S(1)} %get-tuple-element.51), channel_id=1, source_target_pairs={{0,8},{1,9},{8,2},{9,3},{2,10},{3,11},{10,4},{11,5},{4,12},{5,13},... | collective-permute-start | bytes 344072 | tf_op jit(solution)/shard_map/ppermute | solution.py:315
  17.4 13.5 %collective-permute-start.10 = (bf16[2,14,16,128]{3,2,1,0:T(8,128)(2,1)S(1)}, bf16[2,14,16,128]{3,2,1,0:T(8,128)(2,1)S(1)}, u32[]{:S(2)}, u32[]{:S(2)}) collective-permute-start(bf16[2,14,16,128]{3,2,1,0:T(8,128)(2,1)S(1)} %get-tuple-element.54), channel_id=1, source_target_pairs={{0,10},{1,11},{8,4},{9,5},{2,12},{3,13},{10,6},{11,7},{4,14},{5,15... | collective-permute-start | bytes 344072 | tf_op jit(solution)/shard_map/ppermute | solution.py:315
  21.9 13.4 %collective-permute-start.13 = (bf16[2,14,16,128]{3,2,1,0:T(8,128)(2,1)S(1)}, bf16[2,14,16,128]{3,2,1,0:T(8,128)(2,1)S(1)}, u32[]{:S(2)}, u32[]{:S(2)}) collective-permute-start(bf16[2,14,16,128]{3,2,1,0:T(8,128)(2,1)S(1)} %get-tuple-element.57), channel_id=1, source_target_pairs={{0,6},{1,7},{8,14},{9,15},{2,0},{3,1},{10,8},{11,9},{4,2},{5,3},{1... | collective-permute-start | bytes 344072 | tf_op jit(solution)/shard_map/ppermute | solution.py:315
  35.9 15.0 %collective-permute-start.19 = (bf16[2,4,14,16,128]{4,3,2,1,0:T(8,128)(2,1)S(1)}, bf16[2,4,14,16,128]{4,3,2,1,0:T(8,128)(2,1)S(1)}, u32[]{:S(2)}, u32[]{:S(2)}) collective-permute-start(bf16[2,4,14,16,128]{4,3,2,1,0:T(8,128)(2,1)S(1)} %get-tuple-element.62), channel_id=1, source_target_pairs={{0,17},{1,16},{8,25},{9,24},{2,19},{3,18},{10,27},{11,26},{4,21},{... | collective-permute-start | bytes 1376264 | tf_op jit(solution)/shard_map/ppermute | solution.py:315
  38.2 16.0 %collective-permute-start.17 = (bf16[2,4,14,16,128]{4,3,2,1,0:T(8,128)(2,1)S(1)}, bf16[2,4,14,16,128]{4,3,2,1,0:T(8,128)(2,1)S(1)}, u32[]{:S(2)}, u32[]{:S(2)}) collective-permute-start(bf16[2,4,14,16,128]{4,3,2,1,0:T(8,128)(2,1)S(1)} %get-tuple-element.62), channel_id=1, source_target_pairs={{0,1},{1,0},{8,9},{9,8},{2,3},{3,2},{10,11},{11,10},{4,5},{5,4},{1... | collective-permute-start | bytes 1376264 | tf_op jit(solution)/shard_map/ppermute | solution.py:315
  38.2 22.5 %collective-permute-start.18 = (bf16[2,4,14,16,128]{4,3,2,1,0:T(8,128)(2,1)S(1)}, bf16[2,4,14,16,128]{4,3,2,1,0:T(8,128)(2,1)S(1)}, u32[]{:S(2)}, u32[]{:S(2)}) collective-permute-start(bf16[2,4,14,16,128]{4,3,2,1,0:T(8,128)(2,1)S(1)} %get-tuple-element.58.refs_8_.own0), channel_id=1, source_target_pairs={{0,16},{1,17},{8,24},{9,25},{2,18},{3,19},{10,26},{11,27},{4,20},{... | collective-permute-start | bytes 1376264 | tf_op jit(solution)/shard_map/ppermute | solution.py:315
  39.5 29.8 %collective-permute-start = (bf16[2,14,16,128]{3,2,1,0:T(8,128)(2,1)S(1)}, bf16[2,14,16,128]{3,2,1,0:T(8,128)(2,1)S(1)}, u32[]{:S(2)}, u32[]{:S(2)}) collective-permute-start(bf16[2,14,16,128]{3,2,1,0:T(8,128)(2,1)S(1)} %get-tuple-element.43), channel_id=1, source_target_pairs={{0,8},{1,9},{8,2},{9,3},{2,10},{3,11},{10,4},{11,5},{4,12},{5,13},... | collective-permute-start | bytes 344072 | tf_op jit(solution)/shard_map/ppermute | solution.py:315
  40.4 29.6 %collective-permute-start.1 = (bf16[2,14,16,128]{3,2,1,0:T(8,128)(2,1)S(1)}, bf16[2,14,16,128]{3,2,1,0:T(8,128)(2,1)S(1)}, u32[]{:S(2)}, u32[]{:S(2)}) collective-permute-start(bf16[2,14,16,128]{3,2,1,0:T(8,128)(2,1)S(1)} %get-tuple-element.44), channel_id=1, source_target_pairs={{0,14},{1,15},{8,0},{9,1},{2,8},{3,9},{10,2},{11,3},{4,10},{5,11},... | collective-permute-start | bytes 344072 | tf_op jit(solution)/shard_map/ppermute | solution.py:315
  50.9 22.1 %collective-permute-start.2 = (bf16[2,14,16,128]{3,2,1,0:T(8,128)(2,1)S(1)}, bf16[2,14,16,128]{3,2,1,0:T(8,128)(2,1)S(1)}, u32[]{:S(2)}, u32[]{:S(2)}) collective-permute-start(bf16[2,14,16,128]{3,2,1,0:T(8,128)(2,1)S(1)} %get-tuple-element.45), channel_id=1, source_target_pairs={{0,4},{1,5},{8,12},{9,13},{2,6},{3,7},{10,14},{11,15},{4,0},{5,1},... | collective-permute-start | bytes 344072 | tf_op jit(solution)/shard_map/ppermute | solution.py:315
  54.3 20.3 %collective-permute-start.3 = (bf16[2,14,16,128]{3,2,1,0:T(8,128)(2,1)S(1)}, bf16[2,14,16,128]{3,2,1,0:T(8,128)(2,1)S(1)}, u32[]{:S(2)}, u32[]{:S(2)}) collective-permute-start(bf16[2,14,16,128]{3,2,1,0:T(8,128)(2,1)S(1)} %get-tuple-element.46), channel_id=1, source_target_pairs={{0,10},{1,11},{8,4},{9,5},{2,12},{3,13},{10,6},{11,7},{4,14},{5,15... | collective-permute-start | bytes 344072 | tf_op jit(solution)/shard_map/ppermute | solution.py:315
  60.8 15.5 %collective-permute-start.4 = (bf16[2,14,16,128]{3,2,1,0:T(8,128)(2,1)S(1)}, bf16[2,14,16,128]{3,2,1,0:T(8,128)(2,1)S(1)}, u32[]{:S(2)}, u32[]{:S(2)}) collective-permute-start(bf16[2,14,16,128]{3,2,1,0:T(8,128)(2,1)S(1)} %get-tuple-element.47), channel_id=1, source_target_pairs={{0,12},{1,13},{8,6},{9,7},{2,14},{3,15},{10,0},{11,1},{4,8},{5,9},... | collective-permute-start | bytes 344072 | tf_op jit(solution)/shard_map/ppermute | solution.py:315
  72.9 18.5 %collective-permute-start.27 = (bf16[2,2,8,16,128]{4,3,2,1,0:T(8,128)(2,1)S(1)}, bf16[2,2,8,16,128]{4,3,2,1,0:T(8,128)(2,1)S(1)}, u32[]{:S(2)}, u32[]{:S(2)}) collective-permute-start(bf16[2,2,8,16,128]{4,3,2,1,0:T(8,128)(2,1)S(1)} %get-tuple-element.72), channel_id=1, source_target_pairs={{0,8},{1,9},{8,2},{9,3},{2,10},{3,11},{10,4},{11,5},{4,12},{5,13},... | collective-permute-start | bytes 393224 | tf_op jit(solution)/shard_map/ppermute | solution.py:315
  74.6 16.8 %collective-permute-start.28 = (bf16[2,2,8,16,128]{4,3,2,1,0:T(8,128)(2,1)S(1)}, bf16[2,2,8,16,128]{4,3,2,1,0:T(8,128)(2,1)S(1)}, u32[]{:S(2)}, u32[]{:S(2)}) collective-permute-start(bf16[2,2,8,16,128]{4,3,2,1,0:T(8,128)(2,1)S(1)} %get-tuple-element.73), channel_id=1, source_target_pairs={{0,14},{1,15},{8,0},{9,1},{2,8},{3,9},{10,2},{11,3},{4,10},{5,11},... | collective-permute-start | bytes 393224 | tf_op jit(solution)/shard_map/ppermute | solution.py:315
  76.3 23.0 %collective-permute-start.29 = (bf16[2,2,8,16,128]{4,3,2,1,0:T(8,128)(2,1)S(1)}, bf16[2,2,8,16,128]{4,3,2,1,0:T(8,128)(2,1)S(1)}, u32[]{:S(2)}, u32[]{:S(2)}) collective-permute-start(bf16[2,2,8,16,128]{4,3,2,1,0:T(8,128)(2,1)S(1)} %get-tuple-element.74), channel_id=1, source_target_pairs={{0,4},{1,5},{8,12},{9,13},{2,6},{3,7},{10,14},{11,15},{4,0},{5,1},... | collective-permute-start | bytes 393224 | tf_op jit(solution)/shard_map/ppermute | solution.py:315
  78.7 20.9 %collective-permute-start.30 = (bf16[2,2,8,16,128]{4,3,2,1,0:T(8,128)(2,1)S(1)}, bf16[2,2,8,16,128]{4,3,2,1,0:T(8,128)(2,1)S(1)}, u32[]{:S(2)}, u32[]{:S(2)}) collective-permute-start(bf16[2,2,8,16,128]{4,3,2,1,0:T(8,128)(2,1)S(1)} %get-tuple-element.75), channel_id=1, source_target_pairs={{0,10},{1,11},{8,4},{9,5},{2,12},{3,13},{10,6},{11,7},{4,14},{5,15... | collective-permute-start | bytes 393224 | tf_op jit(solution)/shard_map/ppermute | solution.py:315
  79.4 22.0 %collective-permute-start.31 = (bf16[2,2,8,16,128]{4,3,2,1,0:T(8,128)(2,1)S(1)}, bf16[2,2,8,16,128]{4,3,2,1,0:T(8,128)(2,1)S(1)}, u32[]{:S(2)}, u32[]{:S(2)}) collective-permute-start(bf16[2,2,8,16,128]{4,3,2,1,0:T(8,128)(2,1)S(1)} %get-tuple-element.76), channel_id=1, source_target_pairs={{0,12},{1,13},{8,6},{9,7},{2,14},{3,15},{10,0},{11,1},{4,8},{5,9},... | collective-permute-start | bytes 393224 | tf_op jit(solution)/shard_map/ppermute | solution.py:315
  99.3 13.2 %collective-permute-start.15 = (bf16[2,4,14,16,128]{4,3,2,1,0:T(8,128)(2,1)S(1)}, bf16[2,4,14,16,128]{4,3,2,1,0:T(8,128)(2,1)S(1)}, u32[]{:S(2)}, u32[]{:S(2)}) collective-permute-start(bf16[2,4,14,16,128]{4,3,2,1,0:T(8,128)(2,1)S(1)} %get-tuple-element.60.own0), channel_id=1, source_target_pairs={{0,16},{1,17},{8,24},{9,25},{2,18},{3,19},{10,26},{11,27},{4,20},{... | collective-permute-start | bytes 1376264 | tf_op jit(solution)/shard_map/ppermute | solution.py:315
  99.6 24.2 %collective-permute-start.16 = (bf16[2,4,14,16,128]{4,3,2,1,0:T(8,128)(2,1)S(1)}, bf16[2,4,14,16,128]{4,3,2,1,0:T(8,128)(2,1)S(1)}, u32[]{:S(2)}, u32[]{:S(2)}) collective-permute-start(bf16[2,4,14,16,128]{4,3,2,1,0:T(8,128)(2,1)S(1)} %get-tuple-element.61), channel_id=1, source_target_pairs={{0,17},{1,16},{8,25},{9,24},{2,19},{3,18},{10,27},{11,26},{4,21},{... | collective-permute-start | bytes 1376264 | tf_op jit(solution)/shard_map/ppermute | solution.py:315
  101.4 22.4 %collective-permute-start.14 = (bf16[2,4,14,16,128]{4,3,2,1,0:T(8,128)(2,1)S(1)}, bf16[2,4,14,16,128]{4,3,2,1,0:T(8,128)(2,1)S(1)}, u32[]{:S(2)}, u32[]{:S(2)}) collective-permute-start(bf16[2,4,14,16,128]{4,3,2,1,0:T(8,128)(2,1)S(1)} %get-tuple-element.61), channel_id=1, source_target_pairs={{0,1},{1,0},{8,9},{9,8},{2,3},{3,2},{10,11},{11,10},{4,5},{5,4},{1... | collective-permute-start | bytes 1376264 | tf_op jit(solution)/shard_map/ppermute | solution.py:315
  103.3 44.5 %collective-permute-start.34 = (bf16[2,8,128,128]{3,2,1,0:T(8,128)(2,1)S(1)}, bf16[2,8,128,128]{3,2,1,0:T(8,128)(2,1)S(1)}, u32[]{:S(2)}, u32[]{:S(2)}) collective-permute-start(bf16[2,8,128,128]{3,2,1,0:T(8,128)(2,1)S(1)} %turn.4.refs_8_), channel_id=1, source_target_pairs={{0,1},{1,0},{8,9},{9,8},{2,3},{3,2},{10,11},{11,10},{4,5},{5,4},{1... | collective-permute-start | bytes 1572872 | tf_op jit(solution)/shard_map/ppermute | solution.py:315
  129.1 17.4 %collective-permute-start.20 = (bf16[2,2,8,16,128]{4,3,2,1,0:T(8,128)(2,1)S(1)}, bf16[2,2,8,16,128]{4,3,2,1,0:T(8,128)(2,1)S(1)}, u32[]{:S(2)}, u32[]{:S(2)}) collective-permute-start(bf16[2,2,8,16,128]{4,3,2,1,0:T(8,128)(2,1)S(1)} %get-tuple-element.65), channel_id=1, source_target_pairs={{0,8},{1,9},{8,2},{9,3},{2,10},{3,11},{10,4},{11,5},{4,12},{5,13},... | collective-permute-start | bytes 393224 | tf_op jit(solution)/shard_map/ppermute | solution.py:315
  129.2 17.4 %collective-permute-start.21 = (bf16[2,2,8,16,128]{4,3,2,1,0:T(8,128)(2,1)S(1)}, bf16[2,2,8,16,128]{4,3,2,1,0:T(8,128)(2,1)S(1)}, u32[]{:S(2)}, u32[]{:S(2)}) collective-permute-start(bf16[2,2,8,16,128]{4,3,2,1,0:T(8,128)(2,1)S(1)} %get-tuple-element.66), channel_id=1, source_target_pairs={{0,14},{1,15},{8,0},{9,1},{2,8},{3,9},{10,2},{11,3},{4,10},{5,11},... | collective-permute-start | bytes 393224 | tf_op jit(solution)/shard_map/ppermute | solution.py:315
  131.9 21.0 %collective-permute-start.22 = (bf16[2,2,8,16,128]{4,3,2,1,0:T(8,128)(2,1)S(1)}, bf16[2,2,8,16,128]{4,3,2,1,0:T(8,128)(2,1)S(1)}, u32[]{:S(2)}, u32[]{:S(2)}) collective-permute-start(bf16[2,2,8,16,128]{4,3,2,1,0:T(8,128)(2,1)S(1)} %get-tuple-element.67), channel_id=1, source_target_pairs={{0,4},{1,5},{8,12},{9,13},{2,6},{3,7},{10,14},{11,15},{4,0},{5,1},... | collective-permute-start | bytes 393224 | tf_op jit(solution)/shard_map/ppermute | solution.py:315
  133.7 19.2 %collective-permute-start.23 = (bf16[2,2,8,16,128]{4,3,2,1,0:T(8,128)(2,1)S(1)}, bf16[2,2,8,16,128]{4,3,2,1,0:T(8,128)(2,1)S(1)}, u32[]{:S(2)}, u32[]{:S(2)}) collective-permute-start(bf16[2,2,8,16,128]{4,3,2,1,0:T(8,128)(2,1)S(1)} %get-tuple-element.68), channel_id=1, source_target_pairs={{0,10},{1,11},{8,4},{9,5},{2,12},{3,13},{10,6},{11,7},{4,14},{5,15... | collective-permute-start | bytes 393224 | tf_op jit(solution)/shard_map/ppermute | solution.py:315
  (13 other events, 124.8 us)

commit v10 on v9

--- a/solution.py
+++ b/solution.py
@@ -162,7 +162,7 @@
                 res[pl.ds(start, CH), :] = bottom + sign * top
         return carry
 
-    lax.fori_loop(0, FC, one_bin, 0, unroll=2)
+    lax.fori_loop(0, FC, one_bin, 0, unroll=4)
     for r in range(8):
         dst = (z + r) & 7
         for crel in range(2):
@@ -181,8 +181,8 @@
         in_specs=[SM] + [VM] * 4 + [ANY] * len(after),
         out_specs=[VM] * 8,
         scratch_shapes=[
-            pltpu.VMEM((32 * WIN * FC, 128), F32),
-            pltpu.VMEM((4 * FC * CH, 128), F32),
+            pltpu.VMEM((32 * WIN * FC + FC, 128), F32),
+            pltpu.VMEM((4 * FC * CH + CH, 128), F32),
         ],
         compiler_params=params(),
         cost_estimate=pl.CostEstimate(
@@ -195,7 +195,9 @@
 def turn_kernel(pos_ref, *refs):
     ins, (out, buf) = refs[:8], refs[-2:]
     z = pos_ref[0]
-    for rnd in range(2):
+
+    @pl.loop(0, 2)
+    def _(rnd):
         for i in range(8):
             slot = i & 1
             for n, r in enumerate(ORDER):
@@ -228,11 +230,8 @@
         for i in range(4):
             cols = [p[0, i, k * CH : (k + 1) * CH] for p in parts]
             rows.append(jnp.concatenate(cols, axis=1))
-        start = k * BINS + chunk * CBINS
         total += jnp.dot(
-            jnp.concatenate(rows, axis=0),
-            table[start : start + CBINS],
-            preferred_element_type=F32,
+            jnp.concatenate(rows, axis=0), table[k], preferred_element_type=F32
         )
     total = total.reshape(4, CH, LAG_COUNT)
     for ref in sums:
@@ -251,7 +250,7 @@
         out_shape=jax.ShapeDtypeStruct((2, 8, CH, LAG_COUNT), dtype),
         grid=(2, 2),
         in_specs=[part] * 2
-        + [pl.BlockSpec((2 * BINS, LAG_COUNT), lambda r, i: (0, 0))]
+        + [pl.BlockSpec((2, CBINS, LAG_COUNT), lambda r, i: (0, chunk, 0))]
         + [block] * len(sums),
         out_specs=block,
         compiler_params=params(),
@@ -259,7 +258,7 @@
             flops=1024 * 1024 * 1024, bytes_accessed=6 << 20, transcendentals=0
         ),
         name="invert",
-    )(*parts, table, *sums)
+    )(*parts, table.reshape(2, BINS, LAG_COUNT), *sums)
 
 
 def turns(freq_ids, delay_ids):

time: 167 us -> 165 us (0.988)
    pallas_call x2, Pallas kernels: 10.8 us -> 8.81 us  [cross(): pl.pallas_call(cross_kernel, out_shape=[shape] * 8, in_specs=[SM] + [VM]...]
where the time goes in v10:
time: 165 us; the launch traced here: 164 us
  waiting for transfers between devices  73.5 us (45%)
  starting transfers between devices  59.9 us (36%)
  Pallas kernels  26 us (16%)
  other arithmetic  2.92 us (2%)
  local copies, waits for them, and re-layouts  1.9 us (1%)
    ppermute x36, waiting for transfers between devices, send(): lax.ppermute(value, ALL, [(device(*d), device(*target(*d))) for d in EVERY])  73.5 us
    ppermute x36, starting transfers between devices, send(): lax.ppermute(value, ALL, [(device(*d), device(*target(*d))) for d in EVERY])  59.9 us
    pallas_call x2, Pallas kernels, cross(): pl.pallas_call(cross_kernel, out_shape=[shape] * 8, in_specs=[SM] + [VM]...  8.81 us
    pallas_call x1, Pallas kernels, whiten(): pl.pallas_call(whiten_kernel, out_shape=[shape] * (8 * CHUNKS) + [jax.Sha...  5.71 us
    pallas_call x2, Pallas kernels, invert(): pl.pallas_call(functools.partial(invert_kernel, scaling, chunk), out_shap...  4.88 us
    pallas_call x4, Pallas kernels, turn(): pl.pallas_call(turn_kernel, out_shape=jax.ShapeDtypeStruct((2, 8, 128, 8...  3.94 us
  transfers between devices with their start and end apart: 36, of which 13 were waited for; matrix products, arithmetic and copies ran while one was open for 2% of the time, Pallas kernels for 10%

profile of v10, /device:TPU:5, one launch (start us, length us, event | category | flops | bytes accessed | tf_op | source)
XLA Modules:
  0.0 164.5 jit_solution(15448706547355078950)
XLA Ops:
  2.0 5.7 %whiten.1 = (bf16[2,14,16,128]{3,2,1,0:T(8,128)(2,1)S(1)}, bf16[2,14,16,128]{3,2,1,0:T(8,128)(2,1)S(1)}, bf16[2,14,16,128]{3,2,1,0:T(8,128)(2,1)S(1)}, bf16[2,14...) custom-call(s32[2]{0:T(128)S(1)} %pad_add_fusion.pos_ref, ...), custom_call_target="tpu_custom_call" | custom-call | flops 1409286144 | bytes 4194304 | tf_op jit(solution)/shard_map/whiten/pallas_call | solution.py:85
  9.4 4.0 %collective-permute-start.8 = (bf16[2,14,16,128]{3,2,1,0:T(8,128)(2,1)S(1)}, bf16[2,14,16,128]{3,2,1,0:T(8,128)(2,1)S(1)}, u32[]{:S(2)}, u32[]{:S(2)}) collective-permute-start(bf16[2,14,16,128]{3,2,1,0:T(8,128)(2,1)S(1)} %get-tuple-element.52), channel_id=1, source_target_pairs={{0,14},{1,15},{8,0},{9,1},{2,8},{3,9},{10,2},{11,3},{4,10},{5,11},... | collective-permute-start | bytes 344072 | tf_op jit(solution)/shard_map/ppermute | solution.py:314
  13.5 3.9 %collective-permute-start.9 = (bf16[2,14,16,128]{3,2,1,0:T(8,128)(2,1)S(1)}, bf16[2,14,16,128]{3,2,1,0:T(8,128)(2,1)S(1)}, u32[]{:S(2)}, u32[]{:S(2)}) collective-permute-start(bf16[2,14,16,128]{3,2,1,0:T(8,128)(2,1)S(1)} %get-tuple-element.53), channel_id=1, source_target_pairs={{0,4},{1,5},{8,12},{9,13},{2,6},{3,7},{10,14},{11,15},{4,0},{5,1},... | collective-permute-start | bytes 344072 | tf_op jit(solution)/shard_map/ppermute | solution.py:314
  17.8 4.0 %collective-permute-start.11 = (bf16[2,14,16,128]{3,2,1,0:T(8,128)(2,1)S(1)}, bf16[2,14,16,128]{3,2,1,0:T(8,128)(2,1)S(1)}, u32[]{:S(2)}, u32[]{:S(2)}) collective-permute-start(bf16[2,14,16,128]{3,2,1,0:T(8,128)(2,1)S(1)} %get-tuple-element.55), channel_id=1, source_target_pairs={{0,12},{1,13},{8,6},{9,7},{2,14},{3,15},{10,0},{11,1},{4,8},{5,9},... | collective-permute-start | bytes 344072 | tf_op jit(solution)/shard_map/ppermute | solution.py:314
  21.9 3.6 %collective-permute-start.13 = (bf16[2,14,16,128]{3,2,1,0:T(8,128)(2,1)S(1)}, bf16[2,14,16,128]{3,2,1,0:T(8,128)(2,1)S(1)}, u32[]{:S(2)}, u32[]{:S(2)}) collective-permute-start(bf16[2,14,16,128]{3,2,1,0:T(8,128)(2,1)S(1)} %get-tuple-element.57), channel_id=1, source_target_pairs={{0,6},{1,7},{8,14},{9,15},{2,0},{3,1},{10,8},{11,9},{4,2},{5,3},{1... | collective-permute-start | bytes 344072 | tf_op jit(solution)/shard_map/ppermute | solution.py:314
  25.4 5.4 %collective-permute-done.10.refs_4_ = bf16[2,14,16,128]{3,2,1,0:T(8,128)(2,1)S(1)} collective-permute-done((bf16[2,14,16,128]{3,2,1,0:T(8,128)(2,1)S(1)}, bf16[2,14,16,128]{3,2,1,0:T(8,128)(2,1)S(1)}, u32[]{:S(2)}, u32[]{:S(2)}) %collective-permute-start.10) | collective-permute-done | bytes 114720 | tf_op jit(solution)/shard_map/ppermute | solution.py:314
  31.4 3.9 %collective-permute-done.13.refs_7_ = bf16[2,14,16,128]{3,2,1,0:T(8,128)(2,1)S(1)} collective-permute-done((bf16[2,14,16,128]{3,2,1,0:T(8,128)(2,1)S(1)}, bf16[2,14,16,128]{3,2,1,0:T(8,128)(2,1)S(1)}, u32[]{:S(2)}, u32[]{:S(2)}) %collective-permute-start.13) | collective-permute-done | bytes 114720 | tf_op jit(solution)/shard_map/ppermute | solution.py:314
  42.2 8.7 %collective-permute-done.19.prev1 = bf16[2,4,14,16,128]{4,3,2,1,0:T(8,128)(2,1)S(1)} collective-permute-done((bf16[2,4,14,16,128]{4,3,2,1,0:T(8,128)(2,1)S(1)}, bf16[2,4,14,16,128]{4,3,2,1,0:T(8,128)(2,1)S(1)}, u32[]{:S(2)}, u32[]{:S(2)}) %collective-permute-start.19) | collective-permute-done | bytes 458784 | tf_op jit(solution)/shard_map/ppermute | solution.py:314
  50.9 3.4 %collective-permute-start.2 = (bf16[2,14,16,128]{3,2,1,0:T(8,128)(2,1)S(1)}, bf16[2,14,16,128]{3,2,1,0:T(8,128)(2,1)S(1)}, u32[]{:S(2)}, u32[]{:S(2)}) collective-permute-start(bf16[2,14,16,128]{3,2,1,0:T(8,128)(2,1)S(1)} %get-tuple-element.45), channel_id=1, source_target_pairs={{0,4},{1,5},{8,12},{9,13},{2,6},{3,7},{10,14},{11,15},{4,0},{5,1},... | collective-permute-start | bytes 344072 | tf_op jit(solution)/shard_map/ppermute | solution.py:314
  55.1 5.7 %collective-permute-done.18.prev0 = bf16[2,4,14,16,128]{4,3,2,1,0:T(8,128)(2,1)S(1)} collective-permute-done((bf16[2,4,14,16,128]{4,3,2,1,0:T(8,128)(2,1)S(1)}, bf16[2,4,14,16,128]{4,3,2,1,0:T(8,128)(2,1)S(1)}, u32[]{:S(2)}, u32[]{:S(2)}) %collective-permute-start.18) | collective-permute-done | bytes 458784 | tf_op jit(solution)/shard_map/ppermute | solution.py:314
  60.8 3.1 %collective-permute-start.4 = (bf16[2,14,16,128]{3,2,1,0:T(8,128)(2,1)S(1)}, bf16[2,14,16,128]{3,2,1,0:T(8,128)(2,1)S(1)}, u32[]{:S(2)}, u32[]{:S(2)}) collective-permute-start(bf16[2,14,16,128]{3,2,1,0:T(8,128)(2,1)S(1)} %get-tuple-element.47), channel_id=1, source_target_pairs={{0,12},{1,13},{8,6},{9,7},{2,14},{3,15},{10,0},{11,1},{4,8},{5,9},... | collective-permute-start | bytes 344072 | tf_op jit(solution)/shard_map/ppermute | solution.py:314
  63.9 4.4 %cross.2 = (bf16[2,2,8,16,128]{4,3,2,1,0:T(8,128)(2,1)S(1)}, bf16[2,2,8,16,128]{4,3,2,1,0:T(8,128)(2,1)S(1)}, bf16[2,2,8,16,128]{4,3,2,1,0:T(8,128)(2,1)S(1)}, b...) custom-call(s32[2]{0:T(128)S(1)} %pad_add_fusion.pos_ref, ...), custom_call_target="tpu_custom_call" | custom-call | flops 536870912 | bytes 3145728 | tf_op jit(solution)/shard_map/cross/pallas_call | solution.py:178
  69.1 2.9 %collective-permute-start.6 = (bf16[2,14,16,128]{3,2,1,0:T(8,128)(2,1)S(1)}, bf16[2,14,16,128]{3,2,1,0:T(8,128)(2,1)S(1)}, u32[]{:S(2)}, u32[]{:S(2)}) collective-permute-start(bf16[2,14,16,128]{3,2,1,0:T(8,128)(2,1)S(1)} %get-tuple-element.49), channel_id=1, source_target_pairs={{0,6},{1,7},{8,14},{9,15},{2,0},{3,1},{10,8},{11,9},{4,2},{5,3},{1... | collective-permute-start | bytes 344072 | tf_op jit(solution)/shard_map/ppermute | solution.py:314
  78.4 3.8 %collective-permute-start.31 = (bf16[2,2,8,16,128]{4,3,2,1,0:T(8,128)(2,1)S(1)}, bf16[2,2,8,16,128]{4,3,2,1,0:T(8,128)(2,1)S(1)}, u32[]{:S(2)}, u32[]{:S(2)}) collective-permute-start(bf16[2,2,8,16,128]{4,3,2,1,0:T(8,128)(2,1)S(1)} %get-tuple-element.76), channel_id=1, source_target_pairs={{0,12},{1,13},{8,6},{9,7},{2,14},{3,15},{10,0},{11,1},{4,8},{5,9},... | collective-permute-start | bytes 393224 | tf_op jit(solution)/shard_map/ppermute | solution.py:314
  82.2 8.3 %collective-permute-done.27.refs_1_ = bf16[2,2,8,16,128]{4,3,2,1,0:T(8,128)(2,1)S(1)} collective-permute-done((bf16[2,2,8,16,128]{4,3,2,1,0:T(8,128)(2,1)S(1)}, bf16[2,2,8,16,128]{4,3,2,1,0:T(8,128)(2,1)S(1)}, u32[]{:S(2)}, u32[]{:S(2)}) %collective-permute-start.27) | collective-permute-done | bytes 131104 | tf_op jit(solution)/shard_map/ppermute | solution.py:314
  90.5 3.6 %collective-permute-start.33 = (bf16[2,2,8,16,128]{4,3,2,1,0:T(8,128)(2,1)S(1)}, bf16[2,2,8,16,128]{4,3,2,1,0:T(8,128)(2,1)S(1)}, u32[]{:S(2)}, u32[]{:S(2)}) collective-permute-start(bf16[2,2,8,16,128]{4,3,2,1,0:T(8,128)(2,1)S(1)} %get-tuple-element.78), channel_id=1, source_target_pairs={{0,6},{1,7},{8,14},{9,15},{2,0},{3,1},{10,8},{11,9},{4,2},{5,3},{1... | collective-permute-start | bytes 393224 | tf_op jit(solution)/shard_map/ppermute | solution.py:314
  103.0 8.3 %collective-permute-done.15.prev0 = bf16[2,4,14,16,128]{4,3,2,1,0:T(8,128)(2,1)S(1)} collective-permute-done((bf16[2,4,14,16,128]{4,3,2,1,0:T(8,128)(2,1)S(1)}, bf16[2,4,14,16,128]{4,3,2,1,0:T(8,128)(2,1)S(1)}, u32[]{:S(2)}, u32[]{:S(2)}) %collective-permute-start.15) | collective-permute-done | bytes 458784 | tf_op jit(solution)/shard_map/ppermute | solution.py:314
  111.3 11.3 %collective-permute-done.16.prev1 = bf16[2,4,14,16,128]{4,3,2,1,0:T(8,128)(2,1)S(1)} collective-permute-done((bf16[2,4,14,16,128]{4,3,2,1,0:T(8,128)(2,1)S(1)}, bf16[2,4,14,16,128]{4,3,2,1,0:T(8,128)(2,1)S(1)}, u32[]{:S(2)}, u32[]{:S(2)}) %collective-permute-start.16) | collective-permute-done | bytes 458784 | tf_op jit(solution)/shard_map/ppermute | solution.py:314
  122.6 4.4 %cross.3 = (bf16[2,2,8,16,128]{4,3,2,1,0:T(8,128)(2,1)S(1)}, bf16[2,2,8,16,128]{4,3,2,1,0:T(8,128)(2,1)S(1)}, bf16[2,2,8,16,128]{4,3,2,1,0:T(8,128)(2,1)S(1)}, b...) custom-call(s32[2]{0:T(128)S(1)} %pad_add_fusion.pos_ref, ...), custom_call_target="tpu_custom_call" | custom-call | flops 536870912 | bytes 3145728 | tf_op jit(solution)/shard_map/cross/pallas_call | solution.py:178
  127.1 2.7 %collective-permute-start.21 = (bf16[2,2,8,16,128]{4,3,2,1,0:T(8,128)(2,1)S(1)}, bf16[2,2,8,16,128]{4,3,2,1,0:T(8,128)(2,1)S(1)}, u32[]{:S(2)}, u32[]{:S(2)}) collective-permute-start(bf16[2,2,8,16,128]{4,3,2,1,0:T(8,128)(2,1)S(1)} %get-tuple-element.66), channel_id=1, source_target_pairs={{0,14},{1,15},{8,0},{9,1},{2,8},{3,9},{10,2},{11,3},{4,10},{5,11},... | collective-permute-start | bytes 393224 | tf_op jit(solution)/shard_map/ppermute | solution.py:314
  132.7 11.8 %collective-permute-done.20.refs_1_ = bf16[2,2,8,16,128]{4,3,2,1,0:T(8,128)(2,1)S(1)} collective-permute-done((bf16[2,2,8,16,128]{4,3,2,1,0:T(8,128)(2,1)S(1)}, bf16[2,2,8,16,128]{4,3,2,1,0:T(8,128)(2,1)S(1)}, u32[]{:S(2)}, u32[]{:S(2)}) %collective-permute-start.20) | collective-permute-done | bytes 131104 | tf_op jit(solution)/shard_map/ppermute | solution.py:314
  151.0 4.1 %collective-permute-done.24.refs_5_ = bf16[2,2,8,16,128]{4,3,2,1,0:T(8,128)(2,1)S(1)} collective-permute-done((bf16[2,2,8,16,128]{4,3,2,1,0:T(8,128)(2,1)S(1)}, bf16[2,2,8,16,128]{4,3,2,1,0:T(8,128)(2,1)S(1)}, u32[]{:S(2)}, u32[]{:S(2)}) %collective-permute-start.24) | collective-permute-done | bytes 131104 | tf_op jit(solution)/shard_map/ppermute | solution.py:314
  155.1 3.4 %collective-permute-done.26.refs_7_ = bf16[2,2,8,16,128]{4,3,2,1,0:T(8,128)(2,1)S(1)} collective-permute-done((bf16[2,2,8,16,128]{4,3,2,1,0:T(8,128)(2,1)S(1)}, bf16[2,2,8,16,128]{4,3,2,1,0:T(8,128)(2,1)S(1)}, u32[]{:S(2)}, u32[]{:S(2)}) %collective-permute-start.26) | collective-permute-done | bytes 131104 | tf_op jit(solution)/shard_map/ppermute | solution.py:314
  161.4 3.0 %invert.3 = bf16[2,8,64,1024]{3,2,1,0:T(8,128)(2,1)} custom-call(bf16[2,8,128,128]{3,2,1,0:T(8,128)(2,1)S(1)} %turn.7.refs_0_, bf16[2,8,128,128]{3,2,1,0:T(8,128)(2,1)S(1)} %collective-permute-done.35.refs_1_, bf16[2,512,1024]{2,1,0:T(8,128)(2,1)S(1)} %bitcast.8, f32[2,8,64,1024]{3,2,1,0:T(8,128)S(1)} %invert.2.refs_8_.refs_3_), custom_call_target="tpu_custom_call" | custom-call | flops 1073741824 | bytes 6291456 | tf_op jit(solution)/shard_map/invert/pallas_call | solution.py:248
  (68 shorter events, 41.1 us)
Async XLA Ops:
  7.7 14.1 %collective-permute-start.7 = (bf16[2,14,16,128]{3,2,1,0:T(8,128)(2,1)S(1)}, bf16[2,14,16,128]{3,2,1,0:T(8,128)(2,1)S(1)}, u32[]{:S(2)}, u32[]{:S(2)}) collective-permute-start(bf16[2,14,16,128]{3,2,1,0:T(8,128)(2,1)S(1)} %get-tuple-element.51), channel_id=1, source_target_pairs={{0,8},{1,9},{8,2},{9,3},{2,10},{3,11},{10,4},{11,5},{4,12},{5,13},... | collective-permute-start | bytes 344072 | tf_op jit(solution)/shard_map/ppermute | solution.py:314
  17.4 13.5 %collective-permute-start.10 = (bf16[2,14,16,128]{3,2,1,0:T(8,128)(2,1)S(1)}, bf16[2,14,16,128]{3,2,1,0:T(8,128)(2,1)S(1)}, u32[]{:S(2)}, u32[]{:S(2)}) collective-permute-start(bf16[2,14,16,128]{3,2,1,0:T(8,128)(2,1)S(1)} %get-tuple-element.54), channel_id=1, source_target_pairs={{0,10},{1,11},{8,4},{9,5},{2,12},{3,13},{10,6},{11,7},{4,14},{5,15... | collective-permute-start | bytes 344072 | tf_op jit(solution)/shard_map/ppermute | solution.py:314
  17.8 13.0 %collective-permute-start.11 = (bf16[2,14,16,128]{3,2,1,0:T(8,128)(2,1)S(1)}, bf16[2,14,16,128]{3,2,1,0:T(8,128)(2,1)S(1)}, u32[]{:S(2)}, u32[]{:S(2)}) collective-permute-start(bf16[2,14,16,128]{3,2,1,0:T(8,128)(2,1)S(1)} %get-tuple-element.55), channel_id=1, source_target_pairs={{0,12},{1,13},{8,6},{9,7},{2,14},{3,15},{10,0},{11,1},{4,8},{5,9},... | collective-permute-start | bytes 344072 | tf_op jit(solution)/shard_map/ppermute | solution.py:314
  21.9 13.4 %collective-permute-start.13 = (bf16[2,14,16,128]{3,2,1,0:T(8,128)(2,1)S(1)}, bf16[2,14,16,128]{3,2,1,0:T(8,128)(2,1)S(1)}, u32[]{:S(2)}, u32[]{:S(2)}) collective-permute-start(bf16[2,14,16,128]{3,2,1,0:T(8,128)(2,1)S(1)} %get-tuple-element.57), channel_id=1, source_target_pairs={{0,6},{1,7},{8,14},{9,15},{2,0},{3,1},{10,8},{11,9},{4,2},{5,3},{1... | collective-permute-start | bytes 344072 | tf_op jit(solution)/shard_map/ppermute | solution.py:314
  35.9 15.0 %collective-permute-start.19 = (bf16[2,4,14,16,128]{4,3,2,1,0:T(8,128)(2,1)S(1)}, bf16[2,4,14,16,128]{4,3,2,1,0:T(8,128)(2,1)S(1)}, u32[]{:S(2)}, u32[]{:S(2)}) collective-permute-start(bf16[2,4,14,16,128]{4,3,2,1,0:T(8,128)(2,1)S(1)} %get-tuple-element.62), channel_id=1, source_target_pairs={{0,17},{1,16},{8,25},{9,24},{2,19},{3,18},{10,27},{11,26},{4,21},{... | collective-permute-start | bytes 1376264 | tf_op jit(solution)/shard_map/ppermute | solution.py:314
  38.2 16.0 %collective-permute-start.17 = (bf16[2,4,14,16,128]{4,3,2,1,0:T(8,128)(2,1)S(1)}, bf16[2,4,14,16,128]{4,3,2,1,0:T(8,128)(2,1)S(1)}, u32[]{:S(2)}, u32[]{:S(2)}) collective-permute-start(bf16[2,4,14,16,128]{4,3,2,1,0:T(8,128)(2,1)S(1)} %get-tuple-element.62), channel_id=1, source_target_pairs={{0,1},{1,0},{8,9},{9,8},{2,3},{3,2},{10,11},{11,10},{4,5},{5,4},{1... | collective-permute-start | bytes 1376264 | tf_op jit(solution)/shard_map/ppermute | solution.py:314
  38.2 22.5 %collective-permute-start.18 = (bf16[2,4,14,16,128]{4,3,2,1,0:T(8,128)(2,1)S(1)}, bf16[2,4,14,16,128]{4,3,2,1,0:T(8,128)(2,1)S(1)}, u32[]{:S(2)}, u32[]{:S(2)}) collective-permute-start(bf16[2,4,14,16,128]{4,3,2,1,0:T(8,128)(2,1)S(1)} %get-tuple-element.58.refs_8_.own0), channel_id=1, source_target_pairs={{0,16},{1,17},{8,24},{9,25},{2,18},{3,19},{10,26},{11,27},{4,20},{... | collective-permute-start | bytes 1376264 | tf_op jit(solution)/shard_map/ppermute | solution.py:314
  39.5 28.8 %collective-permute-start = (bf16[2,14,16,128]{3,2,1,0:T(8,128)(2,1)S(1)}, bf16[2,14,16,128]{3,2,1,0:T(8,128)(2,1)S(1)}, u32[]{:S(2)}, u32[]{:S(2)}) collective-permute-start(bf16[2,14,16,128]{3,2,1,0:T(8,128)(2,1)S(1)} %get-tuple-element.43), channel_id=1, source_target_pairs={{0,8},{1,9},{8,2},{9,3},{2,10},{3,11},{10,4},{11,5},{4,12},{5,13},... | collective-permute-start | bytes 344072 | tf_op jit(solution)/shard_map/ppermute | solution.py:314
  40.4 28.6 %collective-permute-start.1 = (bf16[2,14,16,128]{3,2,1,0:T(8,128)(2,1)S(1)}, bf16[2,14,16,128]{3,2,1,0:T(8,128)(2,1)S(1)}, u32[]{:S(2)}, u32[]{:S(2)}) collective-permute-start(bf16[2,14,16,128]{3,2,1,0:T(8,128)(2,1)S(1)} %get-tuple-element.44), channel_id=1, source_target_pairs={{0,14},{1,15},{8,0},{9,1},{2,8},{3,9},{10,2},{11,3},{4,10},{5,11},... | collective-permute-start | bytes 344072 | tf_op jit(solution)/shard_map/ppermute | solution.py:314
  50.9 21.1 %collective-permute-start.2 = (bf16[2,14,16,128]{3,2,1,0:T(8,128)(2,1)S(1)}, bf16[2,14,16,128]{3,2,1,0:T(8,128)(2,1)S(1)}, u32[]{:S(2)}, u32[]{:S(2)}) collective-permute-start(bf16[2,14,16,128]{3,2,1,0:T(8,128)(2,1)S(1)} %get-tuple-element.45), channel_id=1, source_target_pairs={{0,4},{1,5},{8,12},{9,13},{2,6},{3,7},{10,14},{11,15},{4,0},{5,1},... | collective-permute-start | bytes 344072 | tf_op jit(solution)/shard_map/ppermute | solution.py:314
  54.3 19.4 %collective-permute-start.3 = (bf16[2,14,16,128]{3,2,1,0:T(8,128)(2,1)S(1)}, bf16[2,14,16,128]{3,2,1,0:T(8,128)(2,1)S(1)}, u32[]{:S(2)}, u32[]{:S(2)}) collective-permute-start(bf16[2,14,16,128]{3,2,1,0:T(8,128)(2,1)S(1)} %get-tuple-element.46), channel_id=1, source_target_pairs={{0,10},{1,11},{8,4},{9,5},{2,12},{3,13},{10,6},{11,7},{4,14},{5,15... | collective-permute-start | bytes 344072 | tf_op jit(solution)/shard_map/ppermute | solution.py:314
  60.8 14.5 %collective-permute-start.4 = (bf16[2,14,16,128]{3,2,1,0:T(8,128)(2,1)S(1)}, bf16[2,14,16,128]{3,2,1,0:T(8,128)(2,1)S(1)}, u32[]{:S(2)}, u32[]{:S(2)}) collective-permute-start(bf16[2,14,16,128]{3,2,1,0:T(8,128)(2,1)S(1)} %get-tuple-element.47), channel_id=1, source_target_pairs={{0,12},{1,13},{8,6},{9,7},{2,14},{3,15},{10,0},{11,1},{4,8},{5,9},... | collective-permute-start | bytes 344072 | tf_op jit(solution)/shard_map/ppermute | solution.py:314
  71.9 18.5 %collective-permute-start.27 = (bf16[2,2,8,16,128]{4,3,2,1,0:T(8,128)(2,1)S(1)}, bf16[2,2,8,16,128]{4,3,2,1,0:T(8,128)(2,1)S(1)}, u32[]{:S(2)}, u32[]{:S(2)}) collective-permute-start(bf16[2,2,8,16,128]{4,3,2,1,0:T(8,128)(2,1)S(1)} %get-tuple-element.72), channel_id=1, source_target_pairs={{0,8},{1,9},{8,2},{9,3},{2,10},{3,11},{10,4},{11,5},{4,12},{5,13},... | collective-permute-start | bytes 393224 | tf_op jit(solution)/shard_map/ppermute | solution.py:314
  73.6 16.9 %collective-permute-start.28 = (bf16[2,2,8,16,128]{4,3,2,1,0:T(8,128)(2,1)S(1)}, bf16[2,2,8,16,128]{4,3,2,1,0:T(8,128)(2,1)S(1)}, u32[]{:S(2)}, u32[]{:S(2)}) collective-permute-start(bf16[2,2,8,16,128]{4,3,2,1,0:T(8,128)(2,1)S(1)} %get-tuple-element.73), channel_id=1, source_target_pairs={{0,14},{1,15},{8,0},{9,1},{2,8},{3,9},{10,2},{11,3},{4,10},{5,11},... | collective-permute-start | bytes 393224 | tf_op jit(solution)/shard_map/ppermute | solution.py:314
  75.3 23.0 %collective-permute-start.29 = (bf16[2,2,8,16,128]{4,3,2,1,0:T(8,128)(2,1)S(1)}, bf16[2,2,8,16,128]{4,3,2,1,0:T(8,128)(2,1)S(1)}, u32[]{:S(2)}, u32[]{:S(2)}) collective-permute-start(bf16[2,2,8,16,128]{4,3,2,1,0:T(8,128)(2,1)S(1)} %get-tuple-element.74), channel_id=1, source_target_pairs={{0,4},{1,5},{8,12},{9,13},{2,6},{3,7},{10,14},{11,15},{4,0},{5,1},... | collective-permute-start | bytes 393224 | tf_op jit(solution)/shard_map/ppermute | solution.py:314
  77.7 20.7 %collective-permute-start.30 = (bf16[2,2,8,16,128]{4,3,2,1,0:T(8,128)(2,1)S(1)}, bf16[2,2,8,16,128]{4,3,2,1,0:T(8,128)(2,1)S(1)}, u32[]{:S(2)}, u32[]{:S(2)}) collective-permute-start(bf16[2,2,8,16,128]{4,3,2,1,0:T(8,128)(2,1)S(1)} %get-tuple-element.75), channel_id=1, source_target_pairs={{0,10},{1,11},{8,4},{9,5},{2,12},{3,13},{10,6},{11,7},{4,14},{5,15... | collective-permute-start | bytes 393224 | tf_op jit(solution)/shard_map/ppermute | solution.py:314
  78.4 21.8 %collective-permute-start.31 = (bf16[2,2,8,16,128]{4,3,2,1,0:T(8,128)(2,1)S(1)}, bf16[2,2,8,16,128]{4,3,2,1,0:T(8,128)(2,1)S(1)}, u32[]{:S(2)}, u32[]{:S(2)}) collective-permute-start(bf16[2,2,8,16,128]{4,3,2,1,0:T(8,128)(2,1)S(1)} %get-tuple-element.76), channel_id=1, source_target_pairs={{0,12},{1,13},{8,6},{9,7},{2,14},{3,15},{10,0},{11,1},{4,8},{5,9},... | collective-permute-start | bytes 393224 | tf_op jit(solution)/shard_map/ppermute | solution.py:314
  98.4 24.2 %collective-permute-start.16 = (bf16[2,4,14,16,128]{4,3,2,1,0:T(8,128)(2,1)S(1)}, bf16[2,4,14,16,128]{4,3,2,1,0:T(8,128)(2,1)S(1)}, u32[]{:S(2)}, u32[]{:S(2)}) collective-permute-start(bf16[2,4,14,16,128]{4,3,2,1,0:T(8,128)(2,1)S(1)} %get-tuple-element.61), channel_id=1, source_target_pairs={{0,17},{1,16},{8,25},{9,24},{2,19},{3,18},{10,27},{11,26},{4,21},{... | collective-permute-start | bytes 1376264 | tf_op jit(solution)/shard_map/ppermute | solution.py:314
  100.2 22.4 %collective-permute-start.14 = (bf16[2,4,14,16,128]{4,3,2,1,0:T(8,128)(2,1)S(1)}, bf16[2,4,14,16,128]{4,3,2,1,0:T(8,128)(2,1)S(1)}, u32[]{:S(2)}, u32[]{:S(2)}) collective-permute-start(bf16[2,4,14,16,128]{4,3,2,1,0:T(8,128)(2,1)S(1)} %get-tuple-element.61), channel_id=1, source_target_pairs={{0,1},{1,0},{8,9},{9,8},{2,3},{3,2},{10,11},{11,10},{4,5},{5,4},{1... | collective-permute-start | bytes 1376264 | tf_op jit(solution)/shard_map/ppermute | solution.py:314
  102.4 43.3 %collective-permute-start.34 = (bf16[2,8,128,128]{3,2,1,0:T(8,128)(2,1)S(1)}, bf16[2,8,128,128]{3,2,1,0:T(8,128)(2,1)S(1)}, u32[]{:S(2)}, u32[]{:S(2)}) collective-permute-start(bf16[2,8,128,128]{3,2,1,0:T(8,128)(2,1)S(1)} %turn.4.refs_8_), channel_id=1, source_target_pairs={{0,1},{1,0},{8,9},{9,8},{2,3},{3,2},{10,11},{11,10},{4,5},{5,4},{1... | collective-permute-start | bytes 1572872 | tf_op jit(solution)/shard_map/ppermute | solution.py:314
  127.0 17.5 %collective-permute-start.20 = (bf16[2,2,8,16,128]{4,3,2,1,0:T(8,128)(2,1)S(1)}, bf16[2,2,8,16,128]{4,3,2,1,0:T(8,128)(2,1)S(1)}, u32[]{:S(2)}, u32[]{:S(2)}) collective-permute-start(bf16[2,2,8,16,128]{4,3,2,1,0:T(8,128)(2,1)S(1)} %get-tuple-element.65), channel_id=1, source_target_pairs={{0,8},{1,9},{8,2},{9,3},{2,10},{3,11},{10,4},{11,5},{4,12},{5,13},... | collective-permute-start | bytes 393224 | tf_op jit(solution)/shard_map/ppermute | solution.py:314
  127.1 17.4 %collective-permute-start.21 = (bf16[2,2,8,16,128]{4,3,2,1,0:T(8,128)(2,1)S(1)}, bf16[2,2,8,16,128]{4,3,2,1,0:T(8,128)(2,1)S(1)}, u32[]{:S(2)}, u32[]{:S(2)}) collective-permute-start(bf16[2,2,8,16,128]{4,3,2,1,0:T(8,128)(2,1)S(1)} %get-tuple-element.66), channel_id=1, source_target_pairs={{0,14},{1,15},{8,0},{9,1},{2,8},{3,9},{10,2},{11,3},{4,10},{5,11},... | collective-permute-start | bytes 393224 | tf_op jit(solution)/shard_map/ppermute | solution.py:314
  129.7 21.2 %collective-permute-start.22 = (bf16[2,2,8,16,128]{4,3,2,1,0:T(8,128)(2,1)S(1)}, bf16[2,2,8,16,128]{4,3,2,1,0:T(8,128)(2,1)S(1)}, u32[]{:S(2)}, u32[]{:S(2)}) collective-permute-start(bf16[2,2,8,16,128]{4,3,2,1,0:T(8,128)(2,1)S(1)} %get-tuple-element.67), channel_id=1, source_target_pairs={{0,4},{1,5},{8,12},{9,13},{2,6},{3,7},{10,14},{11,15},{4,0},{5,1},... | collective-permute-start | bytes 393224 | tf_op jit(solution)/shard_map/ppermute | solution.py:314
  131.5 19.4 %collective-permute-start.23 = (bf16[2,2,8,16,128]{4,3,2,1,0:T(8,128)(2,1)S(1)}, bf16[2,2,8,16,128]{4,3,2,1,0:T(8,128)(2,1)S(1)}, u32[]{:S(2)}, u32[]{:S(2)}) collective-permute-start(bf16[2,2,8,16,128]{4,3,2,1,0:T(8,128)(2,1)S(1)} %get-tuple-element.68), channel_id=1, source_target_pairs={{0,10},{1,11},{8,4},{9,5},{2,12},{3,13},{10,6},{11,7},{4,14},{5,15... | collective-permute-start | bytes 393224 | tf_op jit(solution)/shard_map/ppermute | solution.py:314
  (13 other events, 124.3 us)

commit v11 on v10

--- a/solution.py
+++ b/solution.py
@@ -21,6 +21,7 @@
 FC = 32 // CHUNKS
 CBINS = BINS // CHUNKS
 ORDER = (0, 1, 7, 4, 3, 5, 2, 6)
+FAR = (0, 4, 3, 5, 2, 6, 1, 7)
 F32 = jnp.float32
 BF16 = jnp.bfloat16
 
@@ -192,7 +193,7 @@
     )(pos, own0, own1, prev0, prev1, *after)
 
 
-def turn_kernel(pos_ref, *refs):
+def turn_kernel(order, pos_ref, *refs):
     ins, (out, buf) = refs[:8], refs[-2:]
     z = pos_ref[0]
 
@@ -200,17 +201,17 @@
     def _(rnd):
         for i in range(8):
             slot = i & 1
-            for n, r in enumerate(ORDER):
+            for n, r in enumerate(order):
                 start = pl.multiple_of(((z - r) & 7) * FC, FC)
                 buf[slot, pl.ds(start, FC), :] = ins[n][0, rnd, i].astype(F32)
             out[rnd, i] = buf[slot].T.astype(BF16)
 
 
-def turn(crel, pieces, pos, *after):
+def turn(order, crel, pieces, pos, *after):
     half = pl.BlockSpec((1, 2, 8, FC, 128), lambda n: (crel, 0, 0, 0, 0))
     whole = pl.BlockSpec((2, 8, 128, 8 * FC), lambda n: (0, 0, 0, 0))
     return pl.pallas_call(
-        turn_kernel,
+        functools.partial(turn_kernel, order),
         out_shape=jax.ShapeDtypeStruct((2, 8, 128, 8 * FC), BF16),
         grid=(1,),
         in_specs=[SM] + [half] * 8 + [ANY] * len(after),
@@ -314,9 +315,9 @@
     return lax.ppermute(value, ALL, [(device(*d), device(*target(*d))) for d in EVERY])
 
 
-def round_ring(pieces):
+def round_ring(pieces, order=ORDER):
     got = []
-    for r in ORDER:
+    for r in order:
         got.append(send(pieces[r], lambda m, z, c: (m, z + r, c)) if r else pieces[r])
     return got
 
@@ -343,10 +344,11 @@
         own1 = other_core(other)
         out = cross(same, own1, prev0, prev1, pos, *crossed)
         crossed = (out[0],)
-        got = round_ring(out)
-        other = turn(1, got, pos, *sums)
+        order = ORDER if k == 0 else FAR
+        got = round_ring(out, order)
+        other = turn(order, 1, got, pos, *sums)
         received = other_core(other)
-        same = turn(0, got, pos, other)
+        same = turn(order, 0, got, pos, other)
         sums = (invert(k, [same, received], table, sums, scaling),)
     return sums[0]
 

time: 165 us -> 162 us (0.982)
  waiting for transfers between devices: 73.5 us -> 69.3 us
    ppermute x36, waiting for transfers between devices: 73.5 us -> 69.3 us  [send(): lax.ppermute(value, ALL, [(device(*d), device(*target(*d))) for d in EVERY])]
where the time goes in v11:
time: 162 us
  waiting for transfers between devices  69.3 us (43%)
  starting transfers between devices  61.3 us (38%)
  Pallas kernels  26 us (16%)
  other arithmetic  2.92 us (2%)
  local copies, waits for them, and re-layouts  1.9 us (1%)
    ppermute x36, waiting for transfers between devices, send(): lax.ppermute(value, ALL, [(device(*d), device(*target(*d))) for d in EVERY])  69.3 us
    ppermute x36, starting transfers between devices, send(): lax.ppermute(value, ALL, [(device(*d), device(*target(*d))) for d in EVERY])  61.3 us
    pallas_call x2, Pallas kernels, cross(): pl.pallas_call(cross_kernel, out_shape=[shape] * 8, in_specs=[SM] + [VM]...  8.81 us
    pallas_call x1, Pallas kernels, whiten(): pl.pallas_call(whiten_kernel, out_shape=[shape] * (8 * CHUNKS) + [jax.Sha...  5.71 us
    pallas_call x2, Pallas kernels, invert(): pl.pallas_call(functools.partial(invert_kernel, scaling, chunk), out_shap...  4.88 us
    pallas_call x4, Pallas kernels, turn(): pl.pallas_call(functools.partial(turn_kernel, order), out_shape=jax.Shape...  3.93 us
  transfers between devices with their start and end apart: 36, of which 13 were waited for; matrix products, arithmetic and copies ran while one was open for 2% of the time, Pallas kernels for 10%

profile of v11, /device:TPU:5, one launch (start us, length us, event | category | flops | bytes accessed | tf_op | source)
XLA Modules:
  0.0 161.6 jit_solution(4449444079162668949)
XLA Ops:
  2.0 5.7 %whiten.1 = (bf16[2,14,16,128]{3,2,1,0:T(8,128)(2,1)S(1)}, bf16[2,14,16,128]{3,2,1,0:T(8,128)(2,1)S(1)}, bf16[2,14,16,128]{3,2,1,0:T(8,128)(2,1)S(1)}, bf16[2,14...) custom-call(s32[2]{0:T(128)S(1)} %pad_add_fusion.pos_ref, ...), custom_call_target="tpu_custom_call" | custom-call | flops 1409286144 | bytes 4194304 | tf_op jit(solution)/shard_map/whiten/pallas_call | solution.py:86
  9.4 4.0 %collective-permute-start.8 = (bf16[2,14,16,128]{3,2,1,0:T(8,128)(2,1)S(1)}, bf16[2,14,16,128]{3,2,1,0:T(8,128)(2,1)S(1)}, u32[]{:S(2)}, u32[]{:S(2)}) collective-permute-start(bf16[2,14,16,128]{3,2,1,0:T(8,128)(2,1)S(1)} %get-tuple-element.52), channel_id=1, source_target_pairs={{0,14},{1,15},{8,0},{9,1},{2,8},{3,9},{10,2},{11,3},{4,10},{5,11},... | collective-permute-start | bytes 344072 | tf_op jit(solution)/shard_map/ppermute | solution.py:315
  13.5 3.9 %collective-permute-start.9 = (bf16[2,14,16,128]{3,2,1,0:T(8,128)(2,1)S(1)}, bf16[2,14,16,128]{3,2,1,0:T(8,128)(2,1)S(1)}, u32[]{:S(2)}, u32[]{:S(2)}) collective-permute-start(bf16[2,14,16,128]{3,2,1,0:T(8,128)(2,1)S(1)} %get-tuple-element.53), channel_id=1, source_target_pairs={{0,4},{1,5},{8,12},{9,13},{2,6},{3,7},{10,14},{11,15},{4,0},{5,1},... | collective-permute-start | bytes 344072 | tf_op jit(solution)/shard_map/ppermute | solution.py:315
  17.8 4.0 %collective-permute-start.11 = (bf16[2,14,16,128]{3,2,1,0:T(8,128)(2,1)S(1)}, bf16[2,14,16,128]{3,2,1,0:T(8,128)(2,1)S(1)}, u32[]{:S(2)}, u32[]{:S(2)}) collective-permute-start(bf16[2,14,16,128]{3,2,1,0:T(8,128)(2,1)S(1)} %get-tuple-element.55), channel_id=1, source_target_pairs={{0,12},{1,13},{8,6},{9,7},{2,14},{3,15},{10,0},{11,1},{4,8},{5,9},... | collective-permute-start | bytes 344072 | tf_op jit(solution)/shard_map/ppermute | solution.py:315
  21.9 3.6 %collective-permute-start.13 = (bf16[2,14,16,128]{3,2,1,0:T(8,128)(2,1)S(1)}, bf16[2,14,16,128]{3,2,1,0:T(8,128)(2,1)S(1)}, u32[]{:S(2)}, u32[]{:S(2)}) collective-permute-start(bf16[2,14,16,128]{3,2,1,0:T(8,128)(2,1)S(1)} %get-tuple-element.57), channel_id=1, source_target_pairs={{0,6},{1,7},{8,14},{9,15},{2,0},{3,1},{10,8},{11,9},{4,2},{5,3},{1... | collective-permute-start | bytes 344072 | tf_op jit(solution)/shard_map/ppermute | solution.py:315
  25.4 5.4 %collective-permute-done.10.refs_4_ = bf16[2,14,16,128]{3,2,1,0:T(8,128)(2,1)S(1)} collective-permute-done((bf16[2,14,16,128]{3,2,1,0:T(8,128)(2,1)S(1)}, bf16[2,14,16,128]{3,2,1,0:T(8,128)(2,1)S(1)}, u32[]{:S(2)}, u32[]{:S(2)}) %collective-permute-start.10) | collective-permute-done | bytes 114720 | tf_op jit(solution)/shard_map/ppermute | solution.py:315
  31.4 3.9 %collective-permute-done.13.refs_7_ = bf16[2,14,16,128]{3,2,1,0:T(8,128)(2,1)S(1)} collective-permute-done((bf16[2,14,16,128]{3,2,1,0:T(8,128)(2,1)S(1)}, bf16[2,14,16,128]{3,2,1,0:T(8,128)(2,1)S(1)}, u32[]{:S(2)}, u32[]{:S(2)}) %collective-permute-start.13) | collective-permute-done | bytes 114720 | tf_op jit(solution)/shard_map/ppermute | solution.py:315
  42.2 8.7 %collective-permute-done.19.prev1 = bf16[2,4,14,16,128]{4,3,2,1,0:T(8,128)(2,1)S(1)} collective-permute-done((bf16[2,4,14,16,128]{4,3,2,1,0:T(8,128)(2,1)S(1)}, bf16[2,4,14,16,128]{4,3,2,1,0:T(8,128)(2,1)S(1)}, u32[]{:S(2)}, u32[]{:S(2)}) %collective-permute-start.19) | collective-permute-done | bytes 458784 | tf_op jit(solution)/shard_map/ppermute | solution.py:315
  50.9 3.4 %collective-permute-start.2 = (bf16[2,14,16,128]{3,2,1,0:T(8,128)(2,1)S(1)}, bf16[2,14,16,128]{3,2,1,0:T(8,128)(2,1)S(1)}, u32[]{:S(2)}, u32[]{:S(2)}) collective-permute-start(bf16[2,14,16,128]{3,2,1,0:T(8,128)(2,1)S(1)} %get-tuple-element.45), channel_id=1, source_target_pairs={{0,4},{1,5},{8,12},{9,13},{2,6},{3,7},{10,14},{11,15},{4,0},{5,1},... | collective-permute-start | bytes 344072 | tf_op jit(solution)/shard_map/ppermute | solution.py:315
  55.1 5.7 %collective-permute-done.18.prev0 = bf16[2,4,14,16,128]{4,3,2,1,0:T(8,128)(2,1)S(1)} collective-permute-done((bf16[2,4,14,16,128]{4,3,2,1,0:T(8,128)(2,1)S(1)}, bf16[2,4,14,16,128]{4,3,2,1,0:T(8,128)(2,1)S(1)}, u32[]{:S(2)}, u32[]{:S(2)}) %collective-permute-start.18) | collective-permute-done | bytes 458784 | tf_op jit(solution)/shard_map/ppermute | solution.py:315
  60.8 3.1 %collective-permute-start.4 = (bf16[2,14,16,128]{3,2,1,0:T(8,128)(2,1)S(1)}, bf16[2,14,16,128]{3,2,1,0:T(8,128)(2,1)S(1)}, u32[]{:S(2)}, u32[]{:S(2)}) collective-permute-start(bf16[2,14,16,128]{3,2,1,0:T(8,128)(2,1)S(1)} %get-tuple-element.47), channel_id=1, source_target_pairs={{0,12},{1,13},{8,6},{9,7},{2,14},{3,15},{10,0},{11,1},{4,8},{5,9},... | collective-permute-start | bytes 344072 | tf_op jit(solution)/shard_map/ppermute | solution.py:315
  63.9 4.4 %cross.2 = (bf16[2,2,8,16,128]{4,3,2,1,0:T(8,128)(2,1)S(1)}, bf16[2,2,8,16,128]{4,3,2,1,0:T(8,128)(2,1)S(1)}, bf16[2,2,8,16,128]{4,3,2,1,0:T(8,128)(2,1)S(1)}, b...) custom-call(s32[2]{0:T(128)S(1)} %pad_add_fusion.pos_ref, ...), custom_call_target="tpu_custom_call" | custom-call | flops 536870912 | bytes 3145728 | tf_op jit(solution)/shard_map/cross/pallas_call | solution.py:179
  69.1 2.9 %collective-permute-start.6 = (bf16[2,14,16,128]{3,2,1,0:T(8,128)(2,1)S(1)}, bf16[2,14,16,128]{3,2,1,0:T(8,128)(2,1)S(1)}, u32[]{:S(2)}, u32[]{:S(2)}) collective-permute-start(bf16[2,14,16,128]{3,2,1,0:T(8,128)(2,1)S(1)} %get-tuple-element.49), channel_id=1, source_target_pairs={{0,6},{1,7},{8,14},{9,15},{2,0},{3,1},{10,8},{11,9},{4,2},{5,3},{1... | collective-permute-start | bytes 344072 | tf_op jit(solution)/shard_map/ppermute | solution.py:315
  78.4 3.8 %collective-permute-start.31 = (bf16[2,2,8,16,128]{4,3,2,1,0:T(8,128)(2,1)S(1)}, bf16[2,2,8,16,128]{4,3,2,1,0:T(8,128)(2,1)S(1)}, u32[]{:S(2)}, u32[]{:S(2)}) collective-permute-start(bf16[2,2,8,16,128]{4,3,2,1,0:T(8,128)(2,1)S(1)} %get-tuple-element.76), channel_id=1, source_target_pairs={{0,12},{1,13},{8,6},{9,7},{2,14},{3,15},{10,0},{11,1},{4,8},{5,9},... | collective-permute-start | bytes 393224 | tf_op jit(solution)/shard_map/ppermute | solution.py:315
  82.2 8.3 %collective-permute-done.27.refs_1_ = bf16[2,2,8,16,128]{4,3,2,1,0:T(8,128)(2,1)S(1)} collective-permute-done((bf16[2,2,8,16,128]{4,3,2,1,0:T(8,128)(2,1)S(1)}, bf16[2,2,8,16,128]{4,3,2,1,0:T(8,128)(2,1)S(1)}, u32[]{:S(2)}, u32[]{:S(2)}) %collective-permute-start.27) | collective-permute-done | bytes 131104 | tf_op jit(solution)/shard_map/ppermute | solution.py:315
  90.5 3.6 %collective-permute-start.33 = (bf16[2,2,8,16,128]{4,3,2,1,0:T(8,128)(2,1)S(1)}, bf16[2,2,8,16,128]{4,3,2,1,0:T(8,128)(2,1)S(1)}, u32[]{:S(2)}, u32[]{:S(2)}) collective-permute-start(bf16[2,2,8,16,128]{4,3,2,1,0:T(8,128)(2,1)S(1)} %get-tuple-element.78), channel_id=1, source_target_pairs={{0,6},{1,7},{8,14},{9,15},{2,0},{3,1},{10,8},{11,9},{4,2},{5,3},{1... | collective-permute-start | bytes 393224 | tf_op jit(solution)/shard_map/ppermute | solution.py:315
  103.0 8.3 %collective-permute-done.15.prev0 = bf16[2,4,14,16,128]{4,3,2,1,0:T(8,128)(2,1)S(1)} collective-permute-done((bf16[2,4,14,16,128]{4,3,2,1,0:T(8,128)(2,1)S(1)}, bf16[2,4,14,16,128]{4,3,2,1,0:T(8,128)(2,1)S(1)}, u32[]{:S(2)}, u32[]{:S(2)}) %collective-permute-start.15) | collective-permute-done | bytes 458784 | tf_op jit(solution)/shard_map/ppermute | solution.py:315
  111.3 11.3 %collective-permute-done.16.prev1 = bf16[2,4,14,16,128]{4,3,2,1,0:T(8,128)(2,1)S(1)} collective-permute-done((bf16[2,4,14,16,128]{4,3,2,1,0:T(8,128)(2,1)S(1)}, bf16[2,4,14,16,128]{4,3,2,1,0:T(8,128)(2,1)S(1)}, u32[]{:S(2)}, u32[]{:S(2)}) %collective-permute-start.16) | collective-permute-done | bytes 458784 | tf_op jit(solution)/shard_map/ppermute | solution.py:315
  122.6 4.4 %cross.3 = (bf16[2,2,8,16,128]{4,3,2,1,0:T(8,128)(2,1)S(1)}, bf16[2,2,8,16,128]{4,3,2,1,0:T(8,128)(2,1)S(1)}, bf16[2,2,8,16,128]{4,3,2,1,0:T(8,128)(2,1)S(1)}, b...) custom-call(s32[2]{0:T(128)S(1)} %pad_add_fusion.pos_ref, ...), custom_call_target="tpu_custom_call" | custom-call | flops 536870912 | bytes 3145728 | tf_op jit(solution)/shard_map/cross/pallas_call | solution.py:179
  128.9 4.5 %collective-permute-start.22 = (bf16[2,2,8,16,128]{4,3,2,1,0:T(8,128)(2,1)S(1)}, bf16[2,2,8,16,128]{4,3,2,1,0:T(8,128)(2,1)S(1)}, u32[]{:S(2)}, u32[]{:S(2)}) collective-permute-start(bf16[2,2,8,16,128]{4,3,2,1,0:T(8,128)(2,1)S(1)} %get-tuple-element.67), channel_id=1, source_target_pairs={{0,12},{1,13},{8,6},{9,7},{2,14},{3,15},{10,0},{11,1},{4,8},{5,9},... | collective-permute-start | bytes 393224 | tf_op jit(solution)/shard_map/ppermute | solution.py:315
  133.6 6.8 %collective-permute-done.20.refs_1_ = bf16[2,2,8,16,128]{4,3,2,1,0:T(8,128)(2,1)S(1)} collective-permute-done((bf16[2,2,8,16,128]{4,3,2,1,0:T(8,128)(2,1)S(1)}, bf16[2,2,8,16,128]{4,3,2,1,0:T(8,128)(2,1)S(1)}, u32[]{:S(2)}, u32[]{:S(2)}) %collective-permute-start.20) | collective-permute-done | bytes 131104 | tf_op jit(solution)/shard_map/ppermute | solution.py:315
  140.4 8.4 %collective-permute-done.21.refs_2_ = bf16[2,2,8,16,128]{4,3,2,1,0:T(8,128)(2,1)S(1)} collective-permute-done((bf16[2,2,8,16,128]{4,3,2,1,0:T(8,128)(2,1)S(1)}, bf16[2,2,8,16,128]{4,3,2,1,0:T(8,128)(2,1)S(1)}, u32[]{:S(2)}, u32[]{:S(2)}) %collective-permute-start.21) | collective-permute-done | bytes 131104 | tf_op jit(solution)/shard_map/ppermute | solution.py:315
  148.8 2.7 %collective-permute-start.26 = (bf16[2,2,8,16,128]{4,3,2,1,0:T(8,128)(2,1)S(1)}, bf16[2,2,8,16,128]{4,3,2,1,0:T(8,128)(2,1)S(1)}, u32[]{:S(2)}, u32[]{:S(2)}) collective-permute-start(bf16[2,2,8,16,128]{4,3,2,1,0:T(8,128)(2,1)S(1)} %get-tuple-element.71), channel_id=1, source_target_pairs={{0,14},{1,15},{8,0},{9,1},{2,8},{3,9},{10,2},{11,3},{4,10},{5,11},... | collective-permute-start | bytes 393224 | tf_op jit(solution)/shard_map/ppermute | solution.py:315
  158.6 3.0 %invert.3 = bf16[2,8,64,1024]{3,2,1,0:T(8,128)(2,1)} custom-call(bf16[2,8,128,128]{3,2,1,0:T(8,128)(2,1)S(1)} %turn.7.refs_0_, bf16[2,8,128,128]{3,2,1,0:T(8,128)(2,1)S(1)} %collective-permute-done.35.refs_1_, bf16[2,512,1024]{2,1,0:T(8,128)(2,1)S(1)} %bitcast.8, f32[2,8,64,1024]{3,2,1,0:T(8,128)S(1)} %invert.2.refs_8_.refs_3_), custom_call_target="tpu_custom_call" | custom-call | flops 1073741824 | bytes 6291456 | tf_op jit(solution)/shard_map/invert/pallas_call | solution.py:249
  (68 shorter events, 37.8 us)
Async XLA Ops:
  7.7 14.1 %collective-permute-start.7 = (bf16[2,14,16,128]{3,2,1,0:T(8,128)(2,1)S(1)}, bf16[2,14,16,128]{3,2,1,0:T(8,128)(2,1)S(1)}, u32[]{:S(2)}, u32[]{:S(2)}) collective-permute-start(bf16[2,14,16,128]{3,2,1,0:T(8,128)(2,1)S(1)} %get-tuple-element.51), channel_id=1, source_target_pairs={{0,8},{1,9},{8,2},{9,3},{2,10},{3,11},{10,4},{11,5},{4,12},{5,13},... | collective-permute-start | bytes 344072 | tf_op jit(solution)/shard_map/ppermute | solution.py:315
  17.4 13.5 %collective-permute-start.10 = (bf16[2,14,16,128]{3,2,1,0:T(8,128)(2,1)S(1)}, bf16[2,14,16,128]{3,2,1,0:T(8,128)(2,1)S(1)}, u32[]{:S(2)}, u32[]{:S(2)}) collective-permute-start(bf16[2,14,16,128]{3,2,1,0:T(8,128)(2,1)S(1)} %get-tuple-element.54), channel_id=1, source_target_pairs={{0,10},{1,11},{8,4},{9,5},{2,12},{3,13},{10,6},{11,7},{4,14},{5,15... | collective-permute-start | bytes 344072 | tf_op jit(solution)/shard_map/ppermute | solution.py:315
  21.9 13.4 %collective-permute-start.13 = (bf16[2,14,16,128]{3,2,1,0:T(8,128)(2,1)S(1)}, bf16[2,14,16,128]{3,2,1,0:T(8,128)(2,1)S(1)}, u32[]{:S(2)}, u32[]{:S(2)}) collective-permute-start(bf16[2,14,16,128]{3,2,1,0:T(8,128)(2,1)S(1)} %get-tuple-element.57), channel_id=1, source_target_pairs={{0,6},{1,7},{8,14},{9,15},{2,0},{3,1},{10,8},{11,9},{4,2},{5,3},{1... | collective-permute-start | bytes 344072 | tf_op jit(solution)/shard_map/ppermute | solution.py:315
  35.9 15.0 %collective-permute-start.19 = (bf16[2,4,14,16,128]{4,3,2,1,0:T(8,128)(2,1)S(1)}, bf16[2,4,14,16,128]{4,3,2,1,0:T(8,128)(2,1)S(1)}, u32[]{:S(2)}, u32[]{:S(2)}) collective-permute-start(bf16[2,4,14,16,128]{4,3,2,1,0:T(8,128)(2,1)S(1)} %get-tuple-element.62), channel_id=1, source_target_pairs={{0,17},{1,16},{8,25},{9,24},{2,19},{3,18},{10,27},{11,26},{4,21},{... | collective-permute-start | bytes 1376264 | tf_op jit(solution)/shard_map/ppermute | solution.py:315
  38.2 16.0 %collective-permute-start.17 = (bf16[2,4,14,16,128]{4,3,2,1,0:T(8,128)(2,1)S(1)}, bf16[2,4,14,16,128]{4,3,2,1,0:T(8,128)(2,1)S(1)}, u32[]{:S(2)}, u32[]{:S(2)}) collective-permute-start(bf16[2,4,14,16,128]{4,3,2,1,0:T(8,128)(2,1)S(1)} %get-tuple-element.62), channel_id=1, source_target_pairs={{0,1},{1,0},{8,9},{9,8},{2,3},{3,2},{10,11},{11,10},{4,5},{5,4},{1... | collective-permute-start | bytes 1376264 | tf_op jit(solution)/shard_map/ppermute | solution.py:315
  38.2 22.5 %collective-permute-start.18 = (bf16[2,4,14,16,128]{4,3,2,1,0:T(8,128)(2,1)S(1)}, bf16[2,4,14,16,128]{4,3,2,1,0:T(8,128)(2,1)S(1)}, u32[]{:S(2)}, u32[]{:S(2)}) collective-permute-start(bf16[2,4,14,16,128]{4,3,2,1,0:T(8,128)(2,1)S(1)} %get-tuple-element.58.refs_8_.own0), channel_id=1, source_target_pairs={{0,16},{1,17},{8,24},{9,25},{2,18},{3,19},{10,26},{11,27},{4,20},{... | collective-permute-start | bytes 1376264 | tf_op jit(solution)/shard_map/ppermute | solution.py:315
  39.5 28.8 %collective-permute-start = (bf16[2,14,16,128]{3,2,1,0:T(8,128)(2,1)S(1)}, bf16[2,14,16,128]{3,2,1,0:T(8,128)(2,1)S(1)}, u32[]{:S(2)}, u32[]{:S(2)}) collective-permute-start(bf16[2,14,16,128]{3,2,1,0:T(8,128)(2,1)S(1)} %get-tuple-element.43), channel_id=1, source_target_pairs={{0,8},{1,9},{8,2},{9,3},{2,10},{3,11},{10,4},{11,5},{4,12},{5,13},... | collective-permute-start | bytes 344072 | tf_op jit(solution)/shard_map/ppermute | solution.py:315
  40.4 28.6 %collective-permute-start.1 = (bf16[2,14,16,128]{3,2,1,0:T(8,128)(2,1)S(1)}, bf16[2,14,16,128]{3,2,1,0:T(8,128)(2,1)S(1)}, u32[]{:S(2)}, u32[]{:S(2)}) collective-permute-start(bf16[2,14,16,128]{3,2,1,0:T(8,128)(2,1)S(1)} %get-tuple-element.44), channel_id=1, source_target_pairs={{0,14},{1,15},{8,0},{9,1},{2,8},{3,9},{10,2},{11,3},{4,10},{5,11},... | collective-permute-start | bytes 344072 | tf_op jit(solution)/shard_map/ppermute | solution.py:315
  50.9 21.1 %collective-permute-start.2 = (bf16[2,14,16,128]{3,2,1,0:T(8,128)(2,1)S(1)}, bf16[2,14,16,128]{3,2,1,0:T(8,128)(2,1)S(1)}, u32[]{:S(2)}, u32[]{:S(2)}) collective-permute-start(bf16[2,14,16,128]{3,2,1,0:T(8,128)(2,1)S(1)} %get-tuple-element.45), channel_id=1, source_target_pairs={{0,4},{1,5},{8,12},{9,13},{2,6},{3,7},{10,14},{11,15},{4,0},{5,1},... | collective-permute-start | bytes 344072 | tf_op jit(solution)/shard_map/ppermute | solution.py:315
  54.3 19.4 %collective-permute-start.3 = (bf16[2,14,16,128]{3,2,1,0:T(8,128)(2,1)S(1)}, bf16[2,14,16,128]{3,2,1,0:T(8,128)(2,1)S(1)}, u32[]{:S(2)}, u32[]{:S(2)}) collective-permute-start(bf16[2,14,16,128]{3,2,1,0:T(8,128)(2,1)S(1)} %get-tuple-element.46), channel_id=1, source_target_pairs={{0,10},{1,11},{8,4},{9,5},{2,12},{3,13},{10,6},{11,7},{4,14},{5,15... | collective-permute-start | bytes 344072 | tf_op jit(solution)/shard_map/ppermute | solution.py:315
  60.8 14.5 %collective-permute-start.4 = (bf16[2,14,16,128]{3,2,1,0:T(8,128)(2,1)S(1)}, bf16[2,14,16,128]{3,2,1,0:T(8,128)(2,1)S(1)}, u32[]{:S(2)}, u32[]{:S(2)}) collective-permute-start(bf16[2,14,16,128]{3,2,1,0:T(8,128)(2,1)S(1)} %get-tuple-element.47), channel_id=1, source_target_pairs={{0,12},{1,13},{8,6},{9,7},{2,14},{3,15},{10,0},{11,1},{4,8},{5,9},... | collective-permute-start | bytes 344072 | tf_op jit(solution)/shard_map/ppermute | solution.py:315
  71.9 18.5 %collective-permute-start.27 = (bf16[2,2,8,16,128]{4,3,2,1,0:T(8,128)(2,1)S(1)}, bf16[2,2,8,16,128]{4,3,2,1,0:T(8,128)(2,1)S(1)}, u32[]{:S(2)}, u32[]{:S(2)}) collective-permute-start(bf16[2,2,8,16,128]{4,3,2,1,0:T(8,128)(2,1)S(1)} %get-tuple-element.72), channel_id=1, source_target_pairs={{0,8},{1,9},{8,2},{9,3},{2,10},{3,11},{10,4},{11,5},{4,12},{5,13},... | collective-permute-start | bytes 393224 | tf_op jit(solution)/shard_map/ppermute | solution.py:315
  73.6 16.9 %collective-permute-start.28 = (bf16[2,2,8,16,128]{4,3,2,1,0:T(8,128)(2,1)S(1)}, bf16[2,2,8,16,128]{4,3,2,1,0:T(8,128)(2,1)S(1)}, u32[]{:S(2)}, u32[]{:S(2)}) collective-permute-start(bf16[2,2,8,16,128]{4,3,2,1,0:T(8,128)(2,1)S(1)} %get-tuple-element.73), channel_id=1, source_target_pairs={{0,14},{1,15},{8,0},{9,1},{2,8},{3,9},{10,2},{11,3},{4,10},{5,11},... | collective-permute-start | bytes 393224 | tf_op jit(solution)/shard_map/ppermute | solution.py:315
  75.3 23.0 %collective-permute-start.29 = (bf16[2,2,8,16,128]{4,3,2,1,0:T(8,128)(2,1)S(1)}, bf16[2,2,8,16,128]{4,3,2,1,0:T(8,128)(2,1)S(1)}, u32[]{:S(2)}, u32[]{:S(2)}) collective-permute-start(bf16[2,2,8,16,128]{4,3,2,1,0:T(8,128)(2,1)S(1)} %get-tuple-element.74), channel_id=1, source_target_pairs={{0,4},{1,5},{8,12},{9,13},{2,6},{3,7},{10,14},{11,15},{4,0},{5,1},... | collective-permute-start | bytes 393224 | tf_op jit(solution)/shard_map/ppermute | solution.py:315
  77.7 20.7 %collective-permute-start.30 = (bf16[2,2,8,16,128]{4,3,2,1,0:T(8,128)(2,1)S(1)}, bf16[2,2,8,16,128]{4,3,2,1,0:T(8,128)(2,1)S(1)}, u32[]{:S(2)}, u32[]{:S(2)}) collective-permute-start(bf16[2,2,8,16,128]{4,3,2,1,0:T(8,128)(2,1)S(1)} %get-tuple-element.75), channel_id=1, source_target_pairs={{0,10},{1,11},{8,4},{9,5},{2,12},{3,13},{10,6},{11,7},{4,14},{5,15... | collective-permute-start | bytes 393224 | tf_op jit(solution)/shard_map/ppermute | solution.py:315
  78.4 21.8 %collective-permute-start.31 = (bf16[2,2,8,16,128]{4,3,2,1,0:T(8,128)(2,1)S(1)}, bf16[2,2,8,16,128]{4,3,2,1,0:T(8,128)(2,1)S(1)}, u32[]{:S(2)}, u32[]{:S(2)}) collective-permute-start(bf16[2,2,8,16,128]{4,3,2,1,0:T(8,128)(2,1)S(1)} %get-tuple-element.76), channel_id=1, source_target_pairs={{0,12},{1,13},{8,6},{9,7},{2,14},{3,15},{10,0},{11,1},{4,8},{5,9},... | collective-permute-start | bytes 393224 | tf_op jit(solution)/shard_map/ppermute | solution.py:315
  98.4 24.2 %collective-permute-start.16 = (bf16[2,4,14,16,128]{4,3,2,1,0:T(8,128)(2,1)S(1)}, bf16[2,4,14,16,128]{4,3,2,1,0:T(8,128)(2,1)S(1)}, u32[]{:S(2)}, u32[]{:S(2)}) collective-permute-start(bf16[2,4,14,16,128]{4,3,2,1,0:T(8,128)(2,1)S(1)} %get-tuple-element.61), channel_id=1, source_target_pairs={{0,17},{1,16},{8,25},{9,24},{2,19},{3,18},{10,27},{11,26},{4,21},{... | collective-permute-start | bytes 1376264 | tf_op jit(solution)/shard_map/ppermute | solution.py:315
  100.2 22.4 %collective-permute-start.14 = (bf16[2,4,14,16,128]{4,3,2,1,0:T(8,128)(2,1)S(1)}, bf16[2,4,14,16,128]{4,3,2,1,0:T(8,128)(2,1)S(1)}, u32[]{:S(2)}, u32[]{:S(2)}) collective-permute-start(bf16[2,4,14,16,128]{4,3,2,1,0:T(8,128)(2,1)S(1)} %get-tuple-element.61), channel_id=1, source_target_pairs={{0,1},{1,0},{8,9},{9,8},{2,3},{3,2},{10,11},{11,10},{4,5},{5,4},{1... | collective-permute-start | bytes 1376264 | tf_op jit(solution)/shard_map/ppermute | solution.py:315
  102.4 46.4 %collective-permute-start.34 = (bf16[2,8,128,128]{3,2,1,0:T(8,128)(2,1)S(1)}, bf16[2,8,128,128]{3,2,1,0:T(8,128)(2,1)S(1)}, u32[]{:S(2)}, u32[]{:S(2)}) collective-permute-start(bf16[2,8,128,128]{3,2,1,0:T(8,128)(2,1)S(1)} %turn.4.refs_8_), channel_id=1, source_target_pairs={{0,1},{1,0},{8,9},{9,8},{2,3},{3,2},{10,11},{11,10},{4,5},{5,4},{1... | collective-permute-start | bytes 1572872 | tf_op jit(solution)/shard_map/ppermute | solution.py:315
  127.0 13.4 %collective-permute-start.20 = (bf16[2,2,8,16,128]{4,3,2,1,0:T(8,128)(2,1)S(1)}, bf16[2,2,8,16,128]{4,3,2,1,0:T(8,128)(2,1)S(1)}, u32[]{:S(2)}, u32[]{:S(2)}) collective-permute-start(bf16[2,2,8,16,128]{4,3,2,1,0:T(8,128)(2,1)S(1)} %get-tuple-element.65), channel_id=1, source_target_pairs={{0,4},{1,5},{8,12},{9,13},{2,6},{3,7},{10,14},{11,15},{4,0},{5,1},... | collective-permute-start | bytes 393224 | tf_op jit(solution)/shard_map/ppermute | solution.py:315
  128.8 20.0 %collective-permute-start.21 = (bf16[2,2,8,16,128]{4,3,2,1,0:T(8,128)(2,1)S(1)}, bf16[2,2,8,16,128]{4,3,2,1,0:T(8,128)(2,1)S(1)}, u32[]{:S(2)}, u32[]{:S(2)}) collective-permute-start(bf16[2,2,8,16,128]{4,3,2,1,0:T(8,128)(2,1)S(1)} %get-tuple-element.66), channel_id=1, source_target_pairs={{0,10},{1,11},{8,4},{9,5},{2,12},{3,13},{10,6},{11,7},{4,14},{5,15... | collective-permute-start | bytes 393224 | tf_op jit(solution)/shard_map/ppermute | solution.py:315
  128.9 25.5 %collective-permute-start.22 = (bf16[2,2,8,16,128]{4,3,2,1,0:T(8,128)(2,1)S(1)}, bf16[2,2,8,16,128]{4,3,2,1,0:T(8,128)(2,1)S(1)}, u32[]{:S(2)}, u32[]{:S(2)}) collective-permute-start(bf16[2,2,8,16,128]{4,3,2,1,0:T(8,128)(2,1)S(1)} %get-tuple-element.67), channel_id=1, source_target_pairs={{0,12},{1,13},{8,6},{9,7},{2,14},{3,15},{10,0},{11,1},{4,8},{5,9},... | collective-permute-start | bytes 393224 | tf_op jit(solution)/shard_map/ppermute | solution.py:315
  133.3 21.1 %collective-permute-start.23 = (bf16[2,2,8,16,128]{4,3,2,1,0:T(8,128)(2,1)S(1)}, bf16[2,2,8,16,128]{4,3,2,1,0:T(8,128)(2,1)S(1)}, u32[]{:S(2)}, u32[]{:S(2)}) collective-permute-start(bf16[2,2,8,16,128]{4,3,2,1,0:T(8,128)(2,1)S(1)} %get-tuple-element.68), channel_id=1, source_target_pairs={{0,2},{1,3},{8,10},{9,11},{2,4},{3,5},{10,12},{11,13},{4,6},{5,7},... | collective-permute-start | bytes 393224 | tf_op jit(solution)/shard_map/ppermute | solution.py:315
  140.4 14.0 %collective-permute-start.24 = (bf16[2,2,8,16,128]{4,3,2,1,0:T(8,128)(2,1)S(1)}, bf16[2,2,8,16,128]{4,3,2,1,0:T(8,128)(2,1)S(1)}, u32[]{:S(2)}, u32[]{:S(2)}) collective-permute-start(bf16[2,2,8,16,128]{4,3,2,1,0:T(8,128)(2,1)S(1)} %get-tuple-element.69), channel_id=1, source_target_pairs={{0,6},{1,7},{8,14},{9,15},{2,0},{3,1},{10,8},{11,9},{4,2},{5,3},{1... | collective-permute-start | bytes 393224 | tf_op jit(solution)/shard_map/ppermute | solution.py:315
  (13 other events, 115.9 us)
